TPU v7x, 32 devices: a whole 2x2x4 slice. The times are simulated.
32 devices in a mesh: dp: 8 (over y, x, core), tensor: 4 (over z).
Axes of the slice: x: 2, y: 2, z: 4, core: 2. Of those that a mesh axis runs over, the one named last changes fastest.
Arguments:
- images: bfloat16 [64, 257, 1664], P(('dp', 'tensor')), may hold values from -6 to 6
- first_gain: float32 [1664], replicated, may hold values from 0.5 to 1.5
- first_shift: float32 [1664], replicated, may hold values from -4 to 4
- qkv_weight: bfloat16 [3, 1664, 1664], P(None, None, 'tensor'), as said below
- qv_bias: float32 [2, 1664], P(None, 'tensor'), may hold values from -6 to 6
- out_weight: bfloat16 [1664, 1664], P('tensor'), may hold values from -0.625 to 0.625
- out_bias: float32 [1664], replicated, may hold values from -4 to 4
- second_gain: float32 [1664], replicated, may hold values from 0.5 to 1.5
- second_shift: float32 [1664], replicated, may hold values from -4 to 4
- up_weight: bfloat16 [1664, 8192], P(None, 'tensor'), may hold values from -0.15625 to 0.15625
- up_bias: float32 [8192], P('tensor'), may hold values from -6 to 6
- down_weight: bfloat16 [8192, 1664], P('tensor'), may hold values from -0.0625 to 0.0625
- down_bias: float32 [1664], replicated, may hold values from -4 to 4
- cotangent: bfloat16 [64, 257, 1664], P(('dp', 'tensor')), may hold values from -6 to 6
Outputs:
- result: bfloat16 [64, 257, 1664], P(('dp', 'tensor'))
- grad_images: bfloat16 [64, 257, 1664], P(('dp', 'tensor'))
- grad_first_gain: float32 [1664], replicated
- grad_first_shift: float32 [1664], replicated
- grad_qkv_weight: float32 [3, 1664, 1664], P(None, None, 'tensor')
- grad_qv_bias: float32 [2, 1664], P(None, 'tensor')
- grad_out_weight: float32 [1664, 1664], P('tensor')
- grad_out_bias: float32 [1664], replicated
- grad_second_gain: float32 [1664], replicated
- grad_second_shift: float32 [1664], replicated
- grad_up_weight: float32 [1664, 8192], P(None, 'tensor')
- grad_up_bias: float32 [8192], P('tensor')
- grad_down_weight: float32 [8192, 1664], P('tensor')
- grad_down_bias: float32 [1664], replicated
Inputs may be any that keep to these rules, and one draw needn't show every extreme that they name: `qkv_weight`: the three parts are query, keys and values, in this order.
All inputs are finite; a program needn't handle non-finite values.
Results may differ from a plain program's by a relative error of at most 0.02.
Values may be sent and summed in bfloat16 or wider, within the bound.
A program may use at most 256 MiB of HBM per device.

v0:
```python
import jax
import jax.numpy as jnp
from jax import lax
from jax.sharding import PartitionSpec as P

HD = 104


epsilon = 1e-06
inv_root_two = 0.7071067811865476
inv_root_tau = 0.3989422804014327


def normalize(rows):
    centre = jnp.mean(rows, axis=-1, keepdims=True)
    centred = rows - centre
    spread = jnp.mean(centred * centred, axis=-1, keepdims=True)
    inverse = lax.rsqrt(spread + epsilon)
    return (centred * inverse, inverse)


def norm_back(grad, unit, inverse, gain):
    scaled = grad * gain
    first = jnp.mean(scaled, axis=-1, keepdims=True)
    second = jnp.mean(scaled * unit, axis=-1, keepdims=True)
    return inverse * (scaled - first - unit * second)


def attend_block(query, keys, values):
    factor = query.shape[-1] ** (-0.5)
    scores = jnp.einsum("bshd,bthd->bhst", query, keys, preferred_element_type=jnp.float32) * factor
    top = jnp.max(scores, axis=-1, keepdims=True)
    raised = jnp.exp(scores - top)
    total = jnp.sum(raised, axis=-1, keepdims=True)
    weights = (raised / total).astype(jnp.bfloat16)
    mixed = jnp.einsum("bhst,bthd->bshd", weights, values, preferred_element_type=jnp.float32)
    return (mixed, (top + jnp.log(total))[..., 0])


def attend_back(query, keys, values, grad_out, log_total):
    factor = query.shape[-1] ** (-0.5)
    scores = jnp.einsum("bshd,bthd->bhst", query, keys, preferred_element_type=jnp.float32) * factor
    probs = jnp.exp(scores - log_total[..., None])
    grad_values = jnp.einsum(
        "bhst,bshd->bthd", probs.astype(jnp.bfloat16), grad_out, preferred_element_type=jnp.float32
    )
    grad_probs = jnp.einsum("bshd,bthd->bhst", grad_out, values, preferred_element_type=jnp.float32)
    inner = jnp.sum(probs * grad_probs, axis=-1, keepdims=True)
    grad_scores = (probs * (grad_probs - inner)).astype(jnp.bfloat16)
    grad_query = (
        jnp.einsum("bhst,bthd->bshd", grad_scores, keys, preferred_element_type=jnp.float32)
        * factor
    )
    grad_keys = (
        jnp.einsum("bhst,bshd->bthd", grad_scores, query, preferred_element_type=jnp.float32)
        * factor
    )
    return (
        grad_query.astype(jnp.bfloat16),
        grad_keys.astype(jnp.bfloat16),
        grad_values.astype(jnp.bfloat16),
    )


def on_device(
    images,
    first_gain,
    first_shift,
    qkv_weight,
    qv_bias,
    out_weight,
    out_bias,
    second_gain,
    second_shift,
    up_weight,
    up_bias,
    down_weight,
    down_bias,
    cotangent,
):
    seq_len = images.shape[1]
    columns = qkv_weight.shape[2]
    heads_here = columns // HD
    inputs = images.astype(jnp.float32)
    unit_first, inverse_first = normalize(inputs)
    normed_local = (unit_first * first_gain + first_shift).astype(jnp.bfloat16)
    normed_first = lax.all_gather(normed_local, "tensor", axis=0, tiled=True)
    count = normed_first.shape[0]
    projected = jnp.einsum(
        "isd,nde->nise", normed_first, qkv_weight, preferred_element_type=jnp.float32
    )
    query = (projected[0] + qv_bias[0]).astype(jnp.bfloat16)
    keys = projected[1].astype(jnp.bfloat16)
    values = (projected[2] + qv_bias[1]).astype(jnp.bfloat16)
    split = (count // 2, 2, seq_len, heads_here, HD)
    query_blocks = query.reshape(split)
    key_blocks = keys.reshape(split)
    value_blocks = values.reshape(split)
    mixed, log_total = lax.map(
        lambda triple: attend_block(triple[0], triple[1], triple[2]),
        (query_blocks, key_blocks, value_blocks),
    )
    heads_out = mixed.reshape(count, seq_len, columns).astype(jnp.bfloat16)
    piece = heads_out
    attention = lax.psum_scatter(
        jnp.einsum("isc,cd->isd", piece, out_weight, preferred_element_type=jnp.float32).astype(
            jnp.bfloat16
        ),
        "tensor",
        scatter_dimension=0,
        tiled=True,
    ).astype(jnp.float32)
    middle = inputs + (attention + out_bias)
    unit_second, inverse_second = normalize(middle)
    normed_second = lax.all_gather(
        (unit_second * second_gain + second_shift).astype(jnp.bfloat16),
        "tensor",
        axis=0,
        tiled=True,
    )
    hidden = (
        jnp.einsum("isd,df->isf", normed_second, up_weight, preferred_element_type=jnp.float32)
        + up_bias
    )
    active = jax.nn.gelu(hidden, approximate=False).astype(jnp.bfloat16)
    piece = active
    result = (
        middle
        + lax.psum_scatter(
            jnp.einsum(
                "isf,fd->isd", piece, down_weight, preferred_element_type=jnp.float32
            ).astype(jnp.bfloat16),
            "tensor",
            scatter_dimension=0,
            tiled=True,
        ).astype(jnp.float32)
        + down_bias
    ).astype(jnp.bfloat16)
    seed_rows = lax.all_gather(cotangent, "tensor", axis=0, tiled=True)
    grad_down_weight = jnp.einsum(
        "isf,isd->fd", active, seed_rows, preferred_element_type=jnp.float32
    )
    grad_down_bias = jnp.sum(cotangent, axis=(0, 1), dtype=jnp.float32)
    grad_active = jnp.einsum(
        "isd,fd->isf", seed_rows, down_weight, preferred_element_type=jnp.float32
    )
    normal_cdf = 0.5 * (1.0 + lax.erf(hidden * inv_root_two))
    density = jnp.exp(-0.5 * hidden * hidden) * inv_root_tau
    grad_hidden = (grad_active * (normal_cdf + hidden * density)).astype(jnp.bfloat16)
    grad_up_weight = jnp.einsum(
        "isd,isf->df", normed_second, grad_hidden, preferred_element_type=jnp.float32
    )
    grad_up_bias = jnp.sum(grad_hidden, axis=(0, 1), dtype=jnp.float32)
    piece = grad_hidden
    grad_normed_second = lax.psum_scatter(
        jnp.einsum("isf,df->isd", piece, up_weight, preferred_element_type=jnp.float32).astype(
            jnp.bfloat16
        ),
        "tensor",
        scatter_dimension=0,
        tiled=True,
    ).astype(jnp.float32)
    grad_second_gain = jnp.sum(grad_normed_second * unit_second, axis=(0, 1))
    grad_second_shift = jnp.sum(grad_normed_second, axis=(0, 1))
    grad_middle = cotangent.astype(jnp.float32) + norm_back(
        grad_normed_second, unit_second, inverse_second, second_gain
    )
    grad_branch = grad_middle.astype(jnp.bfloat16)
    grad_out_bias = jnp.sum(grad_branch, axis=(0, 1), dtype=jnp.float32)
    branch_rows = lax.all_gather(grad_branch, "tensor", axis=0, tiled=True)
    grad_out_weight = jnp.einsum(
        "isc,isd->cd", heads_out, branch_rows, preferred_element_type=jnp.float32
    )
    grad_heads = jnp.einsum(
        "isd,cd->isc", branch_rows, out_weight, preferred_element_type=jnp.float32
    ).astype(jnp.bfloat16)
    grad_query, grad_keys, grad_values = lax.map(
        lambda parts: attend_back(parts[0], parts[1], parts[2], parts[3], parts[4]),
        (query_blocks, key_blocks, value_blocks, grad_heads.reshape(split), log_total),
    )
    grad_projected = jnp.stack(
        [
            grad_query.reshape(count, seq_len, columns),
            grad_keys.reshape(count, seq_len, columns),
            grad_values.reshape(count, seq_len, columns),
        ]
    )
    grad_qkv_weight = jnp.einsum(
        "isd,nisc->ndc", normed_first, grad_projected, preferred_element_type=jnp.float32
    )
    grad_qv_bias = jnp.stack(
        [
            jnp.sum(grad_projected[0], axis=(0, 1), dtype=jnp.float32),
            jnp.sum(grad_projected[2], axis=(0, 1), dtype=jnp.float32),
        ]
    )
    piece = grad_projected
    grad_normed_first = lax.psum_scatter(
        jnp.einsum("nisc,ndc->isd", piece, qkv_weight, preferred_element_type=jnp.float32).astype(
            jnp.bfloat16
        ),
        "tensor",
        scatter_dimension=0,
        tiled=True,
    ).astype(jnp.float32)
    grad_first_gain = jnp.sum(grad_normed_first * unit_first, axis=(0, 1))
    grad_first_shift = jnp.sum(grad_normed_first, axis=(0, 1))
    grad_images = (
        grad_middle + norm_back(grad_normed_first, unit_first, inverse_first, first_gain)
    ).astype(jnp.bfloat16)
    (
        grad_qkv_weight,
        grad_qv_bias,
        grad_out_weight,
        grad_up_weight,
        grad_up_bias,
        grad_down_weight,
    ) = (
        lax.psum(grad_qkv_weight.astype(jnp.bfloat16), "dp").astype(jnp.float32),
        lax.psum(grad_qv_bias.astype(jnp.bfloat16), "dp").astype(jnp.float32),
        lax.psum(grad_out_weight.astype(jnp.bfloat16), "dp").astype(jnp.float32),
        lax.psum(grad_up_weight.astype(jnp.bfloat16), "dp").astype(jnp.float32),
        lax.psum(grad_up_bias.astype(jnp.bfloat16), "dp").astype(jnp.float32),
        lax.psum(grad_down_weight.astype(jnp.bfloat16), "dp").astype(jnp.float32),
    )
    (
        grad_first_gain,
        grad_first_shift,
        grad_out_bias,
        grad_second_gain,
        grad_second_shift,
        grad_down_bias,
    ) = lax.psum(
        (
            grad_first_gain,
            grad_first_shift,
            grad_out_bias,
            grad_second_gain,
            grad_second_shift,
            grad_down_bias,
        ),
        ("dp", "tensor"),
    )
    return (
        result,
        grad_images,
        grad_first_gain,
        grad_first_shift,
        grad_qkv_weight,
        grad_qv_bias,
        grad_out_weight,
        grad_out_bias,
        grad_second_gain,
        grad_second_shift,
        grad_up_weight,
        grad_up_bias,
        grad_down_weight,
        grad_down_bias,
    )


def solution(mesh):
    return jax.shard_map(
        on_device,
        mesh=mesh,
        in_specs=(
            P(("dp", "tensor"), None, None),
            P(),
            P(),
            P(None, None, "tensor"),
            P(None, "tensor"),
            P("tensor", None),
            P(),
            P(),
            P(),
            P(None, "tensor"),
            P("tensor"),
            P("tensor", None),
            P(),
            P(("dp", "tensor"), None, None),
        ),
        out_specs=(
            P(("dp", "tensor"), None, None),
            P(("dp", "tensor"), None, None),
            P(),
            P(),
            P(None, None, "tensor"),
            P(None, "tensor"),
            P("tensor", None),
            P(),
            P(),
            P(),
            P(None, "tensor"),
            P("tensor"),
            P("tensor", None),
            P(),
        ),
        check_vma=False,
    )
```

profile of v0, /device:TPU:0, one launch (start us, length us, event | category | flops | bytes accessed | tf_op | source)
XLA Modules:
  0.0 1597.8 jit_solution(3615522905375342727)
XLA Ops:
  9.1 2.1 fusion.109
  11.8 2.6 fusion.104
  14.7 130.0 %all-gather.5.cloned.1.call-done = bf16[8,257,1664]{2,1,0:T(8,128)(2,1)} async-done(((bf16[2,257,1664]{2,1,0:T(8,128)(2,1)}), bf16[8,257,1664]{2,1,0:T(8,128)(2,1)}) %all-gather.5.cloned.1.call-update) | async-done | bytes 6842384 | tf_op jit(solution)/shard_map/all_gather | solution.py:87
  144.7 15.5 convolution_bitcast_fusion
  160.2 4.5 fusion.122
  166.4 5.9 reshape.134
  172.3 2.9 fusion.93
  175.2 2.2 copy.78
  177.4 5.9 reshape.135
  183.4 2.9 fusion.92
  186.3 2.1 copy.79
  188.4 4.5 reshape.136
  193.0 3.3 copy.80
  196.2 24.7 %while.26 = (s32[]{:T(128)}, bf16[4,2,257,4,104]{4,2,3,1,0:T(8,128)(2,1)}, f32[4,2,4,257]{3,2,1,0:T(4,128)}, bf16[4,2,257,4,104]{4,2,3,1,0:T(8,128)(2,1)}, bf16[...) while((s32[]{:T(128)}, bf16[4,2,257,4,104]{4,2,3,1,0:T(8,128)(2,1)}, ...), condition=%wide.region_5.6_spmd, body=%wide.region_2.5_spmd.sunk | while | flops 224564544 | bytes 9116557 | solution.py:99
  199.8 2.9 fusion.156
  205.9 2.9 fusion.156
  212.0 2.9 fusion.156
  218.0 2.9 fusion.156
  220.9 3.7 copy.113
  224.6 4.6 reshape.141
  229.2 8.2 convolution_convert_fusion
  237.5 121.2 %reduce-scatter.5.cloned.1.call-done = bf16[2,257,1664]{2,1,0:T(8,128)(2,1)} async-done(((bf16[8,257,1664]{2,1,0:T(8,128)(2,1)}), bf16[2,257,1664]{2,1,0:T(8,128)(2,1)}) %reduce-scatter.5.cloned.1.call-update) | async-done | bytes 1710608 | tf_op jit(solution)/shard_map/reduce_scatter | solution.py:105
  358.6 2.2 fusion.119
  361.8 2.2 add_convert_fusion.1
  364.0 2.8 copy.83
  366.9 125.1 %all-gather.7.cloned.1.call-done = bf16[8,257,1664]{2,1,0:T(8,128)(2,1)} async-done(((bf16[2,257,1664]{2,1,0:T(8,128)(2,1)}), bf16[8,257,1664]{2,1,0:T(8,128)(2,1)}) %all-gather.7.cloned.1.call-update) | async-done | bytes 6842384 | tf_op jit(solution)/shard_map/all_gather | solution.py:115
  492.0 28.4 %fusion.91 = (u8[257,2048]{1,0:T(8,128)(4,1)}, u8[257,2048]{1,0:T(8,128)(4,1)}, f32[8,257,2048]{2,1,0:T(8,128)}) fusion(f32[2048]{0:T(1024)S(1)} %copy-done.39, bf16[8,257,1664]{2,1,0:T(8,128)(2,1)} %all-gather.7.cloned.1.call-done, bf16[1664,2048]{1,0:T(8,128)(2,1)} %param.27), kind=kOutput, calls=%fused_computation.123 | convolution fusion | flops 14071066624 | bytes 31561728 | tf_op jit(solution)/shard_map/isd,df->isf/dot_general | solution.py:122
  520.5 99.3 %all-gather.9.cloned.1.call-done = bf16[8,257,1664]{2,1,0:T(8,128)(2,1)} async-done(((bf16[2,257,1664]{2,1,0:T(8,128)(2,1)}), bf16[8,257,1664]{2,1,0:T(8,128)(2,1)}) %all-gather.9.cloned.1.call-update) | async-done | bytes 6842384 | tf_op jit(solution)/shard_map/all_gather | solution.py:139
  619.8 29.1 %fusion.123 = (bf16[2048]{0:T(1024)(128)(2,1)}, bf16[8,257,2048]{2,1,0:T(8,128)(2,1)S(1)}) fusion(f32[8,257,2048]{2,1,0:T(8,128)} %get-tuple-element.253, f32[2048]{0:T(1024)S(1)} %copy-done.39, bf16[8,257,1664]{2,1,0:T(8,128)(2,1)} %all-gather.9.cloned.1.call-done, bf16[2048,1664]{1,0:T(8,128)(2,1)} %param.29), kind=kOutput, calls=%fused_computation.175 | convolution fusion | flops 14063695872 | bytes 38934528 | tf_op jit(solution)/shard_map/isd,fd->isf/dot_general | solution.py:144
  648.9 3.5 copy-done.43
  652.4 20.8 %fusion.78 = bf16[8,257,1664]{2,1,0:T(8,128)(2,1)} fusion(bf16[8,257,2048]{2,1,0:T(8,128)(2,1)S(1)} %get-tuple-element.255, bf16[1664,2048]{1,0:T(8,128)(2,1)} %param.27), kind=kOutput, calls=%fused_computation.102 | convolution fusion | flops 14016590848 | bytes 22079488 | tf_op jit(solution)/shard_map/isf,df->isd/dot_general | solution.py:156
  673.3 121.2 %reduce-scatter.9.cloned.1.call-done = bf16[2,257,1664]{2,1,0:T(8,128)(2,1)} async-done(((bf16[8,257,1664]{2,1,0:T(8,128)(2,1)}), bf16[2,257,1664]{2,1,0:T(8,128)(2,1)}) %reduce-scatter.9.cloned.1.call-update) | async-done | bytes 1710608 | tf_op jit(solution)/shard_map/reduce_scatter | solution.py:155
  794.4 4.3 fusion.114
  798.8 4.0 convert_reduce_fusion.4
  802.9 42.6 %fusion.52 = bf16[8,257,2048]{2,1,0:T(8,128)(2,1)S(1)} fusion(f32[8,257,2048]{2,1,0:T(8,128)} %get-tuple-element.253, f32[2048]{0:T(1024)S(1)} %copy-done.39, u8[257,2048]{1,0:T(8,128)(4,1)} %get-tuple-element.189, u8[257,2048]{1,0:T(8,128)(4,1)} %get-tuple-element.188), kind=kLoop, calls=%fused_computation.60 | loop fusion | flops 298958848 | bytes 26324992 | tf_op jit(solution)/shard_map/convert_element_type | solution.py:125
  845.6 25.8 %bitcast_convert_fusion.1 = bf16[2048,1664]{1,0:T(8,128)(2,1)} fusion(bf16[8,257,2048]{2,1,0:T(8,128)(2,1)S(1)} %fusion.52, bf16[8,257,1664]{2,1,0:T(8,128)(2,1)} %all-gather.9.cloned.1.call-done), kind=kOutput, calls=%fused_computation.86 | convolution fusion | flops 14016577536 | bytes 22079488 | tf_op jit(solution)/shard_map/isf,isd->fd/dot_general | solution.py:140
  871.5 18.5 %bitcast_convert_fusion.2 = bf16[1664,2048]{1,0:T(8,128)(2,1)} fusion(bf16[8,257,1664]{2,1,0:T(8,128)(2,1)S(1)} %bitcast.177, bf16[8,257,2048]{2,1,0:T(8,128)(2,1)S(1)} %bitcast.179), kind=kOutput, calls=%fused_computation.87 | convolution fusion | flops 14016577536 | bytes 22079488 | tf_op jit(solution)/shard_map/isd,isf->df/dot_general | solution.py:150
  889.9 41.0 %all-gather.11.cloned.1.call-done = bf16[8,257,1664]{2,1,0:T(8,128)(2,1)} async-done(((bf16[2,257,1664]{2,1,0:T(8,128)(2,1)}), bf16[8,257,1664]{2,1,0:T(8,128)(2,1)}) %all-gather.11.cloned.1.call-update) | async-done | bytes 6842384 | tf_op jit(solution)/shard_map/all_gather | solution.py:170
  931.0 8.4 convolution_convert_fusion.1
  939.4 4.8 reshape.137
  944.2 50.2 %while.27 = (s32[]{:T(128)}, bf16[4,2,257,4,104]{4,2,3,1,0:T(8,128)(2,1)}, bf16[4,2,257,4,104]{4,3,2,1,0:T(4,128)(2,1)}, bf16[4,2,257,4,104]{4,2,3,1,0:T(8,128)(...) while((s32[]{:T(128)}, ...), condition=%wide.region_15.16_spmd, body=%wide.region_13.15_spmd.sunk | while | flops 556935424 | bytes 23355692 | solution.py:177
  973.0 2.0 multiply_reduce_fusion.6
  994.3 3.7 copy.110
  998.1 3.3 reshape.138
  1002.9 3.3 reshape.139
  1006.2 3.8 copy.112
  1010.0 4.5 reshape.140
  1018.4 8.0 fusion.116
  1026.4 15.5 fusion.98
  1042.0 15.3 bitcast_convert_fusion
  1057.4 21.5 %fusion.81 = bf16[8,257,1664]{2,1,0:T(8,128)(2,1)} fusion(bf16[8,257,2048]{2,1,0:T(8,128)(2,1)} %copy-done.9, bf16[2048,1664]{1,0:T(8,128)(2,1)} %param.29), kind=kOutput, calls=%fused_computation.103 | convolution fusion | flops 14016590848 | bytes 22079488 | tf_op jit(solution)/shard_map/isf,fd->isd/dot_general | solution.py:130
  1080.9 2.1 reduce.4
  1083.2 15.6 all-reduce.1
  1100.0 186.0 %all-reduce.5.cloned.1.call-done = (bf16[3,1664,416]{1,2,0:T(8,128)(2,1)}, bf16[416,1664]{1,0:T(8,128)(2,1)}, bf16[1664,2048]{1,0:T(8,128)(2,1)}, bf16[2048,1664]{1,0:T(8,128)(2,1)}) async-done(((bf16[3,1664,416]{1,2,0:T(8,128)(2,1)}, bf16[416,1664]{1,0:T(8,128)(2,1)}, bf16[1664,2048]{1,0:T(8,128)(2,1)}, bf16[2048,1664]{1,0:T(8,128)(2,1)}), (bf16[3,1664,416]{1,2,0:T(8,128)(2,1)}, ...) | async-done | bytes 19169296 | tf_op jit(solution)/shard_map/psum | solution.py:219
  1286.0 10.6 convert_element_type.181
  1296.6 6.0 convert_element_type.184
  1302.6 3.9 convert_element_type.173
  1308.3 102.9 %reduce-scatter.11.cloned.1.call-done = bf16[2,257,1664]{2,1,0:T(8,128)(2,1)} async-done(((bf16[8,257,1664]{2,1,0:T(8,128)(2,1)}), bf16[2,257,1664]{2,1,0:T(8,128)(2,1)}) %reduce-scatter.11.cloned.1.call-update) | async-done | bytes 1710608 | tf_op jit(solution)/shard_map/reduce_scatter | solution.py:198
  1411.2 3.0 fusion.115
  1414.2 122.8 %reduce-scatter.7.cloned.1.call-done = bf16[2,257,1664]{2,1,0:T(8,128)(2,1)} async-done(((bf16[8,257,1664]{2,1,0:T(8,128)(2,1)}), bf16[2,257,1664]{2,1,0:T(8,128)(2,1)}) %reduce-scatter.7.cloned.1.call-update) | async-done | bytes 1710608 | tf_op jit(solution)/shard_map/reduce_scatter | solution.py:129
  1537.1 6.5 fusion.108
  1543.7 2.5 copy.97
  1546.2 2.5 copy.98
  1548.7 42.1 %all-reduce = (f32[1664]{0:T(1024)}, f32[1664]{0:T(1024)}, f32[1664]{0:T(1024)}, f32[1664]{0:T(1024)}, f32[1664]{0:T(1024)}, /*index=5*/f32[1664]{0:T(1024)}) all-reduce(f32[1664]{0:T(1024)S(1)} %get-tuple-element.192, f32[1664]{0:T(1024)S(1)} %get-tuple-element.197, ...), channel_id=1, replica_groups=mesh['dp'=8,'tensor'=4] {'dp','tensor'}, use_global_device_ids=true, to_apply=%region_20.21 | all-reduce | flops 9984 | bytes 79872 | tf_op jit(solution)/shard_map/psum | solution.py:233
  (192 shorter events, 77.2 us)
Async XLA Ops:
  7.2 222.0 %copy-start = (bf16[416,1664]{1,0:T(8,128)(2,1)S(1)}, bf16[416,1664]{1,0:T(8,128)(2,1)}, u32[]{:S(2)}) copy-start(bf16[416,1664]{1,0:T(8,128)(2,1)} %param.23) | copy-start | bytes 4153348
  7.2 4.6 copy-start.2
  7.2 137.5 %all-gather.5.cloned.1.call-start = ((), (), s32[]{:S(2)}) async-start(), calls=%async_computation.4 | async-start | bytes 8785920 | tf_op jit(solution)/shard_map/all_gather | solution.py:87
  9.1 5.4 copy-start.42
  9.1 2.1 copy-start.25
  11.2 0.6 copy-start.28
  14.5 344.2 %reduce-scatter.5.cloned.1.call-start = ((), (), s32[]{:S(2)}) async-start(), calls=%async_computation.5 | async-start | bytes 8785920 | tf_op jit(solution)/shard_map/reduce_scatter | solution.py:105
  237.4 121.3 %copy-start.17 = (f32[1664]{0:T(1024)S(1)}, f32[1664]{0:T(1024)}, u32[]{:S(2)}) copy-start(f32[1664]{0:T(1024)} %param.24) | copy-start | bytes 19972
  237.4 124.4 %copy-start.19 = (f32[1664]{0:T(1024)S(1)}, f32[1664]{0:T(1024)}, u32[]{:S(2)}) copy-start(f32[1664]{0:T(1024)} %param.25) | copy-start | bytes 19972
  237.4 124.3 %copy-start.38 = (f32[1664]{0:T(1024)S(1)}, f32[1664]{0:T(1024)}, u32[]{:S(2)}) copy-start(f32[1664]{0:T(1024)} %param.26) | copy-start | bytes 19972
  237.4 254.6 %all-gather.7.cloned.1.call-start = ((), (), s32[]{:S(2)}) async-start(), calls=%async_computation.6 | async-start | bytes 8785920 | tf_op jit(solution)/shard_map/all_gather | solution.py:115
  358.6 2.2 copy-start.4
  360.8 438.0 %copy-start.21 = (f32[2,257]{1,0:T(2,128)}, f32[2,257]{1,0:T(2,128)S(1)}, u32[]{:S(2)}) copy-start(f32[2,257]{1,0:T(2,128)S(1)} %broadcast_multiply_fusion.4) | copy-start | bytes 6172
  361.7 437.0 %copy-start.23 = (f32[2,257]{1,0:T(2,128)}, f32[2,257]{1,0:T(2,128)S(1)}, u32[]{:S(2)}) copy-start(f32[2,257]{1,0:T(2,128)S(1)} %add_rsqrt_fusion) | copy-start | bytes 6172
  363.9 128.1 %copy-start.39 = (f32[2048]{0:T(1024)S(1)}, f32[2048]{0:T(1024)}, u32[]{:S(2)}) copy-start(f32[2048]{0:T(1024)} %param.28) | copy-start | bytes 24580
  364.0 255.8 %all-gather.9.cloned.1.call-start = ((), (), s32[]{:S(2)}) async-start(), calls=%async_computation.8 | async-start | bytes 8785920 | tf_op jit(solution)/shard_map/all_gather | solution.py:139
  366.9 427.6 %reduce-scatter.9.cloned.1.call-start = ((), (), s32[]{:S(2)}) async-start(), calls=%async_computation.9 | async-start | bytes 8785920 | tf_op jit(solution)/shard_map/reduce_scatter | solution.py:155
  648.9 3.5 copy-start.43
  673.2 257.8 %all-gather.11.cloned.1.call-start = ((), (), s32[]{:S(2)}) async-start(), calls=%async_computation.10 | async-start | bytes 8785920 | tf_op jit(solution)/shard_map/all_gather | solution.py:170
  794.4 4.3 copy-start.5
  794.4 4.4 copy-start.7
  794.4 4.4 copy-start.8
  798.8 4.1 copy-start.34
  798.8 4.1 copy-start.36
  802.9 483.1 %all-reduce.5.cloned.1.call-start = ((), (), s32[]{:S(2)}) async-start(), calls=%async_computation.12 | async-start | bytes 38338560 | tf_op jit(solution)/shard_map/psum | solution.py:219
  802.9 68.5 %slice-start = ((s8[7028736]{0:T(1024)(128)(4,1)}), s8[4194304]{0:T(1024)(128)(4,1)S(1)}, s32[]{:S(2)}) async-start(s8[7028736]{0:T(1024)(128)(4,1)} %bitcast.176), calls=%async_computation.13 | async-start | bytes 8388608
  802.9 68.5 %slice-start.2 = ((s8[8650752]{0:T(1024)(128)(4,1)}), s8[4194304]{0:T(1024)(128)(4,1)S(1)}, s32[]{:S(2)}) async-start(s8[8650752]{0:T(1024)(128)(4,1)} %bitcast.178), calls=%async_computation.15 | async-start | bytes 8388608
  845.5 25.9 %copy-start.9 = (bf16[8,257,2048]{2,1,0:T(8,128)(2,1)}, bf16[8,257,2048]{2,1,0:T(8,128)(2,1)S(1)}, u32[]{:S(2)}) copy-start(bf16[8,257,2048]{2,1,0:T(8,128)(2,1)S(1)} %fusion.52) | copy-start | bytes 25264132
  845.6 25.9 %slice-start.1 = ((s8[7028736]{0:T(1024)(128)(4,1)}), s8[2834432]{0:T(1024)(128)(4,1)S(1)}, s32[]{:S(2)}) async-start(s8[7028736]{0:T(1024)(128)(4,1)} %bitcast.176), calls=%async_computation.14 | async-start | bytes 5668864
  845.6 25.9 %slice-start.3 = ((s8[8650752]{0:T(1024)(128)(4,1)}), s8[4194304]{0:T(1024)(128)(4,1)S(1)}, s32[]{:S(2)}) async-start(s8[8650752]{0:T(1024)(128)(4,1)} %bitcast.178), calls=%async_computation.16 | async-start | bytes 8388608
  845.6 25.9 %slice-start.4 = ((s8[8650752]{0:T(1024)(128)(4,1)}), s8[262144]{0:T(1024)(128)(4,1)S(1)}, s32[]{:S(2)}) async-start(s8[8650752]{0:T(1024)(128)(4,1)} %bitcast.178), calls=%async_computation.17 | async-start | bytes 524288
  939.4 4.8 copy-start.6
  1014.5 2.4 copy-start.11
  1014.5 3.9 copy-start.14
  1018.4 8.0 copy-start.16
  1041.9 369.3 %reduce-scatter.11.cloned.1.call-start = ((), (), s32[]{:S(2)}) async-start(), calls=%async_computation.11 | async-start | bytes 8785920 | tf_op jit(solution)/shard_map/reduce_scatter | solution.py:198
  1057.3 479.7 %reduce-scatter.7.cloned.1.call-start = ((), (), s32[]{:S(2)}) async-start(), calls=%async_computation.7 | async-start | bytes 8785920 | tf_op jit(solution)/shard_map/reduce_scatter | solution.py:129
  1078.8 1.7 copy-start.10
  1080.5 2.7 copy-start.41
  1286.0 10.6 copy-start.12
  1296.6 6.0 copy-start.13
  1302.6 3.9 copy-start.15
  1306.5 104.7 %copy-start.3 = (bf16[2,257,1664]{2,0,1:T(2,128)(2,1)S(1)}, bf16[2,257,1664]{2,0,1:T(2,128)(2,1)}, u32[]{:S(2)}) copy-start(bf16[2,257,1664]{2,0,1:T(2,128)(2,1)} %param.18) | copy-start | bytes 5131780
  1306.5 104.7 %copy-start.26 = (f32[2,257]{1,0:T(2,128)S(1)}, f32[2,257]{1,0:T(2,128)}, u32[]{:S(2)}) copy-start(f32[2,257]{1,0:T(2,128)} %copy-done.25) | copy-start | bytes 6172
  1306.5 104.7 %copy-start.27 = (f32[1664]{0:T(1024)S(1)}, f32[1664]{0:T(1024)}, u32[]{:S(2)}) copy-start(f32[1664]{0:T(1024)} %param.19) | copy-start | bytes 19972
  1306.5 104.7 %copy-start.29 = (f32[2,257]{1,0:T(2,128)S(1)}, f32[2,257]{1,0:T(2,128)}, u32[]{:S(2)}) copy-start(f32[2,257]{1,0:T(2,128)} %copy-done.28) | copy-start | bytes 6172
  1306.5 230.6 %copy-start.18 = (f32[1664]{0:T(1024)S(1)}, f32[1664]{0:T(1024)}, u32[]{:S(2)}) copy-start(f32[1664]{0:T(1024)} %param.24) | copy-start | bytes 19972
  1306.5 230.6 %copy-start.20 = (f32[1664]{0:T(1024)S(1)}, f32[1664]{0:T(1024)}, u32[]{:S(2)}) copy-start(f32[1664]{0:T(1024)} %param.25) | copy-start | bytes 19972
  1306.5 230.5 %copy-start.22 = (f32[2,257]{1,0:T(2,128)S(1)}, f32[2,257]{1,0:T(2,128)}, u32[]{:S(2)}) copy-start(f32[2,257]{1,0:T(2,128)} %copy-done.21) | copy-start | bytes 6172
  1306.5 230.5 %copy-start.24 = (f32[2,257]{1,0:T(2,128)S(1)}, f32[2,257]{1,0:T(2,128)}, u32[]{:S(2)}) copy-start(f32[2,257]{1,0:T(2,128)} %copy-done.23) | copy-start | bytes 6172
  1306.5 230.5 %copy-start.35 = (f32[2,257]{1,0:T(2,128)S(1)}, f32[2,257]{1,0:T(2,128)}, u32[]{:S(2)}) copy-start(f32[2,257]{1,0:T(2,128)} %copy-done.34) | copy-start | bytes 6172
  1306.5 230.5 %copy-start.37 = (f32[2,257]{1,0:T(2,128)S(1)}, f32[2,257]{1,0:T(2,128)}, u32[]{:S(2)}) copy-start(f32[2,257]{1,0:T(2,128)} %copy-done.36) | copy-start | bytes 6172
  1306.6 230.5 %copy-start.40 = (f32[1664]{0:T(1024)S(1)}, f32[1664]{0:T(1024)}, u32[]{:S(2)}) copy-start(f32[1664]{0:T(1024)} %param.30) | copy-start | bytes 19972
  1537.1 53.7 %copy-start.1 = (bf16[416,1664]{1,0:T(8,128)(2,1)S(1)}, bf16[416,1664]{1,0:T(8,128)(2,1)}, u32[]{:S(2)}) copy-start(bf16[416,1664]{1,0:T(8,128)(2,1)} %param.23) | copy-start | bytes 4153348
  1543.6 5.1 copy-start.30
  1543.6 5.1 copy-start.31
  1543.7 5.0 copy-start.32
  1543.7 5.0 copy-start.33
Sparse Core Ops, SparseCore 0:
  14.6 130.0 all-gather.4
  237.5 121.0 reduce-scatter.4
  364.1 127.9 all-gather.6
  494.1 125.6 all-gather.8
  673.3 121.0 reduce-scatter.8
  803.0 127.9 all-gather.10
  1042.0 243.8 all-reduce.4
  1288.3 122.8 reduce-scatter.10
  1413.6 123.3 reduce-scatter.6
where the time goes:
time: 1610 us; the launch traced here: 1600 us
  waiting for transfers between devices  1050 us (65%)
  matrix products  269 us (17%)
  other arithmetic  112 us (7%)
  local copies, waits for them, and re-layouts  93.3 us (6%)
  blocking collectives  57.6 us (4%)
    psum x1, waiting for transfers between devices, on_device(): lax.psum(grad_qkv_weight.astype(jnp.bfloat16), 'dp').astype(jnp.float32)  186 us
    all_gather x1, waiting for transfers between devices, on_device(): normed_first = lax.all_gather(normed_local, 'tensor', axis=0, tiled=True)  130 us
    all_gather x1, waiting for transfers between devices, on_device(): lax.all_gather((unit_second * second_gain + second_shift).astype(jnp.bflo...  125 us
    reduce_scatter x1, waiting for transfers between devices, on_device(): lax.psum_scatter(jnp.einsum('isf,fd->isd', piece, down_weight, preferred_...  123 us
    reduce_scatter x1, waiting for transfers between devices, on_device(): lax.psum_scatter(jnp.einsum('isc,cd->isd', piece, out_weight, preferred_e...  121 us
    reduce_scatter x1, waiting for transfers between devices, on_device(): lax.psum_scatter(jnp.einsum('isf,df->isd', piece, up_weight, preferred_el...  121 us
    reduce_scatter x1, waiting for transfers between devices, on_device(): lax.psum_scatter(jnp.einsum('nisc,ndc->isd', piece, qkv_weight, preferred...  103 us
    all_gather x1, waiting for transfers between devices, on_device(): seed_rows = lax.all_gather(cotangent, 'tensor', axis=0, tiled=True)  99.3 us
  transfers between devices with their start and end apart: 9, of which 9 were waited for; matrix products, arithmetic and copies ran while one was open for 12% of the time, Pallas kernels for 0%

commit v1 on v0

v1 whole, which is shorter than its diff:
```python
import jax
import jax.numpy as jnp
import numpy as np
from jax import lax
from jax.sharding import PartitionSpec as P

HD = 104

epsilon = 1e-06
inv_root_two = 0.7071067811865476
inv_root_tau = 0.3989422804014327
BF = jnp.bfloat16
F32 = jnp.float32


def normalize(rows):
    centre = jnp.mean(rows, axis=-1, keepdims=True)
    centred = rows - centre
    spread = jnp.mean(centred * centred, axis=-1, keepdims=True)
    inverse = lax.rsqrt(spread + epsilon)
    return (centred * inverse, inverse)


def norm_back(grad, unit, inverse, gain):
    scaled = grad * gain
    first = jnp.mean(scaled, axis=-1, keepdims=True)
    second = jnp.mean(scaled * unit, axis=-1, keepdims=True)
    return inverse * (scaled - first - unit * second)


def attend_block(query, keys, values):
    factor = query.shape[-1] ** (-0.5)
    scores = jnp.einsum("bshd,bthd->bhst", query, keys, preferred_element_type=F32) * factor
    top = jnp.max(scores, axis=-1, keepdims=True)
    raised = jnp.exp(scores - top)
    total = jnp.sum(raised, axis=-1, keepdims=True)
    weights = (raised / total).astype(BF)
    mixed = jnp.einsum("bhst,bthd->bshd", weights, values, preferred_element_type=F32)
    return (mixed, (top + jnp.log(total))[..., 0])


def attend_back(query, keys, values, grad_out, log_total):
    factor = query.shape[-1] ** (-0.5)
    scores = jnp.einsum("bshd,bthd->bhst", query, keys, preferred_element_type=F32) * factor
    probs = jnp.exp(scores - log_total[..., None])
    grad_values = jnp.einsum(
        "bhst,bshd->bthd", probs.astype(BF), grad_out, preferred_element_type=F32
    )
    grad_probs = jnp.einsum("bshd,bthd->bhst", grad_out, values, preferred_element_type=F32)
    inner = jnp.sum(probs * grad_probs, axis=-1, keepdims=True)
    grad_scores = (probs * (grad_probs - inner)).astype(BF)
    grad_query = (
        jnp.einsum("bhst,bthd->bshd", grad_scores, keys, preferred_element_type=F32) * factor
    )
    grad_keys = (
        jnp.einsum("bhst,bshd->bthd", grad_scores, query, preferred_element_type=F32) * factor
    )
    return (grad_query.astype(BF), grad_keys.astype(BF), grad_values.astype(BF))


class Layout:
    def __init__(self, dp, tensor):
        self.dp, self.tensor = dp, tensor
        self.n_p, self.n_hi = dp // 2, tensor // 2
        self.bits = [1 << b for b in range(self.n_p.bit_length() - 1)]

    def move(self, x, p=0, c=0, hi=0, lo=0):
        dp_mask, tensor_mask = 2 * p + c, 2 * hi + lo
        pairs = [
            (d * self.tensor + t, (d ^ dp_mask) * self.tensor + (t ^ tensor_mask))
            for d in range(self.dp)
            for t in range(self.tensor)
        ]
        return lax.ppermute(x, ("dp", "tensor"), pairs)

    def spread(self, block, order):
        have = {0: block}
        for bit in order:
            masks = sorted(have)
            got = self.move(jnp.stack([have[m] for m in masks]), p=bit)
            for i, m in enumerate(masks):
                have[m ^ bit] = got[i]
        return [have[m] for m in range(self.n_p)]

    def collect(self, blocks, order):
        have = dict(enumerate(blocks))
        for bit in order:
            keep = [m for m in sorted(have) if not m & bit]
            got = self.move(jnp.stack([have[m | bit] for m in keep]), p=bit)
            have = {
                m: (have[m].astype(F32) + got[i].astype(F32)).astype(BF)
                for i, m in enumerate(keep)
            }
        return have[0]


def on_device(
    lay,
    images,
    first_gain,
    first_shift,
    qkv_weight,
    qv_bias,
    out_weight,
    out_bias,
    second_gain,
    second_shift,
    up_weight,
    up_bias,
    down_weight,
    down_bias,
    cotangent,
):
    n_p, n_hi = lay.n_p, lay.n_hi
    seq_len = images.shape[1]
    width = images.shape[2]
    columns = qkv_weight.shape[2]
    units = up_weight.shape[1]
    hc, hu = columns // 2, units // 2
    dp = lax.axis_index("dp")
    p, c = dp // 2, dp % 2
    d_block, u_block = width // n_p, hu // n_p
    up_order, down_order = lay.bits, lay.bits[::-1]

    def half(x, axis):
        n = x.shape[axis] // 2
        return lax.dynamic_slice_in_dim(x, c * n, n, axis)

    def relative(x, axis):
        n = x.shape[axis] // n_p
        return [lax.dynamic_slice_in_dim(x, (p ^ m) * n, n, axis) for m in range(n_p)]

    def absolute(blocks, axis):
        stacked = jnp.stack(blocks)
        return jnp.concatenate(
            [lax.dynamic_index_in_dim(stacked, p ^ a, 0, keepdims=False) for a in range(n_p)], axis
        )

    def fetch(x, axis, order):
        mine = relative(x, axis)
        return [mine] + [
            lay.spread(lay.move(mine[0], hi=k), order) for k in range(1, n_hi)
        ]

    qkv_half = half(qkv_weight, 2)
    out_half = half(out_weight, 0)
    qkv_parts = fetch(qkv_half, 1, up_order)
    out_parts = fetch(out_half, 1, down_order)
    qkv_work = jnp.concatenate(
        [qkv_half] + [absolute(b, 1) for b in qkv_parts[1:]], 2
    )
    out_work = jnp.concatenate([out_half] + [absolute(b, 1) for b in out_parts[1:]], 0)
    up_parts = fetch(half(up_weight, 1), 1, up_order)
    down_parts = fetch(half(down_weight, 0), 0, down_order)
    up_work = jnp.concatenate([b for part in up_parts for b in part], 1)
    down_work = jnp.concatenate([b for part in down_parts for b in part], 0)
    qv_half, upb_half = half(qv_bias, 1), half(up_bias, 0)
    bias_all = [jnp.concatenate([qv_half.reshape(-1), upb_half])]
    bias_all += [lay.move(bias_all[0], hi=k) for k in range(1, n_hi)]
    qv_work = jnp.concatenate([b[: 2 * hc].reshape(2, hc) for b in bias_all], 1)
    upb_work = jnp.concatenate([s for b in bias_all for s in relative(b[2 * hc :], 0)])

    def gather(x):
        x_c = lay.move(x, c=1)
        x_z = lay.move(x, lo=1)
        x_zc = lay.move(x_z, c=1)
        return jnp.concatenate([x, x_c, x_z, x_zc])

    def scatter(partial):
        n = partial.shape[0] // 4
        own, other, far, far_other = [partial[i * n : (i + 1) * n] for i in range(4)]
        got_far = lay.move(far_other, c=1)
        far_sum = (far.astype(F32) + got_far.astype(F32)).astype(BF)
        got_z = lay.move(far_sum, lo=1)
        got = lay.move(other, c=1)
        return own.astype(F32) + got.astype(F32) + got_z.astype(F32)

    inputs = images.astype(F32)
    unit_first, inverse_first = normalize(inputs)
    normed_first = gather((unit_first * first_gain + first_shift).astype(BF))
    seed_rows = gather(cotangent)
    count = normed_first.shape[0]
    work_columns = qkv_work.shape[2]
    heads_here = work_columns // HD
    projected = jnp.einsum("isd,nde->nise", normed_first, qkv_work, preferred_element_type=F32)
    query = (projected[0] + qv_work[0]).astype(BF)
    keys = projected[1].astype(BF)
    values = (projected[2] + qv_work[1]).astype(BF)
    split = (count // 2, 2, seq_len, heads_here, HD)
    query_blocks = query.reshape(split)
    key_blocks = keys.reshape(split)
    value_blocks = values.reshape(split)
    mixed, log_total = lax.map(
        lambda triple: attend_block(*triple), (query_blocks, key_blocks, value_blocks)
    )
    heads_out = mixed.reshape(count, seq_len, work_columns).astype(BF)
    attention = scatter(
        jnp.einsum("isc,cd->isd", heads_out, out_work, preferred_element_type=F32).astype(BF)
    )
    middle = inputs + (attention + out_bias)
    unit_second, inverse_second = normalize(middle)
    normed_second = gather((unit_second * second_gain + second_shift).astype(BF))
    hidden = (
        jnp.einsum("isd,df->isf", normed_second, up_work, preferred_element_type=F32) + upb_work
    )
    active = jax.nn.gelu(hidden, approximate=False).astype(BF)
    result = (
        middle
        + scatter(
            jnp.einsum("isf,fd->isd", active, down_work, preferred_element_type=F32).astype(BF)
        )
        + down_bias
    ).astype(BF)
    grad_down_work = jnp.einsum("isf,isd->fd", active, seed_rows, preferred_element_type=F32)
    grad_down_bias = jnp.sum(cotangent, axis=(0, 1), dtype=F32)
    grad_active = jnp.einsum("isd,fd->isf", seed_rows, down_work, preferred_element_type=F32)
    normal_cdf = 0.5 * (1.0 + lax.erf(hidden * inv_root_two))
    density = jnp.exp(-0.5 * hidden * hidden) * inv_root_tau
    grad_hidden = (grad_active * (normal_cdf + hidden * density)).astype(BF)
    grad_up_work = jnp.einsum("isd,isf->df", normed_second, grad_hidden, preferred_element_type=F32)
    grad_up_bias = jnp.sum(grad_hidden, axis=(0, 1), dtype=F32)
    grad_normed_second = scatter(
        jnp.einsum("isf,df->isd", grad_hidden, up_work, preferred_element_type=F32).astype(BF)
    )
    grad_second_gain = jnp.sum(grad_normed_second * unit_second, axis=(0, 1))
    grad_second_shift = jnp.sum(grad_normed_second, axis=(0, 1))
    grad_middle = cotangent.astype(F32) + norm_back(
        grad_normed_second, unit_second, inverse_second, second_gain
    )
    grad_branch = grad_middle.astype(BF)
    grad_out_bias = jnp.sum(grad_branch, axis=(0, 1), dtype=F32)
    branch_rows = gather(grad_branch)
    grad_out_work = jnp.einsum("isc,isd->cd", heads_out, branch_rows, preferred_element_type=F32)
    grad_heads = jnp.einsum(
        "isd,cd->isc", branch_rows, out_work, preferred_element_type=F32
    ).astype(BF)
    grad_query, grad_keys, grad_values = lax.map(
        lambda parts: attend_back(*parts),
        (query_blocks, key_blocks, value_blocks, grad_heads.reshape(split), log_total),
    )
    grad_projected = jnp.stack(
        [g.reshape(count, seq_len, work_columns) for g in (grad_query, grad_keys, grad_values)]
    )
    grad_qkv_work = jnp.einsum(
        "isd,nisc->ndc", normed_first, grad_projected, preferred_element_type=F32
    )
    grad_qv_work = jnp.stack(
        [jnp.sum(grad_projected[i], axis=(0, 1), dtype=F32) for i in (0, 2)]
    )
    grad_normed_first = scatter(
        jnp.einsum("nisc,ndc->isd", grad_projected, qkv_work, preferred_element_type=F32).astype(BF)
    )
    grad_first_gain = jnp.sum(grad_normed_first * unit_first, axis=(0, 1))
    grad_first_shift = jnp.sum(grad_normed_first, axis=(0, 1))
    grad_images = (
        grad_middle + norm_back(grad_normed_first, unit_first, inverse_first, first_gain)
    ).astype(BF)

    def settle(parts, order):
        sums = lay.collect(
            [jnp.stack([part[m] for part in parts]) for m in range(n_p)], order
        )
        total = sums[0].astype(F32)
        for k in range(1, n_hi):
            total = total + lay.move(sums[k], hi=k).astype(F32)
        return lay.spread(total.astype(BF), order[::-1])

    def whole(blocks, axis):
        mine = absolute(blocks, axis)
        other = lay.move(mine, c=1)
        first = jnp.where(c == 0, mine, other)
        second = jnp.where(c == 0, other, mine)
        return first.astype(F32), second.astype(F32)

    def block_list(x, start, size, axis):
        return [
            lax.slice_in_dim(x, start + m * size, start + (m + 1) * size, axis=axis)
            for m in range(n_p)
        ]

    grad_down_low, grad_up_low = grad_down_work.astype(BF), grad_up_work.astype(BF)
    down_settled = settle(
        [block_list(grad_down_low, k * hu, u_block, 0) for k in range(n_hi)], down_order
    )
    up_settled = settle(
        [block_list(grad_up_low, k * hu, u_block, 1) for k in range(n_hi)], up_order
    )
    grad_out_low, grad_qkv_low = grad_out_work.astype(BF), grad_qkv_work.astype(BF)
    out_settled = settle(
        [relative(grad_out_low[k * hc : (k + 1) * hc], 1) for k in range(n_hi)], down_order
    )
    qkv_settled = settle(
        [relative(grad_qkv_low[:, :, k * hc : (k + 1) * hc], 1) for k in range(n_hi)], up_order
    )
    grad_down_weight = jnp.concatenate(whole(down_settled, 0), 0)
    grad_up_weight = jnp.concatenate(whole(up_settled, 1), 1)
    grad_out_weight = jnp.concatenate(whole(out_settled, 1), 0)
    grad_qkv_weight = jnp.concatenate(whole(qkv_settled, 1), 2)

    tensor_at = lax.axis_index("tensor")
    all_units, all_columns = units * lay.tensor, columns * lay.tensor
    wide_up = jnp.zeros((all_units,), F32)
    wide_qv = jnp.zeros((2, all_columns), F32)
    for k in range(n_hi):
        shard = tensor_at ^ (2 * k)
        blocks = [
            grad_up_bias[k * hu + m * u_block : k * hu + (m + 1) * u_block] for m in range(n_p)
        ]
        wide_up = lax.dynamic_update_slice(
            wide_up, absolute(blocks, 0), (shard * units + c * hu,)
        )
        wide_qv = lax.dynamic_update_slice(
            wide_qv, grad_qv_work[:, k * hc : (k + 1) * hc], (0, shard * columns + c * hc)
        )

    def total_of(vector):
        for bit in lay.bits:
            vector = vector + lay.move(vector, p=bit)
        vector = vector + lay.move(vector, c=1)
        for k in [1 << b for b in range(lay.tensor.bit_length() - 1)]:
            vector = vector + lay.move(vector, lo=k & 1, hi=k >> 1)
        return vector

    early = total_of(
        jnp.concatenate([grad_down_bias, wide_up, grad_second_gain, grad_second_shift, grad_out_bias])
    )
    late = total_of(jnp.concatenate([wide_qv.reshape(-1), grad_first_gain, grad_first_shift]))
    grad_down_bias, early = early[:width], early[width:]
    grad_up_bias = lax.dynamic_slice(early, (tensor_at * units,), (units,))
    early = early[all_units:].reshape(3, width)
    grad_qv_bias = lax.dynamic_slice(
        late[: 2 * all_columns].reshape(2, all_columns), (0, tensor_at * columns), (2, columns)
    )
    late = late[2 * all_columns :].reshape(2, width)
    return (
        result,
        grad_images,
        late[0],
        late[1],
        grad_qkv_weight,
        grad_qv_bias,
        grad_out_weight,
        early[2],
        early[0],
        early[1],
        grad_up_weight,
        grad_up_bias,
        grad_down_weight,
        grad_down_bias,
    )


def solution(mesh):
    lay = Layout(mesh.shape["dp"], mesh.shape["tensor"])

    def run(*args):
        return on_device(lay, *args)

    return jax.shard_map(
        run,
        mesh=mesh,
        in_specs=(
            P(("dp", "tensor"), None, None),
            P(),
            P(),
            P(None, None, "tensor"),
            P(None, "tensor"),
            P("tensor", None),
            P(),
            P(),
            P(),
            P(None, "tensor"),
            P("tensor"),
            P("tensor", None),
            P(),
            P(("dp", "tensor"), None, None),
        ),
        out_specs=(
            P(("dp", "tensor"), None, None),
            P(("dp", "tensor"), None, None),
            P(),
            P(),
            P(None, None, "tensor"),
            P(None, "tensor"),
            P("tensor", None),
            P(),
            P(),
            P(),
            P(None, "tensor"),
            P("tensor"),
            P("tensor", None),
            P(),
        ),
        check_vma=False,
    )
```

time: 1610 us -> 1140 us (0.71)
  waiting for transfers between devices: 1050 us -> 388 us
  local copies, waits for them, and re-layouts: 93.3 us -> 234 us
  starting transfers between devices: 0.37 us -> 65.4 us
  other arithmetic: 112 us -> 174 us
  blocking collectives: 57.6 us -> 0 us
    reduce_scatter x4 -> x0, waiting for transfers between devices: 468 us -> none  [the longest x1 123 us: on_device(): lax.psum_scatter(jnp.einsum('isf,fd->isd', piece, down_weight, preferred_...]
    all_gather x4 -> x0, waiting for transfers between devices: 395 us -> none  [the longest x1 130 us: on_device(): normed_first = lax.all_gather(normed_local, 'tensor', axis=0, tiled=True)]
    ppermute x0 -> x71, waiting for transfers between devices: none -> 388 us  [move(): return lax.ppermute(x, ('dp', 'tensor'), pairs)]
    psum x1 -> x0, waiting for transfers between devices: 186 us -> none  [on_device(): lax.psum(grad_qkv_weight.astype(jnp.bfloat16), 'dp').astype(jnp.float32)]
    ppermute x0 -> x71, starting transfers between devices: none -> 65.4 us  [move(): return lax.ppermute(x, ('dp', 'tensor'), pairs)]
    psum x2 -> x0, blocking collectives: 57.6 us -> none  [the longest x1 42.1 us: on_device(): lax.psum((grad_first_gain, grad_first_shift, grad_out_bias, grad_second_g...]
    unnamed x103 -> x250, local copies, waits for them, and re-layouts: 17.7 us -> 52.9 us
    concatenate x0 -> x9, other arithmetic: none -> 29.4 us  [the longest x2 8.83 us: absolute(): jnp.concatenate([lax.dynamic_index_in_dim(stacked, p ^ a, 0, keepdims=Fal...]
  transfers between devices with their start and end apart: 9 -> 71, of which waited for: 9 -> 29; matrix products, arithmetic and copies ran while one was open for 12% -> 41% of each run, Pallas kernels for 0% -> 0%
where the time goes in v1:
time: 1140 us; the launch traced here: 1130 us
  waiting for transfers between devices  388 us (34%)
  matrix products  261 us (23%)
  local copies, waits for them, and re-layouts  234 us (21%)
  other arithmetic  174 us (15%)
  starting transfers between devices  65.4 us (6%)
    ppermute x71, waiting for transfers between devices, move(): return lax.ppermute(x, ('dp', 'tensor'), pairs)  388 us
    ppermute x71, starting transfers between devices, move(): return lax.ppermute(x, ('dp', 'tensor'), pairs)  65.4 us
    unnamed x250, local copies, waits for them, and re-layouts  52.9 us
    convert_element_type x1, other arithmetic, on_device(): active = jax.nn.gelu(hidden, approximate=False).astype(BF)  41.5 us
    dot_general x1, matrix products, on_device(): jnp.einsum('isd,fd->isf', seed_rows, down_work, preferred_element_type=F32)  28.9 us
    dot_general x1, matrix products, on_device(): jnp.einsum('isd,df->isf', normed_second, up_work, preferred_element_type=...  26.8 us
  transfers between devices with their start and end apart: 71, of which 29 were waited for; matrix products, arithmetic and copies ran while one was open for 41% of the time, Pallas kernels for 0%

profile of v1, /device:TPU:0, one launch (start us, length us, event | category | flops | bytes accessed | tf_op | source)
XLA Modules:
  0.0 1126.4 jit_solution(9687107386977402120)
XLA Ops:
  28.9 35.5 %collective-permute-done = bf16[3,416,208]{1,2,0:T(8,128)(2,1)} collective-permute-done((bf16[3,416,208]{1,2,0:T(8,128)(2,1)S(1)}, bf16[3,416,208]{1,2,0:T(8,128)(2,1)}, u32[]{:S(2)}, u32[]{:S(2)}) %collective-permute-start) | collective-permute-done | bytes 519200 | tf_op jit(solution)/shard_map/ppermute | solution.py:74
  75.1 3.6 collective-permute-done.1
  91.6 3.7 collective-permute-done.9
  113.7 5.2 concatenate.115
  120.9 17.6 %fusion.77 = f32[3,8,257,416]{3,2,1,0:T(8,128)} fusion(bf16[3,1664,208]{1,2,0:T(8,128)(2,1)} %concatenate.115, bf16[3,1664,208]{1,2,0:T(8,128)(2,1)} %constant_dynamic-slice_fusion.15, bf16[2,257,1664]{2,1,0:T(8,128)(2,1)S(1)} %copy.83, bf16[2,257,1664]{2,1,0:T(8,128)(2,1)} %copy.82, bf16[2,257,1664]{2,1,0:T(8,128)(2,1)} %copy.81, ...), kind=kOutput, calls=%fused_computation.107 | convolution fusion | flops 8574951424 | bytes 21259264 | tf_op jit(solution)/shard_map/isd,nde->nise/dot_general | solution.py:185
  138.5 8.3 fusion.149
  146.8 3.8 slice.564
  150.7 5.9 reshape.327
  161.7 5.9 reshape.328
  172.7 4.5 reshape.329
  180.5 25.5 %while.26 = (s32[]{:T(128)}, bf16[4,2,257,4,104]{4,2,3,1,0:T(8,128)(2,1)}, f32[4,2,4,257]{3,2,1,0:T(4,128)}, bf16[4,2,257,4,104]{4,2,3,1,0:T(8,128)(2,1)}, bf16[...) while((s32[]{:T(128)}, bf16[4,2,257,4,104]{4,2,3,1,0:T(8,128)(2,1)}, ...), condition=%wide.region_5.6_spmd, body=%wide.region_2.5_spmd.sunk | while | flops 224564544 | bytes 23939440 | solution.py:193
  206.0 3.7 copy.160
  209.7 4.9 reshape.334
  214.7 6.1 convolution_convert_fusion
  244.0 8.8 collective-permute-done.17
  254.1 5.1 collective-permute-done.20
  264.0 11.9 %collective-permute-done.12 = bf16[2,257,1664]{2,0,1:T(2,128)(2,1)S(1)} collective-permute-done((bf16[2,257,1664]{2,0,1:T(2,128)(2,1)S(1)}, bf16[2,257,1664]{2,0,1:T(2,128)(2,1)S(1)}, u32[]{:S(2)}, u32[]{:S(2)}) %collective-permute-start.12) | collective-permute-done | bytes 1710624 | tf_op jit(solution)/shard_map/ppermute | solution.py:74
  286.1 11.4 %collective-permute-done.18 = bf16[2,1664,256]{2,1,0:T(8,128)(2,1)S(1)} collective-permute-done((bf16[2,1664,256]{2,1,0:T(8,128)(2,1)S(1)}, bf16[2,1664,256]{2,1,0:T(8,128)(2,1)S(1)}, u32[]{:S(2)}, u32[]{:S(2)}) %collective-permute-start.18) | collective-permute-done | bytes 1703968 | tf_op jit(solution)/shard_map/ppermute | solution.py:74
  299.6 19.6 %collective-permute-done.14 = bf16[2,257,1664]{2,0,1:T(2,128)(2,1)S(1)} collective-permute-done((bf16[2,257,1664]{2,0,1:T(2,128)(2,1)S(1)}, bf16[2,257,1664]{2,0,1:T(2,128)(2,1)S(1)}, u32[]{:S(2)}, u32[]{:S(2)}) %collective-permute-start.14) | collective-permute-done | bytes 1710624 | tf_op jit(solution)/shard_map/ppermute | solution.py:74
  324.1 26.8 %fusion.89 = (u8[257,2048]{1,0:T(8,128)(4,1)S(1)}, u8[257,2048]{1,0:T(8,128)(4,1)S(1)}, f32[8,257,2048]{2,1,0:T(8,128)}) fusion(f32[2048]{0:T(1024)S(1)} %constant_dynamic-update-slice_fusion.9, bf16[1664,2048]{1,0:T(8,128)(2,1)} %fusion.126, bf16[2,257,1664]{2,1,0:T(8,128)(2,1)S(1)} %copy.102, bf16[2,257,1664]{2,1,0:T(8,128)(2,1)S(1)} %copy.101, ...), kind=kOutput, calls=%fused_computation.120 | convolution fusion | flops 14081330176 | bytes 31561728 | tf_op jit(solution)/shard_map/isd,df->isf/dot_general | solution.py:204
  350.9 28.9 %convert_reduce_fusion = (f32[2048]{0:T(1024)}, bf16[8,257,2048]{2,1,0:T(8,128)(2,1)}) fusion(f32[8,257,2048]{2,1,0:T(8,128)} %get-tuple-element.354, f32[2048]{0:T(1024)S(1)} %constant_dynamic-update-slice_fusion.9, bf16[8,257,1664]{2,1,0:T(8,128)(2,1)S(1)} %bitcast.408, bf16[2048,1664]{1,0:T(8,128)(2,1)} %fusion.124), kind=kOutput, calls=%fused_computation.72 | convolution fusion | flops 14067906560 | bytes 38938624 | tf_op jit(solution)/shard_map/isd,fd->isf/dot_general | solution.py:216
  379.8 21.3 %fusion.82 = bf16[8,257,1664]{2,1,0:T(8,128)(2,1)} fusion(bf16[8,257,2048]{2,1,0:T(8,128)(2,1)} %get-tuple-element.356, bf16[1664,2048]{1,0:T(8,128)(2,1)} %fusion.126), kind=kOutput, calls=%fused_computation.109 | convolution fusion | flops 14016590848 | bytes 22079488 | tf_op jit(solution)/shard_map/isf,df->isd/dot_general | solution.py:223
  401.1 21.0 %bitcast_convert_fusion.2 = bf16[1664,2048]{1,0:T(8,128)(2,1)} fusion(bf16[8,257,2048]{2,1,0:T(8,128)(2,1)} %get-tuple-element.356, bf16[2,257,1664]{2,1,0:T(8,128)(2,1)S(1)} %copy.102, bf16[2,257,1664]{2,1,0:T(8,128)(2,1)S(1)} %copy.101, bf16[2,257,1664]{2,1,0:T(8,128)(2,1)S(1)} %copy.100, bf16[2,257,1664]{2,1,0:T(8,128)(2,1)S(1)} %add_convert_fusion.4), kind=kOutput, calls=%fused_computation.88 | convolution fusion | flops 14026841088 | bytes 22079488 | tf_op jit(solution)/shard_map/isd,isf->df/dot_general | solution.py:220
  422.1 41.5 %fusion.52 = bf16[8,257,2048]{2,1,0:T(8,128)(2,1)S(1)} fusion(f32[8,257,2048]{2,1,0:T(8,128)} %get-tuple-element.354, f32[2048]{0:T(1024)S(1)} %constant_dynamic-update-slice_fusion.9, u8[257,2048]{1,0:T(8,128)(4,1)S(1)} %get-tuple-element.189, u8[257,2048]{1,0:T(8,128)(4,1)S(1)} %get-tuple-element.188), kind=kLoop, calls=%fused_computation.60 | loop fusion | flops 298958848 | bytes 26324992 | tf_op jit(solution)/shard_map/convert_element_type | solution.py:206
  463.6 19.4 %fusion.85 = bf16[8,257,1664]{2,1,0:T(8,128)(2,1)S(1)} fusion(bf16[8,257,2048]{2,1,0:T(8,128)(2,1)S(1)} %fusion.52, bf16[2048,1664]{1,0:T(8,128)(2,1)} %fusion.124), kind=kOutput, calls=%fused_computation.110 | convolution fusion | flops 14016590848 | bytes 22079488 | tf_op jit(solution)/shard_map/isf,fd->isd/dot_general | solution.py:210
  483.0 21.0 %bitcast_convert_fusion.1 = bf16[2048,1664]{1,0:T(8,128)(2,1)S(1)} fusion(bf16[8,257,2048]{2,1,0:T(8,128)(2,1)S(1)} %fusion.52, bf16[8,257,1664]{2,1,0:T(8,128)(2,1)} %copy_dynamic-update-slice_fusion.1), kind=kOutput, calls=%fused_computation.87 | convolution fusion | flops 14016577536 | bytes 22079488 | tf_op jit(solution)/shard_map/isf,isd->fd/dot_general | solution.py:214
  507.3 5.7 slice_bitcast_fusion.16
  540.1 53.1 %collective-permute-done.59 = bf16[2,2,1664,256]{3,2,1,0:T(8,128)(2,1)} collective-permute-done((bf16[2,2,1664,256]{3,2,1,0:T(8,128)(2,1)}, bf16[2,2,1664,256]{3,2,1,0:T(8,128)(2,1)}, u32[]{:S(2)}, u32[]{:S(2)}) %collective-permute-start.59) | collective-permute-done | bytes 3407904 | tf_op jit(solution)/shard_map/ppermute | solution.py:74
  602.3 4.5 multiply_reduce_fusion.2
  606.8 25.1 %collective-permute-done.24 = bf16[2,257,1664]{2,0,1:T(2,128)(2,1)} collective-permute-done((bf16[2,257,1664]{2,0,1:T(2,128)(2,1)}, bf16[2,257,1664]{2,0,1:T(2,128)(2,1)}, u32[]{:S(2)}, u32[]{:S(2)}) %collective-permute-start.24) | collective-permute-done | bytes 1710624 | tf_op jit(solution)/shard_map/ppermute | solution.py:74
  631.9 5.5 convert_reduce_fusion.5
  651.6 58.3 %collective-permute-done.32 = bf16[2,257,1664]{2,0,1:T(2,128)(2,1)} collective-permute-done((bf16[2,257,1664]{2,0,1:T(2,128)(2,1)}, bf16[2,257,1664]{2,0,1:T(2,128)(2,1)}, u32[]{:S(2)}, u32[]{:S(2)}) %collective-permute-start.32) | collective-permute-done | bytes 1710624 | tf_op jit(solution)/shard_map/ppermute | solution.py:74
  712.9 7.1 collective-permute-done.67
  722.9 4.0 copy.143
  728.8 4.3 collective-permute-done.62
  735.7 6.4 collective-permute-done.68
  746.8 6.9 convolution_convert_fusion.1
  753.6 4.7 reshape.330
  758.3 50.4 %while.27 = (s32[]{:T(128)}, bf16[4,2,257,4,104]{4,2,3,1,0:T(8,128)(2,1)}, bf16[4,2,257,4,104]{4,3,2,1,0:T(4,128)(2,1)}, bf16[4,2,257,4,104]{4,2,3,1,0:T(8,128)(...) while((s32[]{:T(128)}, ...), condition=%wide.region_12.13_spmd, body=%wide.region_10.12_spmd.sunk | while | flops 556935424 | bytes 23353668 | solution.py:237
  817.3 4.5 reshape.332
  823.9 4.6 reshape.333
  832.4 12.8 %bitcast_convert_fusion = bf16[8,257,1664]{2,1,0:T(8,128)(2,1)S(1)} fusion(bf16[3,8,257,416]{3,2,0,1:T(8,128)(2,1)} %constant_dynamic-update-slice_fusion.5, bf16[3,1664,208]{1,2,0:T(8,128)(2,1)S(1)} %copy-done.61, bf16[3,1664,208]{1,2,0:T(8,128)(2,1)S(1)} %copy-done.60), kind=kOutput, calls=%fused_computation.86 | convolution fusion | flops 8551003136 | bytes 16127488 | tf_op jit(solution)/shard_map/nisc,ndc->isd/dot_general | solution.py:251
  845.3 20.3 %fusion.98 = bf16[3,1664,416]{1,2,0:T(8,128)(2,1)} fusion(bf16[3,8,257,416]{3,2,0,1:T(8,128)(2,1)} %constant_dynamic-update-slice_fusion.5, bf16[2,257,1664]{2,1,0:T(8,128)(2,1)} %copy-done.64, bf16[2,257,1664]{2,1,0:T(8,128)(2,1)S(1)} %copy-done.63, bf16[2,257,1664]{2,1,0:T(8,128)(2,1)} %copy.81, bf16[2,257,1664]{2,1,0:T(8,128)(2,1)S(1)} %copy-done.33), kind=kOutput, calls=%fused_computation.131 | convolution fusion | flops 8551615488 | bytes 16127488 | tf_op jit(solution)/shard_map/isd,nisc->ndc/dot_general | solution.py:244
  865.6 6.4 fusion.116
  881.6 6.2 collective-permute-done.48
  890.1 6.9 dynamic-slice_bitcast_fusion.13
  901.1 6.5 collective-permute-done.50
  908.6 7.3 collective-permute-done.51
  927.9 38.4 %collective-permute-done.42 = bf16[2,2,3,416,208]{3,4,2,1,0:T(8,128)(2,1)S(1)} collective-permute-done((bf16[2,2,3,416,208]{3,4,2,1,0:T(8,128)(2,1)S(1)}, bf16[2,2,3,416,208]{3,4,2,1,0:T(8,128)(2,1)S(1)}, u32[]{:S(2)}, u32[]{:S(2)}) %collective-permute-start.42) | collective-permute-done | bytes 2076704 | tf_op jit(solution)/shard_map/ppermute | solution.py:74
  970.8 6.6 pad_maximum_fusion.9
  981.0 9.4 collective-permute-done.43
  993.3 4.4 collective-permute-done.36
  997.7 4.1 fusion.110
  1003.5 5.3 convert_reduce_fusion.2
  1016.4 11.8 %collective-permute-done.40 = f32[6656]{0:T(1024)S(1)} collective-permute-done((f32[6656]{0:T(1024)S(1)}, f32[6656]{0:T(1024)S(1)}, u32[]{:S(2)}, u32[]{:S(2)}) %collective-permute-start.40) | collective-permute-done | bytes 26656 | tf_op jit(solution)/shard_map/ppermute | solution.py:74
  1031.7 13.1 %collective-permute-done.44 = bf16[3,416,208]{1,2,0:T(8,128)(2,1)S(1)} collective-permute-done((bf16[3,416,208]{1,2,0:T(8,128)(2,1)S(1)}, bf16[3,416,208]{1,2,0:T(8,128)(2,1)S(1)}, u32[]{:S(2)}, u32[]{:S(2)}) %collective-permute-start.44) | collective-permute-done | bytes 519200 | tf_op jit(solution)/shard_map/ppermute | solution.py:74
  1055.6 4.5 collective-permute-done.58
  1062.7 5.1 broadcast_select_fusion.3
  1067.8 22.8 %collective-permute-done.46 = bf16[2,3,416,208]{2,3,1,0:T(8,128)(2,1)S(1)} collective-permute-done((bf16[2,3,416,208]{2,3,1,0:T(8,128)(2,1)S(1)}, bf16[2,3,416,208]{2,3,1,0:T(8,128)(2,1)S(1)}, u32[]{:S(2)}, u32[]{:S(2)}) %collective-permute-start.46) | collective-permute-done | bytes 1038368 | tf_op jit(solution)/shard_map/ppermute | solution.py:74
  1092.7 5.2 concatenate.129
  1097.9 8.7 maximum_convert_fusion
  1106.6 6.9 broadcast_select_fusion.1
  1113.5 6.0 maximum_convert_fusion.1
  1122.1 3.9 maximum_convert_fusion.2
  (609 shorter events, 360.8 us)
Async XLA Ops:
  9.7 61.1 %collective-permute-start.4 = (bf16[2,257,1664]{2,0,1:T(2,128)(2,1)}, bf16[2,257,1664]{2,0,1:T(2,128)(2,1)}, u32[]{:S(2)}, u32[]{:S(2)}) collective-permute-start(bf16[2,257,1664]{2,0,1:T(2,128)(2,1)} %copy.79), channel_id=1, source_target_pairs={{0,1},{1,0},{2,3},{3,2},{4,5},{5,4},{6,7},{7,6},{8,9},{9,8},{10,11... | collective-permute-start | bytes 5131784 | tf_op jit(solution)/shard_map/ppermute | solution.py:74
  12.7 94.7 %collective-permute-start.3 = (bf16[2,257,1664]{2,0,1:T(2,128)(2,1)}, bf16[2,257,1664]{2,0,1:T(2,128)(2,1)}, u32[]{:S(2)}, u32[]{:S(2)}) collective-permute-start(bf16[2,257,1664]{2,0,1:T(2,128)(2,1)} %copy.79), channel_id=1, source_target_pairs={{0,4},{1,5},{2,6},{3,7},{4,0},{5,1},{6,2},{7,3},{8,12},{9,13},{10,... | collective-permute-start | bytes 5131784 | tf_op jit(solution)/shard_map/ppermute | solution.py:74
  14.2 50.1 %collective-permute-start = (bf16[3,416,208]{1,2,0:T(8,128)(2,1)S(1)}, bf16[3,416,208]{1,2,0:T(8,128)(2,1)}, u32[]{:S(2)}, u32[]{:S(2)}) collective-permute-start(bf16[3,416,208]{1,2,0:T(8,128)(2,1)S(1)} %constant_dynamic-slice_fusion.14), channel_id=1, source_target_pairs={{0,2},{1,3},{2,0},{3,1},{4,6},{5,7},{6,4},{7,5},{8,10},{9,11},{10,... | collective-permute-start | bytes 1557512 | tf_op jit(solution)/shard_map/ppermute | solution.py:74
  17.1 70.6 %collective-permute-start.6 = (f32[1440]{0:T(1024)S(1)}, f32[1440]{0:T(1024)S(1)}, u32[]{:S(2)}, u32[]{:S(2)}) collective-permute-start(f32[1440]{0:T(1024)S(1)} %pad_maximum_fusion.33), channel_id=1, source_target_pairs={{0,2},{1,3},{2,0},{3,1},{4,6},{5,7},{6,4},{7,5},{8,10},{9,11},{10,... | collective-permute-start | bytes 17288 | tf_op jit(solution)/shard_map/ppermute | solution.py:74
  19.2 54.3 %collective-permute-start.7 = (bf16[208,416]{1,0:T(8,128)(2,1)}, bf16[208,416]{1,0:T(8,128)(2,1)}, u32[]{:S(2)}, u32[]{:S(2)}) collective-permute-start(bf16[208,416]{1,0:T(8,128)(2,1)} %dynamic_slice.275), channel_id=1, source_target_pairs={{0,2},{1,3},{2,0},{3,1},{4,6},{5,7},{6,4},{7,5},{8,10},{9,11},{10,... | collective-permute-start | bytes 519176 | tf_op jit(solution)/shard_map/ppermute | solution.py:74
  64.3 14.4 %collective-permute-start.1 = (bf16[1,3,416,208]{2,3,1,0:T(8,128)(2,1)}, bf16[1,3,416,208]{2,3,1,0:T(8,128)(2,1)}, u32[]{:S(2)}, u32[]{:S(2)}) collective-permute-start(bf16[1,3,416,208]{2,3,1,0:T(8,128)(2,1)} %bitcast.17), channel_id=1, source_target_pairs={{0,8},{1,9},{2,10},{3,11},{4,12},{5,13},{6,14},{7,15},{8,0},{9,1},... | collective-permute-start | bytes 1557512 | tf_op jit(solution)/shard_map/ppermute | solution.py:74
  70.8 48.2 %collective-permute-start.5 = (bf16[2,257,1664]{2,0,1:T(2,128)(2,1)}, bf16[2,257,1664]{2,0,1:T(2,128)(2,1)}, u32[]{:S(2)}, u32[]{:S(2)}) collective-permute-start(bf16[2,257,1664]{2,0,1:T(2,128)(2,1)} %collective-permute-done.4), channel_id=1, source_target_pairs={{0,4},{1,5},{2,6},{3,7},{4,0},{5,1},{6,2},{7,3},{8,12},{9,13},{10,... | collective-permute-start | bytes 5131784 | tf_op jit(solution)/shard_map/ppermute | solution.py:74
  73.6 9.2 collective-permute-start.8
  81.2 29.0 %collective-permute-start.2 = (bf16[2,3,416,208]{2,3,1,0:T(8,128)(2,1)}, bf16[2,3,416,208]{2,3,1,0:T(8,128)(2,1)}, u32[]{:S(2)}, u32[]{:S(2)}) collective-permute-start(bf16[2,3,416,208]{2,3,1,0:T(8,128)(2,1)} %pad_maximum_fusion.19), channel_id=1, source_target_pairs={{0,16},{1,17},{2,18},{3,19},{4,20},{5,21},{6,22},{7,23},{8,24},{9,... | collective-permute-start | bytes 3115016 | tf_op jit(solution)/shard_map/ppermute | solution.py:74
  85.2 10.1 collective-permute-start.9
  87.7 143.7 %collective-permute-start.16 = (bf16[1664,256]{1,0:T(8,128)(2,1)}, bf16[1664,256]{1,0:T(8,128)(2,1)}, u32[]{:S(2)}, u32[]{:S(2)}) collective-permute-start(bf16[1664,256]{1,0:T(8,128)(2,1)} %get-tuple-element.238), channel_id=1, source_target_pairs={{0,2},{1,3},{2,0},{3,1},{4,6},{5,7},{6,4},{7,5},{8,10},{9,11},{10,... | collective-permute-start | bytes 2555912 | tf_op jit(solution)/shard_map/ppermute | solution.py:74
  95.3 167.7 %collective-permute-start.26 = (bf16[2,257,1664]{2,0,1:T(2,128)(2,1)S(1)}, bf16[2,257,1664]{2,0,1:T(2,128)(2,1)}, u32[]{:S(2)}, u32[]{:S(2)}) collective-permute-start(bf16[2,257,1664]{2,0,1:T(2,128)(2,1)S(1)} %copy-done.10), channel_id=1, source_target_pairs={{0,1},{1,0},{2,3},{3,2},{4,5},{5,4},{6,7},{7,6},{8,9},{9,8},{10,11... | collective-permute-start | bytes 5131784 | tf_op jit(solution)/shard_map/ppermute | solution.py:74
  107.4 130.7 %collective-permute-start.19 = (bf16[256,1664]{1,0:T(8,128)(2,1)}, bf16[256,1664]{1,0:T(8,128)(2,1)}, u32[]{:S(2)}, u32[]{:S(2)}) collective-permute-start(bf16[256,1664]{1,0:T(8,128)(2,1)} %get-tuple-element.234), channel_id=1, source_target_pairs={{0,2},{1,3},{2,0},{3,1},{4,6},{5,7},{6,4},{7,5},{8,10},{9,11},{10,... | collective-permute-start | bytes 2555912 | tf_op jit(solution)/shard_map/ppermute | solution.py:74
  222.3 11.0 collective-permute-start.11
  231.4 21.4 %collective-permute-start.17 = (bf16[1,1664,256]{2,1,0:T(8,128)(2,1)}, bf16[1,1664,256]{2,1,0:T(8,128)(2,1)S(1)}, u32[]{:S(2)}, u32[]{:S(2)}) collective-permute-start(bf16[1,1664,256]{2,1,0:T(8,128)(2,1)} %bitcast.32), channel_id=1, source_target_pairs={{0,8},{1,9},{2,10},{3,11},{4,12},{5,13},{6,14},{7,15},{8,0},{9,1},... | collective-permute-start | bytes 2555912 | tf_op jit(solution)/shard_map/ppermute | solution.py:74
  233.0 30.9 %collective-permute-start.10 = (bf16[2,257,1664]{2,0,1:T(2,128)(2,1)S(1)}, bf16[2,257,1664]{2,0,1:T(2,128)(2,1)S(1)}, u32[]{:S(2)}, u32[]{:S(2)}) collective-permute-start(bf16[2,257,1664]{2,0,1:T(2,128)(2,1)S(1)} %copy.92), channel_id=1, source_target_pairs={{0,4},{1,5},{2,6},{3,7},{4,0},{5,1},{6,2},{7,3},{8,12},{9,13},{10,... | collective-permute-start | bytes 5131784 | tf_op jit(solution)/shard_map/ppermute | solution.py:74
  235.0 40.9 %collective-permute-start.12 = (bf16[2,257,1664]{2,0,1:T(2,128)(2,1)S(1)}, bf16[2,257,1664]{2,0,1:T(2,128)(2,1)S(1)}, u32[]{:S(2)}, u32[]{:S(2)}) collective-permute-start(bf16[2,257,1664]{2,0,1:T(2,128)(2,1)S(1)} %copy.96), channel_id=1, source_target_pairs={{0,1},{1,0},{2,3},{3,2},{4,5},{5,4},{6,7},{7,6},{8,9},{9,8},{10,11... | collective-permute-start | bytes 5131784 | tf_op jit(solution)/shard_map/ppermute | solution.py:74
  238.1 21.1 %collective-permute-start.20 = (bf16[1,256,1664]{2,1,0:T(8,128)(2,1)}, bf16[1,256,1664]{2,1,0:T(8,128)(2,1)S(1)}, u32[]{:S(2)}, u32[]{:S(2)}) collective-permute-start(bf16[1,256,1664]{2,1,0:T(8,128)(2,1)} %bitcast.37), channel_id=1, source_target_pairs={{0,16},{1,17},{2,18},{3,19},{4,20},{5,21},{6,22},{7,23},{8,24},{9,... | collective-permute-start | bytes 2555912 | tf_op jit(solution)/shard_map/ppermute | solution.py:74
  252.8 29.0 %collective-permute-start.25 = (bf16[2,257,1664]{2,0,1:T(2,128)(2,1)S(1)}, bf16[2,257,1664]{2,0,1:T(2,128)(2,1)S(1)}, u32[]{:S(2)}, u32[]{:S(2)}) collective-permute-start(bf16[2,257,1664]{2,0,1:T(2,128)(2,1)S(1)} %copy-done.10), channel_id=1, source_target_pairs={{0,4},{1,5},{2,6},{3,7},{4,0},{5,1},{6,2},{7,3},{8,12},{9,13},{10,... | collective-permute-start | bytes 5131784 | tf_op jit(solution)/shard_map/ppermute | solution.py:74
  259.2 38.3 %collective-permute-start.18 = (bf16[2,1664,256]{2,1,0:T(8,128)(2,1)S(1)}, bf16[2,1664,256]{2,1,0:T(8,128)(2,1)S(1)}, u32[]{:S(2)}, u32[]{:S(2)}) collective-permute-start(bf16[2,1664,256]{2,1,0:T(8,128)(2,1)S(1)} %pad_maximum_fusion.15), channel_id=1, source_target_pairs={{0,16},{1,17},{2,18},{3,19},{4,20},{5,21},{6,22},{7,23},{8,24},{9,... | collective-permute-start | bytes 5111816 | tf_op jit(solution)/shard_map/ppermute | solution.py:74
  263.0 56.1 %collective-permute-start.21 = (bf16[2,256,1664]{2,1,0:T(8,128)(2,1)S(1)}, bf16[2,256,1664]{2,1,0:T(8,128)(2,1)S(1)}, u32[]{:S(2)}, u32[]{:S(2)}) collective-permute-start(bf16[2,256,1664]{2,1,0:T(8,128)(2,1)S(1)} %pad_maximum_fusion.16), channel_id=1, source_target_pairs={{0,8},{1,9},{2,10},{3,11},{4,12},{5,13},{6,14},{7,15},{8,0},{9,1},... | collective-permute-start | bytes 5111816 | tf_op jit(solution)/shard_map/ppermute | solution.py:74
  264.0 58.2 %collective-permute-start.27 = (bf16[2,257,1664]{2,0,1:T(2,128)(2,1)}, bf16[2,257,1664]{2,0,1:T(2,128)(2,1)S(1)}, u32[]{:S(2)}, u32[]{:S(2)}) collective-permute-start(bf16[2,257,1664]{2,0,1:T(2,128)(2,1)} %collective-permute-done.26), channel_id=1, source_target_pairs={{0,4},{1,5},{2,6},{3,7},{4,0},{5,1},{6,2},{7,3},{8,12},{9,13},{10,... | collective-permute-start | bytes 5131784 | tf_op jit(solution)/shard_map/ppermute | solution.py:74
  280.0 39.1 %collective-permute-start.14 = (bf16[2,257,1664]{2,0,1:T(2,128)(2,1)S(1)}, bf16[2,257,1664]{2,0,1:T(2,128)(2,1)S(1)}, u32[]{:S(2)}, u32[]{:S(2)}) collective-permute-start(bf16[2,257,1664]{2,0,1:T(2,128)(2,1)S(1)} %copy.98), channel_id=1, source_target_pairs={{0,1},{1,0},{2,3},{3,2},{4,5},{5,4},{6,7},{7,6},{8,9},{9,8},{10,11... | collective-permute-start | bytes 5131784 | tf_op jit(solution)/shard_map/ppermute | solution.py:74
  299.6 24.1 %collective-permute-start.13 = (bf16[2,257,1664]{2,0,1:T(2,128)(2,1)S(1)}, bf16[2,257,1664]{2,0,1:T(2,128)(2,1)S(1)}, u32[]{:S(2)}, u32[]{:S(2)}) collective-permute-start(bf16[2,257,1664]{2,0,1:T(2,128)(2,1)S(1)} %copy.98), channel_id=1, source_target_pairs={{0,4},{1,5},{2,6},{3,7},{4,0},{5,1},{6,2},{7,3},{8,12},{9,13},{10,... | collective-permute-start | bytes 5131784 | tf_op jit(solution)/shard_map/ppermute | solution.py:74
  506.8 25.6 %collective-permute-start.29 = (bf16[2,257,1664]{2,0,1:T(2,128)(2,1)}, bf16[2,257,1664]{2,0,1:T(2,128)(2,1)}, u32[]{:S(2)}, u32[]{:S(2)}) collective-permute-start(bf16[2,257,1664]{2,0,1:T(2,128)(2,1)} %copy.116), channel_id=1, source_target_pairs={{0,4},{1,5},{2,6},{3,7},{4,0},{5,1},{6,2},{7,3},{8,12},{9,13},{10,... | collective-permute-start | bytes 5131784 | tf_op jit(solution)/shard_map/ppermute | solution.py:74
  517.3 75.9 %collective-permute-start.59 = (bf16[2,2,1664,256]{3,2,1,0:T(8,128)(2,1)}, bf16[2,2,1664,256]{3,2,1,0:T(8,128)(2,1)}, u32[]{:S(2)}, u32[]{:S(2)}) collective-permute-start(bf16[2,2,1664,256]{3,2,1,0:T(8,128)(2,1)} %pad_maximum_fusion.4), channel_id=1, source_target_pairs={{0,8},{1,9},{2,10},{3,11},{4,12},{5,13},{6,14},{7,15},{8,0},{9,1},... | collective-permute-start | bytes 10223624 | tf_op jit(solution)/shard_map/ppermute | solution.py:74
  523.8 75.4 %collective-permute-start.65 = (bf16[2,2,256,1664]{3,2,1,0:T(8,128)(2,1)S(1)}, bf16[2,2,256,1664]{3,2,1,0:T(8,128)(2,1)S(1)}, u32[]{:S(2)}, u32[]{:S(2)}) collective-permute-start(bf16[2,2,256,1664]{3,2,1,0:T(8,128)(2,1)S(1)} %pad_maximum_fusion.7), channel_id=1, source_target_pairs={{0,16},{1,17},{2,18},{3,19},{4,20},{5,21},{6,22},{7,23},{8,24},{9,... | collective-permute-start | bytes 10223624 | tf_op jit(solution)/shard_map/ppermute | solution.py:74
  526.9 8.7 collective-permute-start.23
  529.5 71.6 %collective-permute-start.28 = (bf16[2,257,1664]{2,0,1:T(2,128)(2,1)}, bf16[2,257,1664]{2,0,1:T(2,128)(2,1)}, u32[]{:S(2)}, u32[]{:S(2)}) collective-permute-start(bf16[2,257,1664]{2,0,1:T(2,128)(2,1)} %copy.114), channel_id=1, source_target_pairs={{0,4},{1,5},{2,6},{3,7},{4,0},{5,1},{6,2},{7,3},{8,12},{9,13},{10,... | collective-permute-start | bytes 5131784 | tf_op jit(solution)/shard_map/ppermute | solution.py:74
  532.5 74.4 %collective-permute-start.22 = (bf16[2,257,1664]{2,0,1:T(2,128)(2,1)}, bf16[2,257,1664]{2,0,1:T(2,128)(2,1)}, u32[]{:S(2)}, u32[]{:S(2)}) collective-permute-start(bf16[2,257,1664]{2,0,1:T(2,128)(2,1)} %copy.103), channel_id=1, source_target_pairs={{0,4},{1,5},{2,6},{3,7},{4,0},{5,1},{6,2},{7,3},{8,12},{9,13},{10,... | collective-permute-start | bytes 5131784 | tf_op jit(solution)/shard_map/ppermute | solution.py:74
  535.6 66.7 %collective-permute-start.30 = (bf16[2,257,1664]{2,0,1:T(2,128)(2,1)S(1)}, bf16[2,257,1664]{2,0,1:T(2,128)(2,1)}, u32[]{:S(2)}, u32[]{:S(2)}) collective-permute-start(bf16[2,257,1664]{2,0,1:T(2,128)(2,1)S(1)} %copy.118), channel_id=1, source_target_pairs={{0,1},{1,0},{2,3},{3,2},{4,5},{5,4},{6,7},{7,6},{8,9},{9,8},{10,11... | collective-permute-start | bytes 5131784 | tf_op jit(solution)/shard_map/ppermute | solution.py:74
  593.2 38.7 %collective-permute-start.24 = (bf16[2,257,1664]{2,0,1:T(2,128)(2,1)}, bf16[2,257,1664]{2,0,1:T(2,128)(2,1)}, u32[]{:S(2)}, u32[]{:S(2)}) collective-permute-start(bf16[2,257,1664]{2,0,1:T(2,128)(2,1)} %copy.107), channel_id=1, source_target_pairs={{0,1},{1,0},{2,3},{3,2},{4,5},{5,4},{6,7},{7,6},{8,9},{9,8},{10,11... | collective-permute-start | bytes 5131784 | tf_op jit(solution)/shard_map/ppermute | solution.py:74
  599.2 42.2 %collective-permute-start.60 = (bf16[1,2,1664,256]{3,2,1,0:T(8,128)(2,1)}, bf16[1,2,1664,256]{3,2,1,0:T(8,128)(2,1)}, u32[]{:S(2)}, u32[]{:S(2)}) collective-permute-start(bf16[1,2,1664,256]{3,2,1,0:T(8,128)(2,1)} %add_convert_fusion.7), channel_id=1, source_target_pairs={{0,16},{1,17},{2,18},{3,19},{4,20},{5,21},{6,22},{7,23},{8,24},{9,... | collective-permute-start | bytes 5111816 | tf_op jit(solution)/shard_map/ppermute | solution.py:74
  601.1 44.7 %collective-permute-start.66 = (bf16[1,2,256,1664]{3,2,1,0:T(8,128)(2,1)S(1)}, bf16[1,2,256,1664]{3,2,1,0:T(8,128)(2,1)}, u32[]{:S(2)}, u32[]{:S(2)}) collective-permute-start(bf16[1,2,256,1664]{3,2,1,0:T(8,128)(2,1)S(1)} %add_convert_fusion.6), channel_id=1, source_target_pairs={{0,8},{1,9},{2,10},{3,11},{4,12},{5,13},{6,14},{7,15},{8,0},{9,1},... | collective-permute-start | bytes 5111816 | tf_op jit(solution)/shard_map/ppermute | solution.py:74
  639.9 70.0 %collective-permute-start.32 = (bf16[2,257,1664]{2,0,1:T(2,128)(2,1)}, bf16[2,257,1664]{2,0,1:T(2,128)(2,1)}, u32[]{:S(2)}, u32[]{:S(2)}) collective-permute-start(bf16[2,257,1664]{2,0,1:T(2,128)(2,1)} %copy.120), channel_id=1, source_target_pairs={{0,1},{1,0},{2,3},{3,2},{4,5},{5,4},{6,7},{7,6},{8,9},{9,8},{10,11... | collective-permute-start | bytes 5131784 | tf_op jit(solution)/shard_map/ppermute | solution.py:74
  645.1 64.8 %collective-permute-start.61 = (bf16[1664,256]{1,0:T(8,128)(2,1)}, bf16[1664,256]{1,0:T(8,128)(2,1)}, u32[]{:S(2)}, u32[]{:S(2)}) collective-permute-start(bf16[1664,256]{1,0:T(8,128)(2,1)} %slice_bitcast_fusion.13), channel_id=1, source_target_pairs={{0,2},{1,3},{2,0},{3,1},{4,6},{5,7},{6,4},{7,5},{8,10},{9,11},{10,... | collective-permute-start | bytes 2555912 | tf_op jit(solution)/shard_map/ppermute | solution.py:74
  649.4 70.6 %collective-permute-start.67 = (bf16[256,1664]{1,0:T(8,128)(2,1)}, bf16[256,1664]{1,0:T(8,128)(2,1)}, u32[]{:S(2)}, u32[]{:S(2)}) collective-permute-start(bf16[256,1664]{1,0:T(8,128)(2,1)} %slice_bitcast_fusion.3), channel_id=1, source_target_pairs={{0,2},{1,3},{2,0},{3,1},{4,6},{5,7},{6,4},{7,5},{8,10},{9,11},{10,... | collective-permute-start | bytes 2555912 | tf_op jit(solution)/shard_map/ppermute | solution.py:74
  651.6 76.9 %collective-permute-start.31 = (bf16[2,257,1664]{2,0,1:T(2,128)(2,1)}, bf16[2,257,1664]{2,0,1:T(2,128)(2,1)S(1)}, u32[]{:S(2)}, u32[]{:S(2)}) collective-permute-start(bf16[2,257,1664]{2,0,1:T(2,128)(2,1)} %copy.120), channel_id=1, source_target_pairs={{0,4},{1,5},{2,6},{3,7},{4,0},{5,1},{6,2},{7,3},{8,12},{9,13},{10,... | collective-permute-start | bytes 5131784 | tf_op jit(solution)/shard_map/ppermute | solution.py:74
  710.0 35.4 %collective-permute-start.33 = (bf16[2,257,1664]{2,0,1:T(2,128)(2,1)}, bf16[2,257,1664]{2,0,1:T(2,128)(2,1)S(1)}, u32[]{:S(2)}, u32[]{:S(2)}) collective-permute-start(bf16[2,257,1664]{2,0,1:T(2,128)(2,1)} %collective-permute-done.32), channel_id=1, source_target_pairs={{0,4},{1,5},{2,6},{3,7},{4,0},{5,1},{6,2},{7,3},{8,12},{9,13},{10,... | collective-permute-start | bytes 5131784 | tf_op jit(solution)/shard_map/ppermute | solution.py:74
  711.6 21.4 %collective-permute-start.62 = (bf16[1,1664,256]{2,1,0:T(8,128)(2,1)S(1)}, bf16[1,1664,256]{2,1,0:T(8,128)(2,1)S(1)}, u32[]{:S(2)}, u32[]{:S(2)}) collective-permute-start(bf16[1,1664,256]{2,1,0:T(8,128)(2,1)S(1)} %fusion.122), channel_id=1, source_target_pairs={{0,16},{1,17},{2,18},{3,19},{4,20},{5,21},{6,22},{7,23},{8,24},{9,... | collective-permute-start | bytes 2555912 | tf_op jit(solution)/shard_map/ppermute | solution.py:74
  721.6 20.5 %collective-permute-start.68 = (bf16[1,256,1664]{2,1,0:T(8,128)(2,1)S(1)}, bf16[1,256,1664]{2,1,0:T(8,128)(2,1)S(1)}, u32[]{:S(2)}, u32[]{:S(2)}) collective-permute-start(bf16[1,256,1664]{2,1,0:T(8,128)(2,1)S(1)} %fusion.123), channel_id=1, source_target_pairs={{0,8},{1,9},{2,10},{3,11},{4,12},{5,13},{6,14},{7,15},{8,0},{9,1},... | collective-permute-start | bytes 2555912 | tf_op jit(solution)/shard_map/ppermute | solution.py:74
  734.5 182.0 %collective-permute-start.63 = (bf16[2,1664,256]{2,1,0:T(8,128)(2,1)}, bf16[2,1664,256]{2,1,0:T(8,128)(2,1)}, u32[]{:S(2)}, u32[]{:S(2)}) collective-permute-start(bf16[2,1664,256]{2,1,0:T(8,128)(2,1)} %pad_maximum_fusion.17), channel_id=1, source_target_pairs={{0,8},{1,9},{2,10},{3,11},{4,12},{5,13},{6,14},{7,15},{8,0},{9,1},... | collective-permute-start | bytes 5111816 | tf_op jit(solution)/shard_map/ppermute | solution.py:74
  743.6 224.6 %collective-permute-start.69 = (bf16[2,256,1664]{2,1,0:T(8,128)(2,1)}, bf16[2,256,1664]{2,1,0:T(8,128)(2,1)}, u32[]{:S(2)}, u32[]{:S(2)}) collective-permute-start(bf16[2,256,1664]{2,1,0:T(8,128)(2,1)} %pad_maximum_fusion.18), channel_id=1, source_target_pairs={{0,16},{1,17},{2,18},{3,19},{4,20},{5,21},{6,22},{7,23},{8,24},{9,... | collective-permute-start | bytes 5111816 | tf_op jit(solution)/shard_map/ppermute | solution.py:74
  873.9 14.0 %collective-permute-start.48 = (bf16[2,2,208,416]{3,2,1,0:T(8,128)(2,1)S(1)}, bf16[2,2,208,416]{3,2,1,0:T(8,128)(2,1)S(1)}, u32[]{:S(2)}, u32[]{:S(2)}) collective-permute-start(bf16[2,2,208,416]{3,2,1,0:T(8,128)(2,1)S(1)} %pad_maximum_fusion.28), channel_id=1, source_target_pairs={{0,16},{1,17},{2,18},{3,19},{4,20},{5,21},{6,22},{7,23},{8,24},{9,... | collective-permute-start | bytes 2076680 | tf_op jit(solution)/shard_map/ppermute | solution.py:74
  877.0 46.0 %collective-permute-start.35 = (bf16[2,257,1664]{2,0,1:T(2,128)(2,1)}, bf16[2,257,1664]{2,0,1:T(2,128)(2,1)}, u32[]{:S(2)}, u32[]{:S(2)}) collective-permute-start(bf16[2,257,1664]{2,0,1:T(2,128)(2,1)} %copy.138), channel_id=1, source_target_pairs={{0,4},{1,5},{2,6},{3,7},{4,0},{5,1},{6,2},{7,3},{8,12},{9,13},{10,... | collective-permute-start | bytes 5131784 | tf_op jit(solution)/shard_map/ppermute | solution.py:74
  879.5 113.8 %collective-permute-start.34 = (bf16[2,257,1664]{2,0,1:T(2,128)(2,1)}, bf16[2,257,1664]{2,0,1:T(2,128)(2,1)}, u32[]{:S(2)}, u32[]{:S(2)}) collective-permute-start(bf16[2,257,1664]{2,0,1:T(2,128)(2,1)} %copy.136), channel_id=1, source_target_pairs={{0,4},{1,5},{2,6},{3,7},{4,0},{5,1},{6,2},{7,3},{8,12},{9,13},{10,... | collective-permute-start | bytes 5131784 | tf_op jit(solution)/shard_map/ppermute | solution.py:74
  888.0 9.2 collective-permute-start.49
  899.1 8.5 collective-permute-start.50
  907.7 8.3 collective-permute-start.51
  916.0 50.3 %collective-permute-start.42 = (bf16[2,2,3,416,208]{3,4,2,1,0:T(8,128)(2,1)S(1)}, bf16[2,2,3,416,208]{3,4,2,1,0:T(8,128)(2,1)S(1)}, u32[]{:S(2)}, u32[]{:S(2)}) collective-permute-start(bf16[2,2,3,416,208]{3,4,2,1,0:T(8,128)(2,1)S(1)} %pad_maximum_fusion.13), channel_id=1, source_target_pairs={{0,8},{1,9},{2,10},{3,11},{4,12},{5,13},{6,14},{7,15},{8,0},{9,1},... | collective-permute-start | bytes 6230024 | tf_op jit(solution)/shard_map/ppermute | solution.py:74
  916.5 60.9 %collective-permute-start.52 = (bf16[2,208,416]{2,1,0:T(8,128)(2,1)S(1)}, bf16[2,208,416]{2,1,0:T(8,128)(2,1)S(1)}, u32[]{:S(2)}, u32[]{:S(2)}) collective-permute-start(bf16[2,208,416]{2,1,0:T(8,128)(2,1)S(1)} %pad_maximum_fusion.31), channel_id=1, source_target_pairs={{0,16},{1,17},{2,18},{3,19},{4,20},{5,21},{6,22},{7,23},{8,24},{9,... | collective-permute-start | bytes 1038344 | tf_op jit(solution)/shard_map/ppermute | solution.py:74
  923.0 139.7 %collective-permute-start.64 = (bf16[1664,1024]{1,0:T(8,128)(2,1)}, bf16[1664,1024]{1,0:T(8,128)(2,1)}, u32[]{:S(2)}, u32[]{:S(2)}) collective-permute-start(bf16[1664,1024]{1,0:T(8,128)(2,1)} %pad_maximum_fusion.6), channel_id=1, source_target_pairs={{0,4},{1,5},{2,6},{3,7},{4,0},{5,1},{6,2},{7,3},{8,12},{9,13},{10,... | collective-permute-start | bytes 10223624 | tf_op jit(solution)/shard_map/ppermute | solution.py:74
  966.2 31.4 %collective-permute-start.36 = (bf16[2,257,1664]{2,0,1:T(2,128)(2,1)}, bf16[2,257,1664]{2,0,1:T(2,128)(2,1)S(1)}, u32[]{:S(2)}, u32[]{:S(2)}) collective-permute-start(bf16[2,257,1664]{2,0,1:T(2,128)(2,1)} %copy.140), channel_id=1, source_target_pairs={{0,1},{1,0},{2,3},{3,2},{4,5},{5,4},{6,7},{7,6},{8,9},{9,8},{10,11... | collective-permute-start | bytes 5131784 | tf_op jit(solution)/shard_map/ppermute | solution.py:74
  968.1 22.3 %collective-permute-start.43 = (bf16[1,2,3,416,208]{3,4,2,1,0:T(8,128)(2,1)}, bf16[1,2,3,416,208]{3,4,2,1,0:T(8,128)(2,1)}, u32[]{:S(2)}, u32[]{:S(2)}) collective-permute-start(bf16[1,2,3,416,208]{3,4,2,1,0:T(8,128)(2,1)} %add_convert_fusion.8), channel_id=1, source_target_pairs={{0,16},{1,17},{2,18},{3,19},{4,20},{5,21},{6,22},{7,23},{8,24},{9,... | collective-permute-start | bytes 3115016 | tf_op jit(solution)/shard_map/ppermute | solution.py:74
  977.5 129.2 %collective-permute-start.70 = (bf16[1024,1664]{1,0:T(8,128)(2,1)}, bf16[1024,1664]{1,0:T(8,128)(2,1)}, u32[]{:S(2)}, u32[]{:S(2)}) collective-permute-start(bf16[1024,1664]{1,0:T(8,128)(2,1)} %pad_maximum_fusion.9), channel_id=1, source_target_pairs={{0,4},{1,5},{2,6},{3,7},{4,0},{5,1},{6,2},{7,3},{8,12},{9,13},{10,... | collective-permute-start | bytes 10223624 | tf_op jit(solution)/shard_map/ppermute | solution.py:74
  990.4 25.0 %collective-permute-start.53 = (bf16[208,1664]{1,0:T(8,128)(2,1)}, bf16[208,1664]{1,0:T(8,128)(2,1)S(1)}, u32[]{:S(2)}, u32[]{:S(2)}) collective-permute-start(bf16[208,1664]{1,0:T(8,128)(2,1)} %concatenate.132), channel_id=1, source_target_pairs={{0,4},{1,5},{2,6},{3,7},{4,0},{5,1},{6,2},{7,3},{8,12},{9,13},{10,... | collective-permute-start | bytes 2076680 | tf_op jit(solution)/shard_map/ppermute | solution.py:74
  1014.5 30.3 %collective-permute-start.44 = (bf16[3,416,208]{1,2,0:T(8,128)(2,1)S(1)}, bf16[3,416,208]{1,2,0:T(8,128)(2,1)S(1)}, u32[]{:S(2)}, u32[]{:S(2)}) collective-permute-start(bf16[3,416,208]{1,2,0:T(8,128)(2,1)S(1)} %slice_bitcast_fusion.27), channel_id=1, source_target_pairs={{0,2},{1,3},{2,0},{3,1},{4,6},{5,7},{6,4},{7,5},{8,10},{9,11},{10,... | collective-permute-start | bytes 1557512 | tf_op jit(solution)/shard_map/ppermute | solution.py:74
  1014.5 17.1 %collective-permute-start.55 = (f32[14848]{0:T(1024)S(1)}, f32[14848]{0:T(1024)S(1)}, u32[]{:S(2)}, u32[]{:S(2)}) collective-permute-start(f32[14848]{0:T(1024)S(1)} %add.473), channel_id=1, source_target_pairs={{0,16},{1,17},{2,18},{3,19},{4,20},{5,21},{6,22},{7,23},{8,24},{9,... | collective-permute-start | bytes 178184 | tf_op jit(solution)/shard_map/ppermute | solution.py:74
  1015.4 12.8 %collective-permute-start.40 = (f32[6656]{0:T(1024)S(1)}, f32[6656]{0:T(1024)S(1)}, u32[]{:S(2)}, u32[]{:S(2)}) collective-permute-start(f32[6656]{0:T(1024)S(1)} %add.454), channel_id=1, source_target_pairs={{0,1},{1,0},{2,3},{3,2},{4,5},{5,4},{6,7},{7,6},{8,9},{9,8},{10,11... | collective-permute-start | bytes 79880 | tf_op jit(solution)/shard_map/ppermute | solution.py:74
  1028.3 22.2 %collective-permute-start.41 = (f32[6656]{0:T(1024)S(1)}, f32[6656]{0:T(1024)S(1)}, u32[]{:S(2)}, u32[]{:S(2)}) collective-permute-start(f32[6656]{0:T(1024)S(1)} %add.455), channel_id=1, source_target_pairs={{0,2},{1,3},{2,0},{3,1},{4,6},{5,7},{6,4},{7,5},{8,10},{9,11},{10,... | collective-permute-start | bytes 79880 | tf_op jit(solution)/shard_map/ppermute | solution.py:74
  1031.7 18.9 %collective-permute-start.56 = (f32[14848]{0:T(1024)S(1)}, f32[14848]{0:T(1024)S(1)}, u32[]{:S(2)}, u32[]{:S(2)}) collective-permute-start(f32[14848]{0:T(1024)S(1)} %add.474), channel_id=1, source_target_pairs={{0,4},{1,5},{2,6},{3,7},{4,0},{5,1},{6,2},{7,3},{8,12},{9,13},{10,... | collective-permute-start | bytes 178184 | tf_op jit(solution)/shard_map/ppermute | solution.py:74
  1045.0 16.3 %collective-permute-start.45 = (bf16[1,3,416,208]{2,3,1,0:T(8,128)(2,1)S(1)}, bf16[1,3,416,208]{2,3,1,0:T(8,128)(2,1)S(1)}, u32[]{:S(2)}, u32[]{:S(2)}) collective-permute-start(bf16[1,3,416,208]{2,3,1,0:T(8,128)(2,1)S(1)} %fusion.130), channel_id=1, source_target_pairs={{0,16},{1,17},{2,18},{3,19},{4,20},{5,21},{6,22},{7,23},{8,24},{9,... | collective-permute-start | bytes 1557512 | tf_op jit(solution)/shard_map/ppermute | solution.py:74
  1061.4 29.1 %collective-permute-start.46 = (bf16[2,3,416,208]{2,3,1,0:T(8,128)(2,1)S(1)}, bf16[2,3,416,208]{2,3,1,0:T(8,128)(2,1)S(1)}, u32[]{:S(2)}, u32[]{:S(2)}) collective-permute-start(bf16[2,3,416,208]{2,3,1,0:T(8,128)(2,1)S(1)} %pad_maximum_fusion.20), channel_id=1, source_target_pairs={{0,8},{1,9},{2,10},{3,11},{4,12},{5,13},{6,14},{7,15},{8,0},{9,1},... | collective-permute-start | bytes 3115016 | tf_op jit(solution)/shard_map/ppermute | solution.py:74
  1097.9 21.6 %collective-permute-start.47 = (bf16[3,1664,208]{1,2,0:T(8,128)(2,1)}, bf16[3,1664,208]{1,2,0:T(8,128)(2,1)}, u32[]{:S(2)}, u32[]{:S(2)}) collective-permute-start(bf16[3,1664,208]{1,2,0:T(8,128)(2,1)} %concatenate.129), channel_id=1, source_target_pairs={{0,4},{1,5},{2,6},{3,7},{4,0},{5,1},{6,2},{7,3},{8,12},{9,13},{10,... | collective-permute-start | bytes 6230024 | tf_op jit(solution)/shard_map/ppermute | solution.py:74
  (124 other events, 1705.8 us)

commit v2 on v0

v2 whole, which is shorter than its diff:
```python
import functools

import jax
import jax.numpy as jnp
from jax import lax
from jax.experimental import pallas as pl
from jax.experimental.pallas import tpu as pltpu
from jax.sharding import PartitionSpec as P

HD = 104
PAD = 16
BF = jnp.bfloat16
F32 = jnp.float32


def dot(a, b, ca, cb):
    return lax.dot_general(a, b, (((ca,), (cb,)), ((), ())), preferred_element_type=F32)


def whole_spec(shape):
    return pl.BlockSpec(shape, lambda *_: (0,) * len(shape), pipeline_mode=pl.Buffered(1))


def head_mask(heads):
    lane = lax.broadcasted_iota(jnp.int32, (8, heads * HD), 1)
    row = lax.broadcasted_iota(jnp.int32, (8, heads * HD), 0)
    return (lane >= row * HD) & (lane < row * HD + HD)


def attend_fwd_kernel(n_i, main, heads, n_add, n_ref, w_ref, b_ref, wo_ref, *refs):
    adds = refs[:n_add]
    qkv_ref, ho_ref, lse_ref, lset_ref, out_ref = refs[n_add:]
    hc = heads * HD
    tail = pl.ds(n_i * main, PAD)
    qkv_ref[...] = (dot(n_ref[...], w_ref[...], 1, 0) + b_ref[...]).astype(BF)
    ho_ref[tail, :] = jnp.zeros((PAD, hc), BF)
    factor = HD ** -0.5
    tail_row = lax.broadcasted_iota(jnp.int32, (PAD, 1), 0)
    per_head = head_mask(heads)

    def image(i, carry):
        rows = pl.ds(pl.multiple_of(i * main, main), main)
        here = tail_row == i
        bar = jnp.where(here, 0.0, -1e30)
        bar_all = jnp.concatenate([jnp.zeros((main, 1), F32), bar], 0)

        def both(cols):
            return jnp.concatenate([qkv_ref[rows, cols], qkv_ref[tail, cols]], 0)

        q_t = jnp.sum(jnp.where(here, qkv_ref[tail, 0:hc].astype(F32), 0.0), 0, keepdims=True)
        q_b = jnp.where(per_head, q_t, 0.0).astype(BF)
        s = dot(both(slice(hc, 2 * hc)), q_b, 1, 1) * factor + bar_all
        top = jnp.max(s, 0, keepdims=True)
        e = jnp.exp(s - top)
        total = jnp.sum(e, 0, keepdims=True)
        o = dot((e * (1.0 / total)).astype(BF), both(slice(2 * hc, 3 * hc)), 0, 0)
        o = jnp.sum(jnp.where(per_head, o, 0.0), 0, keepdims=True).astype(BF)
        ho_ref[tail, :] = jnp.where(here, o, ho_ref[tail, :])
        lset_ref[pl.ds(i, 1), 0:8] = top + jnp.log(total)
        for h in range(heads):
            cols = [slice(t * hc + h * HD, t * hc + (h + 1) * HD) for t in range(3)]
            q = qkv_ref[rows, cols[0]]
            s = dot(qkv_ref[rows, cols[1]], q, 1, 1) * factor
            s_t = dot(qkv_ref[tail, cols[1]], q, 1, 1) * factor + bar
            top = jnp.maximum(jnp.max(s, 0, keepdims=True), jnp.max(s_t, 0, keepdims=True))
            e, e_t = jnp.exp(s - top), jnp.exp(s_t - top)
            total = jnp.sum(e, 0, keepdims=True) + jnp.sum(e_t, 0, keepdims=True)
            inv = 1.0 / total
            o = dot((e * inv).astype(BF), qkv_ref[rows, cols[2]], 0, 0)
            o = o + dot((e_t * inv).astype(BF), qkv_ref[tail, cols[2]], 0, 0)
            ho_ref[rows, h * HD : (h + 1) * HD] = o.astype(BF)
            lse_ref[h : h + 1, rows] = top + jnp.log(total)
        return carry

    lax.fori_loop(0, n_i, image, 0)
    total = dot(ho_ref[...], wo_ref[0:hc, :], 1, 0)
    for ref in adds:
        total = total + ref[...].astype(F32)
    out_ref[...] = total.astype(BF)


def attend_fwd(n_i, n, w, b, wo, adds=()):
    rows, width = n.shape
    hc = w.shape[1] // 3
    main = (rows - PAD) // n_i
    shapes = (
        ((rows, 3 * hc), BF),
        ((rows, hc), BF),
        ((8, n_i * main), F32),
        ((8, 128), F32),
        ((rows, width), BF),
    )
    flops = 2 * rows * width * 4 * hc + 4 * n_i * main * main * hc
    return call(
        functools.partial(attend_fwd_kernel, n_i, main, hc // HD, len(adds)),
        [n, w, b, wo, *adds],
        shapes,
        flops=flops,
        name="attend_fwd",
    )


def attend_bwd_kernel(n_i, main, heads, n_half, n_add, g_ref, *refs):
    halves = [refs[5 * k : 5 * k + 5] for k in range(n_half)]
    adds = refs[5 * n_half : 5 * n_half + n_add]
    refs = refs[5 * n_half + n_add :]
    total = None
    for k, half in enumerate(halves):
        attend_bwd_half(n_i, main, heads, g_ref, *half, refs[2 * k], refs[2 * k + 1], *refs[-2:])
        part = dot(refs[2 * k][...], half[3][...], 1, 1)
        total = part if total is None else total + part
    for ref in adds:
        total = total + ref[...].astype(F32)
    refs[2 * n_half][...] = total.astype(BF)


def attend_bwd_half(
    n_i, main, heads, g_ref, qkv_ref, lse_ref, lset_ref, w_ref, wo_ref, d_ref, gb_ref, gh_ref, kv_ref
):
    hc = heads * HD
    tail = pl.ds(n_i * main, PAD)
    gh_ref[...] = dot(g_ref[...], wo_ref[0:hc, :], 1, 1).astype(BF)
    d_ref[tail, :] = jnp.zeros((PAD, 3 * hc), BF)
    factor = HD ** -0.5
    tail_row = lax.broadcasted_iota(jnp.int32, (PAD, 1), 0)
    per_head = head_mask(heads)

    def image(i, carry):
        rows = pl.ds(pl.multiple_of(i * main, main), main)
        here = tail_row == i
        bar = jnp.where(here, 0.0, -1e30)
        bar_all = jnp.concatenate([jnp.zeros((main, 1), F32), bar], 0)

        def both(cols):
            return jnp.concatenate([qkv_ref[rows, cols], qkv_ref[tail, cols]], 0)

        def last(ref, cols):
            row = jnp.sum(jnp.where(here, ref[tail, cols].astype(F32), 0.0), 0, keepdims=True)
            return jnp.where(per_head, row, 0.0).astype(BF)

        q_b, go_b = last(qkv_ref, slice(0, hc)), last(gh_ref, slice(0, hc))
        k_all, v_all = both(slice(hc, 2 * hc)), both(slice(2 * hc, 3 * hc))
        p = jnp.exp(dot(k_all, q_b, 1, 1) * factor + bar_all - lset_ref[pl.ds(i, 1), 0:8])
        dp = dot(v_all, go_b, 1, 1)
        ds = (p * (dp - jnp.sum(p * dp, 0, keepdims=True))).astype(BF)
        dq = dot(ds, k_all, 0, 0) * factor
        dq = jnp.sum(jnp.where(per_head, dq, 0.0), 0, keepdims=True).astype(BF)
        d_ref[tail, 0:hc] = jnp.where(here, dq, d_ref[tail, 0:hc])
        kv_ref[:, 0:hc] = dot(ds, q_b, 1, 0)
        kv_ref[:, hc : 2 * hc] = dot(p.astype(BF), go_b, 1, 0)
        for h in range(heads):
            head = slice(h * HD, (h + 1) * HD)
            cols = [slice(t * hc + h * HD, t * hc + (h + 1) * HD) for t in range(3)]
            q, go = qkv_ref[rows, cols[0]], gh_ref[rows, head]
            k, k_t = qkv_ref[rows, cols[1]], qkv_ref[tail, cols[1]]
            v, v_t = qkv_ref[rows, cols[2]], qkv_ref[tail, cols[2]]
            lse = lse_ref[h : h + 1, rows]
            p = jnp.exp(dot(k, q, 1, 1) * factor - lse)
            p_t = jnp.exp(dot(k_t, q, 1, 1) * factor + bar - lse)
            dp, dp_t = dot(v, go, 1, 1), dot(v_t, go, 1, 1)
            inner = jnp.sum(p * dp, 0, keepdims=True) + jnp.sum(p_t * dp_t, 0, keepdims=True)
            ds = (p * (dp - inner)).astype(BF)
            ds_t = (p_t * (dp_t - inner)).astype(BF)
            d_ref[rows, cols[0]] = ((dot(ds, k, 0, 0) + dot(ds_t, k_t, 0, 0)) * factor).astype(BF)
            dk = ((dot(ds, q, 1, 0) + kv_ref[0:main, head]) * factor).astype(BF)
            dk_t = ((dot(ds_t, q, 1, 0) + kv_ref[main:, head]) * factor).astype(BF)
            head_v = slice(hc + h * HD, hc + (h + 1) * HD)
            dv = (dot(p.astype(BF), go, 1, 0) + kv_ref[0:main, head_v]).astype(BF)
            dv_t = (dot(p_t.astype(BF), go, 1, 0) + kv_ref[main:, head_v]).astype(BF)
            d_ref[rows, cols[1]] = dk
            d_ref[rows, cols[2]] = dv
            d_ref[tail, cols[1]] = jnp.where(here, dk_t, d_ref[tail, cols[1]])
            d_ref[tail, cols[2]] = jnp.where(here, dv_t, d_ref[tail, cols[2]])
        return carry

    lax.fori_loop(0, n_i, image, 0)
    gb_ref[...] = jnp.sum(d_ref[...].astype(F32), 0, keepdims=True)


def attend_bwd(n_i, g, halves, adds=()):
    rows, width = g.shape
    hc = halves[0][3].shape[1] // 3
    main = (rows - PAD) // n_i
    shapes = [((rows, 3 * hc), BF), ((1, 3 * hc), F32)] * len(halves) + [((rows, width), BF)]
    flops = (2 * rows * width * 4 * hc + 10 * n_i * main * main * hc) * len(halves)
    out = call(
        functools.partial(attend_bwd_kernel, n_i, main, hc // HD, len(halves), len(adds)),
        [g] + [x for half in halves for x in half] + list(adds),
        shapes,
        scratch=[pltpu.VMEM((rows, hc), BF), pltpu.VMEM((main + PAD, 2 * hc), F32)],
        flops=flops,
        name="attend_bwd",
    )
    return out[0:-1:2], out[1:-1:2], out[-1]


epsilon = 1e-06
inv_root_two = 0.7071067811865476
inv_root_tau = 0.3989422804014327
def step_of(rows):
    return next(s for s in (48, 64, 32, 16) if rows % s == 0)


def call(kernel, ins, outs, scratch=(), flops=0, name=None, in_specs=None, **grid):
    moved = sum(x.size * x.dtype.itemsize for x in ins)
    moved += sum(int(jnp.dtype(d).itemsize) * functools.reduce(lambda a, b: a * b, s) for s, d in outs)
    vmem = pl.BlockSpec(memory_space=pltpu.VMEM)
    return pl.pallas_call(
        kernel,
        in_specs=in_specs or [vmem] * len(ins),
        out_specs=grid.pop("out_specs", [vmem] * len(outs)),
        out_shape=[jax.ShapeDtypeStruct(*s) for s in outs],
        scratch_shapes=list(scratch),
        compiler_params=pltpu.CompilerParams(vmem_limit_bytes=60 * 2**20),
        cost_estimate=pl.CostEstimate(flops=int(flops), bytes_accessed=int(moved), transcendentals=0),
        name=name,
        **grid,
    )(*ins)


def mean_parts(rows):
    centred = rows - jnp.mean(rows, axis=1, keepdims=True)
    spread = jnp.mean(centred * centred, axis=1, keepdims=True)
    inverse = lax.rsqrt(spread + epsilon)
    return centred * inverse, inverse


def fold(x):
    total = x[0:8]
    for at in range(8, x.shape[0], 8):
        total = total + x[at : at + 8]
    return total


def pack_kernel(n_i, main, norm, img_ref, gain_ref, shift_ref, x_ref, other_ref):
    width = x_ref.shape[1]

    def emit(at, x, count):
        x_ref[pl.ds(at, count), :] = x
        if norm:
            unit, _ = mean_parts(x.astype(F32))
            other_ref[pl.ds(at, count), :] = (unit * gain_ref[...] + shift_ref[...]).astype(BF)

    size = step_of(main)
    if not norm:
        other_ref[...] = jnp.zeros(other_ref.shape, F32)
    tail_row = lax.broadcasted_iota(jnp.int32, (PAD, 1), 0)
    tails = jnp.zeros((PAD, width), F32)
    for i in range(n_i):

        def step(r, carry, i=i):
            at = pl.multiple_of(r * size, size)
            x = img_ref[i, pl.ds(at, size), :]
            emit(pl.multiple_of(i * main + r * size, size), x, size)
            if not norm:
                other_ref[...] += fold(x.astype(F32))
            return carry

        lax.fori_loop(0, main // size, step, 0)
        tails = jnp.where(tail_row == i, img_ref[i, main : main + 1, :].astype(F32), tails)
    emit(n_i * main, tails.astype(BF), PAD)
    if not norm:
        other_ref[...] += fold(tails)


def pack(img, gain, shift, norm):
    n_i, seq, width = img.shape
    rows = n_i * (seq - 1) + PAD
    other = ((rows, width), BF) if norm else ((8, width), F32)
    return call(
        functools.partial(pack_kernel, n_i, seq - 1, norm),
        [img, gain, shift],
        [((rows, width), BF), other],
        name="pack",
    )


def loop_rows(rows, step):
    size = step_of(rows)

    def one(r, carry):
        step(pl.ds(pl.multiple_of(r * size, size), size))
        return carry

    lax.fori_loop(0, rows // size, one, 0)


def norm_kernel(x_ref, a_ref, b_ref, c_ref, bias_ref, gain_ref, shift_ref, mid_ref, n_ref):
    def step(at):
        moved = a_ref[at, :].astype(F32) + b_ref[at, :].astype(F32) + c_ref[at, :].astype(F32)
        middle = x_ref[at, :].astype(F32) + (moved + bias_ref[...])
        mid_ref[at, :] = middle
        unit, _ = mean_parts(middle)
        n_ref[at, :] = (unit * gain_ref[...] + shift_ref[...]).astype(BF)

    loop_rows(x_ref.shape[0], step)


def norm_second(x, parts, bias, gain, shift):
    return call(
        norm_kernel,
        [x, *parts, bias, gain, shift],
        [(x.shape, F32), (x.shape, BF)],
        name="norm_second",
    )


def norm_back_kernel(res_f32, x_ref, a_ref, b_ref, c_ref, add_ref, gain_ref, *outs):
    out_ref, low_ref, gain_out, shift_out, bias_out = outs
    for ref in (gain_out, shift_out, bias_out):
        ref[...] = jnp.zeros(ref.shape, F32)

    def step(at):
        grad = a_ref[at, :].astype(F32) + b_ref[at, :].astype(F32) + c_ref[at, :].astype(F32)
        unit, inverse = mean_parts(x_ref[at, :].astype(F32))
        scaled = grad * gain_ref[...]
        first = jnp.mean(scaled, axis=1, keepdims=True)
        second = jnp.mean(scaled * unit, axis=1, keepdims=True)
        total = add_ref[at, :].astype(F32) + inverse * (scaled - first - unit * second)
        low = total.astype(BF)
        low_ref[at, :] = low
        if res_f32:
            out_ref[at, :] = total
            bias_out[...] += fold(low.astype(F32))
        gain_out[...] += fold(grad * unit)
        shift_out[...] += fold(grad)

    loop_rows(x_ref.shape[0], step)


def norm_back(x, parts, add, gain, keep):
    rows, width = x.shape
    full = (x.shape, F32) if keep else ((8, width), F32)
    return call(
        functools.partial(norm_back_kernel, keep),
        [x, *parts, add, gain],
        [full, (x.shape, BF)] + [((8, width), F32)] * 3,
        name="norm_back",
    )


def unpack_kernel(n_i, main, sum_parts, *refs):
    size = step_of(main)
    if sum_parts:
        mid_ref, a_ref, b_ref, c_ref, bias_ref, out_ref = refs
    else:
        mid_ref, out_ref = refs

    def value(at):
        x = mid_ref[at, :]
        if sum_parts:
            moved = a_ref[at, :].astype(F32) + b_ref[at, :].astype(F32) + c_ref[at, :].astype(F32)
            x = (x.astype(F32) + moved + bias_ref[...]).astype(BF)
        return x

    for i in range(n_i):

        def step(r, carry, i=i):
            at = pl.multiple_of(i * main + r * size, size)
            out_ref[i, pl.ds(pl.multiple_of(r * size, size), size), :] = value(pl.ds(at, size))
            return carry

        lax.fori_loop(0, main // size, step, 0)
    tails = value(pl.ds(n_i * main, PAD)).astype(F32)
    for i in range(n_i):
        out_ref[i, main : main + 1, :] = tails[i : i + 1].astype(BF)


def unpack(n_i, seq, first, parts=(), bias=None):
    width = first.shape[1]
    ins = [first, *parts] + ([bias] if parts else [])
    return call(
        functools.partial(unpack_kernel, n_i, seq - 1, bool(parts)),
        ins,
        [((n_i, seq, width), BF)],
        name="unpack",
    )[0]


def mlp_kernel(n0, n1, c0, c1, up_ref, upb_ref, down_ref, act_ref, gh_ref, g0, g1, gub_ref, acc):
    j, last = pl.program_id(0), pl.num_programs(0) - 1
    size = n0.shape[0]
    for i, (n_ref, c_ref) in enumerate(((n0, c0), (n1, c1))):
        rows = slice(i * size, (i + 1) * size)
        h = dot(n_ref[...], up_ref[...], 1, 0) + upb_ref[...]
        da = dot(c_ref[...], down_ref[...], 1, 1)
        cdf = 0.5 * (1.0 + lax.erf(h * inv_root_two))
        act_ref[rows, :] = (h * cdf).astype(BF)
        gh = (da * (cdf + h * (jnp.exp(-0.5 * h * h) * inv_root_tau))).astype(BF)
        gh_ref[rows, :] = gh
        total = jnp.sum(gh.astype(F32), axis=0, keepdims=True)
        gub_ref[...] = total if i == 0 else gub_ref[...] + total
        part = dot(gh, up_ref[...], 1, 1)

        @pl.when(j == 0)
        def _():
            acc[rows, :] = part

        @pl.when(j > 0)
        def _():
            acc[rows, :] += part

    @pl.when(j == last)
    def _():
        g0[...] = acc[0:size, :].astype(BF)
        g1[...] = acc[size : 2 * size, :].astype(BF)


def mlp(n, c, up, upb, down, tile=512):
    rows, width = n[0].shape
    units = up.shape[1]
    here = whole_spec((rows, width))
    return call(
        mlp_kernel,
        [*n, *c, up, upb, down],
        [((2 * rows, units), BF)] * 2 + [((rows, width), BF)] * 2 + [((1, units), F32)],
        scratch=[pltpu.VMEM((2 * rows, width), F32)],
        flops=12 * rows * width * units,
        in_specs=[here] * 4
        + [
            pl.BlockSpec((width, tile), lambda j: (0, j)),
            pl.BlockSpec((1, tile), lambda j: (0, j)),
            pl.BlockSpec((tile, width), lambda j: (j, 0)),
        ],
        out_specs=[pl.BlockSpec((2 * rows, tile), lambda j: (0, j))] * 2
        + [here] * 2
        + [pl.BlockSpec((1, tile), lambda j: (0, j))],
        grid=(units // tile,),
        name="mlp",
    )


def wgrad_kernel(n_left, n_right, index_ref, *refs):
    left, right = refs[:n_left], refs[n_left : n_left + n_right]
    out_ref, held, sems = refs[n_left + n_right :]
    size = right[0].shape[0]
    copies = [
        pltpu.make_async_copy(r, held.at[pl.ds(i * size, size)], sems.at[i])
        for i, r in enumerate(right)
    ]

    @pl.when(pl.program_id(0) == 0)
    def _():
        for copy in copies:
            copy.start()
        for copy in copies:
            copy.wait()

    total, at = None, 0
    for ref in left:
        rows = ref.shape[0]
        part = dot(ref[...], held[at : at + rows, :], 0, 0)
        total = part if total is None else total + part
        at += rows
    out_ref[...] = total.astype(BF)


def wgrad(left, right, index, tile):
    width = right[0].shape[1]
    total = sum(r.shape[0] for r in right)
    blocks = index.shape[0]
    in_specs = [pl.BlockSpec((x.shape[0], tile), lambda j, at: (0, at[j])) for x in left]
    in_specs += [pl.BlockSpec(memory_space=pl.ANY)] * len(right)
    moved = 2 * (total * (width + blocks * tile) + blocks * tile * width)
    return pl.pallas_call(
        functools.partial(wgrad_kernel, len(left), len(right)),
        grid_spec=pltpu.PrefetchScalarGridSpec(
            num_scalar_prefetch=1,
            grid=(blocks,),
            in_specs=in_specs,
            out_specs=pl.BlockSpec((tile, width), lambda j, at: (j, 0)),
            scratch_shapes=[
                pltpu.VMEM((total, width), BF),
                pltpu.SemaphoreType.DMA((len(right),)),
            ],
        ),
        out_shape=jax.ShapeDtypeStruct((blocks * tile, width), BF),
        compiler_params=pltpu.CompilerParams(vmem_limit_bytes=60 * 2**20),
        cost_estimate=pl.CostEstimate(
            flops=2 * total * blocks * tile * width, bytes_accessed=moved, transcendentals=0
        ),
        name="wgrad",
    )(index, *left, *right)


def place_kernel(count, transposed, at_ref, *refs):
    blocks, out_ref = refs[:count], refs[count]
    size = blocks[0].shape[0]
    target = refs[count + 1] if transposed else out_ref
    for i, ref in enumerate(blocks):
        rows = pl.ds(pl.multiple_of(at_ref[i] * size, size), size)
        target[rows, :] = ref[...].astype(target.dtype)
    if transposed:
        for at in range(0, target.shape[0], 256):
            out_ref[:, at : at + 256] = target[at : at + 256, :].astype(F32).T


def place(blocks, at, transposed):
    size, width = blocks[0].shape
    rows = size * len(blocks)
    shape = (width, rows) if transposed else (rows, width)
    vmem = pl.BlockSpec(memory_space=pltpu.VMEM)
    return call(
        functools.partial(place_kernel, len(blocks), transposed),
        [at, *blocks],
        [(shape, F32)],
        scratch=[pltpu.VMEM((rows, width), BF)] if transposed else [],
        in_specs=[pl.BlockSpec(memory_space=pltpu.SMEM)] + [vmem] * len(blocks),
        name="place",
    )[0]


class Order:
    def __init__(self):
        self.last = None

    def gate(self, x):
        return x if self.last is None else lax.optimization_barrier((x, self.last))[0]

    def __call__(self, kernel, x, *rest):
        out = kernel(self.gate(x), *rest)
        self.last = jax.tree.leaves(out)[-1]
        return out

    def meet(self, *arrays):
        self.last = lax.optimization_barrier((self.last, *arrays))[0]


class Layout:
    def __init__(self, dp, tensor):
        self.dp, self.tensor = dp, tensor
        self.n_p, self.n_hi = dp // 2, tensor // 2
        self.bits = [1 << b for b in range(self.n_p.bit_length() - 1)]

    def move(self, x, p=0, c=0, hi=0, lo=0):
        dp_mask, tensor_mask = 2 * p + c, 2 * hi + lo
        pairs = [
            (d * self.tensor + t, (d ^ dp_mask) * self.tensor + (t ^ tensor_mask))
            for d in range(self.dp)
            for t in range(self.tensor)
        ]
        return lax.ppermute(x, ("dp", "tensor"), pairs)

    def place_of(self, p, order):
        n = len(order)
        place = 0
        for i, bit in enumerate(order):
            place = place + (p // bit) % 2 * (1 << (n - 1 - i))
        return place

    def spread(self, block, order):
        have = {0: block}
        for bit in order:
            have.update({m ^ bit: self.move(x, p=bit) for m, x in list(have.items())})
        return have

    def spread_direct(self, block):
        return {m: self.move(block, p=m) if m else block for m in range(self.n_p)}


def on_device(
    lay,
    images,
    first_gain,
    first_shift,
    qkv_weight,
    qv_bias,
    out_weight,
    out_bias,
    second_gain,
    second_shift,
    up_weight,
    up_bias,
    down_weight,
    down_bias,
    cotangent,
):
    n_p, n_hi = lay.n_p, lay.n_hi
    n_i, seq, width = images.shape
    columns = qkv_weight.shape[2]
    units = up_weight.shape[1]
    hc, hu = columns // 2, units // 2
    dp = lax.axis_index("dp")
    p, c = dp // 2, dp % 2
    up_order, down_order = lay.bits, lay.bits[::-1]
    order = Order()
    first_gain, first_shift, out_bias, second_gain, second_shift, down_bias = [
        v.reshape(1, width)
        for v in (first_gain, first_shift, out_bias, second_gain, second_shift, down_bias)
    ]

    def half(x, axis):
        n = x.shape[axis] // 2
        return lax.dynamic_slice_in_dim(x, c * n, n, axis)

    def block(x, axis, at):
        n = x.shape[axis] // n_p
        return lax.dynamic_slice_in_dim(x, at * n, n, axis)

    def put(buf, x, axis, at):
        return lax.dynamic_update_slice_in_dim(buf, x, at, axis)

    qkv_half = half(qkv_weight, 2)
    qkv_mine = jnp.concatenate([qkv_half[i] for i in range(3)], 1)
    pad_rows = -hc % (16 * n_p)
    out_mine = jnp.pad(half(out_weight, 0), ((0, pad_rows), (0, 0)))
    qkv_cut, out_cut = block(qkv_mine, 0, p), block(out_mine, 0, p)
    qkv_hi = [lay.move(qkv_cut, hi=k) for k in range(1, n_hi)]
    out_hi = [lay.move(out_cut, hi=k) for k in range(1, n_hi)]
    qv_half, upb_half = half(qv_bias, 1), half(up_bias, 0)
    bias_all = [jnp.concatenate([qv_half.reshape(-1), upb_half])]
    bias_all += [lay.move(bias_all[0], hi=k) for k in range(1, n_hi)]
    upb_work = jnp.concatenate([b[2 * hc :] for b in bias_all]).reshape(1, -1)
    qkv_bias = [
        jnp.concatenate([b[:hc], jnp.zeros((hc,), F32), b[hc : 2 * hc]]).reshape(1, -1)
        for b in bias_all
    ]

    x_unit, first_own = order(pack, images, first_gain, first_shift, True)
    first_c, first_z = lay.move(first_own, c=1), lay.move(first_own, lo=1)
    seed_unit, grad_down_bias = order(pack, cotangent, first_gain, first_shift, False)
    seed_c = lay.move(seed_unit, c=1)

    qkv_work, out_work = [qkv_mine], [out_mine]
    forward = [[None] * 4 for _ in range(n_hi)]

    def attention(k, u, n, adds=()):
        adds = list(adds) + ([forward[k - 1][u][4]] if k else [])
        forward[k][u] = order(
            lambda x: attend_fwd(n_i, x, qkv_work[k], qkv_bias[k], out_work[k], adds), n
        )
        return forward[k][u][4]

    def spread_work(got_all, axis):
        return [
            [(k * n_p + (p ^ m), x) for m, x in lay.spread_direct(got).items()]
            for k, got in enumerate(got_all, 1)
        ]

    attention(0, 0, first_own)
    up_hi = [lay.move(block(half(order.gate(up_weight), 1), 1, p), hi=k) for k in range(1, n_hi)]
    attention(0, 1, first_c)
    first_zc = lay.move(order.gate(first_z), c=1)
    seed_z = lay.move(lax.optimization_barrier((seed_unit, first_zc))[0], lo=1)
    qkv_got = spread_work([order.gate(x) for x in qkv_hi], 0)
    out_got = spread_work([order.gate(x) for x in out_hi], 0)
    attention(0, 2, first_z)
    down_hi = [
        lay.move(block(half(order.gate(down_weight), 0), 0, p), hi=k) for k in range(1, n_hi)
    ]
    attention(0, 3, first_zc)
    up_got = spread_work([order.gate(x) for x in up_hi], 1)
    for k in range(1, n_hi):
        for got, work, like in ((qkv_got, qkv_work, qkv_mine), (out_got, out_work, out_mine)):
            full = jnp.zeros_like(like)
            for at, x in got[k - 1]:
                full = put(full, x, 0, (at - k * n_p) * x.shape[0])
            work.append(full)
    normed = (first_own, first_c, first_z, first_zc)
    for k in range(1, n_hi - 1):
        for u in range(4):
            attention(k, u, normed[u])
    k = n_hi - 1
    moved_3 = lay.move(attention(k, 3, first_zc), c=1)
    seed_zc = lay.move(order.gate(seed_z), c=1)
    moved_1 = lay.move(attention(k, 1, first_c), c=1)
    down_got = spread_work([order.gate(x) for x in down_hi], 0)
    moved_2 = lay.move(attention(k, 2, first_z, [moved_3]), lo=1)
    attention_parts = (attention(k, 0, first_own), moved_1, moved_2)
    seed = [seed_unit, seed_c, seed_z, seed_zc]
    normed_first = list(normed)

    def fill_up(x):
        work = put(jnp.zeros((width, n_hi * hu), BF), half(x, 1), 1, 0)
        for at, part in (pair for got in up_got for pair in got):
            work = put(work, part, 1, at * part.shape[1])
        return work

    def fill_down(x):
        work = put(jnp.zeros((n_hi * hu, width), BF), half(x, 0), 0, 0)
        for at, part in (pair for got in down_got for pair in got):
            work = put(work, part, 0, at * part.shape[0])
        return work

    up_work = order(fill_up, up_weight)
    down_work = order(fill_down, down_weight)
    middle, second_own = order(
        lambda x: norm_second(x, attention_parts, out_bias, second_gain, second_shift), x_unit
    )
    second_c, second_z = lay.move(second_own, c=1), lay.move(second_own, lo=1)

    near = order(lambda n: mlp([n, second_c], seed[:2], up_work, upb_work, down_work), second_own)
    second_zc = lay.move(order.gate(second_z), c=1)
    other_c = lay.move(near[3], c=1)
    low_near = order(lambda x: dot(x, down_work, 1, 0).astype(BF), near[0])
    far = order(lambda n: mlp([n, second_zc], seed[2:], up_work, upb_work, down_work), second_z)
    normed_second = [second_own, second_c, second_z, second_zc]

    def index(order_of, other):
        top = lay.place_of(p, order_of) // (n_p // 2)
        return jnp.stack([2 * k + (top ^ other) for k in range(n_hi)]).astype(jnp.int32)

    def mlp_grad(which, right, order_of, other):
        return order(
            lambda x: wgrad([x, far[which]], right, index(order_of, other), hu // 2), near[which]
        )

    far_c = lay.move(far[3], c=1)
    down_send = mlp_grad(0, seed, down_order, 1)
    down_recv = lay.move(down_send, p=down_order[0])

    def join(*parts):
        total = parts[0].astype(F32)
        for x in parts[1:]:
            total = total + x.astype(F32)
        return total.astype(BF)

    far_sum = order(lambda x: join(x, far_c), far[2])
    grad_second = (near[2], other_c, lay.move(far_sum, lo=1))
    up_send = mlp_grad(1, normed_second, up_order, 1)
    up_recv = lay.move(up_send, p=up_order[0])
    down_keep = mlp_grad(0, seed, down_order, 0)
    rows = x_unit.shape[0]
    grad_middle, grad_branch, grad_second_gain, grad_second_shift, grad_out_bias = order(
        lambda x: norm_back(x, grad_second, seed_unit, second_gain, True), middle
    )
    branch_c, branch_z = lay.move(grad_branch, c=1), lay.move(grad_branch, lo=1)
    low_far = order(lambda x: dot(x, down_work, 1, 0).astype(BF), far[0])
    low_far_c = lay.move(low_far[rows:], c=1)
    low_near_c = lay.move(low_near[rows:], c=1)
    up_keep = mlp_grad(1, normed_second, up_order, 0)

    def halve(keep, recv, order_of, stage, parts):
        bit = order_of[stage]
        side = (p // bit) % 2
        shape = (parts, 2, keep.shape[0] // (2 * parts), width)

        def pick(x, s):
            x = lax.dynamic_index_in_dim(x.reshape(shape), s, 1, keepdims=False)
            return x.reshape(-1, width)

        send = order(lambda x: join(pick(x, 1 - side), pick(recv, 1 - side)), keep)
        keep = join(pick(keep, side), pick(recv, side))
        return keep, lay.move(send, p=bit)

    def settle_hi(keep, recv):
        size = keep.shape[0] // n_hi
        total = order(lambda x: join(x, recv), keep)
        got = [lay.move(total[k * size : (k + 1) * size], hi=k) for k in range(1, n_hi)]
        return total[:size], got

    def whole_grad(mine, order_of):
        have = lay.spread(mine, order_of[::-1])
        at, out = [], []
        for core in (0, 1):
            for mask, x in have.items():
                at.append((c ^ core) * n_p + lay.place_of(p ^ mask, order_of))
                out.append(lay.move(x, c=1) if core else x)
        return out, jnp.stack(at).astype(jnp.int32)

    backward = [[None] * 4 for _ in range(n_hi)]
    branch = [grad_branch, branch_c, branch_z, None]

    def attention_back(k, u, adds=()):
        adds = list(adds) + ([backward[k + 1][u][2]] if k < n_hi - 1 else [])
        f = forward[k][u]
        backward[k][u] = order(
            lambda g: attend_bwd(n_i, g, [(f[0], f[2], f[3], qkv_work[k], out_work[k])], adds),
            branch[u],
        )
        return backward[k][u][2]

    whole_index = jnp.zeros((1,), jnp.int32)

    def attention_grad(k):
        qkv = order(
            lambda x: wgrad([x] + [b[0][0] for b in backward[k][1:]], normed_first, whole_index, 3 * hc),
            backward[k][0][0][0],
        )
        heads = [f[1] for f in forward[k]]
        out = order(lambda x: wgrad([x] + heads[1:], branch, whole_index, hc), heads[0])
        return jnp.concatenate([qkv, out])

    def attention_send(k, order_of):
        grad = attention_grad(k)
        if order_of != orders[0]:
            blocks = jnp.split(grad, n_p)
            owner = {lay.place_of(q, order_of): lay.place_of(q, orders[0]) for q in range(n_p)}
            grad = jnp.concatenate([blocks[owner[i]] for i in range(n_p)])
        top = lay.place_of(p, order_of) // (n_p // 2)
        size = grad.shape[0] // 2
        send = lax.dynamic_slice_in_dim(grad, (1 - top) * size, size, 0)
        keep = lax.dynamic_slice_in_dim(grad, top * size, size, 0)
        return keep, lay.move(send, p=order_of[0])

    down_pair, up_pair = (down_keep, down_recv), (up_keep, up_recv)
    attn_pairs = [None] * n_hi
    orders = [up_order] + [down_order] * (n_hi - 1)
    n_stage = len(lay.bits)
    k = n_hi - 1
    down_pair = halve(*down_pair, down_order, 1, n_hi)
    attention_back(k, 0)
    branch[3] = lay.move(order.gate(branch_z), c=1)
    attention_back(k, 1)
    up_pair = halve(*up_pair, up_order, 1, n_hi)
    low_far_sum = order(lambda x: join(x, low_far_c), low_far[:rows])
    low_far_z = lay.move(low_far_sum, lo=1)
    attention_back(k, 2)
    attention_back(k, 3)
    for stage in range(2, n_stage):
        down_pair = halve(*down_pair, down_order, stage, n_hi)
        up_pair = halve(*up_pair, up_order, stage, n_hi)
    down_mine, down_hi_got = settle_hi(*down_pair)
    attn_pairs[k] = attention_send(k, orders[k])
    for k in range(n_hi - 2, 0, -1):
        for u in range(4):
            attention_back(k, u)
        attn_pairs[k] = attention_send(k, orders[k])
    moved_3 = lay.move(attention_back(0, 3), c=1)
    up_mine, up_hi_got = settle_hi(*up_pair)
    moved_1 = lay.move(attention_back(0, 1), c=1)
    for k in range(1, n_hi):
        for stage in range(1, n_stage):
            attn_pairs[k] = halve(*attn_pairs[k], orders[k], stage, 1)
    moved_2 = lay.move(attention_back(0, 2, [moved_3]), lo=1)
    down_mine = order(lambda x: join(x, *down_hi_got), down_mine)
    down_all = whole_grad(down_mine, down_order)
    grad_first = (attention_back(0, 0), moved_1, moved_2)
    attn_hi = []
    for k in range(1, n_hi):
        total = order(lambda x, k=k: join(x, attn_pairs[k][1]), attn_pairs[k][0])
        attn_hi.append(lay.move(total, hi=k))
    attn_pairs[0] = attention_send(0, orders[0])
    up_mine = order(lambda x: join(x, *up_hi_got), up_mine)
    up_all = whole_grad(up_mine, up_order)
    result_parts = (low_near[:rows], low_near_c, low_far_z)
    result = order(lambda x: unpack(n_i, seq, x, result_parts, down_bias), middle)
    for stage in range(1, n_stage):
        attn_pairs[0] = halve(*attn_pairs[0], orders[0], stage, 1)
    _, grad_images, grad_first_gain, grad_first_shift, _ = order(
        lambda x: norm_back(x, grad_first, grad_middle, first_gain, False), x_unit
    )
    attn_mine = order(lambda x: join(x, attn_pairs[0][1], *attn_hi), attn_pairs[0][0])
    attn_all = whole_grad(attn_mine, orders[0])
    grad_images = order(lambda x: unpack(n_i, seq, x), grad_images)
    grad_down_weight = order(
        lambda x: place([x] + down_all[0][1:], down_all[1], False), down_all[0][0]
    )
    grad_up_weight = order(lambda x: place([x] + up_all[0][1:], up_all[1], True), up_all[0][0])

    tensor_at = lax.axis_index("tensor")
    all_units, all_columns = units * lay.tensor, columns * lay.tensor
    grad_up_bias = (near[4] + far[4])[0]
    wide_up = jnp.zeros((all_units,), F32)
    wide_qv = jnp.zeros((2, all_columns), F32)
    for k in range(n_hi):
        shard = tensor_at ^ (2 * k)
        wide_up = put(wide_up, grad_up_bias[k * hu : (k + 1) * hu], 0, shard * units + c * hu)
        bias = sum(b[1][0] for b in backward[k])[0]
        bias = jnp.stack([bias[:hc], bias[2 * hc :]])
        wide_qv = put(wide_qv, bias, 1, shard * columns + c * hc)
    sums = (
        grad_first_gain,
        grad_first_shift,
        grad_out_bias,
        grad_second_gain,
        grad_second_shift,
        grad_down_bias,
    )
    vector = jnp.concatenate(
        [jnp.sum(x, axis=0) for x in sums] + [wide_up, wide_qv.reshape(-1)]
    )
    for bit in lay.bits:
        vector = vector + lay.move(vector, p=bit)
    vector = vector + lay.move(vector, c=1)
    for k in [1 << b for b in range(lay.tensor.bit_length() - 1)]:
        vector = vector + lay.move(vector, lo=k & 1, hi=k >> 1)
    norms = vector[: 6 * width].reshape(6, width)
    vector = vector[6 * width :]
    grad_up_bias = lax.dynamic_slice_in_dim(vector, tensor_at * units, units, 0)
    grad_qv_bias = lax.dynamic_slice_in_dim(
        vector[all_units:].reshape(2, all_columns), tensor_at * columns, columns, 1
    )

    buf = jnp.zeros((8 * hc, width), BF)
    for i, x in enumerate(attn_all[0]):
        buf = put(buf, x, 0, attn_all[1][i] * x.shape[0])
    buf = buf.reshape(2, 4, hc, width)
    grad_out_weight = buf[:, 3].reshape(columns, width).astype(F32)
    grad_qkv_weight = jnp.stack([buf[:, i].reshape(columns, width).T for i in range(3)]).astype(F32)
    return (
        result,
        grad_images,
        norms[0],
        norms[1],
        grad_qkv_weight,
        grad_qv_bias,
        grad_out_weight,
        norms[2],
        norms[3],
        norms[4],
        grad_up_weight,
        grad_up_bias,
        grad_down_weight,
        norms[5],
    )


def solution(mesh):
    lay = Layout(mesh.shape["dp"], mesh.shape["tensor"])
    rows = P(("dp", "tensor"), None, None)
    qkv, qv = P(None, None, "tensor"), P(None, "tensor")
    line, up, down, rep = P("tensor"), P(None, "tensor"), P("tensor", None), P()
    return jax.shard_map(
        functools.partial(on_device, lay),
        mesh=mesh,
        in_specs=(rows, rep, rep, qkv, qv, down, rep, rep, rep, up, line, down, rep, rows),
        out_specs=(rows, rows, rep, rep, qkv, qv, down, rep, rep, rep, up, line, down, rep),
        check_vma=False,
    )
```

time: 1610 us -> 914 us (0.57)
  waiting for transfers between devices: 1050 us -> 252 us
  Pallas kernels: 0 us -> 400 us
  matrix products: 269 us -> 26.6 us
  starting transfers between devices: 0.37 us -> 66.5 us
  blocking collectives: 57.6 us -> 0 us
  other arithmetic: 112 us -> 61.4 us
    reduce_scatter x4 -> x0, waiting for transfers between devices: 468 us -> none  [the longest x1 123 us: on_device(): lax.psum_scatter(jnp.einsum('isf,fd->isd', piece, down_weight, preferred_...]
    pallas_call x0 -> x35, Pallas kernels: none -> 400 us  [the longest x27 292 us: call(): pl.pallas_call(kernel, in_specs=in_specs or [vmem] * len(ins), out_specs=...]
    all_gather x4 -> x0, waiting for transfers between devices: 395 us -> none  [the longest x1 130 us: on_device(): normed_first = lax.all_gather(normed_local, 'tensor', axis=0, tiled=True)]
    ppermute x0 -> x78, waiting for transfers between devices: none -> 252 us  [move(): return lax.ppermute(x, ('dp', 'tensor'), pairs)]
    dot_general x40 -> x2, matrix products: 269 us -> 26.6 us  [dot(): lax.dot_general(a, b, (((ca,), (cb,)), ((), ())), preferred_element_type=...]
    psum x1 -> x0, waiting for transfers between devices: 186 us -> none  [on_device(): lax.psum(grad_qkv_weight.astype(jnp.bfloat16), 'dp').astype(jnp.float32)]
    ppermute x0 -> x78, starting transfers between devices: none -> 66.5 us  [move(): return lax.ppermute(x, ('dp', 'tensor'), pairs)]
    psum x2 -> x0, blocking collectives: 57.6 us -> none  [the longest x1 42.1 us: on_device(): lax.psum((grad_first_gain, grad_first_shift, grad_out_bias, grad_second_g...]
  transfers between devices with their start and end apart: 9 -> 78, of which waited for: 9 -> 19; matrix products, arithmetic and copies ran while one was open for 12% -> 18% of each run, Pallas kernels for 0% -> 38%
where the time goes in v2:
time: 914 us; the launch traced here: 904 us
  Pallas kernels  400 us (44%)
  waiting for transfers between devices  252 us (28%)
  local copies, waits for them, and re-layouts  95.4 us (10%)
  starting transfers between devices  66.5 us (7%)
  other arithmetic  61.4 us (7%)
  matrix products  26.6 us (3%)
    pallas_call x27, Pallas kernels, call(): pl.pallas_call(kernel, in_specs=in_specs or [vmem] * len(ins), out_specs=...  292 us
    ppermute x78, waiting for transfers between devices, move(): return lax.ppermute(x, ('dp', 'tensor'), pairs)  252 us
    pallas_call x8, Pallas kernels, wgrad(): pl.pallas_call(functools.partial(wgrad_kernel, len(left), len(right)), gr...  108 us
    ppermute x78, starting transfers between devices, move(): return lax.ppermute(x, ('dp', 'tensor'), pairs)  66.5 us
    convert_element_type x11, other arithmetic, join(): return total.astype(BF)  31.3 us
    dynamic_update_slice x29, local copies, waits for them, and re-layouts, put(): return lax.dynamic_update_slice_in_dim(buf, x, at, axis)  30.5 us
    dot_general x2, matrix products, dot(): lax.dot_general(a, b, (((ca,), (cb,)), ((), ())), preferred_element_type=...  26.6 us
    unnamed x131, local copies, waits for them, and re-layouts  23.1 us
  transfers between devices with their start and end apart: 78, of which 19 were waited for; matrix products, arithmetic and copies ran while one was open for 18% of the time, Pallas kernels for 38%

profile of v2, /device:TPU:0, one launch (start us, length us, event | category | flops | bytes accessed | tf_op | source)
XLA Modules:
  0.0 904.3 jit_solution(16495300709603075034)
XLA Ops:
  6.2 5.5 pack.2
  35.7 18.1 %collective-permute-done.7 = f32[1440]{0:T(1024)S(1)} collective-permute-done((f32[1440]{0:T(1024)S(1)}, f32[1440]{0:T(1024)S(1)}, u32[]{:S(2)}, u32[]{:S(2)}) %collective-permute-start.7) | collective-permute-done | bytes 5792 | tf_op jit(solution)/shard_map/ppermute | solution.py:542
  54.5 8.6 attend_fwd.8
  63.1 8.6 attend_fwd.9
  77.5 8.9 attend_fwd.10
  92.5 4.1 collective-permute-done.4
  96.7 15.6 %collective-permute-done.5 = bf16[416,624]{1,0:T(8,128)(2,1)S(1)} collective-permute-done((bf16[416,624]{1,0:T(8,128)(2,1)S(1)}, bf16[416,624]{1,0:T(8,128)(2,1)S(1)}, u32[]{:S(2)}, u32[]{:S(2)}) %collective-permute-start.5) | collective-permute-done | bytes 519200 | tf_op jit(solution)/shard_map/ppermute | solution.py:542
  112.4 9.3 %attend_fwd.11 = (bf16[528,624]{1,0:T(8,128)(2,1)}, bf16[528,208]{1,0:T(8,128)(2,1)}, f32[8,512]{1,0:T(8,128)}, f32[8,128]{1,0:T(8,128)}, bf16[528,1664]{1,0:T(8,128)(2,1)}) custom-call(bf16[528,1664]{1,0:T(8,128)(2,1)} %collective-permute-done.2.n_ref.refs_7_, bf16[1664,624]{1,0:T(8,128)(2,1)} %copy-done.2, f32[1,624]{1,0:T(1,128)} %reshape.200.b_ref, ...), custom_call_target="tpu_custom_call" | custom-call | flops 1571028992 | bytes 7344576 | tf_op jit(solution)/shard_map/attend_fwd/pallas_call | solution.py:208
  121.8 9.2 %attend_fwd.12 = (bf16[528,624]{1,0:T(8,128)(2,1)}, bf16[528,208]{1,0:T(8,128)(2,1)}, f32[8,512]{1,0:T(8,128)}, f32[8,128]{1,0:T(8,128)}, bf16[528,1664]{1,0:T(8,128)(2,1)}) custom-call(bf16[528,1664]{1,0:T(8,128)(2,1)} %collective-permute-done.2.n_ref.refs_7_, bf16[1664,624]{1,0:T(8,128)(2,1)} %copy-done.3, f32[1,624]{1,0:T(1,128)} %reshape.202.b_ref, ...), custom_call_target="tpu_custom_call" | custom-call | flops 1571028992 | bytes 9101760 | tf_op jit(solution)/shard_map/attend_fwd/pallas_call | solution.py:208
  132.7 3.4 collective-permute-start.13
  139.5 53.1 %collective-permute-done.13 = bf16[1664,256]{1,0:T(8,128)(2,1)} collective-permute-done((bf16[1664,256]{1,0:T(8,128)(2,1)S(1)}, bf16[1664,256]{1,0:T(8,128)(2,1)}, u32[]{:S(2)}, u32[]{:S(2)}) %collective-permute-start.13) | collective-permute-done | bytes 852000 | tf_op jit(solution)/shard_map/ppermute | solution.py:542
  196.1 9.2 %attend_fwd.13 = (bf16[528,624]{1,0:T(8,128)(2,1)}, bf16[528,208]{1,0:T(8,128)(2,1)}, f32[8,512]{1,0:T(8,128)}, f32[8,128]{1,0:T(8,128)}, bf16[528,1664]{1,0:T(8,128)(2,1)}) custom-call(bf16[528,1664]{1,0:T(8,128)(2,1)} %collective-permute-done.1.n_ref.refs_5_, bf16[1664,624]{1,0:T(8,128)(2,1)} %copy-done.3, f32[1,624]{1,0:T(1,128)} %reshape.202.b_ref, ...), custom_call_target="tpu_custom_call" | custom-call | flops 1571028992 | bytes 9101760 | tf_op jit(solution)/shard_map/attend_fwd/pallas_call | solution.py:208
  205.2 5.4 collective-permute-done.17
  212.5 10.2 %attend_fwd.14 = (bf16[528,624]{1,0:T(8,128)(2,1)}, bf16[528,208]{1,0:T(8,128)(2,1)}, f32[8,512]{1,0:T(8,128)}, f32[8,128]{1,0:T(8,128)}, bf16[528,1664]{1,0:T(8,128)(2,1)}) custom-call(bf16[528,1664]{1,0:T(8,128)(2,1)} %collective-permute-done.n_ref.refs_6_, bf16[1664,624]{1,0:T(8,128)(2,1)} %copy-done.3, f32[1,624]{1,0:T(1,128)} %reshape.202.b_ref, ...), custom_call_target="tpu_custom_call" | custom-call | flops 1571028992 | bytes 10858944 | tf_op jit(solution)/shard_map/attend_fwd/pallas_call | solution.py:208
  222.7 9.1 %attend_fwd.15 = (bf16[528,624]{1,0:T(8,128)(2,1)}, bf16[528,208]{1,0:T(8,128)(2,1)}, f32[8,512]{1,0:T(8,128)}, f32[8,128]{1,0:T(8,128)}, bf16[528,1664]{1,0:T(8,128)(2,1)}) custom-call(bf16[528,1664]{1,0:T(8,128)(2,1)} %get-tuple-element.181.n_ref.refs_4_, bf16[1664,624]{1,0:T(8,128)(2,1)} %copy-done.3, f32[1,624]{1,0:T(1,128)} %reshape.202.b_ref, ...), custom_call_target="tpu_custom_call" | custom-call | flops 1571028992 | bytes 9101760 | tf_op jit(solution)/shard_map/attend_fwd/pallas_call | solution.py:208
  245.9 3.3 dynamic_update_slice.103
  257.6 11.5 %collective-permute-done.20 = bf16[256,1664]{1,0:T(8,128)(2,1)S(1)} collective-permute-done((bf16[256,1664]{1,0:T(8,128)(2,1)}, bf16[256,1664]{1,0:T(8,128)(2,1)S(1)}, u32[]{:S(2)}, u32[]{:S(2)}) %collective-permute-start.20) | collective-permute-done | bytes 852000 | tf_op jit(solution)/shard_map/ppermute | solution.py:542
  270.1 9.4 %collective-permute-done.22.c_ref = bf16[528,1664]{1,0:T(8,128)(2,1)} collective-permute-done((bf16[528,1664]{1,0:T(8,128)(2,1)}, bf16[528,1664]{1,0:T(8,128)(2,1)}, u32[]{:S(2)}, u32[]{:S(2)}) %collective-permute-start.22) | collective-permute-done | bytes 1757216 | tf_op jit(solution)/shard_map/ppermute | solution.py:542
  279.5 8.5 norm_second.1
  288.7 28.1 %collective-permute-done.27.c0.refs_4_ = bf16[528,1664]{1,0:T(8,128)(2,1)} collective-permute-done((bf16[528,1664]{1,0:T(8,128)(2,1)S(1)}, bf16[528,1664]{1,0:T(8,128)(2,1)}, u32[]{:S(2)}, u32[]{:S(2)}) %collective-permute-start.27) | collective-permute-done | bytes 1757216 | tf_op jit(solution)/shard_map/ppermute | solution.py:542
  317.0 35.8 %mlp.2 = (bf16[1056,2048]{1,0:T(8,128)(2,1)}, bf16[1056,2048]{1,0:T(8,128)(2,1)}, bf16[528,1664]{1,0:T(8,128)(2,1)}, bf16[528,1664]{1,0:T(8,128)(2,1)}, f32[1,2048]{1,0:T(1,128)}) custom-call(bf16[528,1664]{1,0:T(8,128)(2,1)} %get-tuple-element.192.n0.refs_2_, bf16[528,1664]{1,0:T(8,128)(2,1)} %collective-permute-done.23.n1.refs_3_, ...), custom_call_target="tpu_custom_call" | custom-call | flops 21592276992 | bytes 32841728 | tf_op jit(solution)/shard_map/mlp/pallas_call | solution.py:208
  352.8 4.9 collective-permute-done.25.n0.refs_4_
  357.7 13.6 %convolution_convert_fusion.1 = bf16[1056,1664]{1,0:T(8,128)(2,1)} fusion(bf16[1056,2048]{1,0:T(8,128)(2,1)} %get-tuple-element.210.refs_0_, bf16[2048,1664]{1,0:T(8,128)(2,1)} %constant_dynamic-update-slice_fusion.8.down_ref), kind=kOutput, calls=%fused_computation.1 | convolution fusion | flops 7199182848 | bytes 14655488 | tf_op jit(solution)/shard_map/dot_general | solution.py:17
  372.6 35.7 %mlp.3 = (bf16[1056,2048]{1,0:T(8,128)(2,1)}, bf16[1056,2048]{1,0:T(8,128)(2,1)}, bf16[528,1664]{1,0:T(8,128)(2,1)}, bf16[528,1664]{1,0:T(8,128)(2,1)}, f32[1,2048]{1,0:T(1,128)}) custom-call(bf16[528,1664]{1,0:T(8,128)(2,1)} %copy-done.55, bf16[528,1664]{1,0:T(8,128)(2,1)} %copy-done.56, bf16[528,1664]{1,0:T(8,128)(2,1)} %collective-permute-done.27.c0.refs_4_, ...), custom_call_target="tpu_custom_call" | custom-call | flops 21592276992 | bytes 32841728 | tf_op jit(solution)/shard_map/mlp/pallas_call | solution.py:208
  409.5 16.6 %wgrad.8 = bf16[1024,1664]{1,0:T(8,128)(2,1)} custom-call(s32[2]{0:T(128)} %pad_add_fusion.3.index_ref, bf16[1056,2048]{1,0:T(8,128)(2,1)} %get-tuple-element.210.refs_0_, bf16[1056,2048]{1,0:T(8,128)(2,1)} %get-tuple-element.215.refs_1_, bf16[528,1664]{1,0:T(8,128)(2,1)} %get-tuple-element.200.c0.refs_2_.add_ref, ...), custom_call_target="tpu_custom_call" | custom-call | flops 7197425664 | bytes 14761984 | tf_op jit(solution)/shard_map/wgrad/pallas_call | solution.py:465
  426.2 3.2 add_convert_fusion.1
  434.1 16.9 %wgrad.9 = bf16[1024,1664]{1,0:T(8,128)(2,1)} custom-call(s32[2]{0:T(128)} %pad_add_fusion.2.index_ref, bf16[1056,2048]{1,0:T(8,128)(2,1)} %get-tuple-element.216.refs_0_, bf16[1056,2048]{1,0:T(8,128)(2,1)} %get-tuple-element.209.refs_1_, bf16[528,1664]{1,0:T(8,128)(2,1)} %get-tuple-element.192.n0.refs_2_, ...), custom_call_target="tpu_custom_call" | custom-call | flops 7197425664 | bytes 14761984 | tf_op jit(solution)/shard_map/wgrad/pallas_call | solution.py:465
  452.7 16.5 %wgrad.10 = bf16[1024,1664]{1,0:T(8,128)(2,1)} custom-call(s32[2]{0:T(128)} %pad_add_fusion.1.index_ref, bf16[1056,2048]{1,0:T(8,128)(2,1)} %get-tuple-element.210.refs_0_, bf16[1056,2048]{1,0:T(8,128)(2,1)} %get-tuple-element.215.refs_1_, bf16[528,1664]{1,0:T(8,128)(2,1)} %get-tuple-element.200.c0.refs_2_.add_ref, ...), custom_call_target="tpu_custom_call" | custom-call | flops 7197425664 | bytes 14761984 | tf_op jit(solution)/shard_map/wgrad/pallas_call | solution.py:465
  471.1 10.9 %norm_back.2 = (f32[528,1664]{1,0:T(8,128)}, bf16[528,1664]{1,0:T(8,128)(2,1)}, f32[8,1664]{1,0:T(8,128)}, f32[8,1664]{1,0:T(8,128)}, f32[8,1664]{1,0:T(8,128)}) custom-call(f32[528,1664]{1,0:T(8,128)} %get-tuple-element.288.x_ref.refs_0_, bf16[528,1664]{1,0:T(8,128)(2,1)} %get-tuple-element.212.a_ref, bf16[528,1664]{1,0:T(8,128)(2,1)} %copy-done.20, ...), custom_call_target="tpu_custom_call" | custom-call | bytes 15981056 | tf_op jit(solution)/shard_map/norm_back/pallas_call | solution.py:208
  483.6 12.9 %convolution_convert_fusion = bf16[1056,1664]{1,0:T(8,128)(2,1)} fusion(bf16[1056,2048]{1,0:T(8,128)(2,1)} %get-tuple-element.215.refs_1_, bf16[2048,1664]{1,0:T(8,128)(2,1)} %constant_dynamic-update-slice_fusion.8.down_ref), kind=kOutput, calls=%fused_computation | convolution fusion | flops 7199182848 | bytes 14655488 | tf_op jit(solution)/shard_map/dot_general | solution.py:17
  496.6 16.6 %wgrad.11 = bf16[1024,1664]{1,0:T(8,128)(2,1)} custom-call(s32[2]{0:T(128)} %pad_add_fusion.index_ref, bf16[1056,2048]{1,0:T(8,128)(2,1)} %get-tuple-element.216.refs_0_, bf16[1056,2048]{1,0:T(8,128)(2,1)} %get-tuple-element.209.refs_1_, bf16[528,1664]{1,0:T(8,128)(2,1)} %get-tuple-element.192.n0.refs_2_, ...), custom_call_target="tpu_custom_call" | custom-call | flops 7197425664 | bytes 14761984 | tf_op jit(solution)/shard_map/wgrad/pallas_call | solution.py:465
  513.2 4.2 fusion.10
  517.6 4.6 add_convert_fusion.5
  522.6 9.6 %attend_bwd.8 = (bf16[528,624]{1,0:T(8,128)(2,1)}, f32[1,624]{1,0:T(1,128)}, bf16[528,1664]{1,0:T(8,128)(2,1)}) custom-call(bf16[528,1664]{1,0:T(8,128)(2,1)} %get-tuple-element.272.g_ref.refs_4_, bf16[528,624]{1,0:T(8,128)(2,1)} %get-tuple-element.220.refs_0_, f32[8,512]{1,0:T(8,128)} %get-tuple-element.221.refs_1_, f32[8,128]{1,0:T(8,128)} %get-tuple-element.222.refs_2_, ...), custom_call_target="tpu_custom_call" | custom-call | flops 1734606848 | bytes 7783872 | tf_op jit(solution)/shard_map/attend_bwd/pallas_call | solution.py:208
  532.3 4.1 fusion.9
  542.5 9.8 %attend_bwd.9 = (bf16[528,624]{1,0:T(8,128)(2,1)}, f32[1,624]{1,0:T(1,128)}, bf16[528,1664]{1,0:T(8,128)(2,1)}) custom-call(bf16[528,1664]{1,0:T(8,128)(2,1)} %copy-done.5, bf16[528,624]{1,0:T(8,128)(2,1)} %get-tuple-element.228.refs_0_, f32[8,512]{1,0:T(8,128)} %get-tuple-element.229.refs_1_, f32[8,128]{1,0:T(8,128)} %get-tuple-element.230.refs_2_, ...), custom_call_target="tpu_custom_call" | custom-call | flops 1734606848 | bytes 7783872 | tf_op jit(solution)/shard_map/attend_bwd/pallas_call | solution.py:208
  552.3 5.7 add_convert_fusion.7
  564.0 9.7 %attend_bwd.10 = (bf16[528,624]{1,0:T(8,128)(2,1)}, f32[1,624]{1,0:T(1,128)}, bf16[528,1664]{1,0:T(8,128)(2,1)}) custom-call(bf16[528,1664]{1,0:T(8,128)(2,1)} %collective-permute-done.33.g_ref.refs_6_, bf16[528,624]{1,0:T(8,128)(2,1)} %get-tuple-element.235.refs_0_, f32[8,512]{1,0:T(8,128)} %get-tuple-element.236.refs_1_, ...), custom_call_target="tpu_custom_call" | custom-call | flops 1734606848 | bytes 7783872 | tf_op jit(solution)/shard_map/attend_bwd/pallas_call | solution.py:208
  574.9 10.1 %attend_bwd.11 = (bf16[528,624]{1,0:T(8,128)(2,1)}, f32[1,624]{1,0:T(1,128)}, bf16[528,1664]{1,0:T(8,128)(2,1)}) custom-call(bf16[528,1664]{1,0:T(8,128)(2,1)} %copy-done.6, bf16[528,624]{1,0:T(8,128)(2,1)} %get-tuple-element.240.refs_0_, f32[8,512]{1,0:T(8,128)} %get-tuple-element.241.refs_1_, f32[8,128]{1,0:T(8,128)} %get-tuple-element.242.refs_2_, ...), custom_call_target="tpu_custom_call" | custom-call | flops 1734606848 | bytes 7783872 | tf_op jit(solution)/shard_map/attend_bwd/pallas_call | solution.py:208
  586.9 13.3 %wgrad.12 = bf16[624,1664]{1,0:T(8,128)(2,1)} custom-call(s32[1]{0:T(128)} %constant.468.clone.1.index_ref, bf16[528,624]{1,0:T(8,128)(2,1)} %get-tuple-element.245.refs_0_, bf16[528,624]{1,0:T(8,128)(2,1)} %get-tuple-element.246.refs_1_, bf16[528,624]{1,0:T(8,128)(2,1)} %get-tuple-element.247.refs_2_, bf16[528,624]{1,0:T(8,128)(2,1)} %get-tuple-element.248.refs_3_, ...), custom_call_target="tpu_custom_call" | custom-call | flops 4385931264 | bytes 11741184 | tf_op jit(solution)/shard_map/wgrad/pallas_call | solution.py:465
  600.1 7.7 wgrad.13
  607.8 10.2 %attend_bwd.12 = (bf16[528,624]{1,0:T(8,128)(2,1)}, f32[1,624]{1,0:T(1,128)}, bf16[528,1664]{1,0:T(8,128)(2,1)}) custom-call(bf16[528,1664]{1,0:T(8,128)(2,1)} %copy-done.6, bf16[528,624]{1,0:T(8,128)(2,1)} %get-tuple-element.254.refs_0_, f32[8,512]{1,0:T(8,128)} %get-tuple-element.255.refs_1_, f32[8,128]{1,0:T(8,128)} %get-tuple-element.256.refs_2_, ...), custom_call_target="tpu_custom_call" | custom-call | flops 1734606848 | bytes 9541056 | tf_op jit(solution)/shard_map/attend_bwd/pallas_call | solution.py:208
  619.8 4.5 pad_maximum_fusion
  629.0 10.3 %attend_bwd.13 = (bf16[528,624]{1,0:T(8,128)(2,1)}, f32[1,624]{1,0:T(1,128)}, bf16[528,1664]{1,0:T(8,128)(2,1)}) custom-call(bf16[528,1664]{1,0:T(8,128)(2,1)} %copy-done.5, bf16[528,624]{1,0:T(8,128)(2,1)} %get-tuple-element.261.refs_0_, f32[8,512]{1,0:T(8,128)} %get-tuple-element.262.refs_1_, f32[8,128]{1,0:T(8,128)} %get-tuple-element.263.refs_2_, ...), custom_call_target="tpu_custom_call" | custom-call | flops 1734606848 | bytes 9541056 | tf_op jit(solution)/shard_map/attend_bwd/pallas_call | solution.py:208
  643.0 18.1 %collective-permute-done.40 = bf16[416,1664]{1,0:T(8,128)(2,1)} collective-permute-done((bf16[416,1664]{1,0:T(8,128)(2,1)}, bf16[416,1664]{1,0:T(8,128)(2,1)}, u32[]{:S(2)}, u32[]{:S(2)}) %collective-permute-start.40) | collective-permute-done | bytes 1384480 | tf_op jit(solution)/shard_map/ppermute | solution.py:542
  664.0 10.7 %attend_bwd.14 = (bf16[528,624]{1,0:T(8,128)(2,1)}, f32[1,624]{1,0:T(1,128)}, bf16[528,1664]{1,0:T(8,128)(2,1)}) custom-call(bf16[528,1664]{1,0:T(8,128)(2,1)} %collective-permute-done.33.g_ref.refs_6_, bf16[528,624]{1,0:T(8,128)(2,1)} %get-tuple-element.267.refs_0_, f32[8,512]{1,0:T(8,128)} %get-tuple-element.268.refs_1_, ...), custom_call_target="tpu_custom_call" | custom-call | flops 1734606848 | bytes 11298240 | tf_op jit(solution)/shard_map/attend_bwd/pallas_call | solution.py:208
  674.8 6.0 collective-permute-done.42
  683.1 10.8 %attend_bwd.15 = (bf16[528,624]{1,0:T(8,128)(2,1)}, f32[1,624]{1,0:T(1,128)}, bf16[528,1664]{1,0:T(8,128)(2,1)}) custom-call(bf16[528,1664]{1,0:T(8,128)(2,1)} %get-tuple-element.272.g_ref.refs_4_, bf16[528,624]{1,0:T(8,128)(2,1)} %get-tuple-element.273.refs_0_, f32[8,512]{1,0:T(8,128)} %get-tuple-element.274.refs_1_, f32[8,128]{1,0:T(8,128)} %get-tuple-element.275.refs_2_, ...), custom_call_target="tpu_custom_call" | custom-call | flops 1734606848 | bytes 9541056 | tf_op jit(solution)/shard_map/attend_bwd/pallas_call | solution.py:208
  699.0 13.2 %wgrad.14 = bf16[624,1664]{1,0:T(8,128)(2,1)} custom-call(s32[1]{0:T(128)} %constant.468.clone.1.index_ref, bf16[528,624]{1,0:T(8,128)(2,1)} %get-tuple-element.279.refs_0_, bf16[528,624]{1,0:T(8,128)(2,1)} %get-tuple-element.280.refs_1_, bf16[528,624]{1,0:T(8,128)(2,1)} %get-tuple-element.281.refs_2_, bf16[528,624]{1,0:T(8,128)(2,1)} %get-tuple-element.282.refs_3_, ...), custom_call_target="tpu_custom_call" | custom-call | flops 4385931264 | bytes 11741184 | tf_op jit(solution)/shard_map/wgrad/pallas_call | solution.py:465
  712.3 7.6 wgrad.15
  720.0 4.5 fusion.1
  731.0 5.7 unpack.2
  736.7 21.4 %collective-permute-done.47 = bf16[416,1664]{1,0:T(8,128)(2,1)} collective-permute-done((bf16[416,1664]{1,0:T(8,128)(2,1)}, bf16[416,1664]{1,0:T(8,128)(2,1)}, u32[]{:S(2)}, u32[]{:S(2)}) %collective-permute-start.47) | collective-permute-done | bytes 1384480 | tf_op jit(solution)/shard_map/ppermute | solution.py:542
  762.1 9.6 %norm_back.3 = (f32[8,1664]{1,0:T(8,128)}, bf16[528,1664]{1,0:T(8,128)(2,1)}, f32[8,1664]{1,0:T(8,128)}, f32[8,1664]{1,0:T(8,128)}, f32[8,1664]{1,0:T(8,128)}) custom-call(bf16[528,1664]{1,0:T(8,128)(2,1)} %get-tuple-element.290.x_ref, bf16[528,1664]{1,0:T(8,128)(2,1)} %get-tuple-element.277.a_ref, bf16[528,1664]{1,0:T(8,128)(2,1)} %collective-permute-done.48.b_ref, ...), custom_call_target="tpu_custom_call" | custom-call | bytes 12519936 | tf_op jit(solution)/shard_map/norm_back/pallas_call | solution.py:208
  776.9 19.5 %collective-permute-done.52 = f32[21504]{0:T(1024)S(1)} collective-permute-done((f32[21504]{0:T(1024)S(1)}, f32[21504]{0:T(1024)S(1)}, u32[]{:S(2)}, u32[]{:S(2)}) %collective-permute-start.52) | collective-permute-done | bytes 86048 | tf_op jit(solution)/shard_map/ppermute | solution.py:542
  798.6 18.8 %collective-permute-done.53 = f32[21504]{0:T(1024)S(1)} collective-permute-done((f32[21504]{0:T(1024)S(1)}, f32[21504]{0:T(1024)S(1)}, u32[]{:S(2)}, u32[]{:S(2)}) %collective-permute-start.53) | collective-permute-done | bytes 86048 | tf_op jit(solution)/shard_map/ppermute | solution.py:542
  825.7 6.5 collective-permute-done.50
  832.2 4.7 collective-permute-start.56
  850.5 6.9 collective-permute-done.57
  858.8 3.3 unpack.3
  862.1 4.0 copy.53
  866.1 9.0 place.2
  875.9 10.6 %place.3 = f32[1664,2048]{1,0:T(8,128)} custom-call(s32[8]{0:T(128)} %stack.138.at_ref, bf16[256,1664]{1,0:T(8,128)(2,1)} %add_convert_fusion.8.refs_0_, bf16[256,1664]{1,0:T(8,128)(2,1)} %collective-permute-done.71.refs_1_, bf16[256,1664]{1,0:T(8,128)(2,1)} %copy-done.27, bf16[256,1664]{1,0:T(8,128)(2,1)} %collective-permute-done.73.refs_3_, ...), custom_call_target="tpu_custom_call" | custom-call | bytes 20447264 | tf_op jit(solution)/shard_map/place/pallas_call | solution.py:208
  900.5 3.7 maximum_convert_fusion
  (381 shorter events, 181.1 us)
Async XLA Ops:
  11.7 51.4 %collective-permute-start.1 = (bf16[528,1664]{1,0:T(8,128)(2,1)}, bf16[528,1664]{1,0:T(8,128)(2,1)}, u32[]{:S(2)}, u32[]{:S(2)}) collective-permute-start(bf16[528,1664]{1,0:T(8,128)(2,1)} %get-tuple-element.181.n_ref.refs_4_), channel_id=1, source_target_pairs={{0,4},{1,5},{2,6},{3,7},{4,0},{5,1},{6,2},{7,3},{8,12},{9,13},{10,... | collective-permute-start | bytes 5271560 | tf_op jit(solution)/shard_map/ppermute | solution.py:542
  12.2 59.5 %collective-permute-start = (bf16[528,1664]{1,0:T(8,128)(2,1)}, bf16[528,1664]{1,0:T(8,128)(2,1)}, u32[]{:S(2)}, u32[]{:S(2)}) collective-permute-start(bf16[528,1664]{1,0:T(8,128)(2,1)} %get-tuple-element.181.n_ref.refs_4_), channel_id=1, source_target_pairs={{0,1},{1,0},{2,3},{3,2},{4,5},{5,4},{6,7},{7,6},{8,9},{9,8},{10,11... | collective-permute-start | bytes 5271560 | tf_op jit(solution)/shard_map/ppermute | solution.py:542
  15.0 38.8 %collective-permute-start.7 = (f32[1440]{0:T(1024)S(1)}, f32[1440]{0:T(1024)S(1)}, u32[]{:S(2)}, u32[]{:S(2)}) collective-permute-start(f32[1440]{0:T(1024)S(1)} %pad_maximum_fusion.2), channel_id=1, source_target_pairs={{0,2},{1,3},{2,0},{3,1},{4,6},{5,7},{6,4},{7,5},{8,10},{9,11},{10,... | collective-permute-start | bytes 17288 | tf_op jit(solution)/shard_map/ppermute | solution.py:542
  18.4 53.9 %collective-permute-start.8 = (bf16[64,1664]{1,0:T(8,128)(2,1)}, bf16[64,1664]{1,0:T(8,128)(2,1)}, u32[]{:S(2)}, u32[]{:S(2)}) collective-permute-start(bf16[64,1664]{1,0:T(8,128)(2,1)} %constant_dynamic-slice_fusion.10), channel_id=1, source_target_pairs={{0,2},{1,3},{2,0},{3,1},{4,6},{5,7},{6,4},{7,5},{8,10},{9,11},{10,... | collective-permute-start | bytes 638984 | tf_op jit(solution)/shard_map/ppermute | solution.py:542
  27.7 48.1 %collective-permute-start.3 = (bf16[416,624]{1,0:T(8,128)(2,1)}, bf16[416,624]{1,0:T(8,128)(2,1)S(1)}, u32[]{:S(2)}, u32[]{:S(2)}) collective-permute-start(bf16[416,624]{1,0:T(8,128)(2,1)} %constant_dynamic-slice_fusion.11), channel_id=1, source_target_pairs={{0,2},{1,3},{2,0},{3,1},{4,6},{5,7},{6,4},{7,5},{8,10},{9,11},{10,... | collective-permute-start | bytes 1557512 | tf_op jit(solution)/shard_map/ppermute | solution.py:542
  71.7 40.8 %collective-permute-start.2 = (bf16[528,1664]{1,0:T(8,128)(2,1)}, bf16[528,1664]{1,0:T(8,128)(2,1)}, u32[]{:S(2)}, u32[]{:S(2)}) collective-permute-start(bf16[528,1664]{1,0:T(8,128)(2,1)} %collective-permute-done.n_ref.refs_6_), channel_id=1, source_target_pairs={{0,4},{1,5},{2,6},{3,7},{4,0},{5,1},{6,2},{7,3},{8,12},{9,13},{10,... | collective-permute-start | bytes 5271560 | tf_op jit(solution)/shard_map/ppermute | solution.py:542
  75.8 20.8 %collective-permute-start.4 = (bf16[416,624]{1,0:T(8,128)(2,1)S(1)}, bf16[416,624]{1,0:T(8,128)(2,1)S(1)}, u32[]{:S(2)}, u32[]{:S(2)}) collective-permute-start(bf16[416,624]{1,0:T(8,128)(2,1)S(1)} %collective-permute-done.3), channel_id=1, source_target_pairs={{0,8},{1,9},{2,10},{3,11},{4,12},{5,13},{6,14},{7,15},{8,0},{9,1},... | collective-permute-start | bytes 1557512 | tf_op jit(solution)/shard_map/ppermute | solution.py:542
  87.4 24.8 %collective-permute-start.5 = (bf16[416,624]{1,0:T(8,128)(2,1)S(1)}, bf16[416,624]{1,0:T(8,128)(2,1)S(1)}, u32[]{:S(2)}, u32[]{:S(2)}) collective-permute-start(bf16[416,624]{1,0:T(8,128)(2,1)S(1)} %collective-permute-done.3), channel_id=1, source_target_pairs={{0,16},{1,17},{2,18},{3,19},{4,20},{5,21},{6,22},{7,23},{8,24},{9,... | collective-permute-start | bytes 1557512 | tf_op jit(solution)/shard_map/ppermute | solution.py:542
  90.0 22.3 %collective-permute-start.6 = (bf16[416,624]{1,0:T(8,128)(2,1)S(1)}, bf16[416,624]{1,0:T(8,128)(2,1)S(1)}, u32[]{:S(2)}, u32[]{:S(2)}) collective-permute-start(bf16[416,624]{1,0:T(8,128)(2,1)S(1)} %collective-permute-done.3), channel_id=1, source_target_pairs={{0,24},{1,25},{2,26},{3,27},{4,28},{5,29},{6,30},{7,31},{8,16},{9,... | collective-permute-start | bytes 1557512 | tf_op jit(solution)/shard_map/ppermute | solution.py:542
  131.0 80.2 %collective-permute-start.12 = (bf16[528,1664]{1,0:T(8,128)(2,1)}, bf16[528,1664]{1,0:T(8,128)(2,1)S(1)}, u32[]{:S(2)}, u32[]{:S(2)}) collective-permute-start(bf16[528,1664]{1,0:T(8,128)(2,1)} %get-tuple-element.176), channel_id=1, source_target_pairs={{0,4},{1,5},{2,6},{3,7},{4,0},{5,1},{6,2},{7,3},{8,12},{9,13},{10,... | collective-permute-start | bytes 5271560 | tf_op jit(solution)/shard_map/ppermute | solution.py:542
  132.7 59.9 %collective-permute-start.13 = (bf16[1664,256]{1,0:T(8,128)(2,1)S(1)}, bf16[1664,256]{1,0:T(8,128)(2,1)}, u32[]{:S(2)}, u32[]{:S(2)}) collective-permute-start(bf16[1664,256]{1,0:T(8,128)(2,1)S(1)} %constant_dynamic-slice_fusion.8), channel_id=1, source_target_pairs={{0,2},{1,3},{2,0},{3,1},{4,6},{5,7},{6,4},{7,5},{8,10},{9,11},{10,... | collective-permute-start | bytes 2555912 | tf_op jit(solution)/shard_map/ppermute | solution.py:542
  137.6 73.1 %collective-permute-start.17 = (bf16[256,1664]{1,0:T(8,128)(2,1)S(1)}, bf16[256,1664]{1,0:T(8,128)(2,1)}, u32[]{:S(2)}, u32[]{:S(2)}) collective-permute-start(bf16[256,1664]{1,0:T(8,128)(2,1)S(1)} %constant_dynamic-slice_fusion.6), channel_id=1, source_target_pairs={{0,2},{1,3},{2,0},{3,1},{4,6},{5,7},{6,4},{7,5},{8,10},{9,11},{10,... | collective-permute-start | bytes 2555912 | tf_op jit(solution)/shard_map/ppermute | solution.py:542
  192.6 44.0 %collective-permute-start.14 = (bf16[1664,256]{1,0:T(8,128)(2,1)}, bf16[1664,256]{1,0:T(8,128)(2,1)}, u32[]{:S(2)}, u32[]{:S(2)}) collective-permute-start(bf16[1664,256]{1,0:T(8,128)(2,1)} %collective-permute-done.13), channel_id=1, source_target_pairs={{0,8},{1,9},{2,10},{3,11},{4,12},{5,13},{6,14},{7,15},{8,0},{9,1},... | collective-permute-start | bytes 2555912 | tf_op jit(solution)/shard_map/ppermute | solution.py:542
  193.1 44.8 %collective-permute-start.15 = (bf16[1664,256]{1,0:T(8,128)(2,1)}, bf16[1664,256]{1,0:T(8,128)(2,1)}, u32[]{:S(2)}, u32[]{:S(2)}) collective-permute-start(bf16[1664,256]{1,0:T(8,128)(2,1)} %collective-permute-done.13), channel_id=1, source_target_pairs={{0,16},{1,17},{2,18},{3,19},{4,20},{5,21},{6,22},{7,23},{8,24},{9,... | collective-permute-start | bytes 2555912 | tf_op jit(solution)/shard_map/ppermute | solution.py:542
  194.5 44.8 %collective-permute-start.16 = (bf16[1664,256]{1,0:T(8,128)(2,1)}, bf16[1664,256]{1,0:T(8,128)(2,1)}, u32[]{:S(2)}, u32[]{:S(2)}) collective-permute-start(bf16[1664,256]{1,0:T(8,128)(2,1)} %collective-permute-done.13), channel_id=1, source_target_pairs={{0,24},{1,25},{2,26},{3,27},{4,28},{5,29},{6,30},{7,31},{8,16},{9,... | collective-permute-start | bytes 2555912 | tf_op jit(solution)/shard_map/ppermute | solution.py:542
  210.6 40.7 %collective-permute-start.18 = (bf16[256,1664]{1,0:T(8,128)(2,1)}, bf16[256,1664]{1,0:T(8,128)(2,1)}, u32[]{:S(2)}, u32[]{:S(2)}) collective-permute-start(bf16[256,1664]{1,0:T(8,128)(2,1)} %collective-permute-done.17), channel_id=1, source_target_pairs={{0,8},{1,9},{2,10},{3,11},{4,12},{5,13},{6,14},{7,15},{8,0},{9,1},... | collective-permute-start | bytes 2555912 | tf_op jit(solution)/shard_map/ppermute | solution.py:542
  211.2 42.5 %collective-permute-start.19 = (bf16[256,1664]{1,0:T(8,128)(2,1)}, bf16[256,1664]{1,0:T(8,128)(2,1)}, u32[]{:S(2)}, u32[]{:S(2)}) collective-permute-start(bf16[256,1664]{1,0:T(8,128)(2,1)} %collective-permute-done.17), channel_id=1, source_target_pairs={{0,16},{1,17},{2,18},{3,19},{4,20},{5,21},{6,22},{7,23},{8,24},{9,... | collective-permute-start | bytes 2555912 | tf_op jit(solution)/shard_map/ppermute | solution.py:542
  236.6 33.5 %collective-permute-start.21 = (bf16[528,1664]{1,0:T(8,128)(2,1)}, bf16[528,1664]{1,0:T(8,128)(2,1)S(1)}, u32[]{:S(2)}, u32[]{:S(2)}) collective-permute-start(bf16[528,1664]{1,0:T(8,128)(2,1)} %get-tuple-element.178), channel_id=1, source_target_pairs={{0,4},{1,5},{2,6},{3,7},{4,0},{5,1},{6,2},{7,3},{8,12},{9,13},{10,... | collective-permute-start | bytes 5271560 | tf_op jit(solution)/shard_map/ppermute | solution.py:542
  238.0 41.5 %collective-permute-start.22 = (bf16[528,1664]{1,0:T(8,128)(2,1)}, bf16[528,1664]{1,0:T(8,128)(2,1)}, u32[]{:S(2)}, u32[]{:S(2)}) collective-permute-start(bf16[528,1664]{1,0:T(8,128)(2,1)} %get-tuple-element.180), channel_id=1, source_target_pairs={{0,1},{1,0},{2,3},{3,2},{4,5},{5,4},{6,7},{7,6},{8,9},{9,8},{10,11... | collective-permute-start | bytes 5271560 | tf_op jit(solution)/shard_map/ppermute | solution.py:542
  239.3 29.8 %collective-permute-start.20 = (bf16[256,1664]{1,0:T(8,128)(2,1)}, bf16[256,1664]{1,0:T(8,128)(2,1)S(1)}, u32[]{:S(2)}, u32[]{:S(2)}) collective-permute-start(bf16[256,1664]{1,0:T(8,128)(2,1)} %collective-permute-done.17), channel_id=1, source_target_pairs={{0,24},{1,25},{2,26},{3,27},{4,28},{5,29},{6,30},{7,31},{8,16},{9,... | collective-permute-start | bytes 2555912 | tf_op jit(solution)/shard_map/ppermute | solution.py:542
  251.3 65.7 %collective-permute-start.24 = (bf16[528,1664]{1,0:T(8,128)(2,1)S(1)}, bf16[528,1664]{1,0:T(8,128)(2,1)}, u32[]{:S(2)}, u32[]{:S(2)}) collective-permute-start(bf16[528,1664]{1,0:T(8,128)(2,1)S(1)} %copy-done.19), channel_id=1, source_target_pairs={{0,4},{1,5},{2,6},{3,7},{4,0},{5,1},{6,2},{7,3},{8,12},{9,13},{10,... | collective-permute-start | bytes 5271560 | tf_op jit(solution)/shard_map/ppermute | solution.py:542
  253.7 63.1 %collective-permute-start.27 = (bf16[528,1664]{1,0:T(8,128)(2,1)S(1)}, bf16[528,1664]{1,0:T(8,128)(2,1)}, u32[]{:S(2)}, u32[]{:S(2)}) collective-permute-start(bf16[528,1664]{1,0:T(8,128)(2,1)S(1)} %copy-done.19), channel_id=1, source_target_pairs={{0,1},{1,0},{2,3},{3,2},{4,5},{5,4},{6,7},{7,6},{8,9},{9,8},{10,11... | collective-permute-start | bytes 5271560 | tf_op jit(solution)/shard_map/ppermute | solution.py:542
  288.0 29.0 %collective-permute-start.23 = (bf16[528,1664]{1,0:T(8,128)(2,1)}, bf16[528,1664]{1,0:T(8,128)(2,1)}, u32[]{:S(2)}, u32[]{:S(2)}) collective-permute-start(bf16[528,1664]{1,0:T(8,128)(2,1)} %get-tuple-element.192.n0.refs_2_), channel_id=1, source_target_pairs={{0,4},{1,5},{2,6},{3,7},{4,0},{5,1},{6,2},{7,3},{8,12},{9,13},{10,... | collective-permute-start | bytes 5271560 | tf_op jit(solution)/shard_map/ppermute | solution.py:542
  316.7 54.6 %collective-permute-start.28 = (bf16[528,1664]{1,0:T(8,128)(2,1)}, bf16[528,1664]{1,0:T(8,128)(2,1)}, u32[]{:S(2)}, u32[]{:S(2)}) collective-permute-start(bf16[528,1664]{1,0:T(8,128)(2,1)} %collective-permute-done.27.c0.refs_4_), channel_id=1, source_target_pairs={{0,4},{1,5},{2,6},{3,7},{4,0},{5,1},{6,2},{7,3},{8,12},{9,13},{10,... | collective-permute-start | bytes 5271560 | tf_op jit(solution)/shard_map/ppermute | solution.py:542
  316.7 41.0 %collective-permute-start.25 = (bf16[528,1664]{1,0:T(8,128)(2,1)}, bf16[528,1664]{1,0:T(8,128)(2,1)S(1)}, u32[]{:S(2)}, u32[]{:S(2)}) collective-permute-start(bf16[528,1664]{1,0:T(8,128)(2,1)} %get-tuple-element.192.n0.refs_2_), channel_id=1, source_target_pairs={{0,1},{1,0},{2,3},{3,2},{4,5},{5,4},{6,7},{7,6},{8,9},{9,8},{10,11... | collective-permute-start | bytes 5271560 | tf_op jit(solution)/shard_map/ppermute | solution.py:542
  409.1 60.1 %collective-permute-start.30 = (bf16[528,1664]{1,0:T(8,128)(2,1)}, bf16[528,1664]{1,0:T(8,128)(2,1)S(1)}, u32[]{:S(2)}, u32[]{:S(2)}) collective-permute-start(bf16[528,1664]{1,0:T(8,128)(2,1)} %get-tuple-element.213), channel_id=1, source_target_pairs={{0,4},{1,5},{2,6},{3,7},{4,0},{5,1},{6,2},{7,3},{8,12},{9,13},{10,... | collective-permute-start | bytes 5271560 | tf_op jit(solution)/shard_map/ppermute | solution.py:542
  429.3 40.5 %collective-permute-start.31 = (bf16[528,1664]{1,0:T(8,128)(2,1)}, bf16[528,1664]{1,0:T(8,128)(2,1)S(1)}, u32[]{:S(2)}, u32[]{:S(2)}) collective-permute-start(bf16[528,1664]{1,0:T(8,128)(2,1)} %add_convert_fusion.1), channel_id=1, source_target_pairs={{0,1},{1,0},{2,3},{3,2},{4,5},{5,4},{6,7},{7,6},{8,9},{9,8},{10,11... | collective-permute-start | bytes 5271560 | tf_op jit(solution)/shard_map/ppermute | solution.py:542
  432.9 84.7 %collective-permute-start.34 = (bf16[1024,1664]{1,0:T(8,128)(2,1)}, bf16[1024,1664]{1,0:T(8,128)(2,1)}, u32[]{:S(2)}, u32[]{:S(2)}) collective-permute-start(bf16[1024,1664]{1,0:T(8,128)(2,1)} %wgrad.8), channel_id=1, source_target_pairs={{0,16},{1,17},{2,18},{3,19},{4,20},{5,21},{6,22},{7,23},{8,24},{9,... | collective-permute-start | bytes 10223624 | tf_op jit(solution)/shard_map/ppermute | solution.py:542
  451.0 101.3 %collective-permute-start.32 = (bf16[1024,1664]{1,0:T(8,128)(2,1)}, bf16[1024,1664]{1,0:T(8,128)(2,1)}, u32[]{:S(2)}, u32[]{:S(2)}) collective-permute-start(bf16[1024,1664]{1,0:T(8,128)(2,1)} %wgrad.9), channel_id=1, source_target_pairs={{0,8},{1,9},{2,10},{3,11},{4,12},{5,13},{6,14},{7,15},{8,0},{9,1},... | collective-permute-start | bytes 10223624 | tf_op jit(solution)/shard_map/ppermute | solution.py:542
  482.0 59.3 %collective-permute-start.36 = (bf16[528,1664]{1,0:T(8,128)(2,1)}, bf16[528,1664]{1,0:T(8,128)(2,1)S(1)}, u32[]{:S(2)}, u32[]{:S(2)}) collective-permute-start(bf16[528,1664]{1,0:T(8,128)(2,1)} %get-tuple-element.272.g_ref.refs_4_), channel_id=1, source_target_pairs={{0,4},{1,5},{2,6},{3,7},{4,0},{5,1},{6,2},{7,3},{8,12},{9,13},{10,... | collective-permute-start | bytes 5271560 | tf_op jit(solution)/shard_map/ppermute | solution.py:542
  482.0 50.2 %collective-permute-start.33 = (bf16[528,1664]{1,0:T(8,128)(2,1)}, bf16[528,1664]{1,0:T(8,128)(2,1)}, u32[]{:S(2)}, u32[]{:S(2)}) collective-permute-start(bf16[528,1664]{1,0:T(8,128)(2,1)} %get-tuple-element.272.g_ref.refs_4_), channel_id=1, source_target_pairs={{0,1},{1,0},{2,3},{3,2},{4,5},{5,4},{6,7},{7,6},{8,9},{9,8},{10,11... | collective-permute-start | bytes 5271560 | tf_op jit(solution)/shard_map/ppermute | solution.py:542
  517.4 41.7 %collective-permute-start.37 = (bf16[528,1664]{1,0:T(8,128)(2,1)}, bf16[528,1664]{1,0:T(8,128)(2,1)}, u32[]{:S(2)}, u32[]{:S(2)}) collective-permute-start(bf16[528,1664]{1,0:T(8,128)(2,1)} %get-tuple-element.348), channel_id=1, source_target_pairs={{0,4},{1,5},{2,6},{3,7},{4,0},{5,1},{6,2},{7,3},{8,12},{9,13},{10,... | collective-permute-start | bytes 5271560 | tf_op jit(solution)/shard_map/ppermute | solution.py:542
  522.2 62.8 %collective-permute-start.38 = (bf16[512,1664]{1,0:T(8,128)(2,1)}, bf16[512,1664]{1,0:T(8,128)(2,1)}, u32[]{:S(2)}, u32[]{:S(2)}) collective-permute-start(bf16[512,1664]{1,0:T(8,128)(2,1)} %bitcast.19), channel_id=1, source_target_pairs={{0,8},{1,9},{2,10},{3,11},{4,12},{5,13},{6,14},{7,15},{8,0},{9,1},... | collective-permute-start | bytes 5111816 | tf_op jit(solution)/shard_map/ppermute | solution.py:542
  532.2 41.4 %collective-permute-start.35 = (bf16[528,1664]{1,0:T(8,128)(2,1)}, bf16[528,1664]{1,0:T(8,128)(2,1)S(1)}, u32[]{:S(2)}, u32[]{:S(2)}) collective-permute-start(bf16[528,1664]{1,0:T(8,128)(2,1)} %collective-permute-done.33.g_ref.refs_6_), channel_id=1, source_target_pairs={{0,4},{1,5},{2,6},{3,7},{4,0},{5,1},{6,2},{7,3},{8,12},{9,13},{10,... | collective-permute-start | bytes 5271560 | tf_op jit(solution)/shard_map/ppermute | solution.py:542
  541.3 187.1 %collective-permute-start.45 = (bf16[528,1664]{1,0:T(8,128)(2,1)}, bf16[528,1664]{1,0:T(8,128)(2,1)}, u32[]{:S(2)}, u32[]{:S(2)}) collective-permute-start(bf16[528,1664]{1,0:T(8,128)(2,1)} %get-tuple-element.345), channel_id=1, source_target_pairs={{0,4},{1,5},{2,6},{3,7},{4,0},{5,1},{6,2},{7,3},{8,12},{9,13},{10,... | collective-permute-start | bytes 5271560 | tf_op jit(solution)/shard_map/ppermute | solution.py:542
  558.0 66.4 %collective-permute-start.39 = (bf16[512,1664]{1,0:T(8,128)(2,1)}, bf16[512,1664]{1,0:T(8,128)(2,1)}, u32[]{:S(2)}, u32[]{:S(2)}) collective-permute-start(bf16[512,1664]{1,0:T(8,128)(2,1)} %bitcast.23), channel_id=1, source_target_pairs={{0,16},{1,17},{2,18},{3,19},{4,20},{5,21},{6,22},{7,23},{8,24},{9,... | collective-permute-start | bytes 5111816 | tf_op jit(solution)/shard_map/ppermute | solution.py:542
  562.2 167.6 %collective-permute-start.46 = (bf16[528,1664]{1,0:T(8,128)(2,1)}, bf16[528,1664]{1,0:T(8,128)(2,1)}, u32[]{:S(2)}, u32[]{:S(2)}) collective-permute-start(bf16[528,1664]{1,0:T(8,128)(2,1)} %add_convert_fusion), channel_id=1, source_target_pairs={{0,1},{1,0},{2,3},{3,2},{4,5},{5,4},{6,7},{7,6},{8,9},{9,8},{10,11... | collective-permute-start | bytes 5271560 | tf_op jit(solution)/shard_map/ppermute | solution.py:542
  618.1 45.6 %collective-permute-start.41 = (bf16[528,1664]{1,0:T(8,128)(2,1)}, bf16[528,1664]{1,0:T(8,128)(2,1)}, u32[]{:S(2)}, u32[]{:S(2)}) collective-permute-start(bf16[528,1664]{1,0:T(8,128)(2,1)} %get-tuple-element.257), channel_id=1, source_target_pairs={{0,4},{1,5},{2,6},{3,7},{4,0},{5,1},{6,2},{7,3},{8,12},{9,13},{10,... | collective-permute-start | bytes 5271560 | tf_op jit(solution)/shard_map/ppermute | solution.py:542
  628.2 33.0 %collective-permute-start.40 = (bf16[416,1664]{1,0:T(8,128)(2,1)}, bf16[416,1664]{1,0:T(8,128)(2,1)}, u32[]{:S(2)}, u32[]{:S(2)}) collective-permute-start(bf16[416,1664]{1,0:T(8,128)(2,1)} %get-tuple-element.356), channel_id=1, source_target_pairs={{0,16},{1,17},{2,18},{3,19},{4,20},{5,21},{6,22},{7,23},{8,24},{9,... | collective-permute-start | bytes 4153352 | tf_op jit(solution)/shard_map/ppermute | solution.py:542
  640.6 40.2 %collective-permute-start.42 = (bf16[256,1664]{1,0:T(8,128)(2,1)}, bf16[256,1664]{1,0:T(8,128)(2,1)S(1)}, u32[]{:S(2)}, u32[]{:S(2)}) collective-permute-start(bf16[256,1664]{1,0:T(8,128)(2,1)} %get-tuple-element.361), channel_id=1, source_target_pairs={{0,2},{1,3},{2,0},{3,1},{4,6},{5,7},{6,4},{7,5},{8,10},{9,11},{10,... | collective-permute-start | bytes 2555912 | tf_op jit(solution)/shard_map/ppermute | solution.py:542
  661.2 99.7 %collective-permute-start.48 = (bf16[528,1664]{1,0:T(8,128)(2,1)}, bf16[528,1664]{1,0:T(8,128)(2,1)}, u32[]{:S(2)}, u32[]{:S(2)}) collective-permute-start(bf16[528,1664]{1,0:T(8,128)(2,1)} %get-tuple-element.264), channel_id=1, source_target_pairs={{0,4},{1,5},{2,6},{3,7},{4,0},{5,1},{6,2},{7,3},{8,12},{9,13},{10,... | collective-permute-start | bytes 5271560 | tf_op jit(solution)/shard_map/ppermute | solution.py:542
  663.7 30.3 %collective-permute-start.43 = (bf16[208,1664]{1,0:T(8,128)(2,1)}, bf16[208,1664]{1,0:T(8,128)(2,1)}, u32[]{:S(2)}, u32[]{:S(2)}) collective-permute-start(bf16[208,1664]{1,0:T(8,128)(2,1)} %get-tuple-element.367), channel_id=1, source_target_pairs={{0,8},{1,9},{2,10},{3,11},{4,12},{5,13},{6,14},{7,15},{8,0},{9,1},... | collective-permute-start | bytes 2076680 | tf_op jit(solution)/shard_map/ppermute | solution.py:542
  681.7 42.8 %collective-permute-start.44 = (bf16[256,1664]{1,0:T(8,128)(2,1)}, bf16[256,1664]{1,0:T(8,128)(2,1)}, u32[]{:S(2)}, u32[]{:S(2)}) collective-permute-start(bf16[256,1664]{1,0:T(8,128)(2,1)} %get-tuple-element.363), channel_id=1, source_target_pairs={{0,2},{1,3},{2,0},{3,1},{4,6},{5,7},{6,4},{7,5},{8,10},{9,11},{10,... | collective-permute-start | bytes 2555912 | tf_op jit(solution)/shard_map/ppermute | solution.py:542
  693.9 67.0 %collective-permute-start.49 = (bf16[528,1664]{1,0:T(8,128)(2,1)}, bf16[528,1664]{1,0:T(8,128)(2,1)}, u32[]{:S(2)}, u32[]{:S(2)}) collective-permute-start(bf16[528,1664]{1,0:T(8,128)(2,1)} %get-tuple-element.270), channel_id=1, source_target_pairs={{0,1},{1,0},{2,3},{3,2},{4,5},{5,4},{6,7},{7,6},{8,9},{9,8},{10,11... | collective-permute-start | bytes 5271560 | tf_op jit(solution)/shard_map/ppermute | solution.py:542
  724.5 33.6 %collective-permute-start.47 = (bf16[416,1664]{1,0:T(8,128)(2,1)}, bf16[416,1664]{1,0:T(8,128)(2,1)}, u32[]{:S(2)}, u32[]{:S(2)}) collective-permute-start(bf16[416,1664]{1,0:T(8,128)(2,1)} %get-tuple-element.354), channel_id=1, source_target_pairs={{0,8},{1,9},{2,10},{3,11},{4,12},{5,13},{6,14},{7,15},{8,0},{9,1},... | collective-permute-start | bytes 4153352 | tf_op jit(solution)/shard_map/ppermute | solution.py:542
  728.4 46.5 %collective-permute-start.64 = (bf16[256,1664]{1,0:T(8,128)(2,1)S(1)}, bf16[256,1664]{1,0:T(8,128)(2,1)}, u32[]{:S(2)}, u32[]{:S(2)}) collective-permute-start(bf16[256,1664]{1,0:T(8,128)(2,1)S(1)} %add_convert_fusion.9.refs_0_), channel_id=1, source_target_pairs={{0,8},{1,9},{2,10},{3,11},{4,12},{5,13},{6,14},{7,15},{8,0},{9,1},... | collective-permute-start | bytes 2555912 | tf_op jit(solution)/shard_map/ppermute | solution.py:542
  729.8 45.3 %collective-permute-start.65 = (bf16[256,1664]{1,0:T(8,128)(2,1)S(1)}, bf16[256,1664]{1,0:T(8,128)(2,1)}, u32[]{:S(2)}, u32[]{:S(2)}) collective-permute-start(bf16[256,1664]{1,0:T(8,128)(2,1)S(1)} %add_convert_fusion.9.refs_0_), channel_id=1, source_target_pairs={{0,16},{1,17},{2,18},{3,19},{4,20},{5,21},{6,22},{7,23},{8,24},{9,... | collective-permute-start | bytes 2555912 | tf_op jit(solution)/shard_map/ppermute | solution.py:542
  758.1 18.8 %collective-permute-start.67 = (bf16[256,1664]{1,0:T(8,128)(2,1)S(1)}, bf16[256,1664]{1,0:T(8,128)(2,1)}, u32[]{:S(2)}, u32[]{:S(2)}) collective-permute-start(bf16[256,1664]{1,0:T(8,128)(2,1)S(1)} %add_convert_fusion.9.refs_0_), channel_id=1, source_target_pairs={{0,4},{1,5},{2,6},{3,7},{4,0},{5,1},{6,2},{7,3},{8,12},{9,13},{10,... | collective-permute-start | bytes 2555912 | tf_op jit(solution)/shard_map/ppermute | solution.py:542
  760.9 36.5 %collective-permute-start.51 = (bf16[208,1664]{1,0:T(8,128)(2,1)}, bf16[208,1664]{1,0:T(8,128)(2,1)S(1)}, u32[]{:S(2)}, u32[]{:S(2)}) collective-permute-start(bf16[208,1664]{1,0:T(8,128)(2,1)} %add_convert_fusion.13), channel_id=1, source_target_pairs={{0,2},{1,3},{2,0},{3,1},{4,6},{5,7},{6,4},{7,5},{8,10},{9,11},{10,... | collective-permute-start | bytes 2076680 | tf_op jit(solution)/shard_map/ppermute | solution.py:542
  760.9 57.3 %collective-permute-start.71 = (bf16[256,1664]{1,0:T(8,128)(2,1)S(1)}, bf16[256,1664]{1,0:T(8,128)(2,1)}, u32[]{:S(2)}, u32[]{:S(2)}) collective-permute-start(bf16[256,1664]{1,0:T(8,128)(2,1)S(1)} %copy-done.16), channel_id=1, source_target_pairs={{0,16},{1,17},{2,18},{3,19},{4,20},{5,21},{6,22},{7,23},{8,24},{9,... | collective-permute-start | bytes 2555912 | tf_op jit(solution)/shard_map/ppermute | solution.py:542
  774.8 43.5 %collective-permute-start.72 = (bf16[256,1664]{1,0:T(8,128)(2,1)S(1)}, bf16[256,1664]{1,0:T(8,128)(2,1)S(1)}, u32[]{:S(2)}, u32[]{:S(2)}) collective-permute-start(bf16[256,1664]{1,0:T(8,128)(2,1)S(1)} %copy-done.16), channel_id=1, source_target_pairs={{0,8},{1,9},{2,10},{3,11},{4,12},{5,13},{6,14},{7,15},{8,0},{9,1},... | collective-permute-start | bytes 2555912 | tf_op jit(solution)/shard_map/ppermute | solution.py:542
  775.1 21.3 %collective-permute-start.52 = (f32[21504]{0:T(1024)S(1)}, f32[21504]{0:T(1024)S(1)}, u32[]{:S(2)}, u32[]{:S(2)}) collective-permute-start(f32[21504]{0:T(1024)S(1)} %constant_dynamic-update-slice_fusion.24), channel_id=1, source_target_pairs={{0,8},{1,9},{2,10},{3,11},{4,12},{5,13},{6,14},{7,15},{8,0},{9,1},... | collective-permute-start | bytes 258056 | tf_op jit(solution)/shard_map/ppermute | solution.py:542
  776.9 41.9 %collective-permute-start.74 = (bf16[256,1664]{1,0:T(8,128)(2,1)S(1)}, bf16[256,1664]{1,0:T(8,128)(2,1)S(1)}, u32[]{:S(2)}, u32[]{:S(2)}) collective-permute-start(bf16[256,1664]{1,0:T(8,128)(2,1)S(1)} %copy-done.16), channel_id=1, source_target_pairs={{0,4},{1,5},{2,6},{3,7},{4,0},{5,1},{6,2},{7,3},{8,12},{9,13},{10,... | collective-permute-start | bytes 2555912 | tf_op jit(solution)/shard_map/ppermute | solution.py:542
  796.4 24.1 %collective-permute-start.66 = (bf16[256,1664]{1,0:T(8,128)(2,1)}, bf16[256,1664]{1,0:T(8,128)(2,1)}, u32[]{:S(2)}, u32[]{:S(2)}) collective-permute-start(bf16[256,1664]{1,0:T(8,128)(2,1)} %collective-permute-done.64.refs_1_), channel_id=1, source_target_pairs={{0,16},{1,17},{2,18},{3,19},{4,20},{5,21},{6,22},{7,23},{8,24},{9,... | collective-permute-start | bytes 2555912 | tf_op jit(solution)/shard_map/ppermute | solution.py:542
  797.4 19.9 %collective-permute-start.53 = (f32[21504]{0:T(1024)S(1)}, f32[21504]{0:T(1024)S(1)}, u32[]{:S(2)}, u32[]{:S(2)}) collective-permute-start(f32[21504]{0:T(1024)S(1)} %add.570), channel_id=1, source_target_pairs={{0,16},{1,17},{2,18},{3,19},{4,20},{5,21},{6,22},{7,23},{8,24},{9,... | collective-permute-start | bytes 258056 | tf_op jit(solution)/shard_map/ppermute | solution.py:542
  818.3 24.2 %collective-permute-start.68 = (bf16[256,1664]{1,0:T(8,128)(2,1)}, bf16[256,1664]{1,0:T(8,128)(2,1)}, u32[]{:S(2)}, u32[]{:S(2)}) collective-permute-start(bf16[256,1664]{1,0:T(8,128)(2,1)} %collective-permute-done.64.refs_1_), channel_id=1, source_target_pairs={{0,4},{1,5},{2,6},{3,7},{4,0},{5,1},{6,2},{7,3},{8,12},{9,13},{10,... | collective-permute-start | bytes 2555912 | tf_op jit(solution)/shard_map/ppermute | solution.py:542
  819.3 24.3 %collective-permute-start.69 = (bf16[256,1664]{1,0:T(8,128)(2,1)}, bf16[256,1664]{1,0:T(8,128)(2,1)}, u32[]{:S(2)}, u32[]{:S(2)}) collective-permute-start(bf16[256,1664]{1,0:T(8,128)(2,1)} %collective-permute-done.65.refs_2_), channel_id=1, source_target_pairs={{0,4},{1,5},{2,6},{3,7},{4,0},{5,1},{6,2},{7,3},{8,12},{9,13},{10,... | collective-permute-start | bytes 2555912 | tf_op jit(solution)/shard_map/ppermute | solution.py:542
  819.8 23.8 %collective-permute-start.73 = (bf16[256,1664]{1,0:T(8,128)(2,1)}, bf16[256,1664]{1,0:T(8,128)(2,1)}, u32[]{:S(2)}, u32[]{:S(2)}) collective-permute-start(bf16[256,1664]{1,0:T(8,128)(2,1)} %collective-permute-done.71.refs_1_), channel_id=1, source_target_pairs={{0,8},{1,9},{2,10},{3,11},{4,12},{5,13},{6,14},{7,15},{8,0},{9,1},... | collective-permute-start | bytes 2555912 | tf_op jit(solution)/shard_map/ppermute | solution.py:542
  825.7 19.1 %collective-permute-start.70 = (bf16[256,1664]{1,0:T(8,128)(2,1)}, bf16[256,1664]{1,0:T(8,128)(2,1)}, u32[]{:S(2)}, u32[]{:S(2)}) collective-permute-start(bf16[256,1664]{1,0:T(8,128)(2,1)} %collective-permute-done.66.refs_3_), channel_id=1, source_target_pairs={{0,4},{1,5},{2,6},{3,7},{4,0},{5,1},{6,2},{7,3},{8,12},{9,13},{10,... | collective-permute-start | bytes 2555912 | tf_op jit(solution)/shard_map/ppermute | solution.py:542
  843.5 31.5 %collective-permute-start.75 = (bf16[256,1664]{1,0:T(8,128)(2,1)}, bf16[256,1664]{1,0:T(8,128)(2,1)S(1)}, u32[]{:S(2)}, u32[]{:S(2)}) collective-permute-start(bf16[256,1664]{1,0:T(8,128)(2,1)} %collective-permute-done.71.refs_1_), channel_id=1, source_target_pairs={{0,4},{1,5},{2,6},{3,7},{4,0},{5,1},{6,2},{7,3},{8,12},{9,13},{10,... | collective-permute-start | bytes 2555912 | tf_op jit(solution)/shard_map/ppermute | solution.py:542
  843.6 31.5 %collective-permute-start.76 = (bf16[256,1664]{1,0:T(8,128)(2,1)S(1)}, bf16[256,1664]{1,0:T(8,128)(2,1)}, u32[]{:S(2)}, u32[]{:S(2)}) collective-permute-start(bf16[256,1664]{1,0:T(8,128)(2,1)S(1)} %copy-done.28), channel_id=1, source_target_pairs={{0,4},{1,5},{2,6},{3,7},{4,0},{5,1},{6,2},{7,3},{8,12},{9,13},{10,... | collective-permute-start | bytes 2555912 | tf_op jit(solution)/shard_map/ppermute | solution.py:542
  844.7 30.4 %collective-permute-start.77 = (bf16[256,1664]{1,0:T(8,128)(2,1)}, bf16[256,1664]{1,0:T(8,128)(2,1)}, u32[]{:S(2)}, u32[]{:S(2)}) collective-permute-start(bf16[256,1664]{1,0:T(8,128)(2,1)} %collective-permute-done.73.refs_3_), channel_id=1, source_target_pairs={{0,4},{1,5},{2,6},{3,7},{4,0},{5,1},{6,2},{7,3},{8,12},{9,13},{10,... | collective-permute-start | bytes 2555912 | tf_op jit(solution)/shard_map/ppermute | solution.py:542
  844.8 41.8 %collective-permute-start.58 = (bf16[208,1664]{1,0:T(8,128)(2,1)}, bf16[208,1664]{1,0:T(8,128)(2,1)}, u32[]{:S(2)}, u32[]{:S(2)}) collective-permute-start(bf16[208,1664]{1,0:T(8,128)(2,1)} %get-tuple-element.337), channel_id=1, source_target_pairs={{0,8},{1,9},{2,10},{3,11},{4,12},{5,13},{6,14},{7,15},{8,0},{9,1},... | collective-permute-start | bytes 2076680 | tf_op jit(solution)/shard_map/ppermute | solution.py:542
  857.4 33.6 %collective-permute-start.59 = (bf16[208,1664]{1,0:T(8,128)(2,1)}, bf16[208,1664]{1,0:T(8,128)(2,1)S(1)}, u32[]{:S(2)}, u32[]{:S(2)}) collective-permute-start(bf16[208,1664]{1,0:T(8,128)(2,1)} %collective-permute-done.57), channel_id=1, source_target_pairs={{0,8},{1,9},{2,10},{3,11},{4,12},{5,13},{6,14},{7,15},{8,0},{9,1},... | collective-permute-start | bytes 2076680 | tf_op jit(solution)/shard_map/ppermute | solution.py:542
  (73 other events, 700.5 us)

commit v3 on v2

--- a/solution.py
+++ b/solution.py
@@ -27,12 +27,12 @@
     return (lane >= row * HD) & (lane < row * HD + HD)
 
 
-def attend_fwd_kernel(n_i, main, heads, n_add, n_ref, w_ref, b_ref, wo_ref, *refs):
+def attend_fwd_kernel(n_i, main, heads, n_add, n_ref, w_ref, b_ref, *refs):
     adds = refs[:n_add]
     qkv_ref, ho_ref, lse_ref, lset_ref, out_ref = refs[n_add:]
     hc = heads * HD
     tail = pl.ds(n_i * main, PAD)
-    qkv_ref[...] = (dot(n_ref[...], w_ref[...], 1, 0) + b_ref[...]).astype(BF)
+    qkv_ref[...] = (dot(n_ref[...], w_ref[0 : 3 * hc, :], 1, 1) + b_ref[...]).astype(BF)
     ho_ref[tail, :] = jnp.zeros((PAD, hc), BF)
     factor = HD ** -0.5
     tail_row = lax.broadcasted_iota(jnp.int32, (PAD, 1), 0)
@@ -73,15 +73,15 @@
         return carry
 
     lax.fori_loop(0, n_i, image, 0)
-    total = dot(ho_ref[...], wo_ref[0:hc, :], 1, 0)
+    total = dot(ho_ref[...], w_ref[3 * hc :, :], 1, 0)
     for ref in adds:
         total = total + ref[...].astype(F32)
     out_ref[...] = total.astype(BF)
 
 
-def attend_fwd(n_i, n, w, b, wo, adds=()):
+def attend_fwd(n_i, n, w, b, adds=()):
     rows, width = n.shape
-    hc = w.shape[1] // 3
+    hc = w.shape[0] // 4
     main = (rows - PAD) // n_i
     shapes = (
         ((rows, 3 * hc), BF),
@@ -93,33 +93,19 @@
     flops = 2 * rows * width * 4 * hc + 4 * n_i * main * main * hc
     return call(
         functools.partial(attend_fwd_kernel, n_i, main, hc // HD, len(adds)),
-        [n, w, b, wo, *adds],
+        [n, w, b, *adds],
         shapes,
         flops=flops,
         name="attend_fwd",
     )
 
 
-def attend_bwd_kernel(n_i, main, heads, n_half, n_add, g_ref, *refs):
-    halves = [refs[5 * k : 5 * k + 5] for k in range(n_half)]
-    adds = refs[5 * n_half : 5 * n_half + n_add]
-    refs = refs[5 * n_half + n_add :]
-    total = None
-    for k, half in enumerate(halves):
-        attend_bwd_half(n_i, main, heads, g_ref, *half, refs[2 * k], refs[2 * k + 1], *refs[-2:])
-        part = dot(refs[2 * k][...], half[3][...], 1, 1)
-        total = part if total is None else total + part
-    for ref in adds:
-        total = total + ref[...].astype(F32)
-    refs[2 * n_half][...] = total.astype(BF)
-
-
-def attend_bwd_half(
-    n_i, main, heads, g_ref, qkv_ref, lse_ref, lset_ref, w_ref, wo_ref, d_ref, gb_ref, gh_ref, kv_ref
-):
+def attend_bwd_kernel(n_i, main, heads, n_add, g_ref, qkv_ref, lse_ref, lset_ref, w_ref, *refs):
+    adds = refs[:n_add]
+    d_ref, gb_ref, gn_ref, gh_ref, kv_ref = refs[n_add:]
     hc = heads * HD
     tail = pl.ds(n_i * main, PAD)
-    gh_ref[...] = dot(g_ref[...], wo_ref[0:hc, :], 1, 1).astype(BF)
+    gh_ref[...] = dot(g_ref[...], w_ref[3 * hc :, :], 1, 1).astype(BF)
     d_ref[tail, :] = jnp.zeros((PAD, 3 * hc), BF)
     factor = HD ** -0.5
     tail_row = lax.broadcasted_iota(jnp.int32, (PAD, 1), 0)
@@ -175,28 +161,31 @@
 
     lax.fori_loop(0, n_i, image, 0)
     gb_ref[...] = jnp.sum(d_ref[...].astype(F32), 0, keepdims=True)
-
-
-def attend_bwd(n_i, g, halves, adds=()):
+    total = dot(d_ref[...], w_ref[0 : 3 * hc, :], 1, 0)
+    for ref in adds:
+        total = total + ref[...].astype(F32)
+    gn_ref[...] = total.astype(BF)
+
+
+def attend_bwd(n_i, g, half, adds=()):
     rows, width = g.shape
-    hc = halves[0][3].shape[1] // 3
+    hc = half[3].shape[0] // 4
     main = (rows - PAD) // n_i
-    shapes = [((rows, 3 * hc), BF), ((1, 3 * hc), F32)] * len(halves) + [((rows, width), BF)]
-    flops = (2 * rows * width * 4 * hc + 10 * n_i * main * main * hc) * len(halves)
-    out = call(
-        functools.partial(attend_bwd_kernel, n_i, main, hc // HD, len(halves), len(adds)),
-        [g] + [x for half in halves for x in half] + list(adds),
+    shapes = [((rows, 3 * hc), BF), ((1, 3 * hc), F32), ((rows, width), BF)]
+    return call(
+        functools.partial(attend_bwd_kernel, n_i, main, hc // HD, len(adds)),
+        [g, *half, *adds],
         shapes,
         scratch=[pltpu.VMEM((rows, hc), BF), pltpu.VMEM((main + PAD, 2 * hc), F32)],
-        flops=flops,
+        flops=2 * rows * width * 4 * hc + 10 * n_i * main * main * hc,
         name="attend_bwd",
     )
-    return out[0:-1:2], out[1:-1:2], out[-1]
 
 
 epsilon = 1e-06
 inv_root_two = 0.7071067811865476
 inv_root_tau = 0.3989422804014327
+HINT = 30
 def step_of(rows):
     return next(s for s in (48, 64, 32, 16) if rows % s == 0)
 
@@ -212,7 +201,9 @@
         out_shape=[jax.ShapeDtypeStruct(*s) for s in outs],
         scratch_shapes=list(scratch),
         compiler_params=pltpu.CompilerParams(vmem_limit_bytes=60 * 2**20),
-        cost_estimate=pl.CostEstimate(flops=int(flops), bytes_accessed=int(moved), transcendentals=0),
+        cost_estimate=pl.CostEstimate(
+            flops=int(flops) * HINT, bytes_accessed=int(moved) * HINT, transcendentals=0
+        ),
         name=name,
         **grid,
     )(*ins)
@@ -377,7 +368,8 @@
     )[0]
 
 
-def mlp_kernel(n0, n1, c0, c1, up_ref, upb_ref, down_ref, act_ref, gh_ref, g0, g1, gub_ref, acc):
+def mlp_kernel(n_add, n0, n1, c0, c1, up_ref, upb_ref, down_ref, *refs):
+    act_ref, gh_ref, g0, g1, gub_ref, acc = refs[2 * n_add :]
     j, last = pl.program_id(0), pl.num_programs(0) - 1
     size = n0.shape[0]
     for i, (n_ref, c_ref) in enumerate(((n0, c0), (n1, c1))):
@@ -402,18 +394,25 @@
 
     @pl.when(j == last)
     def _():
-        g0[...] = acc[0:size, :].astype(BF)
-        g1[...] = acc[size : 2 * size, :].astype(BF)
-
-
-def mlp(n, c, up, upb, down, tile=512):
+        for i, out in enumerate((g0, g1)):
+            total = acc[i * size : (i + 1) * size, :]
+            if n_add:
+                total = total + refs[i][...].astype(F32)
+            out[...] = total.astype(BF)
+
+
+def mlp(k, n_hi, n, c, up, upb, down, before):
     rows, width = n[0].shape
     units = up.shape[1]
+    tile = min(512, units)
+    steps = units // tile
     here = whole_spec((rows, width))
+    held = [] if before is None else [before[2], before[3], before[0], before[1]]
+    wide = pl.BlockSpec((2 * rows, tile), lambda j: (0, k * steps + j))
     return call(
-        mlp_kernel,
-        [*n, *c, up, upb, down],
-        [((2 * rows, units), BF)] * 2 + [((rows, width), BF)] * 2 + [((1, units), F32)],
+        functools.partial(mlp_kernel, len(held) // 2),
+        [*n, *c, up, upb, down, *held],
+        [((2 * rows, n_hi * units), BF)] * 2 + [((rows, width), BF)] * 2 + [((1, units), F32)],
         scratch=[pltpu.VMEM((2 * rows, width), F32)],
         flops=12 * rows * width * units,
         in_specs=[here] * 4
@@ -421,12 +420,35 @@
             pl.BlockSpec((width, tile), lambda j: (0, j)),
             pl.BlockSpec((1, tile), lambda j: (0, j)),
             pl.BlockSpec((tile, width), lambda j: (j, 0)),
-        ],
-        out_specs=[pl.BlockSpec((2 * rows, tile), lambda j: (0, j))] * 2
-        + [here] * 2
-        + [pl.BlockSpec((1, tile), lambda j: (0, j))],
-        grid=(units // tile,),
+        ]
+        + ([here] * 2 + [pl.BlockSpec(memory_space=pl.ANY)] * 2 if held else []),
+        out_specs=[wide] * 2 + [here] * 2 + [pl.BlockSpec((1, tile), lambda j: (0, j))],
+        grid=(steps,),
+        input_output_aliases={9: 0, 10: 1} if held else {},
         name="mlp",
+    )
+
+
+def row_product_kernel(n_parts, act_ref, *refs):
+    parts, outs = refs[:n_parts], refs[n_parts:]
+    size, units = outs[0].shape[0], parts[0].shape[0]
+    for i, out in enumerate(outs):
+        rows = slice(i * size, (i + 1) * size)
+        total = None
+        for k, ref in enumerate(parts):
+            part = dot(act_ref[rows, k * units : (k + 1) * units], ref[...], 1, 0)
+            total = part if total is None else total + part
+        out[...] = total.astype(BF)
+
+
+def row_product(act, parts):
+    rows, width = act.shape[0] // 2, parts[0].shape[1]
+    return call(
+        functools.partial(row_product_kernel, len(parts)),
+        [act, *parts],
+        [((rows, width), BF)] * 2,
+        flops=4 * rows * width * act.shape[1],
+        name="row_product",
     )
 
 
@@ -439,16 +461,22 @@
         for i, r in enumerate(right)
     ]
 
-    @pl.when(pl.program_id(0) == 0)
+    first = pl.program_id(0) == 0
+
+    @pl.when(first)
     def _():
         for copy in copies:
             copy.start()
-        for copy in copies:
-            copy.wait()
 
     total, at = None, 0
     for ref in left:
         rows = ref.shape[0]
+
+        @pl.when(first)
+        def _(at=at, rows=rows):
+            for copy in copies[at // size : (at + rows) // size]:
+                copy.wait()
+
         part = dot(ref[...], held[at : at + rows, :], 0, 0)
         total = part if total is None else total + part
         at += rows
@@ -477,53 +505,143 @@
         out_shape=jax.ShapeDtypeStruct((blocks * tile, width), BF),
         compiler_params=pltpu.CompilerParams(vmem_limit_bytes=60 * 2**20),
         cost_estimate=pl.CostEstimate(
-            flops=2 * total * blocks * tile * width, bytes_accessed=moved, transcendentals=0
+            flops=2 * total * blocks * tile * width * HINT,
+            bytes_accessed=moved * HINT,
+            transcendentals=0,
         ),
         name="wgrad",
     )(index, *left, *right)
 
 
 def place_kernel(count, transposed, at_ref, *refs):
-    blocks, out_ref = refs[:count], refs[count]
-    size = blocks[0].shape[0]
+    pieces, out_ref = refs[:count], refs[count]
+    total = sum(ref.shape[0] for ref in pieces)
+    size = total // at_ref.shape[0]
     target = refs[count + 1] if transposed else out_ref
-    for i, ref in enumerate(blocks):
-        rows = pl.ds(pl.multiple_of(at_ref[i] * size, size), size)
-        target[rows, :] = ref[...].astype(target.dtype)
+    i = 0
+    for ref in pieces:
+        for start in range(0, ref.shape[0], size):
+            rows = pl.ds(pl.multiple_of(at_ref[i] * size, size), size)
+            target[rows, :] = ref[start : start + size, :].astype(target.dtype)
+            i += 1
     if transposed:
-        for at in range(0, target.shape[0], 256):
+        for at in range(0, total, 256):
             out_ref[:, at : at + 256] = target[at : at + 256, :].astype(F32).T
 
 
-def place(blocks, at, transposed):
-    size, width = blocks[0].shape
-    rows = size * len(blocks)
+def place(pieces, at, transposed):
+    width = pieces[0].shape[1]
+    rows = sum(x.shape[0] for x in pieces)
     shape = (width, rows) if transposed else (rows, width)
     vmem = pl.BlockSpec(memory_space=pltpu.VMEM)
     return call(
-        functools.partial(place_kernel, len(blocks), transposed),
-        [at, *blocks],
+        functools.partial(place_kernel, len(pieces), transposed),
+        [at, *pieces],
         [(shape, F32)],
         scratch=[pltpu.VMEM((rows, width), BF)] if transposed else [],
-        in_specs=[pl.BlockSpec(memory_space=pltpu.SMEM)] + [vmem] * len(blocks),
+        in_specs=[pl.BlockSpec(memory_space=pltpu.SMEM)] + [vmem] * len(pieces),
         name="place",
     )[0]
 
 
+def attend_wgrad_kernel(n, rows_of, *refs):
+    d, heads, first, branch = [refs[i * n : (i + 1) * n] for i in range(4)]
+    out_ref, held, sems = refs[4 * n :]
+    size, hc = d[0].shape[0], heads[0].shape[1]
+    sources = list(first) + list(branch)
+    copies = [
+        pltpu.make_async_copy(r, held.at[pl.ds(i * size, size)], sems.at[i])
+        for i, r in enumerate(sources)
+    ]
+    for copy in copies:
+        copy.start()
+    for at, left in ((0, d), (n, heads)):
+        total = None
+        for i, ref in enumerate(left):
+            copies[at + i].wait()
+            part = dot(ref[...], held[(at + i) * size : (at + i + 1) * size, :], 0, 0)
+            total = part if total is None else total + part
+        low = total.astype(BF)
+        for i in range(low.shape[0] // hc):
+            to = rows_of[i if at == 0 else 3] * hc
+            out_ref[to : to + hc, :] = low[i * hc : (i + 1) * hc]
+
+
+def attend_wgrad(d, heads, first, branch, rows_of):
+    size, width = first[0].shape
+    hc = heads[0].shape[1]
+    vmem = pl.BlockSpec(memory_space=pltpu.VMEM)
+    n = len(d)
+    return call(
+        functools.partial(attend_wgrad_kernel, n, tuple(rows_of)),
+        [*d, *heads, *first, *branch],
+        [((4 * hc, width), BF)],
+        scratch=[pltpu.VMEM((2 * n * size, width), BF), pltpu.SemaphoreType.DMA((2 * n,))],
+        flops=8 * n * size * hc * width,
+        in_specs=[vmem] * (2 * n) + [pl.BlockSpec(memory_space=pl.ANY)] * (2 * n),
+        name="attend_wgrad",
+    )[0]
+
+
+def place_heads_kernel(count, at_ref, *refs):
+    pieces, qkv_ref, out_ref, buf = refs[:count], *refs[count:]
+    hc = out_ref.shape[0] // 2
+    size = buf.shape[0] // at_ref.shape[0]
+    i = 0
+    for ref in pieces:
+        for start in range(0, ref.shape[0], size):
+            rows = pl.ds(pl.multiple_of(at_ref[i] * size, size), size)
+            buf[rows, :] = ref[start : start + size, :]
+            i += 1
+    for core in (0, 1):
+        for mat in range(4):
+            x = buf[(core * 4 + mat) * hc : (core * 4 + mat + 1) * hc, :].astype(F32)
+            if mat == 3:
+                out_ref[core * hc : (core + 1) * hc, :] = x
+            else:
+                qkv_ref[mat, core * hc : (core + 1) * hc, :] = x
+
+
+def place_heads(pieces, at):
+    rows, width = sum(x.shape[0] for x in pieces), pieces[0].shape[1]
+    hc = rows // 8
+    size = rows // at.shape[0]
+    if size % 16:
+        buf, i = jnp.zeros((rows, width), BF), 0
+        for x in pieces:
+            for start in range(0, x.shape[0], size):
+                buf = lax.dynamic_update_slice_in_dim(buf, x[start : start + size], at[i] * size, 0)
+                i += 1
+        buf = buf.reshape(2, 4, hc, width).astype(F32)
+        mats = [buf[:, i].reshape(2 * hc, width) for i in range(4)]
+        return jnp.stack(mats[:3]), mats[3]
+    vmem = pl.BlockSpec(memory_space=pltpu.VMEM)
+    return call(
+        functools.partial(place_heads_kernel, len(pieces)),
+        [at, *pieces],
+        [((3, 2 * hc, width), F32), ((2 * hc, width), F32)],
+        scratch=[pltpu.VMEM((rows, width), BF)],
+        in_specs=[pl.BlockSpec(memory_space=pltpu.SMEM)] + [vmem] * len(pieces),
+        name="place_heads",
+    )
+
+
 class Order:
     def __init__(self):
-        self.last = None
+        self.last, self.also = None, ()
 
     def gate(self, x):
-        return x if self.last is None else lax.optimization_barrier((x, self.last))[0]
+        if self.last is None:
+            return x
+        return lax.optimization_barrier((x, self.last, *self.also))[0]
 
     def __call__(self, kernel, x, *rest):
         out = kernel(self.gate(x), *rest)
-        self.last = jax.tree.leaves(out)[-1]
+        self.last, self.also = jax.tree.leaves(out)[-1], ()
         return out
 
     def meet(self, *arrays):
-        self.last = lax.optimization_barrier((self.last, *arrays))[0]
+        self.also += arrays
 
 
 class Layout:
@@ -548,11 +666,11 @@
             place = place + (p // bit) % 2 * (1 << (n - 1 - i))
         return place
 
-    def spread(self, block, order):
-        have = {0: block}
+    def spread_masks(self, order):
+        masks = [0]
         for bit in order:
-            have.update({m ^ bit: self.move(x, p=bit) for m, x in list(have.items())})
-        return have
+            masks += [m ^ bit for m in masks]
+        return masks
 
     def spread_direct(self, block):
         return {m: self.move(block, p=m) if m else block for m in range(self.n_p)}
@@ -600,100 +718,147 @@
     def put(buf, x, axis, at):
         return lax.dynamic_update_slice_in_dim(buf, x, at, axis)
 
-    qkv_half = half(qkv_weight, 2)
-    qkv_mine = jnp.concatenate([qkv_half[i] for i in range(3)], 1)
-    pad_rows = -hc % (16 * n_p)
-    out_mine = jnp.pad(half(out_weight, 0), ((0, pad_rows), (0, 0)))
-    qkv_cut, out_cut = block(qkv_mine, 0, p), block(out_mine, 0, p)
-    qkv_hi = [lay.move(qkv_cut, hi=k) for k in range(1, n_hi)]
-    out_hi = [lay.move(out_cut, hi=k) for k in range(1, n_hi)]
+    x_unit, first_own = order(pack, images, first_gain, first_shift, True)
+    first_c, first_z = lay.move(first_own, c=1), lay.move(first_own, lo=1)
+    head_rows = jnp.swapaxes(qkv_weight, 1, 2)
+
+    def weights_here(x):
+        return jnp.concatenate([half(x[i], 0) for i in range(3)] + [half(out_weight, 0)])
+
+    if n_p == 4:
+
+        def cut_of(x):
+            mat = lax.dynamic_index_in_dim(x, jnp.minimum(p, 2), 0, keepdims=False)
+            return jnp.where(p == 3, half(out_weight, 0), half(mat, 0))
+
+        work_cut = order(cut_of, head_rows)
+    else:
+        work_cut = block(weights_here(head_rows), 0, p)
+    work_hi = [lay.move(work_cut, hi=k) for k in range(1, n_hi)]
     qv_half, upb_half = half(qv_bias, 1), half(up_bias, 0)
     bias_all = [jnp.concatenate([qv_half.reshape(-1), upb_half])]
-    bias_all += [lay.move(bias_all[0], hi=k) for k in range(1, n_hi)]
-    upb_work = jnp.concatenate([b[2 * hc :] for b in bias_all]).reshape(1, -1)
-    qkv_bias = [
-        jnp.concatenate([b[:hc], jnp.zeros((hc,), F32), b[hc : 2 * hc]]).reshape(1, -1)
-        for b in bias_all
-    ]
-
-    x_unit, first_own = order(pack, images, first_gain, first_shift, True)
-    first_c, first_z = lay.move(first_own, c=1), lay.move(first_own, lo=1)
+    work_mine = order(weights_here, head_rows)
+    work = [work_mine]
+    forward = [[None] * 4 for _ in range(n_hi)]
+
+    def qkv_bias_of(b):
+        return jnp.concatenate([b[:hc], jnp.zeros((hc,), F32), b[hc : 2 * hc]]).reshape(1, -1)
+
+    qkv_bias = [qkv_bias_of(bias_all[0])]
+
+    def attention(k, u, n, adds=()):
+        adds = list(adds) + ([forward[k - 1][u][4]] if k else [])
+        forward[k][u] = order(lambda x: attend_fwd(n_i, x, work[k], qkv_bias[k], adds), n)
+        return forward[k][u][4]
+
+    def stage(held, axis, bit):
+        return jnp.concatenate([held, lay.move(held, p=bit)], axis)
+
+    attention(0, 0, first_own)
+    bias_hi = [lay.move(order.gate(bias_all[0]), hi=k) for k in range(1, n_hi)]
+    attention(0, 1, first_c)
     seed_unit, grad_down_bias = order(pack, cotangent, first_gain, first_shift, False)
     seed_c = lay.move(seed_unit, c=1)
-
-    qkv_work, out_work = [qkv_mine], [out_mine]
-    forward = [[None] * 4 for _ in range(n_hi)]
-
-    def attention(k, u, n, adds=()):
-        adds = list(adds) + ([forward[k - 1][u][4]] if k else [])
-        forward[k][u] = order(
-            lambda x: attend_fwd(n_i, x, qkv_work[k], qkv_bias[k], out_work[k], adds), n
-        )
-        return forward[k][u][4]
-
-    def spread_work(got_all, axis):
-        return [
-            [(k * n_p + (p ^ m), x) for m, x in lay.spread_direct(got).items()]
-            for k, got in enumerate(got_all, 1)
-        ]
-
-    attention(0, 0, first_own)
-    up_hi = [lay.move(block(half(order.gate(up_weight), 1), 1, p), hi=k) for k in range(1, n_hi)]
-    attention(0, 1, first_c)
+    order.meet(*work_hi)
+    work_got = [lay.spread_direct(order.gate(x)) for x in work_hi]
     first_zc = lay.move(order.gate(first_z), c=1)
-    seed_z = lay.move(lax.optimization_barrier((seed_unit, first_zc))[0], lo=1)
-    qkv_got = spread_work([order.gate(x) for x in qkv_hi], 0)
-    out_got = spread_work([order.gate(x) for x in out_hi], 0)
     attention(0, 2, first_z)
-    down_hi = [
-        lay.move(block(half(order.gate(down_weight), 0), 0, p), hi=k) for k in range(1, n_hi)
-    ]
+    seed_z = lay.move(seed_unit, lo=1)
     attention(0, 3, first_zc)
-    up_got = spread_work([order.gate(x) for x in up_hi], 1)
-    for k in range(1, n_hi):
-        for got, work, like in ((qkv_got, qkv_work, qkv_mine), (out_got, out_work, out_mine)):
-            full = jnp.zeros_like(like)
-            for at, x in got[k - 1]:
-                full = put(full, x, 0, (at - k * n_p) * x.shape[0])
-            work.append(full)
+    up_cut = order(lambda x: block(half(x, 1), 1, p), up_weight)
+    up_hi = [lay.move(up_cut, hi=k) for k in range(1, n_hi)]
+    down_cut = order(lambda x: block(half(x, 0), 0, p), down_weight)
+    down_hi = [lay.move(down_cut, hi=k) for k in range(1, n_hi)]
+
+    def assemble(got):
+        masks = sorted(got)
+
+        def run(x):
+            full = jnp.zeros_like(work_mine)
+            for mask in masks:
+                x = x if mask == 0 else got[mask]
+                full = put(full, x, 0, (p ^ mask) * x.shape[0])
+            return full
+
+        return order(run, got[0])
+
+    work += [assemble(got) for got in work_got]
+    bias_all += [order.gate(x) for x in bias_hi]
+    qkv_bias += [qkv_bias_of(b) for b in bias_all[1:]]
     normed = (first_own, first_c, first_z, first_zc)
     for k in range(1, n_hi - 1):
         for u in range(4):
             attention(k, u, normed[u])
     k = n_hi - 1
+
+    def widen(pairs, axis):
+        return [order(lambda x, y=y: jnp.concatenate([x, y], axis), x) for x, y in pairs]
+
     moved_3 = lay.move(attention(k, 3, first_zc), c=1)
+    order.meet(seed_c)
+    moved_1 = lay.move(attention(k, 1, first_c), c=1)
+    moved_2 = lay.move(attention(k, 2, first_z, [moved_3]), lo=1)
+    order.meet(moved_1, seed_z, *up_hi)
     seed_zc = lay.move(order.gate(seed_z), c=1)
-    moved_1 = lay.move(attention(k, 1, first_c), c=1)
-    down_got = spread_work([order.gate(x) for x in down_hi], 0)
-    moved_2 = lay.move(attention(k, 2, first_z, [moved_3]), lo=1)
+    up_got = [order.gate(x) for x in up_hi]
+    up_got = [(x, lay.move(x, p=up_order[0])) for x in up_got]
+    down_got = [order.gate(x) for x in down_hi]
+    down_got = [(x, lay.move(x, p=down_order[0])) for x in down_got]
     attention_parts = (attention(k, 0, first_own), moved_1, moved_2)
+    normed_first = list(normed)
+    up_work = [order(lambda x: half(x, 1), up_weight)]
+    down_work = [order(lambda x: half(x, 0), down_weight)]
+    for i in range(1, len(lay.bits)):
+        up_got = [(x, lay.move(x, p=up_order[i])) for x in widen(up_got, 1)]
+        down_got = [(x, lay.move(x, p=down_order[i])) for x in widen(down_got, 0)]
+    order.meet(seed_zc)
     seed = [seed_unit, seed_c, seed_z, seed_zc]
-    normed_first = list(normed)
-
-    def fill_up(x):
-        work = put(jnp.zeros((width, n_hi * hu), BF), half(x, 1), 1, 0)
-        for at, part in (pair for got in up_got for pair in got):
-            work = put(work, part, 1, at * part.shape[1])
-        return work
-
-    def fill_down(x):
-        work = put(jnp.zeros((n_hi * hu, width), BF), half(x, 0), 0, 0)
-        for at, part in (pair for got in down_got for pair in got):
-            work = put(work, part, 0, at * part.shape[0])
-        return work
-
-    up_work = order(fill_up, up_weight)
-    down_work = order(fill_down, down_weight)
+
     middle, second_own = order(
         lambda x: norm_second(x, attention_parts, out_bias, second_gain, second_shift), x_unit
     )
     second_c, second_z = lay.move(second_own, c=1), lay.move(second_own, lo=1)
 
-    near = order(lambda n: mlp([n, second_c], seed[:2], up_work, upb_work, down_work), second_own)
+    def fill(parts, axis, order_of):
+        size = parts[0].shape[axis] * 2 // n_p
+        shape = [width, width]
+        shape[axis] = hu
+        masks = lay.spread_masks(order_of)
+
+        def run(x):
+            full, at = jnp.zeros(shape, BF), 0
+            for part in (x, *parts[1:]):
+                for i in range(part.shape[axis] // size):
+                    piece = lax.slice_in_dim(part, i * size, (i + 1) * size, axis=axis)
+                    full = put(full, piece, axis, (p ^ masks[at]) * size)
+                    at += 1
+            return full
+
+        return order(run, parts[0])
+
+    up_half = [upb_half.reshape(1, -1)] + [b[2 * hc :].reshape(1, -1) for b in bias_all[1:]]
+
+    def mlp_half(k, first, second, seeds, before):
+        return order(
+            lambda x: mlp(k, n_hi, [x, second], seeds, up_work[k], up_half[k], down_work[k], before),
+            first,
+        )
+
+    near = mlp_half(0, second_own, second_c, seed[:2], None)
+    up_work += [fill(parts, 1, up_order) for parts in up_got]
+    down_work += [fill(parts, 0, down_order) for parts in down_got]
+    near_bias, far_bias = [near[4]], []
+    for k in range(1, n_hi):
+        near = mlp_half(k, second_own, second_c, seed[:2], near)
+        near_bias.append(near[4])
     second_zc = lay.move(order.gate(second_z), c=1)
     other_c = lay.move(near[3], c=1)
-    low_near = order(lambda x: dot(x, down_work, 1, 0).astype(BF), near[0])
-    far = order(lambda n: mlp([n, second_zc], seed[2:], up_work, upb_work, down_work), second_z)
+    low_near = order(lambda x: row_product(x, down_work), near[0])
+    low_near_c = lay.move(low_near[1], c=1)
+    far = None
+    for k in range(n_hi):
+        far = mlp_half(k, second_z, second_zc, seed[2:], far)
+        far_bias.append(far[4])
     normed_second = [second_own, second_c, second_z, second_zc]
 
     def index(order_of, other):
@@ -720,14 +885,12 @@
     up_send = mlp_grad(1, normed_second, up_order, 1)
     up_recv = lay.move(up_send, p=up_order[0])
     down_keep = mlp_grad(0, seed, down_order, 0)
-    rows = x_unit.shape[0]
     grad_middle, grad_branch, grad_second_gain, grad_second_shift, grad_out_bias = order(
         lambda x: norm_back(x, grad_second, seed_unit, second_gain, True), middle
     )
     branch_c, branch_z = lay.move(grad_branch, c=1), lay.move(grad_branch, lo=1)
-    low_far = order(lambda x: dot(x, down_work, 1, 0).astype(BF), far[0])
-    low_far_c = lay.move(low_far[rows:], c=1)
-    low_near_c = lay.move(low_near[rows:], c=1)
+    low_far = order(lambda x: row_product(x, down_work), far[0])
+    low_far_c = lay.move(low_far[1], c=1)
     up_keep = mlp_grad(1, normed_second, up_order, 0)
 
     def halve(keep, recv, order_of, stage, parts):
@@ -749,14 +912,27 @@
         got = [lay.move(total[k * size : (k + 1) * size], hi=k) for k in range(1, n_hi)]
         return total[:size], got
 
-    def whole_grad(mine, order_of):
-        have = lay.spread(mine, order_of[::-1])
-        at, out = [], []
-        for core in (0, 1):
-            for mask, x in have.items():
-                at.append((c ^ core) * n_p + lay.place_of(p ^ mask, order_of))
-                out.append(lay.move(x, c=1) if core else x)
-        return out, jnp.stack(at).astype(jnp.int32)
+    class Spread:
+        def __init__(self, mine, order_of):
+            self.pieces, self.order_of, self.bits = [mine], order_of, order_of[::-1]
+            self.got, self.at = lay.move(mine, p=self.bits[0]), 1
+
+        def step(self):
+            self.pieces.append(self.got)
+            held = order(lambda x: jnp.concatenate([x] + self.pieces[1:]), self.pieces[0])
+            if self.at < len(self.bits):
+                self.got = lay.move(held, p=self.bits[self.at])
+            else:
+                self.pieces = [held, lay.move(held, c=1)]
+            self.at += 1
+
+        def finish(self):
+            while self.at <= len(self.bits):
+                self.step()
+            masks = lay.spread_masks(self.bits)
+            places = [lay.place_of(p ^ mask, self.order_of) for mask in masks]
+            at = [c * n_p + x for x in places] + [(1 - c) * n_p + x for x in places]
+            return self.pieces, jnp.stack(at).astype(jnp.int32)
 
     backward = [[None] * 4 for _ in range(n_hi)]
     branch = [grad_branch, branch_c, branch_z, None]
@@ -765,31 +941,31 @@
         adds = list(adds) + ([backward[k + 1][u][2]] if k < n_hi - 1 else [])
         f = forward[k][u]
         backward[k][u] = order(
-            lambda g: attend_bwd(n_i, g, [(f[0], f[2], f[3], qkv_work[k], out_work[k])], adds),
+            lambda g: attend_bwd(n_i, g, (f[0], f[2], f[3], work[k]), adds),
             branch[u],
         )
         return backward[k][u][2]
 
-    whole_index = jnp.zeros((1,), jnp.int32)
-
-    def attention_grad(k):
-        qkv = order(
-            lambda x: wgrad([x] + [b[0][0] for b in backward[k][1:]], normed_first, whole_index, 3 * hc),
-            backward[k][0][0][0],
+    def attention_send(k, order_of):
+        owner = [0] * n_p
+        for q in range(n_p):
+            owner[lay.place_of(q, order_of)] = lay.place_of(q, orders[0])
+        grad = order(
+            lambda x: attend_wgrad(
+                [x] + [b[0] for b in backward[k][1:]],
+                [f[1] for f in forward[k]],
+                normed_first,
+                branch,
+                owner if n_p == 4 else range(4),
+            ),
+            backward[k][0][0],
         )
-        heads = [f[1] for f in forward[k]]
-        out = order(lambda x: wgrad([x] + heads[1:], branch, whole_index, hc), heads[0])
-        return jnp.concatenate([qkv, out])
-
-    def attention_send(k, order_of):
-        grad = attention_grad(k)
-        if order_of != orders[0]:
+        if n_p != 4:
             blocks = jnp.split(grad, n_p)
-            owner = {lay.place_of(q, order_of): lay.place_of(q, orders[0]) for q in range(n_p)}
-            grad = jnp.concatenate([blocks[owner[i]] for i in range(n_p)])
+            grad = jnp.concatenate([blocks[i] for i in owner])
         top = lay.place_of(p, order_of) // (n_p // 2)
         size = grad.shape[0] // 2
-        send = lax.dynamic_slice_in_dim(grad, (1 - top) * size, size, 0)
+        send = order(lambda x: lax.dynamic_slice_in_dim(x, (1 - top) * size, size, 0), grad)
         keep = lax.dynamic_slice_in_dim(grad, top * size, size, 0)
         return keep, lay.move(send, p=order_of[0])
 
@@ -803,60 +979,77 @@
     branch[3] = lay.move(order.gate(branch_z), c=1)
     attention_back(k, 1)
     up_pair = halve(*up_pair, up_order, 1, n_hi)
-    low_far_sum = order(lambda x: join(x, low_far_c), low_far[:rows])
+    low_far_sum = order(lambda x: join(x, low_far_c), low_far[0])
     low_far_z = lay.move(low_far_sum, lo=1)
     attention_back(k, 2)
+    for step in range(2, n_stage):
+        down_pair = halve(*down_pair, down_order, step, n_hi)
+        up_pair = halve(*up_pair, up_order, step, n_hi)
+    down_mine, down_hi_got = settle_hi(*down_pair)
     attention_back(k, 3)
-    for stage in range(2, n_stage):
-        down_pair = halve(*down_pair, down_order, stage, n_hi)
-        up_pair = halve(*up_pair, up_order, stage, n_hi)
-    down_mine, down_hi_got = settle_hi(*down_pair)
     attn_pairs[k] = attention_send(k, orders[k])
+    up_mine, up_hi_got = settle_hi(*up_pair)
+    result_parts = (low_near[0], low_near_c, low_far_z)
+    result = order(lambda x: unpack(n_i, seq, x, result_parts, down_bias), middle)
     for k in range(n_hi - 2, 0, -1):
         for u in range(4):
             attention_back(k, u)
         attn_pairs[k] = attention_send(k, orders[k])
     moved_3 = lay.move(attention_back(0, 3), c=1)
-    up_mine, up_hi_got = settle_hi(*up_pair)
+    down_mine = order(lambda x: join(x, *down_hi_got), down_mine)
+    down_all = Spread(down_mine, down_order)
     moved_1 = lay.move(attention_back(0, 1), c=1)
+    down_all.step()
+    moved_2 = lay.move(attention_back(0, 2, [moved_3]), lo=1)
     for k in range(1, n_hi):
-        for stage in range(1, n_stage):
-            attn_pairs[k] = halve(*attn_pairs[k], orders[k], stage, 1)
-    moved_2 = lay.move(attention_back(0, 2, [moved_3]), lo=1)
-    down_mine = order(lambda x: join(x, *down_hi_got), down_mine)
-    down_all = whole_grad(down_mine, down_order)
+        for step in range(1, n_stage):
+            attn_pairs[k] = halve(*attn_pairs[k], orders[k], step, 1)
+    up_mine = order(lambda x: join(x, *up_hi_got), up_mine)
+    up_all = Spread(up_mine, up_order)
+    order.meet(moved_1)
     grad_first = (attention_back(0, 0), moved_1, moved_2)
+    up_all.step()
     attn_hi = []
     for k in range(1, n_hi):
         total = order(lambda x, k=k: join(x, attn_pairs[k][1]), attn_pairs[k][0])
         attn_hi.append(lay.move(total, hi=k))
-    attn_pairs[0] = attention_send(0, orders[0])
-    up_mine = order(lambda x: join(x, *up_hi_got), up_mine)
-    up_all = whole_grad(up_mine, up_order)
-    result_parts = (low_near[:rows], low_near_c, low_far_z)
-    result = order(lambda x: unpack(n_i, seq, x, result_parts, down_bias), middle)
-    for stage in range(1, n_stage):
-        attn_pairs[0] = halve(*attn_pairs[0], orders[0], stage, 1)
+    down_all = down_all.finish()
+    grad = order(
+        lambda x: attend_wgrad(
+            [x] + [b[0] for b in backward[0][1:]],
+            [f[1] for f in forward[0]],
+            normed_first,
+            branch,
+            range(4),
+        ),
+        backward[0][0][0],
+    )
+    places = [lay.place_of(p ^ mask, orders[0]) for mask in range(n_p)]
+    attn_own = block(grad, 0, places[0])
+    attn_got = []
+    for mask in range(1, n_p):
+        out = order(lambda x, mask=mask: block(x, 0, places[mask]), grad)
+        attn_got.append(lay.move(out, p=mask))
+
+    def place_all(blocks, at, transposed):
+        return order(lambda x: place([x] + blocks[1:], at, transposed), blocks[0])
+
+    grad_down_weight = place_all(*down_all, False)
     _, grad_images, grad_first_gain, grad_first_shift, _ = order(
         lambda x: norm_back(x, grad_first, grad_middle, first_gain, False), x_unit
     )
-    attn_mine = order(lambda x: join(x, attn_pairs[0][1], *attn_hi), attn_pairs[0][0])
-    attn_all = whole_grad(attn_mine, orders[0])
-    grad_images = order(lambda x: unpack(n_i, seq, x), grad_images)
-    grad_down_weight = order(
-        lambda x: place([x] + down_all[0][1:], down_all[1], False), down_all[0][0]
-    )
-    grad_up_weight = order(lambda x: place([x] + up_all[0][1:], up_all[1], True), up_all[0][0])
+    attn_mine = order(lambda x: join(x, *attn_got, *attn_hi), attn_own)
+    attn_all = lay.spread_direct(attn_mine)
 
     tensor_at = lax.axis_index("tensor")
     all_units, all_columns = units * lay.tensor, columns * lay.tensor
-    grad_up_bias = (near[4] + far[4])[0]
+    grad_up_bias = jnp.concatenate([(a + b)[0] for a, b in zip(near_bias, far_bias)])
     wide_up = jnp.zeros((all_units,), F32)
     wide_qv = jnp.zeros((2, all_columns), F32)
     for k in range(n_hi):
         shard = tensor_at ^ (2 * k)
         wide_up = put(wide_up, grad_up_bias[k * hu : (k + 1) * hu], 0, shard * units + c * hu)
-        bias = sum(b[1][0] for b in backward[k])[0]
+        bias = sum(b[1] for b in backward[k])[0]
         bias = jnp.stack([bias[:hc], bias[2 * hc :]])
         wide_qv = put(wide_qv, bias, 1, shard * columns + c * hc)
     sums = (
@@ -870,11 +1063,37 @@
     vector = jnp.concatenate(
         [jnp.sum(x, axis=0) for x in sums] + [wide_up, wide_qv.reshape(-1)]
     )
-    for bit in lay.bits:
-        vector = vector + lay.move(vector, p=bit)
-    vector = vector + lay.move(vector, c=1)
-    for k in [1 << b for b in range(lay.tensor.bit_length() - 1)]:
-        vector = vector + lay.move(vector, lo=k & 1, hi=k >> 1)
+    hops = [dict(c=1)] + [
+        dict(lo=(1 << b) & 1, hi=(1 << b) >> 1) for b in range(lay.tensor.bit_length() - 1)
+    ]
+    hops += [dict(p=bit) for bit in lay.bits]
+
+    def hop(vector):
+        got = lay.move(vector, **hops.pop(0))
+        return vector, got
+
+    def add(pair):
+        return order(lambda x: x + pair[1], pair[0])
+
+    pair = hop(vector)
+    grad_images = order(lambda x: unpack(n_i, seq, x), grad_images)
+    pair = hop(add(pair))
+    for _ in range(lay.tensor.bit_length() - 2):
+        pair = hop(add(pair))
+    up_all = up_all.finish()
+    pair = hop(add(pair))
+    grad_up_weight = place_all(*up_all, True)
+    masks = sorted(attn_all)
+    held = order(
+        lambda x: jnp.concatenate([x] + [attn_all[mask] for mask in masks[1:]]), attn_all[0]
+    )
+    held_c = lay.move(held, c=1)
+    at = [lay.place_of(p ^ mask, orders[0]) for mask in masks]
+    at = [c * n_p + x for x in at] + [(1 - c) * n_p + x for x in at]
+    attn_all = ([held, held_c], jnp.stack(at).astype(jnp.int32))
+    while hops:
+        pair = hop(add(pair))
+    vector = add(pair)
     norms = vector[: 6 * width].reshape(6, width)
     vector = vector[6 * width :]
     grad_up_bias = lax.dynamic_slice_in_dim(vector, tensor_at * units, units, 0)
@@ -882,12 +1101,8 @@
         vector[all_units:].reshape(2, all_columns), tensor_at * columns, columns, 1
     )
 
-    buf = jnp.zeros((8 * hc, width), BF)
-    for i, x in enumerate(attn_all[0]):
-        buf = put(buf, x, 0, attn_all[1][i] * x.shape[0])
-    buf = buf.reshape(2, 4, hc, width)
-    grad_out_weight = buf[:, 3].reshape(columns, width).astype(F32)
-    grad_qkv_weight = jnp.stack([buf[:, i].reshape(columns, width).T for i in range(3)]).astype(F32)
+    grad_qkv_weight, grad_out_weight = place_heads(*attn_all)
+    grad_qkv_weight = jnp.swapaxes(grad_qkv_weight, 1, 2)
     return (
         result,
         grad_images,

time: 914 us -> 838 us (0.917)
  waiting for transfers between devices: 252 us -> 156 us
  Pallas kernels: 400 us -> 451 us
  matrix products: 26.6 us -> 0 us
  other arithmetic: 61.4 us -> 48.1 us
    ppermute x78 -> x62, waiting for transfers between devices: 252 us -> 156 us  [move(): return lax.ppermute(x, ('dp', 'tensor'), pairs)]
    pallas_call x27 -> x34, Pallas kernels: 292 us -> 383 us  [call(): pl.pallas_call(kernel, in_specs=in_specs or [vmem] * len(ins), out_specs=...]
    pallas_call x8 -> x4, Pallas kernels: 108 us -> 67.8 us  [wgrad(): pl.pallas_call(functools.partial(wgrad_kernel, len(left), len(right)), gr...]
    dot_general x2 -> x0, matrix products: 26.6 us -> none  [dot(): lax.dot_general(a, b, (((ca,), (cb,)), ((), ())), preferred_element_type=...]
    dynamic_update_slice x29 -> x16, local copies, waits for them, and re-layouts: 30.5 us -> 17.8 us  [put(): return lax.dynamic_update_slice_in_dim(buf, x, at, axis)]
    unnamed x131 -> x143, local copies, waits for them, and re-layouts: 23.1 us -> 33.5 us
    ppermute x78 -> x62, starting transfers between devices: 66.5 us -> 68.2 us  [move(): return lax.ppermute(x, ('dp', 'tensor'), pairs)]
  transfers between devices with their start and end apart: 78 -> 62, of which waited for: 19 -> 24; matrix products, arithmetic and copies ran while one was open for 18% -> 16% of each run, Pallas kernels for 38% -> 52%
where the time goes in v3:
time: 838 us; the launch traced here: 828 us
  Pallas kernels  451 us (54%)
  waiting for transfers between devices  156 us (19%)
  local copies, waits for them, and re-layouts  103 us (12%)
  starting transfers between devices  68.2 us (8%)
  other arithmetic  48.1 us (6%)
    pallas_call x34, Pallas kernels, call(): pl.pallas_call(kernel, in_specs=in_specs or [vmem] * len(ins), out_specs=...  383 us
    ppermute x62, waiting for transfers between devices, move(): return lax.ppermute(x, ('dp', 'tensor'), pairs)  156 us
    ppermute x62, starting transfers between devices, move(): return lax.ppermute(x, ('dp', 'tensor'), pairs)  68.2 us
    pallas_call x4, Pallas kernels, wgrad(): pl.pallas_call(functools.partial(wgrad_kernel, len(left), len(right)), gr...  67.8 us
    unnamed x143, local copies, waits for them, and re-layouts  33.5 us
    convert_element_type x11, other arithmetic, join(): return total.astype(BF)  30.4 us
    dynamic_update_slice x16, local copies, waits for them, and re-layouts, put(): return lax.dynamic_update_slice_in_dim(buf, x, at, axis)  17.8 us
  transfers between devices with their start and end apart: 62, of which 24 were waited for; matrix products, arithmetic and copies ran while one was open for 16% of the time, Pallas kernels for 52%

profile of v3, /device:TPU:0, one launch (start us, length us, event | category | flops | bytes accessed | tf_op | source)
XLA Modules:
  0.0 827.6 jit_solution(1282015852673804919)
XLA Ops:
  6.1 5.6 pack.2
  21.5 5.5 pad_maximum_fusion.w_ref
  27.7 8.6 %attend_fwd.8 = (bf16[528,624]{1,0:T(8,128)(2,1)}, bf16[528,208]{1,0:T(8,128)(2,1)}, f32[8,512]{1,0:T(8,128)}, f32[8,128]{1,0:T(8,128)}, bf16[528,1664]{1,0:T(8,128)(2,1)}) custom-call(bf16[528,1664]{1,0:T(8,128)(2,1)} %get-tuple-element.226.n_ref.refs_8_, bf16[832,1664]{1,0:T(8,128)(2,1)} %pad_maximum_fusion.w_ref, f32[1,624]{1,0:T(1,128)} %reshape.174.b_ref), custom_call_target="tpu_custom_call" | custom-call | flops 47130869760 | bytes 215544960 | tf_op jit(solution)/shard_map/attend_fwd/pallas_call | solution.py:197
  39.3 8.7 %attend_fwd.9 = (bf16[528,624]{1,0:T(8,128)(2,1)}, bf16[528,208]{1,0:T(8,128)(2,1)}, f32[8,512]{1,0:T(8,128)}, f32[8,128]{1,0:T(8,128)}, bf16[528,1664]{1,0:T(8,128)(2,1)}) custom-call(bf16[528,1664]{1,0:T(8,128)(2,1)} %collective-permute-done.1.n_ref.refs_9_, bf16[832,1664]{1,0:T(8,128)(2,1)} %pad_maximum_fusion.w_ref, f32[1,624]{1,0:T(1,128)} %reshape.174.b_ref), custom_call_target="tpu_custom_call" | custom-call | flops 47130869760 | bytes 215544960 | tf_op jit(solution)/shard_map/attend_fwd/pallas_call | solution.py:197
  49.4 3.0 pack.3
  52.4 15.6 %collective-permute-done.2 = bf16[208,1664]{1,0:T(8,128)(2,1)S(1)} collective-permute-done((bf16[208,1664]{1,0:T(8,128)(2,1)S(1)}, bf16[208,1664]{1,0:T(8,128)(2,1)S(1)}, u32[]{:S(2)}, u32[]{:S(2)}) %collective-permute-start.2) | collective-permute-done | bytes 692256 | tf_op jit(solution)/shard_map/ppermute | solution.py:660
  69.0 8.8 %attend_fwd.10 = (bf16[528,624]{1,0:T(8,128)(2,1)}, bf16[528,208]{1,0:T(8,128)(2,1)}, f32[8,512]{1,0:T(8,128)}, f32[8,128]{1,0:T(8,128)}, bf16[528,1664]{1,0:T(8,128)(2,1)}) custom-call(bf16[528,1664]{1,0:T(8,128)(2,1)} %collective-permute-done.n_ref.refs_10_, bf16[832,1664]{1,0:T(8,128)(2,1)} %pad_maximum_fusion.w_ref, f32[1,624]{1,0:T(1,128)} %reshape.174.b_ref), custom_call_target="tpu_custom_call" | custom-call | flops 47130869760 | bytes 215544960 | tf_op jit(solution)/shard_map/attend_fwd/pallas_call | solution.py:197
  82.5 8.6 %attend_fwd.11 = (bf16[528,624]{1,0:T(8,128)(2,1)}, bf16[528,208]{1,0:T(8,128)(2,1)}, f32[8,512]{1,0:T(8,128)}, f32[8,128]{1,0:T(8,128)}, bf16[528,1664]{1,0:T(8,128)(2,1)}) custom-call(bf16[528,1664]{1,0:T(8,128)(2,1)} %copy-done.57, bf16[832,1664]{1,0:T(8,128)(2,1)} %pad_maximum_fusion.w_ref, f32[1,624]{1,0:T(1,128)} %reshape.174.b_ref), custom_call_target="tpu_custom_call" | custom-call | flops 47130869760 | bytes 215544960 | tf_op jit(solution)/shard_map/attend_fwd/pallas_call | solution.py:197
  100.0 12.1 %collective-permute-done.6 = bf16[208,1664]{1,0:T(8,128)(2,1)} collective-permute-done((bf16[208,1664]{1,0:T(8,128)(2,1)S(1)}, bf16[208,1664]{1,0:T(8,128)(2,1)}, u32[]{:S(2)}, u32[]{:S(2)}) %collective-permute-start.6) | collective-permute-done | bytes 692256 | tf_op jit(solution)/shard_map/ppermute | solution.py:660
  119.0 9.1 %attend_fwd.12 = (bf16[528,624]{1,0:T(8,128)(2,1)}, bf16[528,208]{1,0:T(8,128)(2,1)}, f32[8,512]{1,0:T(8,128)}, f32[8,128]{1,0:T(8,128)}, bf16[528,1664]{1,0:T(8,128)(2,1)}) custom-call(bf16[528,1664]{1,0:T(8,128)(2,1)} %copy-done.57, bf16[832,1664]{1,0:T(8,128)(2,1)} %copy-done.17, f32[1,624]{1,0:T(1,128)} %reshape.176.b_ref, ...), custom_call_target="tpu_custom_call" | custom-call | flops 47130869760 | bytes 268260480 | tf_op jit(solution)/shard_map/attend_fwd/pallas_call | solution.py:197
  128.1 9.1 %attend_fwd.13 = (bf16[528,624]{1,0:T(8,128)(2,1)}, bf16[528,208]{1,0:T(8,128)(2,1)}, f32[8,512]{1,0:T(8,128)}, f32[8,128]{1,0:T(8,128)}, bf16[528,1664]{1,0:T(8,128)(2,1)}) custom-call(bf16[528,1664]{1,0:T(8,128)(2,1)} %collective-permute-done.1.n_ref.refs_9_, bf16[832,1664]{1,0:T(8,128)(2,1)} %copy-done.17, f32[1,624]{1,0:T(1,128)} %reshape.176.b_ref, ...), custom_call_target="tpu_custom_call" | custom-call | flops 47130869760 | bytes 268260480 | tf_op jit(solution)/shard_map/attend_fwd/pallas_call | solution.py:197
  139.0 10.1 %attend_fwd.14 = (bf16[528,624]{1,0:T(8,128)(2,1)}, bf16[528,208]{1,0:T(8,128)(2,1)}, f32[8,512]{1,0:T(8,128)}, f32[8,128]{1,0:T(8,128)}, bf16[528,1664]{1,0:T(8,128)(2,1)}) custom-call(bf16[528,1664]{1,0:T(8,128)(2,1)} %collective-permute-done.n_ref.refs_10_, bf16[832,1664]{1,0:T(8,128)(2,1)} %copy-done.17, f32[1,624]{1,0:T(1,128)} %reshape.176.b_ref, ...), custom_call_target="tpu_custom_call" | custom-call | flops 47130869760 | bytes 320976000 | tf_op jit(solution)/shard_map/attend_fwd/pallas_call | solution.py:197
  151.5 11.3 %collective-permute-done.12.c0.refs_4_ = bf16[528,1664]{1,0:T(8,128)(2,1)} collective-permute-done((bf16[528,1664]{1,0:T(8,128)(2,1)}, bf16[528,1664]{1,0:T(8,128)(2,1)}, u32[]{:S(2)}, u32[]{:S(2)}) %collective-permute-start.12) | collective-permute-done | bytes 1757216 | tf_op jit(solution)/shard_map/ppermute | solution.py:660
  162.9 9.7 %attend_fwd.15 = (bf16[528,624]{1,0:T(8,128)(2,1)}, bf16[528,208]{1,0:T(8,128)(2,1)}, f32[8,512]{1,0:T(8,128)}, f32[8,128]{1,0:T(8,128)}, bf16[528,1664]{1,0:T(8,128)(2,1)}) custom-call(bf16[528,1664]{1,0:T(8,128)(2,1)} %get-tuple-element.226.n_ref.refs_8_, bf16[832,1664]{1,0:T(8,128)(2,1)} %copy-done.17, f32[1,624]{1,0:T(1,128)} %reshape.176.b_ref, ...), custom_call_target="tpu_custom_call" | custom-call | flops 47130869760 | bytes 268260480 | tf_op jit(solution)/shard_map/attend_fwd/pallas_call | solution.py:197
  172.6 9.8 %collective-permute-start.14 = (bf16[1664,256]{1,0:T(8,128)(2,1)}, bf16[1664,256]{1,0:T(8,128)(2,1)S(1)}, u32[]{:S(2)}, u32[]{:S(2)}) collective-permute-start(bf16[1664,256]{1,0:T(8,128)(2,1)} %collective-permute-done.13), channel_id=1, source_target_pairs={{0,8},{1,9},{2,10},{3,11},{4,12},{5,13},{6,14},{7,15},{8,0},{9,1},... | collective-permute-start | bytes 2555912 | tf_op jit(solution)/shard_map/ppermute | solution.py:660
  182.5 4.0 constant_dynamic-slice_fusion.9.up_ref
  190.0 4.0 constant_dynamic-slice_fusion.8.down_ref.refs_0_
  196.2 5.6 collective-permute-done.14
  204.8 3.0 collective-permute-done.15
  212.6 8.5 %norm_second.1 = (f32[528,1664]{1,0:T(8,128)}, bf16[528,1664]{1,0:T(8,128)(2,1)}) custom-call(bf16[528,1664]{1,0:T(8,128)(2,1)} %get-tuple-element.354.x_ref, bf16[528,1664]{1,0:T(8,128)(2,1)} %get-tuple-element.227.a_ref, bf16[528,1664]{1,0:T(8,128)(2,1)} %copy-done.19, bf16[528,1664]{1,0:T(8,128)(2,1)} %copy-done.21, f32[1,1664]{1,0:T(1,128)} %reshape.177.bias_ref, ...), custom_call_target="tpu_custom_call" | custom-call | bytes 369607680 | tf_op jit(solution)/shard_map/norm_second/pallas_call | solution.py:197
  232.7 21.3 %mlp.4 = (bf16[1056,2048]{1,0:T(8,128)(2,1)}, bf16[1056,2048]{1,0:T(8,128)(2,1)}, bf16[528,1664]{1,0:T(8,128)(2,1)}, bf16[528,1664]{1,0:T(8,128)(2,1)}, f32[1,1024]{1,0:T(1,128)}) custom-call(bf16[528,1664]{1,0:T(8,128)(2,1)} %get-tuple-element.240.n0.refs_2_, bf16[528,1664]{1,0:T(8,128)(2,1)} %copy-done.58, ...), custom_call_target="tpu_custom_call" | custom-call | flops 323884154880 | bytes 780533760 | tf_op jit(solution)/shard_map/mlp/pallas_call | solution.py:197
  257.0 9.8 %collective-permute-done.19 = bf16[1664,512]{1,0:T(8,128)(2,1)} collective-permute-done((bf16[1664,512]{1,0:T(8,128)(2,1)}, bf16[1664,512]{1,0:T(8,128)(2,1)}, u32[]{:S(2)}, u32[]{:S(2)}) %collective-permute-start.19) | collective-permute-done | bytes 1703968 | tf_op jit(solution)/shard_map/ppermute | solution.py:660
  277.0 22.6 %mlp.5 = (bf16[1056,2048]{1,0:T(8,128)(2,1)}, bf16[1056,2048]{1,0:T(8,128)(2,1)}, bf16[528,1664]{1,0:T(8,128)(2,1)}, bf16[528,1664]{1,0:T(8,128)(2,1)}, f32[1,1024]{1,0:T(1,128)}) custom-call(bf16[528,1664]{1,0:T(8,128)(2,1)} %get-tuple-element.240.n0.refs_2_, bf16[528,1664]{1,0:T(8,128)(2,1)} %copy-done.58, ...), custom_call_target="tpu_custom_call", output_to_operand_aliasing={{0}: (9, {}), {1}: (10, {})} | custom-call | flops 323884154880 | bytes 1145487360 | tf_op jit(solution)/shard_map/mlp/pallas_call | solution.py:197
  299.7 13.5 %row_product.2 = (bf16[528,1664]{1,0:T(8,128)(2,1)}, bf16[528,1664]{1,0:T(8,128)(2,1)}) custom-call(bf16[1056,2048]{1,0:T(8,128)(2,1)} %get-tuple-element.266.act_ref.refs_0_, bf16[1024,1664]{1,0:T(8,128)(2,1)} %constant_dynamic-slice_fusion.8.down_ref.refs_0_, bf16[1024,1664]{1,0:T(8,128)(2,1)} %copy-done.6), custom_call_target="tpu_custom_call" | custom-call | flops 215922769920 | bytes 439664640 | tf_op jit(solution)/shard_map/row_product/pallas_call | solution.py:197
  313.6 21.1 %mlp.6 = (bf16[1056,2048]{1,0:T(8,128)(2,1)}, bf16[1056,2048]{1,0:T(8,128)(2,1)}, bf16[528,1664]{1,0:T(8,128)(2,1)}, bf16[528,1664]{1,0:T(8,128)(2,1)}, f32[1,1024]{1,0:T(1,128)}) custom-call(bf16[528,1664]{1,0:T(8,128)(2,1)} %collective-permute-done.21.n0.refs_4_, bf16[528,1664]{1,0:T(8,128)(2,1)} %collective-permute-done.22.n1.refs_5_, ...), custom_call_target="tpu_custom_call" | custom-call | flops 323884154880 | bytes 780533760 | tf_op jit(solution)/shard_map/mlp/pallas_call | solution.py:197
  334.8 22.7 %mlp.7 = (bf16[1056,2048]{1,0:T(8,128)(2,1)}, bf16[1056,2048]{1,0:T(8,128)(2,1)}, bf16[528,1664]{1,0:T(8,128)(2,1)}, bf16[528,1664]{1,0:T(8,128)(2,1)}, f32[1,1024]{1,0:T(1,128)}) custom-call(bf16[528,1664]{1,0:T(8,128)(2,1)} %collective-permute-done.21.n0.refs_4_, ...), custom_call_target="tpu_custom_call", output_to_operand_aliasing={{0}: (9, {}), {1}: (10, {})} | custom-call | flops 323884154880 | bytes 1145487360 | tf_op jit(solution)/shard_map/mlp/pallas_call | solution.py:197
  358.1 17.0 %wgrad.4 = bf16[1024,1664]{1,0:T(8,128)(2,1)} custom-call(s32[2]{0:T(128)} %pad_add_fusion.3.index_ref, bf16[1056,2048]{1,0:T(8,128)(2,1)} %get-tuple-element.266.act_ref.refs_0_, bf16[1056,2048]{1,0:T(8,128)(2,1)} %get-tuple-element.271.refs_1_.act_ref, bf16[528,1664]{1,0:T(8,128)(2,1)} %get-tuple-element.219.c0.refs_2_.add_ref, ...), custom_call_target="tpu_custom_call" | custom-call | flops 215922769920 | bytes 442859520 | tf_op jit(solution)/shard_map/wgrad/pallas_call | solution.py:493
  380.2 3.1 add_convert_fusion.1
  385.1 16.9 %wgrad.5 = bf16[1024,1664]{1,0:T(8,128)(2,1)} custom-call(s32[2]{0:T(128)} %pad_add_fusion.2.index_ref, bf16[1056,2048]{1,0:T(8,128)(2,1)} %get-tuple-element.273.refs_0_, bf16[1056,2048]{1,0:T(8,128)(2,1)} %get-tuple-element.265.refs_1_, bf16[528,1664]{1,0:T(8,128)(2,1)} %get-tuple-element.240.n0.refs_2_, bf16[528,1664]{1,0:T(8,128)(2,1)} %copy-done.58, ...), custom_call_target="tpu_custom_call" | custom-call | flops 215922769920 | bytes 442859520 | tf_op jit(solution)/shard_map/wgrad/pallas_call | solution.py:493
  403.5 16.8 %wgrad.6 = bf16[1024,1664]{1,0:T(8,128)(2,1)} custom-call(s32[2]{0:T(128)} %pad_add_fusion.1.index_ref, bf16[1056,2048]{1,0:T(8,128)(2,1)} %get-tuple-element.266.act_ref.refs_0_, bf16[1056,2048]{1,0:T(8,128)(2,1)} %get-tuple-element.271.refs_1_.act_ref, bf16[528,1664]{1,0:T(8,128)(2,1)} %get-tuple-element.219.c0.refs_2_.add_ref, ...), custom_call_target="tpu_custom_call" | custom-call | flops 215922769920 | bytes 442859520 | tf_op jit(solution)/shard_map/wgrad/pallas_call | solution.py:493
  420.2 3.4 collective-permute-done.25.c_ref
  423.7 10.9 %norm_back.2 = (f32[528,1664]{1,0:T(8,128)}, bf16[528,1664]{1,0:T(8,128)(2,1)}, f32[8,1664]{1,0:T(8,128)}, f32[8,1664]{1,0:T(8,128)}, f32[8,1664]{1,0:T(8,128)}) custom-call(f32[528,1664]{1,0:T(8,128)} %get-tuple-element.312.x_ref.refs_0_, bf16[528,1664]{1,0:T(8,128)(2,1)} %get-tuple-element.268.a_ref, bf16[528,1664]{1,0:T(8,128)(2,1)} %collective-permute-done.24.b_ref, ...), custom_call_target="tpu_custom_call" | custom-call | bytes 479431680 | tf_op jit(solution)/shard_map/norm_back/pallas_call | solution.py:197
  434.6 13.5 %row_product.3 = (bf16[528,1664]{1,0:T(8,128)(2,1)}, bf16[528,1664]{1,0:T(8,128)(2,1)}) custom-call(bf16[1056,2048]{1,0:T(8,128)(2,1)} %get-tuple-element.271.refs_1_.act_ref, bf16[1024,1664]{1,0:T(8,128)(2,1)} %constant_dynamic-slice_fusion.8.down_ref.refs_0_, bf16[1024,1664]{1,0:T(8,128)(2,1)} %copy-done.6), custom_call_target="tpu_custom_call" | custom-call | flops 215922769920 | bytes 439664640 | tf_op jit(solution)/shard_map/row_product/pallas_call | solution.py:197
  448.0 17.1 %wgrad.7 = bf16[1024,1664]{1,0:T(8,128)(2,1)} custom-call(s32[2]{0:T(128)} %pad_add_fusion.index_ref, bf16[1056,2048]{1,0:T(8,128)(2,1)} %get-tuple-element.273.refs_0_, bf16[1056,2048]{1,0:T(8,128)(2,1)} %get-tuple-element.265.refs_1_, bf16[528,1664]{1,0:T(8,128)(2,1)} %get-tuple-element.240.n0.refs_2_, bf16[528,1664]{1,0:T(8,128)(2,1)} %copy-done.58, ...), custom_call_target="tpu_custom_call" | custom-call | flops 215922769920 | bytes 442859520 | tf_op jit(solution)/shard_map/wgrad/pallas_call | solution.py:493
  467.4 4.6 add_convert_fusion.5
  472.1 10.0 %attend_bwd.8 = (bf16[528,624]{1,0:T(8,128)(2,1)}, f32[1,624]{1,0:T(1,128)}, bf16[528,1664]{1,0:T(8,128)(2,1)}) custom-call(bf16[528,1664]{1,0:T(8,128)(2,1)} %get-tuple-element.333.g_ref.refs_12_, bf16[528,624]{1,0:T(8,128)(2,1)} %get-tuple-element.277.qkv_ref, f32[8,512]{1,0:T(8,128)} %get-tuple-element.278.lse_ref, f32[8,128]{1,0:T(8,128)} %get-tuple-element.279.lset_ref, ...), custom_call_target="tpu_custom_call" | custom-call | flops 52038205440 | bytes 228723840 | tf_op jit(solution)/shard_map/attend_bwd/pallas_call | solution.py:197
  485.3 9.7 %attend_bwd.9 = (bf16[528,624]{1,0:T(8,128)(2,1)}, f32[1,624]{1,0:T(1,128)}, bf16[528,1664]{1,0:T(8,128)(2,1)}) custom-call(bf16[528,1664]{1,0:T(8,128)(2,1)} %collective-permute-done.30.g_ref.refs_13_, bf16[528,624]{1,0:T(8,128)(2,1)} %get-tuple-element.285.qkv_ref, f32[8,512]{1,0:T(8,128)} %get-tuple-element.286.lse_ref, ...), custom_call_target="tpu_custom_call" | custom-call | flops 52038205440 | bytes 228723840 | tf_op jit(solution)/shard_map/attend_bwd/pallas_call | solution.py:197
  495.0 4.7 add_convert_fusion.7
  500.3 3.1 add_convert_fusion
  503.8 3.3 collective-permute-done.28.g_ref.refs_14_
  507.1 9.7 %attend_bwd.10 = (bf16[528,624]{1,0:T(8,128)(2,1)}, f32[1,624]{1,0:T(1,128)}, bf16[528,1664]{1,0:T(8,128)(2,1)}) custom-call(bf16[528,1664]{1,0:T(8,128)(2,1)} %collective-permute-done.28.g_ref.refs_14_, bf16[528,624]{1,0:T(8,128)(2,1)} %get-tuple-element.292.qkv_ref, f32[8,512]{1,0:T(8,128)} %get-tuple-element.293.lse_ref, ...), custom_call_target="tpu_custom_call" | custom-call | flops 52038205440 | bytes 228723840 | tf_op jit(solution)/shard_map/attend_bwd/pallas_call | solution.py:197
  516.8 6.3 collective-permute-done.32
  529.3 9.8 %attend_bwd.11 = (bf16[528,624]{1,0:T(8,128)(2,1)}, f32[1,624]{1,0:T(1,128)}, bf16[528,1664]{1,0:T(8,128)(2,1)}) custom-call(bf16[528,1664]{1,0:T(8,128)(2,1)} %copy-done.59, bf16[528,624]{1,0:T(8,128)(2,1)} %get-tuple-element.298.qkv_ref, f32[8,512]{1,0:T(8,128)} %get-tuple-element.299.lse_ref, f32[8,128]{1,0:T(8,128)} %get-tuple-element.300.lset_ref, ...), custom_call_target="tpu_custom_call" | custom-call | flops 52038205440 | bytes 228723840 | tf_op jit(solution)/shard_map/attend_bwd/pallas_call | solution.py:197
  539.1 20.2 %attend_wgrad.2 = bf16[832,1664]{1,0:T(8,128)(2,1)} custom-call(bf16[528,624]{1,0:T(8,128)(2,1)} %get-tuple-element.302.refs_0_, bf16[528,624]{1,0:T(8,128)(2,1)} %get-tuple-element.303.refs_1_, bf16[528,624]{1,0:T(8,128)(2,1)} %get-tuple-element.304.refs_2_, bf16[528,624]{1,0:T(8,128)(2,1)} %get-tuple-element.305.refs_3_, ...), custom_call_target="tpu_custom_call" | custom-call | flops 175437250560 | bytes 610222080 | tf_op jit(solution)/shard_map/attend_wgrad/pallas_call | solution.py:197
  564.3 5.7 unpack.2
  570.0 10.7 %attend_bwd.12 = (bf16[528,624]{1,0:T(8,128)(2,1)}, f32[1,624]{1,0:T(1,128)}, bf16[528,1664]{1,0:T(8,128)(2,1)}) custom-call(bf16[528,1664]{1,0:T(8,128)(2,1)} %copy-done.59, bf16[528,624]{1,0:T(8,128)(2,1)} %get-tuple-element.315.qkv_ref, f32[8,512]{1,0:T(8,128)} %get-tuple-element.316.lse_ref, f32[8,128]{1,0:T(8,128)} %get-tuple-element.317.lset_ref, ...), custom_call_target="tpu_custom_call" | custom-call | flops 52038205440 | bytes 281439360 | tf_op jit(solution)/shard_map/attend_bwd/pallas_call | solution.py:197
  583.7 10.2 %attend_bwd.13 = (bf16[528,624]{1,0:T(8,128)(2,1)}, f32[1,624]{1,0:T(1,128)}, bf16[528,1664]{1,0:T(8,128)(2,1)}) custom-call(bf16[528,1664]{1,0:T(8,128)(2,1)} %collective-permute-done.30.g_ref.refs_13_, bf16[528,624]{1,0:T(8,128)(2,1)} %get-tuple-element.321.qkv_ref, f32[8,512]{1,0:T(8,128)} %get-tuple-element.322.lse_ref, ...), custom_call_target="tpu_custom_call" | custom-call | flops 52038205440 | bytes 281439360 | tf_op jit(solution)/shard_map/attend_bwd/pallas_call | solution.py:197
  597.8 5.7 collective-permute-done.38
  606.0 10.7 %attend_bwd.14 = (bf16[528,624]{1,0:T(8,128)(2,1)}, f32[1,624]{1,0:T(1,128)}, bf16[528,1664]{1,0:T(8,128)(2,1)}) custom-call(bf16[528,1664]{1,0:T(8,128)(2,1)} %collective-permute-done.28.g_ref.refs_14_, bf16[528,624]{1,0:T(8,128)(2,1)} %get-tuple-element.327.qkv_ref, f32[8,512]{1,0:T(8,128)} %get-tuple-element.328.lse_ref, ...), custom_call_target="tpu_custom_call" | custom-call | flops 52038205440 | bytes 334154880 | tf_op jit(solution)/shard_map/attend_bwd/pallas_call | solution.py:197
  621.3 14.8 %collective-permute-done.40 = bf16[256,1664]{1,0:T(8,128)(2,1)} collective-permute-done((bf16[256,1664]{1,0:T(8,128)(2,1)}, bf16[256,1664]{1,0:T(8,128)(2,1)}, u32[]{:S(2)}, u32[]{:S(2)}) %collective-permute-start.40) | collective-permute-done | bytes 852000 | tf_op jit(solution)/shard_map/ppermute | solution.py:660
  638.8 10.2 %attend_bwd.15 = (bf16[528,624]{1,0:T(8,128)(2,1)}, f32[1,624]{1,0:T(1,128)}, bf16[528,1664]{1,0:T(8,128)(2,1)}) custom-call(bf16[528,1664]{1,0:T(8,128)(2,1)} %get-tuple-element.333.g_ref.refs_12_, bf16[528,624]{1,0:T(8,128)(2,1)} %get-tuple-element.334.qkv_ref, f32[8,512]{1,0:T(8,128)} %get-tuple-element.335.lse_ref, ...), custom_call_target="tpu_custom_call" | custom-call | flops 52038205440 | bytes 281439360 | tf_op jit(solution)/shard_map/attend_bwd/pallas_call | solution.py:197
  651.2 10.7 %collective-permute-done.42 = bf16[256,1664]{1,0:T(8,128)(2,1)S(1)} collective-permute-done((bf16[256,1664]{1,0:T(8,128)(2,1)S(1)}, bf16[256,1664]{1,0:T(8,128)(2,1)S(1)}, u32[]{:S(2)}, u32[]{:S(2)}) %collective-permute-start.42) | collective-permute-done | bytes 852000 | tf_op jit(solution)/shard_map/ppermute | solution.py:660
  669.3 20.1 %attend_wgrad.3 = bf16[832,1664]{1,0:T(8,128)(2,1)} custom-call(bf16[528,624]{1,0:T(8,128)(2,1)} %get-tuple-element.342.refs_0_, bf16[528,624]{1,0:T(8,128)(2,1)} %get-tuple-element.343.refs_1_, bf16[528,624]{1,0:T(8,128)(2,1)} %get-tuple-element.344.refs_2_, bf16[528,624]{1,0:T(8,128)(2,1)} %get-tuple-element.345.refs_3_, ...), custom_call_target="tpu_custom_call" | custom-call | flops 175437250560 | bytes 610222080 | tf_op jit(solution)/shard_map/attend_wgrad/pallas_call | solution.py:197
  699.4 9.0 %place.2 = f32[2048,1664]{1,0:T(8,128)} custom-call(s32[8]{0:T(128)} %stack.131.at_ref, bf16[1024,1664]{1,0:T(8,128)(2,1)} %constant_dynamic-update-slice_fusion.8.refs_0_, bf16[1024,1664]{1,0:T(8,128)(2,1)} %collective-permute-done.45.refs_1_), custom_call_target="tpu_custom_call" | custom-call | bytes 613417920 | tf_op jit(solution)/shard_map/place/pallas_call | solution.py:197
  710.0 9.8 %norm_back.3 = (f32[8,1664]{1,0:T(8,128)}, bf16[528,1664]{1,0:T(8,128)(2,1)}, f32[8,1664]{1,0:T(8,128)}, f32[8,1664]{1,0:T(8,128)}, f32[8,1664]{1,0:T(8,128)}) custom-call(bf16[528,1664]{1,0:T(8,128)(2,1)} %get-tuple-element.354.x_ref, bf16[528,1664]{1,0:T(8,128)(2,1)} %get-tuple-element.337.a_ref, bf16[528,1664]{1,0:T(8,128)(2,1)} %collective-permute-done.41.b_ref, ...), custom_call_target="tpu_custom_call" | custom-call | bytes 375598080 | tf_op jit(solution)/shard_map/norm_back/pallas_call | solution.py:197
  722.5 6.1 collective-permute-done.48
  731.0 3.0 add_convert_fusion.10
  737.1 4.5 collective-permute-done.52
  743.5 21.6 %collective-permute-done.53 = bf16[512,1664]{1,0:T(8,128)(2,1)S(1)} collective-permute-done((bf16[512,1664]{1,0:T(8,128)(2,1)}, bf16[512,1664]{1,0:T(8,128)(2,1)S(1)}, u32[]{:S(2)}, u32[]{:S(2)}) %collective-permute-start.53) | collective-permute-done | bytes 1703968 | tf_op jit(solution)/shard_map/ppermute | solution.py:660
  771.7 3.8 collective-permute-done.54
  778.2 10.7 %place.3 = f32[1664,2048]{1,0:T(8,128)} custom-call(s32[8]{0:T(128)} %stack.142.at_ref, bf16[1024,1664]{1,0:T(8,128)(2,1)} %constant_dynamic-update-slice_fusion.12.refs_0_, bf16[1024,1664]{1,0:T(8,128)(2,1)} %copy-done.10), custom_call_target="tpu_custom_call" | custom-call | bytes 613417920 | tf_op jit(solution)/shard_map/place/pallas_call | solution.py:197
  792.9 7.7 collective-permute-done.57
  805.3 4.3 collective-permute-done.59
  819.4 7.9 place_heads.1
  (351 shorter events, 186.9 us)
Async XLA Ops:
  11.6 27.7 %collective-permute-start.1 = (bf16[528,1664]{1,0:T(8,128)(2,1)}, bf16[528,1664]{1,0:T(8,128)(2,1)}, u32[]{:S(2)}, u32[]{:S(2)}) collective-permute-start(bf16[528,1664]{1,0:T(8,128)(2,1)} %get-tuple-element.226.n_ref.refs_8_), channel_id=1, source_target_pairs={{0,4},{1,5},{2,6},{3,7},{4,0},{5,1},{6,2},{7,3},{8,12},{9,13},{10,... | collective-permute-start | bytes 5271560 | tf_op jit(solution)/shard_map/ppermute | solution.py:660
  12.1 56.9 %collective-permute-start = (bf16[528,1664]{1,0:T(8,128)(2,1)}, bf16[528,1664]{1,0:T(8,128)(2,1)}, u32[]{:S(2)}, u32[]{:S(2)}) collective-permute-start(bf16[528,1664]{1,0:T(8,128)(2,1)} %get-tuple-element.226.n_ref.refs_8_), channel_id=1, source_target_pairs={{0,1},{1,0},{2,3},{3,2},{4,5},{5,4},{6,7},{7,6},{8,9},{9,8},{10,11... | collective-permute-start | bytes 5271560 | tf_op jit(solution)/shard_map/ppermute | solution.py:660
  16.1 52.0 %collective-permute-start.2 = (bf16[208,1664]{1,0:T(8,128)(2,1)S(1)}, bf16[208,1664]{1,0:T(8,128)(2,1)S(1)}, u32[]{:S(2)}, u32[]{:S(2)}) collective-permute-start(bf16[208,1664]{1,0:T(8,128)(2,1)S(1)} %get-tuple-element.394), channel_id=1, source_target_pairs={{0,2},{1,3},{2,0},{3,1},{4,6},{5,7},{6,4},{7,5},{8,10},{9,11},{10,... | collective-permute-start | bytes 2076680 | tf_op jit(solution)/shard_map/ppermute | solution.py:660
  37.2 80.3 %collective-permute-start.8 = (f32[1440]{0:T(1024)}, f32[1440]{0:T(1024)}, u32[]{:S(2)}, u32[]{:S(2)}) collective-permute-start(f32[1440]{0:T(1024)} %pad_maximum_fusion.1), channel_id=1, source_target_pairs={{0,2},{1,3},{2,0},{3,1},{4,6},{5,7},{6,4},{7,5},{8,10},{9,11},{10,... | collective-permute-start | bytes 17288 | tf_op jit(solution)/shard_map/ppermute | solution.py:660
  69.0 12.3 %collective-permute-start.3 = (bf16[528,1664]{1,0:T(8,128)(2,1)}, bf16[528,1664]{1,0:T(8,128)(2,1)S(1)}, u32[]{:S(2)}, u32[]{:S(2)}) collective-permute-start(bf16[528,1664]{1,0:T(8,128)(2,1)} %collective-permute-done.n_ref.refs_10_), channel_id=1, source_target_pairs={{0,4},{1,5},{2,6},{3,7},{4,0},{5,1},{6,2},{7,3},{8,12},{9,13},{10,... | collective-permute-start | bytes 5271560 | tf_op jit(solution)/shard_map/ppermute | solution.py:660
  77.8 18.4 %collective-permute-start.5 = (bf16[208,1664]{1,0:T(8,128)(2,1)S(1)}, bf16[208,1664]{1,0:T(8,128)(2,1)}, u32[]{:S(2)}, u32[]{:S(2)}) collective-permute-start(bf16[208,1664]{1,0:T(8,128)(2,1)S(1)} %collective-permute-done.2), channel_id=1, source_target_pairs={{0,8},{1,9},{2,10},{3,11},{4,12},{5,13},{6,14},{7,15},{8,0},{9,1},... | collective-permute-start | bytes 2076680 | tf_op jit(solution)/shard_map/ppermute | solution.py:660
  79.5 32.6 %collective-permute-start.6 = (bf16[208,1664]{1,0:T(8,128)(2,1)S(1)}, bf16[208,1664]{1,0:T(8,128)(2,1)}, u32[]{:S(2)}, u32[]{:S(2)}) collective-permute-start(bf16[208,1664]{1,0:T(8,128)(2,1)S(1)} %collective-permute-done.2), channel_id=1, source_target_pairs={{0,16},{1,17},{2,18},{3,19},{4,20},{5,21},{6,22},{7,23},{8,24},{9,... | collective-permute-start | bytes 2076680 | tf_op jit(solution)/shard_map/ppermute | solution.py:660
  81.0 34.6 %collective-permute-start.7 = (bf16[208,1664]{1,0:T(8,128)(2,1)S(1)}, bf16[208,1664]{1,0:T(8,128)(2,1)}, u32[]{:S(2)}, u32[]{:S(2)}) collective-permute-start(bf16[208,1664]{1,0:T(8,128)(2,1)S(1)} %collective-permute-done.2), channel_id=1, source_target_pairs={{0,24},{1,25},{2,26},{3,27},{4,28},{5,29},{6,30},{7,31},{8,16},{9,... | collective-permute-start | bytes 2076680 | tf_op jit(solution)/shard_map/ppermute | solution.py:660
  81.3 46.8 %collective-permute-start.9 = (bf16[528,1664]{1,0:T(8,128)(2,1)}, bf16[528,1664]{1,0:T(8,128)(2,1)}, u32[]{:S(2)}, u32[]{:S(2)}) collective-permute-start(bf16[528,1664]{1,0:T(8,128)(2,1)} %get-tuple-element.219.c0.refs_2_.add_ref), channel_id=1, source_target_pairs={{0,4},{1,5},{2,6},{3,7},{4,0},{5,1},{6,2},{7,3},{8,12},{9,13},{10,... | collective-permute-start | bytes 5271560 | tf_op jit(solution)/shard_map/ppermute | solution.py:660
  96.2 22.1 %copy-start.47 = (f32[208]{0:T(256)S(1)}, f32[208]{0:T(256)}, u32[]{:S(2)}) copy-start(f32[208]{0:T(256)} %copy-done.46) | copy-start | bytes 2500
  96.3 66.6 %collective-permute-start.12 = (bf16[528,1664]{1,0:T(8,128)(2,1)}, bf16[528,1664]{1,0:T(8,128)(2,1)}, u32[]{:S(2)}, u32[]{:S(2)}) collective-permute-start(bf16[528,1664]{1,0:T(8,128)(2,1)} %get-tuple-element.219.c0.refs_2_.add_ref), channel_id=1, source_target_pairs={{0,1},{1,0},{2,3},{3,2},{4,5},{5,4},{6,7},{7,6},{8,9},{9,8},{10,11... | collective-permute-start | bytes 5271560 | tf_op jit(solution)/shard_map/ppermute | solution.py:660
  112.1 50.8 %collective-permute-start.13 = (bf16[1664,256]{1,0:T(8,128)(2,1)}, bf16[1664,256]{1,0:T(8,128)(2,1)}, u32[]{:S(2)}, u32[]{:S(2)}) collective-permute-start(bf16[1664,256]{1,0:T(8,128)(2,1)} %constant_dynamic-slice_fusion.11), channel_id=1, source_target_pairs={{0,2},{1,3},{2,0},{3,1},{4,6},{5,7},{6,4},{7,5},{8,10},{9,11},{10,... | collective-permute-start | bytes 2555912 | tf_op jit(solution)/shard_map/ppermute | solution.py:660
  115.6 71.7 %collective-permute-start.4 = (bf16[256,1664]{1,0:T(8,128)(2,1)}, bf16[256,1664]{1,0:T(8,128)(2,1)}, u32[]{:S(2)}, u32[]{:S(2)}) collective-permute-start(bf16[256,1664]{1,0:T(8,128)(2,1)} %constant_dynamic-slice_fusion.10), channel_id=1, source_target_pairs={{0,2},{1,3},{2,0},{3,1},{4,6},{5,7},{6,4},{7,5},{8,10},{9,11},{10,... | collective-permute-start | bytes 2555912 | tf_op jit(solution)/shard_map/ppermute | solution.py:660
  128.1 9.6 %collective-permute-start.10 = (bf16[528,1664]{1,0:T(8,128)(2,1)}, bf16[528,1664]{1,0:T(8,128)(2,1)S(1)}, u32[]{:S(2)}, u32[]{:S(2)}) collective-permute-start(bf16[528,1664]{1,0:T(8,128)(2,1)} %get-tuple-element.218), channel_id=1, source_target_pairs={{0,4},{1,5},{2,6},{3,7},{4,0},{5,1},{6,2},{7,3},{8,12},{9,13},{10,... | collective-permute-start | bytes 5271560 | tf_op jit(solution)/shard_map/ppermute | solution.py:660
  137.3 25.6 %collective-permute-start.11 = (bf16[528,1664]{1,0:T(8,128)(2,1)}, bf16[528,1664]{1,0:T(8,128)(2,1)S(1)}, u32[]{:S(2)}, u32[]{:S(2)}) collective-permute-start(bf16[528,1664]{1,0:T(8,128)(2,1)} %get-tuple-element.221), channel_id=1, source_target_pairs={{0,4},{1,5},{2,6},{3,7},{4,0},{5,1},{6,2},{7,3},{8,12},{9,13},{10,... | collective-permute-start | bytes 5271560 | tf_op jit(solution)/shard_map/ppermute | solution.py:660
  149.1 62.3 %collective-permute-start.17 = (bf16[528,1664]{1,0:T(8,128)(2,1)}, bf16[528,1664]{1,0:T(8,128)(2,1)S(1)}, u32[]{:S(2)}, u32[]{:S(2)}) collective-permute-start(bf16[528,1664]{1,0:T(8,128)(2,1)} %get-tuple-element.223), channel_id=1, source_target_pairs={{0,1},{1,0},{2,3},{3,2},{4,5},{5,4},{6,7},{7,6},{8,9},{9,8},{10,11... | collective-permute-start | bytes 5271560 | tf_op jit(solution)/shard_map/ppermute | solution.py:660
  162.9 45.9 %collective-permute-start.16 = (bf16[528,1664]{1,0:T(8,128)(2,1)}, bf16[528,1664]{1,0:T(8,128)(2,1)}, u32[]{:S(2)}, u32[]{:S(2)}) collective-permute-start(bf16[528,1664]{1,0:T(8,128)(2,1)} %collective-permute-done.12.c0.refs_4_), channel_id=1, source_target_pairs={{0,4},{1,5},{2,6},{3,7},{4,0},{5,1},{6,2},{7,3},{8,12},{9,13},{10,... | collective-permute-start | bytes 5271560 | tf_op jit(solution)/shard_map/ppermute | solution.py:660
  172.6 29.1 %collective-permute-start.14 = (bf16[1664,256]{1,0:T(8,128)(2,1)}, bf16[1664,256]{1,0:T(8,128)(2,1)S(1)}, u32[]{:S(2)}, u32[]{:S(2)}) collective-permute-start(bf16[1664,256]{1,0:T(8,128)(2,1)} %collective-permute-done.13), channel_id=1, source_target_pairs={{0,8},{1,9},{2,10},{3,11},{4,12},{5,13},{6,14},{7,15},{8,0},{9,1},... | collective-permute-start | bytes 2555912 | tf_op jit(solution)/shard_map/ppermute | solution.py:660
  187.3 20.5 %collective-permute-start.15 = (bf16[256,1664]{1,0:T(8,128)(2,1)}, bf16[256,1664]{1,0:T(8,128)(2,1)S(1)}, u32[]{:S(2)}, u32[]{:S(2)}) collective-permute-start(bf16[256,1664]{1,0:T(8,128)(2,1)} %collective-permute-done.4), channel_id=1, source_target_pairs={{0,16},{1,17},{2,18},{3,19},{4,20},{5,21},{6,22},{7,23},{8,24},{9,... | collective-permute-start | bytes 2555912 | tf_op jit(solution)/shard_map/ppermute | solution.py:660
  221.1 10.4 %collective-permute-start.18 = (bf16[528,1664]{1,0:T(8,128)(2,1)}, bf16[528,1664]{1,0:T(8,128)(2,1)S(1)}, u32[]{:S(2)}, u32[]{:S(2)}) collective-permute-start(bf16[528,1664]{1,0:T(8,128)(2,1)} %get-tuple-element.240.n0.refs_2_), channel_id=1, source_target_pairs={{0,4},{1,5},{2,6},{3,7},{4,0},{5,1},{6,2},{7,3},{8,12},{9,13},{10,... | collective-permute-start | bytes 5271560 | tf_op jit(solution)/shard_map/ppermute | solution.py:660
  226.8 39.9 %collective-permute-start.19 = (bf16[1664,512]{1,0:T(8,128)(2,1)}, bf16[1664,512]{1,0:T(8,128)(2,1)}, u32[]{:S(2)}, u32[]{:S(2)}) collective-permute-start(bf16[1664,512]{1,0:T(8,128)(2,1)} %constant_dynamic-update-slice_fusion), channel_id=1, source_target_pairs={{0,16},{1,17},{2,18},{3,19},{4,20},{5,21},{6,22},{7,23},{8,24},{9,... | collective-permute-start | bytes 5111816 | tf_op jit(solution)/shard_map/ppermute | solution.py:660
  228.4 44.4 %collective-permute-start.20 = (bf16[512,1664]{1,0:T(8,128)(2,1)}, bf16[512,1664]{1,0:T(8,128)(2,1)}, u32[]{:S(2)}, u32[]{:S(2)}) collective-permute-start(bf16[512,1664]{1,0:T(8,128)(2,1)} %constant_dynamic-update-slice_fusion.2), channel_id=1, source_target_pairs={{0,8},{1,9},{2,10},{3,11},{4,12},{5,13},{6,14},{7,15},{8,0},{9,1},... | collective-permute-start | bytes 5111816 | tf_op jit(solution)/shard_map/ppermute | solution.py:660
  229.7 69.9 %collective-permute-start.21 = (bf16[528,1664]{1,0:T(8,128)(2,1)}, bf16[528,1664]{1,0:T(8,128)(2,1)}, u32[]{:S(2)}, u32[]{:S(2)}) collective-permute-start(bf16[528,1664]{1,0:T(8,128)(2,1)} %get-tuple-element.240.n0.refs_2_), channel_id=1, source_target_pairs={{0,1},{1,0},{2,3},{3,2},{4,5},{5,4},{6,7},{7,6},{8,9},{9,8},{10,11... | collective-permute-start | bytes 5271560 | tf_op jit(solution)/shard_map/ppermute | solution.py:660
  299.6 14.1 %collective-permute-start.22 = (bf16[528,1664]{1,0:T(8,128)(2,1)}, bf16[528,1664]{1,0:T(8,128)(2,1)}, u32[]{:S(2)}, u32[]{:S(2)}) collective-permute-start(bf16[528,1664]{1,0:T(8,128)(2,1)} %collective-permute-done.21.n0.refs_4_), channel_id=1, source_target_pairs={{0,4},{1,5},{2,6},{3,7},{4,0},{5,1},{6,2},{7,3},{8,12},{9,13},{10,... | collective-permute-start | bytes 5271560 | tf_op jit(solution)/shard_map/ppermute | solution.py:660
  313.1 251.1 %collective-permute-start.34 = (bf16[528,1664]{1,0:T(8,128)(2,1)}, bf16[528,1664]{1,0:T(8,128)(2,1)}, u32[]{:S(2)}, u32[]{:S(2)}) collective-permute-start(bf16[528,1664]{1,0:T(8,128)(2,1)} %get-tuple-element.249), channel_id=1, source_target_pairs={{0,4},{1,5},{2,6},{3,7},{4,0},{5,1},{6,2},{7,3},{8,12},{9,13},{10,... | collective-permute-start | bytes 5271560 | tf_op jit(solution)/shard_map/ppermute | solution.py:660
  313.6 106.6 %collective-permute-start.24 = (bf16[528,1664]{1,0:T(8,128)(2,1)}, bf16[528,1664]{1,0:T(8,128)(2,1)}, u32[]{:S(2)}, u32[]{:S(2)}) collective-permute-start(bf16[528,1664]{1,0:T(8,128)(2,1)} %get-tuple-element.269), channel_id=1, source_target_pairs={{0,4},{1,5},{2,6},{3,7},{4,0},{5,1},{6,2},{7,3},{8,12},{9,13},{10,... | collective-permute-start | bytes 5271560 | tf_op jit(solution)/shard_map/ppermute | solution.py:660
  357.5 22.7 %collective-permute-start.23 = (bf16[528,1664]{1,0:T(8,128)(2,1)}, bf16[528,1664]{1,0:T(8,128)(2,1)}, u32[]{:S(2)}, u32[]{:S(2)}) collective-permute-start(bf16[528,1664]{1,0:T(8,128)(2,1)} %get-tuple-element.263), channel_id=1, source_target_pairs={{0,4},{1,5},{2,6},{3,7},{4,0},{5,1},{6,2},{7,3},{8,12},{9,13},{10,... | collective-permute-start | bytes 5271560 | tf_op jit(solution)/shard_map/ppermute | solution.py:660
  358.1 22.1 %copy-start.22 = (bf16[528,1664]{1,0:T(8,128)(2,1)S(1)}, bf16[528,1664]{1,0:T(8,128)(2,1)}, u32[]{:S(2)}) copy-start(bf16[528,1664]{1,0:T(8,128)(2,1)} %get-tuple-element.262) | copy-start | bytes 5271556
  375.1 90.6 %collective-permute-start.27 = (bf16[1024,1664]{1,0:T(8,128)(2,1)}, bf16[1024,1664]{1,0:T(8,128)(2,1)}, u32[]{:S(2)}, u32[]{:S(2)}) collective-permute-start(bf16[1024,1664]{1,0:T(8,128)(2,1)} %wgrad.4), channel_id=1, source_target_pairs={{0,16},{1,17},{2,18},{3,19},{4,20},{5,21},{6,22},{7,23},{8,24},{9,... | collective-permute-start | bytes 10223624 | tf_op jit(solution)/shard_map/ppermute | solution.py:660
  383.3 40.3 %collective-permute-start.25 = (bf16[528,1664]{1,0:T(8,128)(2,1)}, bf16[528,1664]{1,0:T(8,128)(2,1)}, u32[]{:S(2)}, u32[]{:S(2)}) collective-permute-start(bf16[528,1664]{1,0:T(8,128)(2,1)} %add_convert_fusion.1), channel_id=1, source_target_pairs={{0,1},{1,0},{2,3},{3,2},{4,5},{5,4},{6,7},{7,6},{8,9},{9,8},{10,11... | collective-permute-start | bytes 5271560 | tf_op jit(solution)/shard_map/ppermute | solution.py:660
  402.0 93.0 %collective-permute-start.26 = (bf16[1024,1664]{1,0:T(8,128)(2,1)}, bf16[1024,1664]{1,0:T(8,128)(2,1)}, u32[]{:S(2)}, u32[]{:S(2)}) collective-permute-start(bf16[1024,1664]{1,0:T(8,128)(2,1)} %wgrad.5), channel_id=1, source_target_pairs={{0,8},{1,9},{2,10},{3,11},{4,12},{5,13},{6,14},{7,15},{8,0},{9,1},... | collective-permute-start | bytes 10223624 | tf_op jit(solution)/shard_map/ppermute | solution.py:660
  448.0 52.3 %collective-permute-start.31 = (bf16[528,1664]{1,0:T(8,128)(2,1)}, bf16[528,1664]{1,0:T(8,128)(2,1)}, u32[]{:S(2)}, u32[]{:S(2)}) collective-permute-start(bf16[528,1664]{1,0:T(8,128)(2,1)} %get-tuple-element.272), channel_id=1, source_target_pairs={{0,4},{1,5},{2,6},{3,7},{4,0},{5,1},{6,2},{7,3},{8,12},{9,13},{10,... | collective-permute-start | bytes 5271560 | tf_op jit(solution)/shard_map/ppermute | solution.py:660
  465.2 18.8 %collective-permute-start.30 = (bf16[528,1664]{1,0:T(8,128)(2,1)}, bf16[528,1664]{1,0:T(8,128)(2,1)}, u32[]{:S(2)}, u32[]{:S(2)}) collective-permute-start(bf16[528,1664]{1,0:T(8,128)(2,1)} %get-tuple-element.333.g_ref.refs_12_), channel_id=1, source_target_pairs={{0,4},{1,5},{2,6},{3,7},{4,0},{5,1},{6,2},{7,3},{8,12},{9,13},{10,... | collective-permute-start | bytes 5271560 | tf_op jit(solution)/shard_map/ppermute | solution.py:660
  465.7 41.4 %collective-permute-start.28 = (bf16[528,1664]{1,0:T(8,128)(2,1)}, bf16[528,1664]{1,0:T(8,128)(2,1)}, u32[]{:S(2)}, u32[]{:S(2)}) collective-permute-start(bf16[528,1664]{1,0:T(8,128)(2,1)} %get-tuple-element.333.g_ref.refs_12_), channel_id=1, source_target_pairs={{0,1},{1,0},{2,3},{3,2},{4,5},{5,4},{6,7},{7,6},{8,9},{9,8},{10,11... | collective-permute-start | bytes 5271560 | tf_op jit(solution)/shard_map/ppermute | solution.py:660
  483.9 39.2 %collective-permute-start.32 = (bf16[512,1664]{1,0:T(8,128)(2,1)}, bf16[512,1664]{1,0:T(8,128)(2,1)}, u32[]{:S(2)}, u32[]{:S(2)}) collective-permute-start(bf16[512,1664]{1,0:T(8,128)(2,1)} %bitcast.22), channel_id=1, source_target_pairs={{0,8},{1,9},{2,10},{3,11},{4,12},{5,13},{6,14},{7,15},{8,0},{9,1},... | collective-permute-start | bytes 5111816 | tf_op jit(solution)/shard_map/ppermute | solution.py:660
  499.7 62.7 %collective-permute-start.33 = (bf16[512,1664]{1,0:T(8,128)(2,1)}, bf16[512,1664]{1,0:T(8,128)(2,1)}, u32[]{:S(2)}, u32[]{:S(2)}) collective-permute-start(bf16[512,1664]{1,0:T(8,128)(2,1)} %bitcast.26), channel_id=1, source_target_pairs={{0,16},{1,17},{2,18},{3,19},{4,20},{5,21},{6,22},{7,23},{8,24},{9,... | collective-permute-start | bytes 5111816 | tf_op jit(solution)/shard_map/ppermute | solution.py:660
  503.4 60.8 %collective-permute-start.35 = (bf16[528,1664]{1,0:T(8,128)(2,1)}, bf16[528,1664]{1,0:T(8,128)(2,1)}, u32[]{:S(2)}, u32[]{:S(2)}) collective-permute-start(bf16[528,1664]{1,0:T(8,128)(2,1)} %add_convert_fusion), channel_id=1, source_target_pairs={{0,1},{1,0},{2,3},{3,2},{4,5},{5,4},{6,7},{7,6},{8,9},{9,8},{10,11... | collective-permute-start | bytes 5271560 | tf_op jit(solution)/shard_map/ppermute | solution.py:660
  507.1 21.0 %collective-permute-start.29 = (bf16[528,1664]{1,0:T(8,128)(2,1)}, bf16[528,1664]{1,0:T(8,128)(2,1)S(1)}, u32[]{:S(2)}, u32[]{:S(2)}) collective-permute-start(bf16[528,1664]{1,0:T(8,128)(2,1)} %collective-permute-done.28.g_ref.refs_14_), channel_id=1, source_target_pairs={{0,4},{1,5},{2,6},{3,7},{4,0},{5,1},{6,2},{7,3},{8,12},{9,13},{10,... | collective-permute-start | bytes 5271560 | tf_op jit(solution)/shard_map/ppermute | solution.py:660
  526.4 54.4 %collective-permute-start.36 = (bf16[256,1664]{1,0:T(8,128)(2,1)}, bf16[256,1664]{1,0:T(8,128)(2,1)}, u32[]{:S(2)}, u32[]{:S(2)}) collective-permute-start(bf16[256,1664]{1,0:T(8,128)(2,1)} %get-tuple-element.406), channel_id=1, source_target_pairs={{0,2},{1,3},{2,0},{3,1},{4,6},{5,7},{6,4},{7,5},{8,10},{9,11},{10,... | collective-permute-start | bytes 2555912 | tf_op jit(solution)/shard_map/ppermute | solution.py:660
  561.9 55.2 %collective-permute-start.37 = (bf16[416,1664]{1,0:T(8,128)(2,1)}, bf16[416,1664]{1,0:T(8,128)(2,1)}, u32[]{:S(2)}, u32[]{:S(2)}) collective-permute-start(bf16[416,1664]{1,0:T(8,128)(2,1)} %constant_dynamic-slice_fusion.6), channel_id=1, source_target_pairs={{0,16},{1,17},{2,18},{3,19},{4,20},{5,21},{6,22},{7,23},{8,24},{9,... | collective-permute-start | bytes 4153352 | tf_op jit(solution)/shard_map/ppermute | solution.py:660
  580.7 25.3 %collective-permute-start.39 = (bf16[528,1664]{1,0:T(8,128)(2,1)}, bf16[528,1664]{1,0:T(8,128)(2,1)}, u32[]{:S(2)}, u32[]{:S(2)}) collective-permute-start(bf16[528,1664]{1,0:T(8,128)(2,1)} %get-tuple-element.318), channel_id=1, source_target_pairs={{0,4},{1,5},{2,6},{3,7},{4,0},{5,1},{6,2},{7,3},{8,12},{9,13},{10,... | collective-permute-start | bytes 5271560 | tf_op jit(solution)/shard_map/ppermute | solution.py:660
  582.1 21.4 %collective-permute-start.38 = (bf16[256,1664]{1,0:T(8,128)(2,1)S(1)}, bf16[256,1664]{1,0:T(8,128)(2,1)S(1)}, u32[]{:S(2)}, u32[]{:S(2)}) collective-permute-start(bf16[256,1664]{1,0:T(8,128)(2,1)S(1)} %add_convert_fusion.9), channel_id=1, source_target_pairs={{0,8},{1,9},{2,10},{3,11},{4,12},{5,13},{6,14},{7,15},{8,0},{9,1},... | collective-permute-start | bytes 2555912 | tf_op jit(solution)/shard_map/ppermute | solution.py:660
  593.9 45.0 %collective-permute-start.41 = (bf16[528,1664]{1,0:T(8,128)(2,1)}, bf16[528,1664]{1,0:T(8,128)(2,1)}, u32[]{:S(2)}, u32[]{:S(2)}) collective-permute-start(bf16[528,1664]{1,0:T(8,128)(2,1)} %get-tuple-element.324), channel_id=1, source_target_pairs={{0,4},{1,5},{2,6},{3,7},{4,0},{5,1},{6,2},{7,3},{8,12},{9,13},{10,... | collective-permute-start | bytes 5271560 | tf_op jit(solution)/shard_map/ppermute | solution.py:660
  595.4 40.6 %collective-permute-start.40 = (bf16[256,1664]{1,0:T(8,128)(2,1)}, bf16[256,1664]{1,0:T(8,128)(2,1)}, u32[]{:S(2)}, u32[]{:S(2)}) collective-permute-start(bf16[256,1664]{1,0:T(8,128)(2,1)} %get-tuple-element.404), channel_id=1, source_target_pairs={{0,2},{1,3},{2,0},{3,1},{4,6},{5,7},{6,4},{7,5},{8,10},{9,11},{10,... | collective-permute-start | bytes 2555912 | tf_op jit(solution)/shard_map/ppermute | solution.py:660
  604.5 62.1 %collective-permute-start.44 = (bf16[512,1664]{1,0:T(8,128)(2,1)}, bf16[512,1664]{1,0:T(8,128)(2,1)}, u32[]{:S(2)}, u32[]{:S(2)}) collective-permute-start(bf16[512,1664]{1,0:T(8,128)(2,1)} %constant_dynamic-update-slice_fusion.4), channel_id=1, source_target_pairs={{0,16},{1,17},{2,18},{3,19},{4,20},{5,21},{6,22},{7,23},{8,24},{9,... | collective-permute-start | bytes 5111816 | tf_op jit(solution)/shard_map/ppermute | solution.py:660
  616.7 91.8 %collective-permute-start.46 = (bf16[528,1664]{1,0:T(8,128)(2,1)}, bf16[528,1664]{1,0:T(8,128)(2,1)}, u32[]{:S(2)}, u32[]{:S(2)}) collective-permute-start(bf16[528,1664]{1,0:T(8,128)(2,1)} %get-tuple-element.330), channel_id=1, source_target_pairs={{0,1},{1,0},{2,3},{3,2},{4,5},{5,4},{6,7},{7,6},{8,9},{9,8},{10,11... | collective-permute-start | bytes 5271560 | tf_op jit(solution)/shard_map/ppermute | solution.py:660
  620.0 42.0 %collective-permute-start.43 = (bf16[208,1664]{1,0:T(8,128)(2,1)}, bf16[208,1664]{1,0:T(8,128)(2,1)}, u32[]{:S(2)}, u32[]{:S(2)}) collective-permute-start(bf16[208,1664]{1,0:T(8,128)(2,1)} %get-tuple-element.408), channel_id=1, source_target_pairs={{0,8},{1,9},{2,10},{3,11},{4,12},{5,13},{6,14},{7,15},{8,0},{9,1},... | collective-permute-start | bytes 2076680 | tf_op jit(solution)/shard_map/ppermute | solution.py:660
  637.4 24.4 %collective-permute-start.42 = (bf16[256,1664]{1,0:T(8,128)(2,1)S(1)}, bf16[256,1664]{1,0:T(8,128)(2,1)S(1)}, u32[]{:S(2)}, u32[]{:S(2)}) collective-permute-start(bf16[256,1664]{1,0:T(8,128)(2,1)S(1)} %add_convert_fusion.8), channel_id=1, source_target_pairs={{0,16},{1,17},{2,18},{3,19},{4,20},{5,21},{6,22},{7,23},{8,24},{9,... | collective-permute-start | bytes 2555912 | tf_op jit(solution)/shard_map/ppermute | solution.py:660
  669.3 28.8 %collective-permute-start.45 = (bf16[1024,1664]{1,0:T(8,128)(2,1)}, bf16[1024,1664]{1,0:T(8,128)(2,1)}, u32[]{:S(2)}, u32[]{:S(2)}) collective-permute-start(bf16[1024,1664]{1,0:T(8,128)(2,1)} %constant_dynamic-update-slice_fusion.8.refs_0_), channel_id=1, source_target_pairs={{0,4},{1,5},{2,6},{3,7},{4,0},{5,1},{6,2},{7,3},{8,12},{9,13},{10,... | collective-permute-start | bytes 10223624 | tf_op jit(solution)/shard_map/ppermute | solution.py:660
  694.6 27.8 %collective-permute-start.49 = (bf16[208,1664]{1,0:T(8,128)(2,1)}, bf16[208,1664]{1,0:T(8,128)(2,1)}, u32[]{:S(2)}, u32[]{:S(2)}) collective-permute-start(bf16[208,1664]{1,0:T(8,128)(2,1)} %constant_dynamic-slice_fusion.2), channel_id=1, source_target_pairs={{0,24},{1,25},{2,26},{3,27},{4,28},{5,29},{6,30},{7,31},{8,16},{9,... | collective-permute-start | bytes 2076680 | tf_op jit(solution)/shard_map/ppermute | solution.py:660
  696.9 31.7 %collective-permute-start.48 = (bf16[208,1664]{1,0:T(8,128)(2,1)}, bf16[208,1664]{1,0:T(8,128)(2,1)}, u32[]{:S(2)}, u32[]{:S(2)}) collective-permute-start(bf16[208,1664]{1,0:T(8,128)(2,1)} %constant_dynamic-slice_fusion.3), channel_id=1, source_target_pairs={{0,16},{1,17},{2,18},{3,19},{4,20},{5,21},{6,22},{7,23},{8,24},{9,... | collective-permute-start | bytes 2076680 | tf_op jit(solution)/shard_map/ppermute | solution.py:660
  697.6 31.5 %collective-permute-start.47 = (bf16[208,1664]{1,0:T(8,128)(2,1)}, bf16[208,1664]{1,0:T(8,128)(2,1)}, u32[]{:S(2)}, u32[]{:S(2)}) collective-permute-start(bf16[208,1664]{1,0:T(8,128)(2,1)} %constant_dynamic-slice_fusion.4), channel_id=1, source_target_pairs={{0,8},{1,9},{2,10},{3,11},{4,12},{5,13},{6,14},{7,15},{8,0},{9,1},... | collective-permute-start | bytes 2076680 | tf_op jit(solution)/shard_map/ppermute | solution.py:660
  698.2 32.8 %collective-permute-start.50 = (bf16[208,1664]{1,0:T(8,128)(2,1)S(1)}, bf16[208,1664]{1,0:T(8,128)(2,1)}, u32[]{:S(2)}, u32[]{:S(2)}) collective-permute-start(bf16[208,1664]{1,0:T(8,128)(2,1)S(1)} %copy-done.24), channel_id=1, source_target_pairs={{0,2},{1,3},{2,0},{3,1},{4,6},{5,7},{6,4},{7,5},{8,10},{9,11},{10,... | collective-permute-start | bytes 2076680 | tf_op jit(solution)/shard_map/ppermute | solution.py:660
  708.5 56.6 %collective-permute-start.53 = (bf16[512,1664]{1,0:T(8,128)(2,1)}, bf16[512,1664]{1,0:T(8,128)(2,1)S(1)}, u32[]{:S(2)}, u32[]{:S(2)}) collective-permute-start(bf16[512,1664]{1,0:T(8,128)(2,1)} %copy-done.25), channel_id=1, source_target_pairs={{0,8},{1,9},{2,10},{3,11},{4,12},{5,13},{6,14},{7,15},{8,0},{9,1},... | collective-permute-start | bytes 5111816 | tf_op jit(solution)/shard_map/ppermute | solution.py:660
  722.4 14.6 %collective-permute-start.51 = (f32[21504]{0:T(1024)S(1)}, f32[21504]{0:T(1024)S(1)}, u32[]{:S(2)}, u32[]{:S(2)}) collective-permute-start(f32[21504]{0:T(1024)S(1)} %constant_dynamic-update-slice_fusion.23), channel_id=1, source_target_pairs={{0,4},{1,5},{2,6},{3,7},{4,0},{5,1},{6,2},{7,3},{8,12},{9,13},{10,... | collective-permute-start | bytes 258056 | tf_op jit(solution)/shard_map/ppermute | solution.py:660
  737.0 4.6 collective-permute-start.52
  766.4 10.0 %collective-permute-start.55 = (bf16[1024,1664]{1,0:T(8,128)(2,1)}, bf16[1024,1664]{1,0:T(8,128)(2,1)S(1)}, u32[]{:S(2)}, u32[]{:S(2)}) collective-permute-start(bf16[1024,1664]{1,0:T(8,128)(2,1)} %constant_dynamic-update-slice_fusion.12.refs_0_), channel_id=1, source_target_pairs={{0,4},{1,5},{2,6},{3,7},{4,0},{5,1},{6,2},{7,3},{8,12},{9,13},{10,... | collective-permute-start | bytes 10223624 | tf_op jit(solution)/shard_map/ppermute | solution.py:660
  766.4 24.5 %collective-permute-start.56 = (bf16[208,1664]{1,0:T(8,128)(2,1)}, bf16[208,1664]{1,0:T(8,128)(2,1)}, u32[]{:S(2)}, u32[]{:S(2)}) collective-permute-start(bf16[208,1664]{1,0:T(8,128)(2,1)} %add_convert_fusion.10), channel_id=1, source_target_pairs={{0,8},{1,9},{2,10},{3,11},{4,12},{5,13},{6,14},{7,15},{8,0},{9,1},... | collective-permute-start | bytes 2076680 | tf_op jit(solution)/shard_map/ppermute | solution.py:660
  767.7 32.8 %collective-permute-start.57 = (bf16[208,1664]{1,0:T(8,128)(2,1)}, bf16[208,1664]{1,0:T(8,128)(2,1)}, u32[]{:S(2)}, u32[]{:S(2)}) collective-permute-start(bf16[208,1664]{1,0:T(8,128)(2,1)} %add_convert_fusion.10), channel_id=1, source_target_pairs={{0,16},{1,17},{2,18},{3,19},{4,20},{5,21},{6,22},{7,23},{8,24},{9,... | collective-permute-start | bytes 2076680 | tf_op jit(solution)/shard_map/ppermute | solution.py:660
  768.4 7.1 collective-permute-start.54
  770.2 32.4 %collective-permute-start.58 = (bf16[208,1664]{1,0:T(8,128)(2,1)}, bf16[208,1664]{1,0:T(8,128)(2,1)}, u32[]{:S(2)}, u32[]{:S(2)}) collective-permute-start(bf16[208,1664]{1,0:T(8,128)(2,1)} %add_convert_fusion.10), channel_id=1, source_target_pairs={{0,24},{1,25},{2,26},{3,27},{4,28},{5,29},{6,30},{7,31},{8,16},{9,... | collective-permute-start | bytes 2076680 | tf_op jit(solution)/shard_map/ppermute | solution.py:660
  804.6 14.9 %collective-permute-start.61 = (bf16[832,1664]{1,0:T(8,128)(2,1)}, bf16[832,1664]{1,0:T(8,128)(2,1)}, u32[]{:S(2)}, u32[]{:S(2)}) collective-permute-start(bf16[832,1664]{1,0:T(8,128)(2,1)} %constant_dynamic-update-slice_fusion.15.refs_0_), channel_id=1, source_target_pairs={{0,4},{1,5},{2,6},{3,7},{4,0},{5,1},{6,2},{7,3},{8,12},{9,13},{10,... | collective-permute-start | bytes 8306696 | tf_op jit(solution)/shard_map/ppermute | solution.py:660
  804.6 4.9 collective-permute-start.59
  810.2 6.3 collective-permute-start.60
  (59 other events, 511.5 us)

commit v4 on v3

--- a/solution.py
+++ b/solution.py
@@ -857,6 +857,8 @@
     low_near_c = lay.move(low_near[1], c=1)
     far = None
     for k in range(n_hi):
+        if k == n_hi - 1:
+            order.meet(other_c, low_near_c)
         far = mlp_half(k, second_z, second_zc, seed[2:], far)
         far_bias.append(far[4])
     normed_second = [second_own, second_c, second_z, second_zc]
@@ -1004,11 +1006,10 @@
     for k in range(1, n_hi):
         for step in range(1, n_stage):
             attn_pairs[k] = halve(*attn_pairs[k], orders[k], step, 1)
+    order.meet(moved_1)
+    grad_first = (attention_back(0, 0), moved_1, moved_2)
     up_mine = order(lambda x: join(x, *up_hi_got), up_mine)
     up_all = Spread(up_mine, up_order)
-    order.meet(moved_1)
-    grad_first = (attention_back(0, 0), moved_1, moved_2)
-    up_all.step()
     attn_hi = []
     for k in range(1, n_hi):
         total = order(lambda x, k=k: join(x, attn_pairs[k][1]), attn_pairs[k][0])
@@ -1030,6 +1031,7 @@
     for mask in range(1, n_p):
         out = order(lambda x, mask=mask: block(x, 0, places[mask]), grad)
         attn_got.append(lay.move(out, p=mask))
+    up_all.step()
 
     def place_all(blocks, at, transposed):
         return order(lambda x: place([x] + blocks[1:], at, transposed), blocks[0])
@@ -1082,12 +1084,12 @@
         pair = hop(add(pair))
     up_all = up_all.finish()
     pair = hop(add(pair))
-    grad_up_weight = place_all(*up_all, True)
     masks = sorted(attn_all)
     held = order(
         lambda x: jnp.concatenate([x] + [attn_all[mask] for mask in masks[1:]]), attn_all[0]
     )
     held_c = lay.move(held, c=1)
+    grad_up_weight = place_all(*up_all, True)
     at = [lay.place_of(p ^ mask, orders[0]) for mask in masks]
     at = [c * n_p + x for x in at] + [(1 - c) * n_p + x for x in at]
     attn_all = ([held, held_c], jnp.stack(at).astype(jnp.int32))

time: 838 us -> 811 us (0.968)
  waiting for transfers between devices: 156 us -> 136 us
    ppermute x62, waiting for transfers between devices: 156 us -> 136 us  [move(): return lax.ppermute(x, ('dp', 'tensor'), pairs)]
    unnamed x143 -> x131, local copies, waits for them, and re-layouts: 33.5 us -> 33.1 us
  transfers between devices with their start and end apart: 62 -> 62, of which waited for: 24 -> 22; matrix products, arithmetic and copies ran while one was open for 16% -> 16% of each run, Pallas kernels for 52% -> 52%
where the time goes in v4:
time: 811 us; the launch traced here: 801 us
  Pallas kernels  451 us (56%)
  waiting for transfers between devices  136 us (17%)
  local copies, waits for them, and re-layouts  102 us (13%)
  starting transfers between devices  64.4 us (8%)
  other arithmetic  46.5 us (6%)
    pallas_call x34, Pallas kernels, call(): pl.pallas_call(kernel, in_specs=in_specs or [vmem] * len(ins), out_specs=...  383 us
    ppermute x62, waiting for transfers between devices, move(): return lax.ppermute(x, ('dp', 'tensor'), pairs)  136 us
    pallas_call x4, Pallas kernels, wgrad(): pl.pallas_call(functools.partial(wgrad_kernel, len(left), len(right)), gr...  67.9 us
    ppermute x62, starting transfers between devices, move(): return lax.ppermute(x, ('dp', 'tensor'), pairs)  64.4 us
    unnamed x131, local copies, waits for them, and re-layouts  33.1 us
    convert_element_type x11, other arithmetic, join(): return total.astype(BF)  29.9 us
    dynamic_update_slice x16, local copies, waits for them, and re-layouts, put(): return lax.dynamic_update_slice_in_dim(buf, x, at, axis)  17.9 us
  transfers between devices with their start and end apart: 62, of which 22 were waited for; matrix products, arithmetic and copies ran while one was open for 16% of the time, Pallas kernels for 52%

profile of v4, /device:TPU:0, one launch (start us, length us, event | category | flops | bytes accessed | tf_op | source)
XLA Modules:
  0.0 801.2 jit_solution(17689871590445743025)
XLA Ops:
  3.2 2.8 copy.32.img_ref
  6.1 5.6 pack.2
  21.5 5.5 pad_maximum_fusion.w_ref
  27.8 8.6 %attend_fwd.8 = (bf16[528,624]{1,0:T(8,128)(2,1)}, bf16[528,208]{1,0:T(8,128)(2,1)}, f32[8,512]{1,0:T(8,128)}, f32[8,128]{1,0:T(8,128)}, bf16[528,1664]{1,0:T(8,128)(2,1)}) custom-call(bf16[528,1664]{1,0:T(8,128)(2,1)} %get-tuple-element.226.n_ref.refs_8_, bf16[832,1664]{1,0:T(8,128)(2,1)} %pad_maximum_fusion.w_ref, f32[1,624]{1,0:T(1,128)} %reshape.174.b_ref), custom_call_target="tpu_custom_call" | custom-call | flops 47130869760 | bytes 215544960 | tf_op jit(solution)/shard_map/attend_fwd/pallas_call | solution.py:197
  39.4 8.7 %attend_fwd.9 = (bf16[528,624]{1,0:T(8,128)(2,1)}, bf16[528,208]{1,0:T(8,128)(2,1)}, f32[8,512]{1,0:T(8,128)}, f32[8,128]{1,0:T(8,128)}, bf16[528,1664]{1,0:T(8,128)(2,1)}) custom-call(bf16[528,1664]{1,0:T(8,128)(2,1)} %collective-permute-done.1.n_ref.refs_9_, bf16[832,1664]{1,0:T(8,128)(2,1)} %pad_maximum_fusion.w_ref, f32[1,624]{1,0:T(1,128)} %reshape.174.b_ref), custom_call_target="tpu_custom_call" | custom-call | flops 47130869760 | bytes 215544960 | tf_op jit(solution)/shard_map/attend_fwd/pallas_call | solution.py:197
  49.5 3.0 pack.3
  52.5 15.6 %collective-permute-done.2 = bf16[208,1664]{1,0:T(8,128)(2,1)S(1)} collective-permute-done((bf16[208,1664]{1,0:T(8,128)(2,1)S(1)}, bf16[208,1664]{1,0:T(8,128)(2,1)S(1)}, u32[]{:S(2)}, u32[]{:S(2)}) %collective-permute-start.2) | collective-permute-done | bytes 692256 | tf_op jit(solution)/shard_map/ppermute | solution.py:660
  69.0 8.8 %attend_fwd.10 = (bf16[528,624]{1,0:T(8,128)(2,1)}, bf16[528,208]{1,0:T(8,128)(2,1)}, f32[8,512]{1,0:T(8,128)}, f32[8,128]{1,0:T(8,128)}, bf16[528,1664]{1,0:T(8,128)(2,1)}) custom-call(bf16[528,1664]{1,0:T(8,128)(2,1)} %collective-permute-done.n_ref.refs_10_, bf16[832,1664]{1,0:T(8,128)(2,1)} %pad_maximum_fusion.w_ref, f32[1,624]{1,0:T(1,128)} %reshape.174.b_ref), custom_call_target="tpu_custom_call" | custom-call | flops 47130869760 | bytes 215544960 | tf_op jit(solution)/shard_map/attend_fwd/pallas_call | solution.py:197
  82.6 8.6 %attend_fwd.11 = (bf16[528,624]{1,0:T(8,128)(2,1)}, bf16[528,208]{1,0:T(8,128)(2,1)}, f32[8,512]{1,0:T(8,128)}, f32[8,128]{1,0:T(8,128)}, bf16[528,1664]{1,0:T(8,128)(2,1)}) custom-call(bf16[528,1664]{1,0:T(8,128)(2,1)} %copy-done.51, bf16[832,1664]{1,0:T(8,128)(2,1)} %pad_maximum_fusion.w_ref, f32[1,624]{1,0:T(1,128)} %reshape.174.b_ref), custom_call_target="tpu_custom_call" | custom-call | flops 47130869760 | bytes 215544960 | tf_op jit(solution)/shard_map/attend_fwd/pallas_call | solution.py:197
  100.1 12.1 %collective-permute-done.6 = bf16[208,1664]{1,0:T(8,128)(2,1)} collective-permute-done((bf16[208,1664]{1,0:T(8,128)(2,1)S(1)}, bf16[208,1664]{1,0:T(8,128)(2,1)}, u32[]{:S(2)}, u32[]{:S(2)}) %collective-permute-start.6) | collective-permute-done | bytes 692256 | tf_op jit(solution)/shard_map/ppermute | solution.py:660
  119.0 9.1 %attend_fwd.12 = (bf16[528,624]{1,0:T(8,128)(2,1)}, bf16[528,208]{1,0:T(8,128)(2,1)}, f32[8,512]{1,0:T(8,128)}, f32[8,128]{1,0:T(8,128)}, bf16[528,1664]{1,0:T(8,128)(2,1)}) custom-call(bf16[528,1664]{1,0:T(8,128)(2,1)} %copy-done.51, bf16[832,1664]{1,0:T(8,128)(2,1)} %copy-done.12, f32[1,624]{1,0:T(1,128)} %reshape.176.b_ref, ...), custom_call_target="tpu_custom_call" | custom-call | flops 47130869760 | bytes 268260480 | tf_op jit(solution)/shard_map/attend_fwd/pallas_call | solution.py:197
  128.2 9.1 %attend_fwd.13 = (bf16[528,624]{1,0:T(8,128)(2,1)}, bf16[528,208]{1,0:T(8,128)(2,1)}, f32[8,512]{1,0:T(8,128)}, f32[8,128]{1,0:T(8,128)}, bf16[528,1664]{1,0:T(8,128)(2,1)}) custom-call(bf16[528,1664]{1,0:T(8,128)(2,1)} %collective-permute-done.1.n_ref.refs_9_, bf16[832,1664]{1,0:T(8,128)(2,1)} %copy-done.12, f32[1,624]{1,0:T(1,128)} %reshape.176.b_ref, ...), custom_call_target="tpu_custom_call" | custom-call | flops 47130869760 | bytes 268260480 | tf_op jit(solution)/shard_map/attend_fwd/pallas_call | solution.py:197
  139.0 10.1 %attend_fwd.14 = (bf16[528,624]{1,0:T(8,128)(2,1)}, bf16[528,208]{1,0:T(8,128)(2,1)}, f32[8,512]{1,0:T(8,128)}, f32[8,128]{1,0:T(8,128)}, bf16[528,1664]{1,0:T(8,128)(2,1)}) custom-call(bf16[528,1664]{1,0:T(8,128)(2,1)} %collective-permute-done.n_ref.refs_10_, bf16[832,1664]{1,0:T(8,128)(2,1)} %copy-done.12, f32[1,624]{1,0:T(1,128)} %reshape.176.b_ref, ...), custom_call_target="tpu_custom_call" | custom-call | flops 47130869760 | bytes 320976000 | tf_op jit(solution)/shard_map/attend_fwd/pallas_call | solution.py:197
  151.5 11.4 %collective-permute-done.12.c0.refs_4_ = bf16[528,1664]{1,0:T(8,128)(2,1)} collective-permute-done((bf16[528,1664]{1,0:T(8,128)(2,1)}, bf16[528,1664]{1,0:T(8,128)(2,1)}, u32[]{:S(2)}, u32[]{:S(2)}) %collective-permute-start.12) | collective-permute-done | bytes 1757216 | tf_op jit(solution)/shard_map/ppermute | solution.py:660
  163.0 9.7 %attend_fwd.15 = (bf16[528,624]{1,0:T(8,128)(2,1)}, bf16[528,208]{1,0:T(8,128)(2,1)}, f32[8,512]{1,0:T(8,128)}, f32[8,128]{1,0:T(8,128)}, bf16[528,1664]{1,0:T(8,128)(2,1)}) custom-call(bf16[528,1664]{1,0:T(8,128)(2,1)} %get-tuple-element.226.n_ref.refs_8_, bf16[832,1664]{1,0:T(8,128)(2,1)} %copy-done.12, f32[1,624]{1,0:T(1,128)} %reshape.176.b_ref, ...), custom_call_target="tpu_custom_call" | custom-call | flops 47130869760 | bytes 268260480 | tf_op jit(solution)/shard_map/attend_fwd/pallas_call | solution.py:197
  172.7 9.9 %collective-permute-start.14 = (bf16[1664,256]{1,0:T(8,128)(2,1)}, bf16[1664,256]{1,0:T(8,128)(2,1)S(1)}, u32[]{:S(2)}, u32[]{:S(2)}) collective-permute-start(bf16[1664,256]{1,0:T(8,128)(2,1)} %collective-permute-done.13), channel_id=1, source_target_pairs={{0,8},{1,9},{2,10},{3,11},{4,12},{5,13},{6,14},{7,15},{8,0},{9,1},... | collective-permute-start | bytes 2555912 | tf_op jit(solution)/shard_map/ppermute | solution.py:660
  182.5 4.0 constant_dynamic-slice_fusion.9.up_ref
  187.3 2.7 collective-permute-start.15
  190.0 4.0 constant_dynamic-slice_fusion.8.down_ref.refs_0_
  196.2 5.6 collective-permute-done.14
  204.9 2.9 collective-permute-done.15
  208.8 2.7 collective-permute-done.17.c_ref
  212.7 8.6 %norm_second.1 = (f32[528,1664]{1,0:T(8,128)}, bf16[528,1664]{1,0:T(8,128)(2,1)}) custom-call(bf16[528,1664]{1,0:T(8,128)(2,1)} %get-tuple-element.354.x_ref, bf16[528,1664]{1,0:T(8,128)(2,1)} %get-tuple-element.227.a_ref, bf16[528,1664]{1,0:T(8,128)(2,1)} %copy-done.14, bf16[528,1664]{1,0:T(8,128)(2,1)} %copy-done.16, f32[1,1664]{1,0:T(1,128)} %reshape.177.bias_ref, ...), custom_call_target="tpu_custom_call" | custom-call | bytes 369607680 | tf_op jit(solution)/shard_map/norm_second/pallas_call | solution.py:197
  232.7 21.2 %mlp.4 = (bf16[1056,2048]{1,0:T(8,128)(2,1)}, bf16[1056,2048]{1,0:T(8,128)(2,1)}, bf16[528,1664]{1,0:T(8,128)(2,1)}, bf16[528,1664]{1,0:T(8,128)(2,1)}, f32[1,1024]{1,0:T(1,128)}) custom-call(bf16[528,1664]{1,0:T(8,128)(2,1)} %get-tuple-element.240.n0.refs_2_, bf16[528,1664]{1,0:T(8,128)(2,1)} %copy-done.52, ...), custom_call_target="tpu_custom_call" | custom-call | flops 323884154880 | bytes 780533760 | tf_op jit(solution)/shard_map/mlp/pallas_call | solution.py:197
  256.9 9.8 %collective-permute-done.19 = bf16[1664,512]{1,0:T(8,128)(2,1)} collective-permute-done((bf16[1664,512]{1,0:T(8,128)(2,1)}, bf16[1664,512]{1,0:T(8,128)(2,1)}, u32[]{:S(2)}, u32[]{:S(2)}) %collective-permute-start.19) | collective-permute-done | bytes 1703968 | tf_op jit(solution)/shard_map/ppermute | solution.py:660
  277.0 22.6 %mlp.5 = (bf16[1056,2048]{1,0:T(8,128)(2,1)}, bf16[1056,2048]{1,0:T(8,128)(2,1)}, bf16[528,1664]{1,0:T(8,128)(2,1)}, bf16[528,1664]{1,0:T(8,128)(2,1)}, f32[1,1024]{1,0:T(1,128)}) custom-call(bf16[528,1664]{1,0:T(8,128)(2,1)} %get-tuple-element.240.n0.refs_2_, bf16[528,1664]{1,0:T(8,128)(2,1)} %copy-done.52, ...), custom_call_target="tpu_custom_call", output_to_operand_aliasing={{0}: (9, {}), {1}: (10, {})} | custom-call | flops 323884154880 | bytes 1145487360 | tf_op jit(solution)/shard_map/mlp/pallas_call | solution.py:197
  299.7 13.5 %row_product.2 = (bf16[528,1664]{1,0:T(8,128)(2,1)}, bf16[528,1664]{1,0:T(8,128)(2,1)}) custom-call(bf16[1056,2048]{1,0:T(8,128)(2,1)} %get-tuple-element.267.act_ref.refs_0_, bf16[1024,1664]{1,0:T(8,128)(2,1)} %constant_dynamic-slice_fusion.8.down_ref.refs_0_, bf16[1024,1664]{1,0:T(8,128)(2,1)} %copy-done.4), custom_call_target="tpu_custom_call" | custom-call | flops 215922769920 | bytes 439664640 | tf_op jit(solution)/shard_map/row_product/pallas_call | solution.py:197
  313.7 21.1 %mlp.6 = (bf16[1056,2048]{1,0:T(8,128)(2,1)}, bf16[1056,2048]{1,0:T(8,128)(2,1)}, bf16[528,1664]{1,0:T(8,128)(2,1)}, bf16[528,1664]{1,0:T(8,128)(2,1)}, f32[1,1024]{1,0:T(1,128)}) custom-call(bf16[528,1664]{1,0:T(8,128)(2,1)} %collective-permute-done.21.n0.refs_4_, bf16[528,1664]{1,0:T(8,128)(2,1)} %collective-permute-done.22.n1.refs_5_, ...), custom_call_target="tpu_custom_call" | custom-call | flops 323884154880 | bytes 780533760 | tf_op jit(solution)/shard_map/mlp/pallas_call | solution.py:197
  334.8 22.8 %mlp.7 = (bf16[1056,2048]{1,0:T(8,128)(2,1)}, bf16[1056,2048]{1,0:T(8,128)(2,1)}, bf16[528,1664]{1,0:T(8,128)(2,1)}, bf16[528,1664]{1,0:T(8,128)(2,1)}, f32[1,1024]{1,0:T(1,128)}) custom-call(bf16[528,1664]{1,0:T(8,128)(2,1)} %collective-permute-done.21.n0.refs_4_, ...), custom_call_target="tpu_custom_call", output_to_operand_aliasing={{0}: (9, {}), {1}: (10, {})} | custom-call | flops 323884154880 | bytes 1145487360 | tf_op jit(solution)/shard_map/mlp/pallas_call | solution.py:197
  358.1 17.0 %wgrad.4 = bf16[1024,1664]{1,0:T(8,128)(2,1)} custom-call(s32[2]{0:T(128)} %pad_add_fusion.3.index_ref, bf16[1056,2048]{1,0:T(8,128)(2,1)} %get-tuple-element.267.act_ref.refs_0_, bf16[1056,2048]{1,0:T(8,128)(2,1)} %get-tuple-element.271.refs_1_.act_ref, bf16[528,1664]{1,0:T(8,128)(2,1)} %get-tuple-element.219.c0.refs_2_.add_ref, ...), custom_call_target="tpu_custom_call" | custom-call | flops 215922769920 | bytes 442859520 | tf_op jit(solution)/shard_map/wgrad/pallas_call | solution.py:493
  380.3 3.1 add_convert_fusion.1
  385.2 16.9 %wgrad.5 = bf16[1024,1664]{1,0:T(8,128)(2,1)} custom-call(s32[2]{0:T(128)} %pad_add_fusion.2.index_ref, bf16[1056,2048]{1,0:T(8,128)(2,1)} %get-tuple-element.273.refs_0_, bf16[1056,2048]{1,0:T(8,128)(2,1)} %get-tuple-element.266.refs_1_, bf16[528,1664]{1,0:T(8,128)(2,1)} %get-tuple-element.240.n0.refs_2_, bf16[528,1664]{1,0:T(8,128)(2,1)} %copy-done.52, ...), custom_call_target="tpu_custom_call" | custom-call | flops 215922769920 | bytes 442859520 | tf_op jit(solution)/shard_map/wgrad/pallas_call | solution.py:493
  403.6 16.9 %wgrad.6 = bf16[1024,1664]{1,0:T(8,128)(2,1)} custom-call(s32[2]{0:T(128)} %pad_add_fusion.1.index_ref, bf16[1056,2048]{1,0:T(8,128)(2,1)} %get-tuple-element.267.act_ref.refs_0_, bf16[1056,2048]{1,0:T(8,128)(2,1)} %get-tuple-element.271.refs_1_.act_ref, bf16[528,1664]{1,0:T(8,128)(2,1)} %get-tuple-element.219.c0.refs_2_.add_ref, ...), custom_call_target="tpu_custom_call" | custom-call | flops 215922769920 | bytes 442859520 | tf_op jit(solution)/shard_map/wgrad/pallas_call | solution.py:493
  420.4 3.3 collective-permute-done.26.c_ref
  423.8 10.9 %norm_back.2 = (f32[528,1664]{1,0:T(8,128)}, bf16[528,1664]{1,0:T(8,128)(2,1)}, f32[8,1664]{1,0:T(8,128)}, f32[8,1664]{1,0:T(8,128)}, f32[8,1664]{1,0:T(8,128)}) custom-call(f32[528,1664]{1,0:T(8,128)} %get-tuple-element.312.x_ref.refs_0_, bf16[528,1664]{1,0:T(8,128)(2,1)} %get-tuple-element.269.a_ref, bf16[528,1664]{1,0:T(8,128)(2,1)} %collective-permute-done.23.b_ref, ...), custom_call_target="tpu_custom_call" | custom-call | bytes 479431680 | tf_op jit(solution)/shard_map/norm_back/pallas_call | solution.py:197
  434.7 13.4 %row_product.3 = (bf16[528,1664]{1,0:T(8,128)(2,1)}, bf16[528,1664]{1,0:T(8,128)(2,1)}) custom-call(bf16[1056,2048]{1,0:T(8,128)(2,1)} %get-tuple-element.271.refs_1_.act_ref, bf16[1024,1664]{1,0:T(8,128)(2,1)} %constant_dynamic-slice_fusion.8.down_ref.refs_0_, bf16[1024,1664]{1,0:T(8,128)(2,1)} %copy-done.4), custom_call_target="tpu_custom_call" | custom-call | flops 215922769920 | bytes 439664640 | tf_op jit(solution)/shard_map/row_product/pallas_call | solution.py:197
  450.3 17.1 %wgrad.7 = bf16[1024,1664]{1,0:T(8,128)(2,1)} custom-call(s32[2]{0:T(128)} %pad_add_fusion.index_ref, bf16[1056,2048]{1,0:T(8,128)(2,1)} %get-tuple-element.273.refs_0_, bf16[1056,2048]{1,0:T(8,128)(2,1)} %get-tuple-element.266.refs_1_, bf16[528,1664]{1,0:T(8,128)(2,1)} %get-tuple-element.240.n0.refs_2_, bf16[528,1664]{1,0:T(8,128)(2,1)} %copy-done.52, ...), custom_call_target="tpu_custom_call" | custom-call | flops 215922769920 | bytes 442859520 | tf_op jit(solution)/shard_map/wgrad/pallas_call | solution.py:493
  467.4 4.6 add_convert_fusion.5
  473.4 10.0 %attend_bwd.8 = (bf16[528,624]{1,0:T(8,128)(2,1)}, f32[1,624]{1,0:T(1,128)}, bf16[528,1664]{1,0:T(8,128)(2,1)}) custom-call(bf16[528,1664]{1,0:T(8,128)(2,1)} %get-tuple-element.332.g_ref.refs_12_, bf16[528,624]{1,0:T(8,128)(2,1)} %get-tuple-element.277.qkv_ref, f32[8,512]{1,0:T(8,128)} %get-tuple-element.278.lse_ref, f32[8,128]{1,0:T(8,128)} %get-tuple-element.279.lset_ref, ...), custom_call_target="tpu_custom_call" | custom-call | flops 52038205440 | bytes 228723840 | tf_op jit(solution)/shard_map/attend_bwd/pallas_call | solution.py:197
  485.3 9.7 %attend_bwd.9 = (bf16[528,624]{1,0:T(8,128)(2,1)}, f32[1,624]{1,0:T(1,128)}, bf16[528,1664]{1,0:T(8,128)(2,1)}) custom-call(bf16[528,1664]{1,0:T(8,128)(2,1)} %collective-permute-done.31.g_ref.refs_13_, bf16[528,624]{1,0:T(8,128)(2,1)} %get-tuple-element.285.qkv_ref, f32[8,512]{1,0:T(8,128)} %get-tuple-element.286.lse_ref, ...), custom_call_target="tpu_custom_call" | custom-call | flops 52038205440 | bytes 228723840 | tf_op jit(solution)/shard_map/attend_bwd/pallas_call | solution.py:197
  495.0 4.7 add_convert_fusion.7
  500.2 3.1 add_convert_fusion
  503.7 9.8 %attend_bwd.10 = (bf16[528,624]{1,0:T(8,128)(2,1)}, f32[1,624]{1,0:T(1,128)}, bf16[528,1664]{1,0:T(8,128)(2,1)}) custom-call(bf16[528,1664]{1,0:T(8,128)(2,1)} %collective-permute-done.29.g_ref.refs_14_, bf16[528,624]{1,0:T(8,128)(2,1)} %get-tuple-element.292.qkv_ref, f32[8,512]{1,0:T(8,128)} %get-tuple-element.293.lse_ref, ...), custom_call_target="tpu_custom_call" | custom-call | flops 52038205440 | bytes 228723840 | tf_op jit(solution)/shard_map/attend_bwd/pallas_call | solution.py:197
  520.2 9.8 %attend_bwd.11 = (bf16[528,624]{1,0:T(8,128)(2,1)}, f32[1,624]{1,0:T(1,128)}, bf16[528,1664]{1,0:T(8,128)(2,1)}) custom-call(bf16[528,1664]{1,0:T(8,128)(2,1)} %copy-done.53, bf16[528,624]{1,0:T(8,128)(2,1)} %get-tuple-element.298.qkv_ref, f32[8,512]{1,0:T(8,128)} %get-tuple-element.299.lse_ref, f32[8,128]{1,0:T(8,128)} %get-tuple-element.300.lset_ref, ...), custom_call_target="tpu_custom_call" | custom-call | flops 52038205440 | bytes 228723840 | tf_op jit(solution)/shard_map/attend_bwd/pallas_call | solution.py:197
  530.0 20.1 %attend_wgrad.2 = bf16[832,1664]{1,0:T(8,128)(2,1)} custom-call(bf16[528,624]{1,0:T(8,128)(2,1)} %get-tuple-element.302.refs_0_, bf16[528,624]{1,0:T(8,128)(2,1)} %get-tuple-element.303.refs_1_, bf16[528,624]{1,0:T(8,128)(2,1)} %get-tuple-element.304.refs_2_, bf16[528,624]{1,0:T(8,128)(2,1)} %get-tuple-element.305.refs_3_, ...), custom_call_target="tpu_custom_call" | custom-call | flops 175437250560 | bytes 610222080 | tf_op jit(solution)/shard_map/attend_wgrad/pallas_call | solution.py:197
  555.6 5.8 collective-permute-done.35.refs_3_
  561.3 5.8 unpack.2
  567.2 10.7 %attend_bwd.12 = (bf16[528,624]{1,0:T(8,128)(2,1)}, f32[1,624]{1,0:T(1,128)}, bf16[528,1664]{1,0:T(8,128)(2,1)}) custom-call(bf16[528,1664]{1,0:T(8,128)(2,1)} %copy-done.53, bf16[528,624]{1,0:T(8,128)(2,1)} %get-tuple-element.315.qkv_ref, f32[8,512]{1,0:T(8,128)} %get-tuple-element.316.lse_ref, f32[8,128]{1,0:T(8,128)} %get-tuple-element.317.lset_ref, ...), custom_call_target="tpu_custom_call" | custom-call | flops 52038205440 | bytes 281439360 | tf_op jit(solution)/shard_map/attend_bwd/pallas_call | solution.py:197
  579.8 10.2 %attend_bwd.13 = (bf16[528,624]{1,0:T(8,128)(2,1)}, f32[1,624]{1,0:T(1,128)}, bf16[528,1664]{1,0:T(8,128)(2,1)}) custom-call(bf16[528,1664]{1,0:T(8,128)(2,1)} %collective-permute-done.31.g_ref.refs_13_, bf16[528,624]{1,0:T(8,128)(2,1)} %get-tuple-element.321.qkv_ref, f32[8,512]{1,0:T(8,128)} %get-tuple-element.322.lse_ref, ...), custom_call_target="tpu_custom_call" | custom-call | flops 52038205440 | bytes 281439360 | tf_op jit(solution)/shard_map/attend_bwd/pallas_call | solution.py:197
  592.8 7.8 collective-permute-done.38
  603.1 10.7 %attend_bwd.14 = (bf16[528,624]{1,0:T(8,128)(2,1)}, f32[1,624]{1,0:T(1,128)}, bf16[528,1664]{1,0:T(8,128)(2,1)}) custom-call(bf16[528,1664]{1,0:T(8,128)(2,1)} %collective-permute-done.29.g_ref.refs_14_, bf16[528,624]{1,0:T(8,128)(2,1)} %get-tuple-element.327.qkv_ref, f32[8,512]{1,0:T(8,128)} %get-tuple-element.328.lse_ref, ...), custom_call_target="tpu_custom_call" | custom-call | flops 52038205440 | bytes 334154880 | tf_op jit(solution)/shard_map/attend_bwd/pallas_call | solution.py:197
  613.8 2.8 fusion
  617.2 10.3 %attend_bwd.15 = (bf16[528,624]{1,0:T(8,128)(2,1)}, f32[1,624]{1,0:T(1,128)}, bf16[528,1664]{1,0:T(8,128)(2,1)}) custom-call(bf16[528,1664]{1,0:T(8,128)(2,1)} %get-tuple-element.332.g_ref.refs_12_, bf16[528,624]{1,0:T(8,128)(2,1)} %get-tuple-element.333.qkv_ref, f32[8,512]{1,0:T(8,128)} %get-tuple-element.334.lse_ref, ...), custom_call_target="tpu_custom_call" | custom-call | flops 52038205440 | bytes 281439360 | tf_op jit(solution)/shard_map/attend_bwd/pallas_call | solution.py:197
  642.0 2.8 constant_dynamic-update-slice_fusion.6.refs_0_
  644.8 20.1 %attend_wgrad.3 = bf16[832,1664]{1,0:T(8,128)(2,1)} custom-call(bf16[528,624]{1,0:T(8,128)(2,1)} %get-tuple-element.341.refs_0_, bf16[528,624]{1,0:T(8,128)(2,1)} %get-tuple-element.342.refs_1_, bf16[528,624]{1,0:T(8,128)(2,1)} %get-tuple-element.343.refs_2_, bf16[528,624]{1,0:T(8,128)(2,1)} %get-tuple-element.344.refs_3_, ...), custom_call_target="tpu_custom_call" | custom-call | flops 175437250560 | bytes 610222080 | tf_op jit(solution)/shard_map/attend_wgrad/pallas_call | solution.py:197
  676.5 9.0 %place.2 = f32[2048,1664]{1,0:T(8,128)} custom-call(s32[8]{0:T(128)} %stack.131.at_ref, bf16[1024,1664]{1,0:T(8,128)(2,1)} %constant_dynamic-update-slice_fusion.6.refs_0_, bf16[1024,1664]{1,0:T(8,128)(2,1)} %collective-permute-done.45.refs_1_), custom_call_target="tpu_custom_call" | custom-call | bytes 613417920 | tf_op jit(solution)/shard_map/place/pallas_call | solution.py:197
  686.1 9.8 %norm_back.3 = (f32[8,1664]{1,0:T(8,128)}, bf16[528,1664]{1,0:T(8,128)(2,1)}, f32[8,1664]{1,0:T(8,128)}, f32[8,1664]{1,0:T(8,128)}, f32[8,1664]{1,0:T(8,128)}) custom-call(bf16[528,1664]{1,0:T(8,128)(2,1)} %get-tuple-element.354.x_ref, bf16[528,1664]{1,0:T(8,128)(2,1)} %get-tuple-element.336.a_ref, bf16[528,1664]{1,0:T(8,128)(2,1)} %collective-permute-done.40.b_ref, ...), custom_call_target="tpu_custom_call" | custom-call | bytes 375598080 | tf_op jit(solution)/shard_map/norm_back/pallas_call | solution.py:197
  698.6 4.6 collective-permute-done.48
  705.8 2.8 unpack.3
  718.6 21.4 %collective-permute-done.53 = bf16[512,1664]{1,0:T(8,128)(2,1)S(1)} collective-permute-done((bf16[512,1664]{1,0:T(8,128)(2,1)}, bf16[512,1664]{1,0:T(8,128)(2,1)S(1)}, u32[]{:S(2)}, u32[]{:S(2)}) %collective-permute-start.53) | collective-permute-done | bytes 1703968 | tf_op jit(solution)/shard_map/ppermute | solution.py:660
  742.3 12.6 %collective-permute-done.55 = bf16[208,1664]{1,0:T(8,128)(2,1)S(1)} collective-permute-done((bf16[208,1664]{1,0:T(8,128)(2,1)S(1)}, bf16[208,1664]{1,0:T(8,128)(2,1)S(1)}, u32[]{:S(2)}, u32[]{:S(2)}) %collective-permute-start.55) | collective-permute-done | bytes 692256 | tf_op jit(solution)/shard_map/ppermute | solution.py:660
  756.7 12.6 %collective-permute-done.57 = bf16[208,1664]{1,0:T(8,128)(2,1)S(1)} collective-permute-done((bf16[208,1664]{1,0:T(8,128)(2,1)S(1)}, bf16[208,1664]{1,0:T(8,128)(2,1)S(1)}, u32[]{:S(2)}, u32[]{:S(2)}) %collective-permute-start.57) | collective-permute-done | bytes 692256 | tf_op jit(solution)/shard_map/ppermute | solution.py:660
  771.4 10.8 %place.3 = f32[1664,2048]{1,0:T(8,128)} custom-call(s32[8]{0:T(128)} %stack.142.at_ref, bf16[1024,1664]{1,0:T(8,128)(2,1)} %constant_dynamic-update-slice_fusion.12.refs_0_, bf16[1024,1664]{1,0:T(8,128)(2,1)} %collective-permute-done.58.refs_1_), custom_call_target="tpu_custom_call" | custom-call | bytes 613417920 | tf_op jit(solution)/shard_map/place/pallas_call | solution.py:197
  790.1 7.9 place_heads.1
  (339 shorter events, 170.4 us)
Async XLA Ops:
  11.7 27.7 %collective-permute-start.1 = (bf16[528,1664]{1,0:T(8,128)(2,1)}, bf16[528,1664]{1,0:T(8,128)(2,1)}, u32[]{:S(2)}, u32[]{:S(2)}) collective-permute-start(bf16[528,1664]{1,0:T(8,128)(2,1)} %get-tuple-element.226.n_ref.refs_8_), channel_id=1, source_target_pairs={{0,4},{1,5},{2,6},{3,7},{4,0},{5,1},{6,2},{7,3},{8,12},{9,13},{10,... | collective-permute-start | bytes 5271560 | tf_op jit(solution)/shard_map/ppermute | solution.py:660
  12.1 56.9 %collective-permute-start = (bf16[528,1664]{1,0:T(8,128)(2,1)}, bf16[528,1664]{1,0:T(8,128)(2,1)}, u32[]{:S(2)}, u32[]{:S(2)}) collective-permute-start(bf16[528,1664]{1,0:T(8,128)(2,1)} %get-tuple-element.226.n_ref.refs_8_), channel_id=1, source_target_pairs={{0,1},{1,0},{2,3},{3,2},{4,5},{5,4},{6,7},{7,6},{8,9},{9,8},{10,11... | collective-permute-start | bytes 5271560 | tf_op jit(solution)/shard_map/ppermute | solution.py:660
  16.1 52.0 %collective-permute-start.2 = (bf16[208,1664]{1,0:T(8,128)(2,1)S(1)}, bf16[208,1664]{1,0:T(8,128)(2,1)S(1)}, u32[]{:S(2)}, u32[]{:S(2)}) collective-permute-start(bf16[208,1664]{1,0:T(8,128)(2,1)S(1)} %get-tuple-element.394), channel_id=1, source_target_pairs={{0,2},{1,3},{2,0},{3,1},{4,6},{5,7},{6,4},{7,5},{8,10},{9,11},{10,... | collective-permute-start | bytes 2076680 | tf_op jit(solution)/shard_map/ppermute | solution.py:660
  37.2 80.3 %collective-permute-start.8 = (f32[1440]{0:T(1024)}, f32[1440]{0:T(1024)}, u32[]{:S(2)}, u32[]{:S(2)}) collective-permute-start(f32[1440]{0:T(1024)} %pad_maximum_fusion.1), channel_id=1, source_target_pairs={{0,2},{1,3},{2,0},{3,1},{4,6},{5,7},{6,4},{7,5},{8,10},{9,11},{10,... | collective-permute-start | bytes 17288 | tf_op jit(solution)/shard_map/ppermute | solution.py:660
  69.0 12.3 %collective-permute-start.3 = (bf16[528,1664]{1,0:T(8,128)(2,1)}, bf16[528,1664]{1,0:T(8,128)(2,1)S(1)}, u32[]{:S(2)}, u32[]{:S(2)}) collective-permute-start(bf16[528,1664]{1,0:T(8,128)(2,1)} %collective-permute-done.n_ref.refs_10_), channel_id=1, source_target_pairs={{0,4},{1,5},{2,6},{3,7},{4,0},{5,1},{6,2},{7,3},{8,12},{9,13},{10,... | collective-permute-start | bytes 5271560 | tf_op jit(solution)/shard_map/ppermute | solution.py:660
  77.9 18.4 %collective-permute-start.5 = (bf16[208,1664]{1,0:T(8,128)(2,1)S(1)}, bf16[208,1664]{1,0:T(8,128)(2,1)}, u32[]{:S(2)}, u32[]{:S(2)}) collective-permute-start(bf16[208,1664]{1,0:T(8,128)(2,1)S(1)} %collective-permute-done.2), channel_id=1, source_target_pairs={{0,8},{1,9},{2,10},{3,11},{4,12},{5,13},{6,14},{7,15},{8,0},{9,1},... | collective-permute-start | bytes 2076680 | tf_op jit(solution)/shard_map/ppermute | solution.py:660
  79.5 32.6 %collective-permute-start.6 = (bf16[208,1664]{1,0:T(8,128)(2,1)S(1)}, bf16[208,1664]{1,0:T(8,128)(2,1)}, u32[]{:S(2)}, u32[]{:S(2)}) collective-permute-start(bf16[208,1664]{1,0:T(8,128)(2,1)S(1)} %collective-permute-done.2), channel_id=1, source_target_pairs={{0,16},{1,17},{2,18},{3,19},{4,20},{5,21},{6,22},{7,23},{8,24},{9,... | collective-permute-start | bytes 2076680 | tf_op jit(solution)/shard_map/ppermute | solution.py:660
  81.1 34.5 %collective-permute-start.7 = (bf16[208,1664]{1,0:T(8,128)(2,1)S(1)}, bf16[208,1664]{1,0:T(8,128)(2,1)}, u32[]{:S(2)}, u32[]{:S(2)}) collective-permute-start(bf16[208,1664]{1,0:T(8,128)(2,1)S(1)} %collective-permute-done.2), channel_id=1, source_target_pairs={{0,24},{1,25},{2,26},{3,27},{4,28},{5,29},{6,30},{7,31},{8,16},{9,... | collective-permute-start | bytes 2076680 | tf_op jit(solution)/shard_map/ppermute | solution.py:660
  81.4 46.8 %collective-permute-start.9 = (bf16[528,1664]{1,0:T(8,128)(2,1)}, bf16[528,1664]{1,0:T(8,128)(2,1)}, u32[]{:S(2)}, u32[]{:S(2)}) collective-permute-start(bf16[528,1664]{1,0:T(8,128)(2,1)} %get-tuple-element.219.c0.refs_2_.add_ref), channel_id=1, source_target_pairs={{0,4},{1,5},{2,6},{3,7},{4,0},{5,1},{6,2},{7,3},{8,12},{9,13},{10,... | collective-permute-start | bytes 5271560 | tf_op jit(solution)/shard_map/ppermute | solution.py:660
  96.2 22.1 %copy-start.41 = (f32[208]{0:T(256)S(1)}, f32[208]{0:T(256)}, u32[]{:S(2)}) copy-start(f32[208]{0:T(256)} %copy-done.40) | copy-start | bytes 2500
  96.3 66.6 %collective-permute-start.12 = (bf16[528,1664]{1,0:T(8,128)(2,1)}, bf16[528,1664]{1,0:T(8,128)(2,1)}, u32[]{:S(2)}, u32[]{:S(2)}) collective-permute-start(bf16[528,1664]{1,0:T(8,128)(2,1)} %get-tuple-element.219.c0.refs_2_.add_ref), channel_id=1, source_target_pairs={{0,1},{1,0},{2,3},{3,2},{4,5},{5,4},{6,7},{7,6},{8,9},{9,8},{10,11... | collective-permute-start | bytes 5271560 | tf_op jit(solution)/shard_map/ppermute | solution.py:660
  112.1 50.8 %collective-permute-start.13 = (bf16[1664,256]{1,0:T(8,128)(2,1)}, bf16[1664,256]{1,0:T(8,128)(2,1)}, u32[]{:S(2)}, u32[]{:S(2)}) collective-permute-start(bf16[1664,256]{1,0:T(8,128)(2,1)} %constant_dynamic-slice_fusion.11), channel_id=1, source_target_pairs={{0,2},{1,3},{2,0},{3,1},{4,6},{5,7},{6,4},{7,5},{8,10},{9,11},{10,... | collective-permute-start | bytes 2555912 | tf_op jit(solution)/shard_map/ppermute | solution.py:660
  115.6 71.7 %collective-permute-start.4 = (bf16[256,1664]{1,0:T(8,128)(2,1)}, bf16[256,1664]{1,0:T(8,128)(2,1)}, u32[]{:S(2)}, u32[]{:S(2)}) collective-permute-start(bf16[256,1664]{1,0:T(8,128)(2,1)} %constant_dynamic-slice_fusion.10), channel_id=1, source_target_pairs={{0,2},{1,3},{2,0},{3,1},{4,6},{5,7},{6,4},{7,5},{8,10},{9,11},{10,... | collective-permute-start | bytes 2555912 | tf_op jit(solution)/shard_map/ppermute | solution.py:660
  128.2 9.6 %collective-permute-start.10 = (bf16[528,1664]{1,0:T(8,128)(2,1)}, bf16[528,1664]{1,0:T(8,128)(2,1)S(1)}, u32[]{:S(2)}, u32[]{:S(2)}) collective-permute-start(bf16[528,1664]{1,0:T(8,128)(2,1)} %get-tuple-element.218), channel_id=1, source_target_pairs={{0,4},{1,5},{2,6},{3,7},{4,0},{5,1},{6,2},{7,3},{8,12},{9,13},{10,... | collective-permute-start | bytes 5271560 | tf_op jit(solution)/shard_map/ppermute | solution.py:660
  137.3 25.6 %collective-permute-start.11 = (bf16[528,1664]{1,0:T(8,128)(2,1)}, bf16[528,1664]{1,0:T(8,128)(2,1)S(1)}, u32[]{:S(2)}, u32[]{:S(2)}) collective-permute-start(bf16[528,1664]{1,0:T(8,128)(2,1)} %get-tuple-element.221), channel_id=1, source_target_pairs={{0,4},{1,5},{2,6},{3,7},{4,0},{5,1},{6,2},{7,3},{8,12},{9,13},{10,... | collective-permute-start | bytes 5271560 | tf_op jit(solution)/shard_map/ppermute | solution.py:660
  149.1 62.4 %collective-permute-start.17 = (bf16[528,1664]{1,0:T(8,128)(2,1)}, bf16[528,1664]{1,0:T(8,128)(2,1)S(1)}, u32[]{:S(2)}, u32[]{:S(2)}) collective-permute-start(bf16[528,1664]{1,0:T(8,128)(2,1)} %get-tuple-element.223), channel_id=1, source_target_pairs={{0,1},{1,0},{2,3},{3,2},{4,5},{5,4},{6,7},{7,6},{8,9},{9,8},{10,11... | collective-permute-start | bytes 5271560 | tf_op jit(solution)/shard_map/ppermute | solution.py:660
  162.9 45.9 %collective-permute-start.16 = (bf16[528,1664]{1,0:T(8,128)(2,1)}, bf16[528,1664]{1,0:T(8,128)(2,1)}, u32[]{:S(2)}, u32[]{:S(2)}) collective-permute-start(bf16[528,1664]{1,0:T(8,128)(2,1)} %collective-permute-done.12.c0.refs_4_), channel_id=1, source_target_pairs={{0,4},{1,5},{2,6},{3,7},{4,0},{5,1},{6,2},{7,3},{8,12},{9,13},{10,... | collective-permute-start | bytes 5271560 | tf_op jit(solution)/shard_map/ppermute | solution.py:660
  172.7 29.1 %collective-permute-start.14 = (bf16[1664,256]{1,0:T(8,128)(2,1)}, bf16[1664,256]{1,0:T(8,128)(2,1)S(1)}, u32[]{:S(2)}, u32[]{:S(2)}) collective-permute-start(bf16[1664,256]{1,0:T(8,128)(2,1)} %collective-permute-done.13), channel_id=1, source_target_pairs={{0,8},{1,9},{2,10},{3,11},{4,12},{5,13},{6,14},{7,15},{8,0},{9,1},... | collective-permute-start | bytes 2555912 | tf_op jit(solution)/shard_map/ppermute | solution.py:660
  187.3 20.5 %collective-permute-start.15 = (bf16[256,1664]{1,0:T(8,128)(2,1)}, bf16[256,1664]{1,0:T(8,128)(2,1)S(1)}, u32[]{:S(2)}, u32[]{:S(2)}) collective-permute-start(bf16[256,1664]{1,0:T(8,128)(2,1)} %collective-permute-done.4), channel_id=1, source_target_pairs={{0,16},{1,17},{2,18},{3,19},{4,20},{5,21},{6,22},{7,23},{8,24},{9,... | collective-permute-start | bytes 2555912 | tf_op jit(solution)/shard_map/ppermute | solution.py:660
  221.2 10.3 %collective-permute-start.18 = (bf16[528,1664]{1,0:T(8,128)(2,1)}, bf16[528,1664]{1,0:T(8,128)(2,1)S(1)}, u32[]{:S(2)}, u32[]{:S(2)}) collective-permute-start(bf16[528,1664]{1,0:T(8,128)(2,1)} %get-tuple-element.240.n0.refs_2_), channel_id=1, source_target_pairs={{0,4},{1,5},{2,6},{3,7},{4,0},{5,1},{6,2},{7,3},{8,12},{9,13},{10,... | collective-permute-start | bytes 5271560 | tf_op jit(solution)/shard_map/ppermute | solution.py:660
  226.8 39.9 %collective-permute-start.19 = (bf16[1664,512]{1,0:T(8,128)(2,1)}, bf16[1664,512]{1,0:T(8,128)(2,1)}, u32[]{:S(2)}, u32[]{:S(2)}) collective-permute-start(bf16[1664,512]{1,0:T(8,128)(2,1)} %constant_dynamic-update-slice_fusion), channel_id=1, source_target_pairs={{0,16},{1,17},{2,18},{3,19},{4,20},{5,21},{6,22},{7,23},{8,24},{9,... | collective-permute-start | bytes 5111816 | tf_op jit(solution)/shard_map/ppermute | solution.py:660
  228.4 44.4 %collective-permute-start.20 = (bf16[512,1664]{1,0:T(8,128)(2,1)}, bf16[512,1664]{1,0:T(8,128)(2,1)}, u32[]{:S(2)}, u32[]{:S(2)}) collective-permute-start(bf16[512,1664]{1,0:T(8,128)(2,1)} %constant_dynamic-update-slice_fusion.2), channel_id=1, source_target_pairs={{0,8},{1,9},{2,10},{3,11},{4,12},{5,13},{6,14},{7,15},{8,0},{9,1},... | collective-permute-start | bytes 5111816 | tf_op jit(solution)/shard_map/ppermute | solution.py:660
  229.7 69.9 %collective-permute-start.21 = (bf16[528,1664]{1,0:T(8,128)(2,1)}, bf16[528,1664]{1,0:T(8,128)(2,1)}, u32[]{:S(2)}, u32[]{:S(2)}) collective-permute-start(bf16[528,1664]{1,0:T(8,128)(2,1)} %get-tuple-element.240.n0.refs_2_), channel_id=1, source_target_pairs={{0,1},{1,0},{2,3},{3,2},{4,5},{5,4},{6,7},{7,6},{8,9},{9,8},{10,11... | collective-permute-start | bytes 5271560 | tf_op jit(solution)/shard_map/ppermute | solution.py:660
  299.6 14.1 %collective-permute-start.22 = (bf16[528,1664]{1,0:T(8,128)(2,1)}, bf16[528,1664]{1,0:T(8,128)(2,1)}, u32[]{:S(2)}, u32[]{:S(2)}) collective-permute-start(bf16[528,1664]{1,0:T(8,128)(2,1)} %collective-permute-done.21.n0.refs_4_), channel_id=1, source_target_pairs={{0,4},{1,5},{2,6},{3,7},{4,0},{5,1},{6,2},{7,3},{8,12},{9,13},{10,... | collective-permute-start | bytes 5271560 | tf_op jit(solution)/shard_map/ppermute | solution.py:660
  313.2 21.6 %collective-permute-start.24 = (bf16[528,1664]{1,0:T(8,128)(2,1)}, bf16[528,1664]{1,0:T(8,128)(2,1)}, u32[]{:S(2)}, u32[]{:S(2)}) collective-permute-start(bf16[528,1664]{1,0:T(8,128)(2,1)} %get-tuple-element.249), channel_id=1, source_target_pairs={{0,4},{1,5},{2,6},{3,7},{4,0},{5,1},{6,2},{7,3},{8,12},{9,13},{10,... | collective-permute-start | bytes 5271560 | tf_op jit(solution)/shard_map/ppermute | solution.py:660
  313.7 21.1 %collective-permute-start.23 = (bf16[528,1664]{1,0:T(8,128)(2,1)}, bf16[528,1664]{1,0:T(8,128)(2,1)}, u32[]{:S(2)}, u32[]{:S(2)}) collective-permute-start(bf16[528,1664]{1,0:T(8,128)(2,1)} %get-tuple-element.253), channel_id=1, source_target_pairs={{0,4},{1,5},{2,6},{3,7},{4,0},{5,1},{6,2},{7,3},{8,12},{9,13},{10,... | collective-permute-start | bytes 5271560 | tf_op jit(solution)/shard_map/ppermute | solution.py:660
  357.5 22.8 %collective-permute-start.25 = (bf16[528,1664]{1,0:T(8,128)(2,1)}, bf16[528,1664]{1,0:T(8,128)(2,1)}, u32[]{:S(2)}, u32[]{:S(2)}) collective-permute-start(bf16[528,1664]{1,0:T(8,128)(2,1)} %get-tuple-element.264), channel_id=1, source_target_pairs={{0,4},{1,5},{2,6},{3,7},{4,0},{5,1},{6,2},{7,3},{8,12},{9,13},{10,... | collective-permute-start | bytes 5271560 | tf_op jit(solution)/shard_map/ppermute | solution.py:660
  358.1 22.2 %copy-start.17 = (bf16[528,1664]{1,0:T(8,128)(2,1)S(1)}, bf16[528,1664]{1,0:T(8,128)(2,1)}, u32[]{:S(2)}) copy-start(bf16[528,1664]{1,0:T(8,128)(2,1)} %get-tuple-element.263) | copy-start | bytes 5271556
  375.2 92.2 %collective-permute-start.28 = (bf16[1024,1664]{1,0:T(8,128)(2,1)}, bf16[1024,1664]{1,0:T(8,128)(2,1)}, u32[]{:S(2)}, u32[]{:S(2)}) collective-permute-start(bf16[1024,1664]{1,0:T(8,128)(2,1)} %wgrad.4), channel_id=1, source_target_pairs={{0,16},{1,17},{2,18},{3,19},{4,20},{5,21},{6,22},{7,23},{8,24},{9,... | collective-permute-start | bytes 10223624 | tf_op jit(solution)/shard_map/ppermute | solution.py:660
  383.5 40.3 %collective-permute-start.26 = (bf16[528,1664]{1,0:T(8,128)(2,1)}, bf16[528,1664]{1,0:T(8,128)(2,1)}, u32[]{:S(2)}, u32[]{:S(2)}) collective-permute-start(bf16[528,1664]{1,0:T(8,128)(2,1)} %add_convert_fusion.1), channel_id=1, source_target_pairs={{0,1},{1,0},{2,3},{3,2},{4,5},{5,4},{6,7},{7,6},{8,9},{9,8},{10,11... | collective-permute-start | bytes 5271560 | tf_op jit(solution)/shard_map/ppermute | solution.py:660
  402.2 92.8 %collective-permute-start.27 = (bf16[1024,1664]{1,0:T(8,128)(2,1)}, bf16[1024,1664]{1,0:T(8,128)(2,1)}, u32[]{:S(2)}, u32[]{:S(2)}) collective-permute-start(bf16[1024,1664]{1,0:T(8,128)(2,1)} %wgrad.5), channel_id=1, source_target_pairs={{0,8},{1,9},{2,10},{3,11},{4,12},{5,13},{6,14},{7,15},{8,0},{9,1},... | collective-permute-start | bytes 10223624 | tf_op jit(solution)/shard_map/ppermute | solution.py:660
  448.1 52.1 %collective-permute-start.32 = (bf16[528,1664]{1,0:T(8,128)(2,1)}, bf16[528,1664]{1,0:T(8,128)(2,1)}, u32[]{:S(2)}, u32[]{:S(2)}) collective-permute-start(bf16[528,1664]{1,0:T(8,128)(2,1)} %get-tuple-element.272), channel_id=1, source_target_pairs={{0,4},{1,5},{2,6},{3,7},{4,0},{5,1},{6,2},{7,3},{8,12},{9,13},{10,... | collective-permute-start | bytes 5271560 | tf_op jit(solution)/shard_map/ppermute | solution.py:660
  448.1 37.1 %collective-permute-start.31 = (bf16[528,1664]{1,0:T(8,128)(2,1)}, bf16[528,1664]{1,0:T(8,128)(2,1)}, u32[]{:S(2)}, u32[]{:S(2)}) collective-permute-start(bf16[528,1664]{1,0:T(8,128)(2,1)} %get-tuple-element.332.g_ref.refs_12_), channel_id=1, source_target_pairs={{0,4},{1,5},{2,6},{3,7},{4,0},{5,1},{6,2},{7,3},{8,12},{9,13},{10,... | collective-permute-start | bytes 5271560 | tf_op jit(solution)/shard_map/ppermute | solution.py:660
  448.6 55.1 %collective-permute-start.29 = (bf16[528,1664]{1,0:T(8,128)(2,1)}, bf16[528,1664]{1,0:T(8,128)(2,1)}, u32[]{:S(2)}, u32[]{:S(2)}) collective-permute-start(bf16[528,1664]{1,0:T(8,128)(2,1)} %get-tuple-element.332.g_ref.refs_12_), channel_id=1, source_target_pairs={{0,1},{1,0},{2,3},{3,2},{4,5},{5,4},{6,7},{7,6},{8,9},{9,8},{10,11... | collective-permute-start | bytes 5271560 | tf_op jit(solution)/shard_map/ppermute | solution.py:660
  472.1 42.0 %collective-permute-start.33 = (bf16[512,1664]{1,0:T(8,128)(2,1)}, bf16[512,1664]{1,0:T(8,128)(2,1)}, u32[]{:S(2)}, u32[]{:S(2)}) collective-permute-start(bf16[512,1664]{1,0:T(8,128)(2,1)} %bitcast.22), channel_id=1, source_target_pairs={{0,8},{1,9},{2,10},{3,11},{4,12},{5,13},{6,14},{7,15},{8,0},{9,1},... | collective-permute-start | bytes 5111816 | tf_op jit(solution)/shard_map/ppermute | solution.py:660
  499.7 54.0 %collective-permute-start.34 = (bf16[512,1664]{1,0:T(8,128)(2,1)}, bf16[512,1664]{1,0:T(8,128)(2,1)}, u32[]{:S(2)}, u32[]{:S(2)}) collective-permute-start(bf16[512,1664]{1,0:T(8,128)(2,1)} %bitcast.26), channel_id=1, source_target_pairs={{0,16},{1,17},{2,18},{3,19},{4,20},{5,21},{6,22},{7,23},{8,24},{9,... | collective-permute-start | bytes 5111816 | tf_op jit(solution)/shard_map/ppermute | solution.py:660
  503.3 58.0 %collective-permute-start.35 = (bf16[528,1664]{1,0:T(8,128)(2,1)}, bf16[528,1664]{1,0:T(8,128)(2,1)}, u32[]{:S(2)}, u32[]{:S(2)}) collective-permute-start(bf16[528,1664]{1,0:T(8,128)(2,1)} %add_convert_fusion), channel_id=1, source_target_pairs={{0,1},{1,0},{2,3},{3,2},{4,5},{5,4},{6,7},{7,6},{8,9},{9,8},{10,11... | collective-permute-start | bytes 5271560 | tf_op jit(solution)/shard_map/ppermute | solution.py:660
  503.7 15.4 %collective-permute-start.30 = (bf16[528,1664]{1,0:T(8,128)(2,1)}, bf16[528,1664]{1,0:T(8,128)(2,1)S(1)}, u32[]{:S(2)}, u32[]{:S(2)}) collective-permute-start(bf16[528,1664]{1,0:T(8,128)(2,1)} %collective-permute-done.29.g_ref.refs_14_), channel_id=1, source_target_pairs={{0,4},{1,5},{2,6},{3,7},{4,0},{5,1},{6,2},{7,3},{8,12},{9,13},{10,... | collective-permute-start | bytes 5271560 | tf_op jit(solution)/shard_map/ppermute | solution.py:660
  517.3 60.6 %collective-permute-start.36 = (bf16[256,1664]{1,0:T(8,128)(2,1)}, bf16[256,1664]{1,0:T(8,128)(2,1)}, u32[]{:S(2)}, u32[]{:S(2)}) collective-permute-start(bf16[256,1664]{1,0:T(8,128)(2,1)} %get-tuple-element.406), channel_id=1, source_target_pairs={{0,2},{1,3},{2,0},{3,1},{4,6},{5,7},{6,4},{7,5},{8,10},{9,11},{10,... | collective-permute-start | bytes 2555912 | tf_op jit(solution)/shard_map/ppermute | solution.py:660
  552.8 61.0 %collective-permute-start.37 = (bf16[416,1664]{1,0:T(8,128)(2,1)}, bf16[416,1664]{1,0:T(8,128)(2,1)}, u32[]{:S(2)}, u32[]{:S(2)}) collective-permute-start(bf16[416,1664]{1,0:T(8,128)(2,1)} %constant_dynamic-slice_fusion.6), channel_id=1, source_target_pairs={{0,16},{1,17},{2,18},{3,19},{4,20},{5,21},{6,22},{7,23},{8,24},{9,... | collective-permute-start | bytes 4153352 | tf_op jit(solution)/shard_map/ppermute | solution.py:660
  577.9 25.2 %collective-permute-start.39 = (bf16[528,1664]{1,0:T(8,128)(2,1)}, bf16[528,1664]{1,0:T(8,128)(2,1)}, u32[]{:S(2)}, u32[]{:S(2)}) collective-permute-start(bf16[528,1664]{1,0:T(8,128)(2,1)} %get-tuple-element.318), channel_id=1, source_target_pairs={{0,4},{1,5},{2,6},{3,7},{4,0},{5,1},{6,2},{7,3},{8,12},{9,13},{10,... | collective-permute-start | bytes 5271560 | tf_op jit(solution)/shard_map/ppermute | solution.py:660
  579.2 21.4 %collective-permute-start.38 = (bf16[256,1664]{1,0:T(8,128)(2,1)S(1)}, bf16[256,1664]{1,0:T(8,128)(2,1)S(1)}, u32[]{:S(2)}, u32[]{:S(2)}) collective-permute-start(bf16[256,1664]{1,0:T(8,128)(2,1)S(1)} %add_convert_fusion.9), channel_id=1, source_target_pairs={{0,8},{1,9},{2,10},{3,11},{4,12},{5,13},{6,14},{7,15},{8,0},{9,1},... | collective-permute-start | bytes 2555912 | tf_op jit(solution)/shard_map/ppermute | solution.py:660
  590.0 27.2 %collective-permute-start.40 = (bf16[528,1664]{1,0:T(8,128)(2,1)}, bf16[528,1664]{1,0:T(8,128)(2,1)}, u32[]{:S(2)}, u32[]{:S(2)}) collective-permute-start(bf16[528,1664]{1,0:T(8,128)(2,1)} %get-tuple-element.324), channel_id=1, source_target_pairs={{0,4},{1,5},{2,6},{3,7},{4,0},{5,1},{6,2},{7,3},{8,12},{9,13},{10,... | collective-permute-start | bytes 5271560 | tf_op jit(solution)/shard_map/ppermute | solution.py:660
  591.6 39.7 %collective-permute-start.41 = (bf16[256,1664]{1,0:T(8,128)(2,1)}, bf16[256,1664]{1,0:T(8,128)(2,1)}, u32[]{:S(2)}, u32[]{:S(2)}) collective-permute-start(bf16[256,1664]{1,0:T(8,128)(2,1)} %get-tuple-element.404), channel_id=1, source_target_pairs={{0,2},{1,3},{2,0},{3,1},{4,6},{5,7},{6,4},{7,5},{8,10},{9,11},{10,... | collective-permute-start | bytes 2555912 | tf_op jit(solution)/shard_map/ppermute | solution.py:660
  601.6 40.4 %collective-permute-start.43 = (bf16[512,1664]{1,0:T(8,128)(2,1)}, bf16[512,1664]{1,0:T(8,128)(2,1)}, u32[]{:S(2)}, u32[]{:S(2)}) collective-permute-start(bf16[512,1664]{1,0:T(8,128)(2,1)} %constant_dynamic-update-slice_fusion.4), channel_id=1, source_target_pairs={{0,16},{1,17},{2,18},{3,19},{4,20},{5,21},{6,22},{7,23},{8,24},{9,... | collective-permute-start | bytes 5111816 | tf_op jit(solution)/shard_map/ppermute | solution.py:660
  613.8 71.8 %collective-permute-start.46 = (bf16[528,1664]{1,0:T(8,128)(2,1)}, bf16[528,1664]{1,0:T(8,128)(2,1)}, u32[]{:S(2)}, u32[]{:S(2)}) collective-permute-start(bf16[528,1664]{1,0:T(8,128)(2,1)} %get-tuple-element.330), channel_id=1, source_target_pairs={{0,1},{1,0},{2,3},{3,2},{4,5},{5,4},{6,7},{7,6},{8,9},{9,8},{10,11... | collective-permute-start | bytes 5271560 | tf_op jit(solution)/shard_map/ppermute | solution.py:660
  616.5 18.7 %collective-permute-start.42 = (bf16[208,1664]{1,0:T(8,128)(2,1)}, bf16[208,1664]{1,0:T(8,128)(2,1)}, u32[]{:S(2)}, u32[]{:S(2)}) collective-permute-start(bf16[208,1664]{1,0:T(8,128)(2,1)} %get-tuple-element.408), channel_id=1, source_target_pairs={{0,8},{1,9},{2,10},{3,11},{4,12},{5,13},{6,14},{7,15},{8,0},{9,1},... | collective-permute-start | bytes 2076680 | tf_op jit(solution)/shard_map/ppermute | solution.py:660
  633.6 38.4 %collective-permute-start.44 = (bf16[256,1664]{1,0:T(8,128)(2,1)}, bf16[256,1664]{1,0:T(8,128)(2,1)}, u32[]{:S(2)}, u32[]{:S(2)}) collective-permute-start(bf16[256,1664]{1,0:T(8,128)(2,1)} %add_convert_fusion.8), channel_id=1, source_target_pairs={{0,16},{1,17},{2,18},{3,19},{4,20},{5,21},{6,22},{7,23},{8,24},{9,... | collective-permute-start | bytes 2555912 | tf_op jit(solution)/shard_map/ppermute | solution.py:660
  637.4 61.1 %collective-permute-start.50 = (bf16[208,1664]{1,0:T(8,128)(2,1)}, bf16[208,1664]{1,0:T(8,128)(2,1)}, u32[]{:S(2)}, u32[]{:S(2)}) collective-permute-start(bf16[208,1664]{1,0:T(8,128)(2,1)} %add_convert_fusion.11), channel_id=1, source_target_pairs={{0,2},{1,3},{2,0},{3,1},{4,6},{5,7},{6,4},{7,5},{8,10},{9,11},{10,... | collective-permute-start | bytes 2076680 | tf_op jit(solution)/shard_map/ppermute | solution.py:660
  644.8 30.2 %collective-permute-start.45 = (bf16[1024,1664]{1,0:T(8,128)(2,1)}, bf16[1024,1664]{1,0:T(8,128)(2,1)}, u32[]{:S(2)}, u32[]{:S(2)}) collective-permute-start(bf16[1024,1664]{1,0:T(8,128)(2,1)} %constant_dynamic-update-slice_fusion.6.refs_0_), channel_id=1, source_target_pairs={{0,4},{1,5},{2,6},{3,7},{4,0},{5,1},{6,2},{7,3},{8,12},{9,13},{10,... | collective-permute-start | bytes 10223624 | tf_op jit(solution)/shard_map/ppermute | solution.py:660
  669.2 29.4 %collective-permute-start.49 = (bf16[208,1664]{1,0:T(8,128)(2,1)}, bf16[208,1664]{1,0:T(8,128)(2,1)}, u32[]{:S(2)}, u32[]{:S(2)}) collective-permute-start(bf16[208,1664]{1,0:T(8,128)(2,1)} %constant_dynamic-slice_fusion.2), channel_id=1, source_target_pairs={{0,24},{1,25},{2,26},{3,27},{4,28},{5,29},{6,30},{7,31},{8,16},{9,... | collective-permute-start | bytes 2076680 | tf_op jit(solution)/shard_map/ppermute | solution.py:660
  672.1 31.1 %collective-permute-start.48 = (bf16[208,1664]{1,0:T(8,128)(2,1)}, bf16[208,1664]{1,0:T(8,128)(2,1)}, u32[]{:S(2)}, u32[]{:S(2)}) collective-permute-start(bf16[208,1664]{1,0:T(8,128)(2,1)} %constant_dynamic-slice_fusion.3), channel_id=1, source_target_pairs={{0,16},{1,17},{2,18},{3,19},{4,20},{5,21},{6,22},{7,23},{8,24},{9,... | collective-permute-start | bytes 2076680 | tf_op jit(solution)/shard_map/ppermute | solution.py:660
  675.0 28.6 %collective-permute-start.47 = (bf16[208,1664]{1,0:T(8,128)(2,1)S(1)}, bf16[208,1664]{1,0:T(8,128)(2,1)}, u32[]{:S(2)}, u32[]{:S(2)}) collective-permute-start(bf16[208,1664]{1,0:T(8,128)(2,1)S(1)} %constant_dynamic-slice_fusion.4), channel_id=1, source_target_pairs={{0,8},{1,9},{2,10},{3,11},{4,12},{5,13},{6,14},{7,15},{8,0},{9,1},... | collective-permute-start | bytes 2076680 | tf_op jit(solution)/shard_map/ppermute | solution.py:660
  685.5 54.5 %collective-permute-start.53 = (bf16[512,1664]{1,0:T(8,128)(2,1)}, bf16[512,1664]{1,0:T(8,128)(2,1)S(1)}, u32[]{:S(2)}, u32[]{:S(2)}) collective-permute-start(bf16[512,1664]{1,0:T(8,128)(2,1)} %copy-done.19), channel_id=1, source_target_pairs={{0,8},{1,9},{2,10},{3,11},{4,12},{5,13},{6,14},{7,15},{8,0},{9,1},... | collective-permute-start | bytes 5111816 | tf_op jit(solution)/shard_map/ppermute | solution.py:660
  698.5 10.1 %collective-permute-start.51 = (f32[21504]{0:T(1024)S(1)}, f32[21504]{0:T(1024)S(1)}, u32[]{:S(2)}, u32[]{:S(2)}) collective-permute-start(f32[21504]{0:T(1024)S(1)} %constant_dynamic-update-slice_fusion.23), channel_id=1, source_target_pairs={{0,4},{1,5},{2,6},{3,7},{4,0},{5,1},{6,2},{7,3},{8,12},{9,13},{10,... | collective-permute-start | bytes 258056 | tf_op jit(solution)/shard_map/ppermute | solution.py:660
  708.6 4.6 collective-permute-start.52
  708.7 46.2 %collective-permute-start.55 = (bf16[208,1664]{1,0:T(8,128)(2,1)S(1)}, bf16[208,1664]{1,0:T(8,128)(2,1)S(1)}, u32[]{:S(2)}, u32[]{:S(2)}) collective-permute-start(bf16[208,1664]{1,0:T(8,128)(2,1)S(1)} %add_convert_fusion.10), channel_id=1, source_target_pairs={{0,8},{1,9},{2,10},{3,11},{4,12},{5,13},{6,14},{7,15},{8,0},{9,1},... | collective-permute-start | bytes 2076680 | tf_op jit(solution)/shard_map/ppermute | solution.py:660
  709.6 46.2 %collective-permute-start.56 = (bf16[208,1664]{1,0:T(8,128)(2,1)S(1)}, bf16[208,1664]{1,0:T(8,128)(2,1)S(1)}, u32[]{:S(2)}, u32[]{:S(2)}) collective-permute-start(bf16[208,1664]{1,0:T(8,128)(2,1)S(1)} %add_convert_fusion.10), channel_id=1, source_target_pairs={{0,16},{1,17},{2,18},{3,19},{4,20},{5,21},{6,22},{7,23},{8,24},{9,... | collective-permute-start | bytes 2076680 | tf_op jit(solution)/shard_map/ppermute | solution.py:660
  710.6 58.7 %collective-permute-start.57 = (bf16[208,1664]{1,0:T(8,128)(2,1)S(1)}, bf16[208,1664]{1,0:T(8,128)(2,1)S(1)}, u32[]{:S(2)}, u32[]{:S(2)}) collective-permute-start(bf16[208,1664]{1,0:T(8,128)(2,1)S(1)} %add_convert_fusion.10), channel_id=1, source_target_pairs={{0,24},{1,25},{2,26},{3,27},{4,28},{5,29},{6,30},{7,31},{8,16},{9,... | collective-permute-start | bytes 2076680 | tf_op jit(solution)/shard_map/ppermute | solution.py:660
  713.2 28.2 %collective-permute-start.54 = (f32[21504]{0:T(1024)S(1)}, f32[21504]{0:T(1024)S(1)}, u32[]{:S(2)}, u32[]{:S(2)}) collective-permute-start(f32[21504]{0:T(1024)S(1)} %add.490), channel_id=1, source_target_pairs={{0,2},{1,3},{2,0},{3,1},{4,6},{5,7},{6,4},{7,5},{8,10},{9,11},{10,... | collective-permute-start | bytes 258056 | tf_op jit(solution)/shard_map/ppermute | solution.py:660
  741.3 30.1 %collective-permute-start.58 = (bf16[1024,1664]{1,0:T(8,128)(2,1)}, bf16[1024,1664]{1,0:T(8,128)(2,1)}, u32[]{:S(2)}, u32[]{:S(2)}) collective-permute-start(bf16[1024,1664]{1,0:T(8,128)(2,1)} %constant_dynamic-update-slice_fusion.12.refs_0_), channel_id=1, source_target_pairs={{0,4},{1,5},{2,6},{3,7},{4,0},{5,1},{6,2},{7,3},{8,12},{9,13},{10,... | collective-permute-start | bytes 10223624 | tf_op jit(solution)/shard_map/ppermute | solution.py:660
  770.2 19.8 %collective-permute-start.61 = (bf16[832,1664]{1,0:T(8,128)(2,1)}, bf16[832,1664]{1,0:T(8,128)(2,1)}, u32[]{:S(2)}, u32[]{:S(2)}) collective-permute-start(bf16[832,1664]{1,0:T(8,128)(2,1)} %constant_dynamic-update-slice_fusion.15.refs_0_), channel_id=1, source_target_pairs={{0,4},{1,5},{2,6},{3,7},{4,0},{5,1},{6,2},{7,3},{8,12},{9,13},{10,... | collective-permute-start | bytes 8306696 | tf_op jit(solution)/shard_map/ppermute | solution.py:660
  770.2 11.9 %collective-permute-start.59 = (f32[21504]{0:T(1024)S(1)}, f32[21504]{0:T(1024)S(1)}, u32[]{:S(2)}, u32[]{:S(2)}) collective-permute-start(f32[21504]{0:T(1024)S(1)} %add.491), channel_id=1, source_target_pairs={{0,8},{1,9},{2,10},{3,11},{4,12},{5,13},{6,14},{7,15},{8,0},{9,1},... | collective-permute-start | bytes 258056 | tf_op jit(solution)/shard_map/ppermute | solution.py:660
  782.8 15.2 %collective-permute-start.60 = (f32[21504]{0:T(1024)}, f32[21504]{0:T(1024)}, u32[]{:S(2)}, u32[]{:S(2)}) collective-permute-start(f32[21504]{0:T(1024)} %add.500), channel_id=1, source_target_pairs={{0,16},{1,17},{2,18},{3,19},{4,20},{5,21},{6,22},{7,23},{8,24},{9,... | collective-permute-start | bytes 258056 | tf_op jit(solution)/shard_map/ppermute | solution.py:660
  (53 other events, 445.4 us)

commit v5 on v4

--- a/solution.py
+++ b/solution.py
@@ -468,19 +468,13 @@
         for copy in copies:
             copy.start()
 
-    total, at = None, 0
-    for ref in left:
-        rows = ref.shape[0]
-
-        @pl.when(first)
-        def _(at=at, rows=rows):
-            for copy in copies[at // size : (at + rows) // size]:
-                copy.wait()
-
-        part = dot(ref[...], held[at : at + rows, :], 0, 0)
-        total = part if total is None else total + part
-        at += rows
-    out_ref[...] = total.astype(BF)
+    @pl.when(first)
+    def _():
+        for copy in copies:
+            copy.wait()
+
+    rows = jnp.concatenate([ref[...] for ref in left], 0)
+    out_ref[...] = dot(rows, held[...], 0, 0).astype(BF)
 
 
 def wgrad(left, right, index, tile):

time: 811 us -> 809 us (level)
  transfers between devices with their start and end apart: 62 -> 62, of which waited for: 22 -> 22; matrix products, arithmetic and copies ran while one was open for 16% -> 16% of each run, Pallas kernels for 52% -> 51%
where the time goes in v5:
time: 809 us; the launch traced here: 798 us
  Pallas kernels  446 us (55%)
  waiting for transfers between devices  138 us (17%)
  local copies, waits for them, and re-layouts  102 us (13%)
  starting transfers between devices  64 us (8%)
  other arithmetic  46.5 us (6%)
    pallas_call x34, Pallas kernels, call(): pl.pallas_call(kernel, in_specs=in_specs or [vmem] * len(ins), out_specs=...  383 us
    ppermute x62, waiting for transfers between devices, move(): return lax.ppermute(x, ('dp', 'tensor'), pairs)  138 us
    ppermute x62, starting transfers between devices, move(): return lax.ppermute(x, ('dp', 'tensor'), pairs)  64 us
    pallas_call x4, Pallas kernels, wgrad(): pl.pallas_call(functools.partial(wgrad_kernel, len(left), len(right)), gr...  63.4 us
    unnamed x131, local copies, waits for them, and re-layouts  33.1 us
    convert_element_type x11, other arithmetic, join(): return total.astype(BF)  29.9 us
    dynamic_update_slice x16, local copies, waits for them, and re-layouts, put(): return lax.dynamic_update_slice_in_dim(buf, x, at, axis)  17.9 us
  transfers between devices with their start and end apart: 62, of which 22 were waited for; matrix products, arithmetic and copies ran while one was open for 16% of the time, Pallas kernels for 51%

profile of v5, /device:TPU:0, one launch (start us, length us, event | category | flops | bytes accessed | tf_op | source)
XLA Modules:
  0.0 798.4 jit_solution(17464565890590775242)
XLA Ops:
  3.2 2.8 copy.32.img_ref
  6.1 5.6 pack.2
  21.5 5.5 pad_maximum_fusion.w_ref
  27.8 8.6 %attend_fwd.8 = (bf16[528,624]{1,0:T(8,128)(2,1)}, bf16[528,208]{1,0:T(8,128)(2,1)}, f32[8,512]{1,0:T(8,128)}, f32[8,128]{1,0:T(8,128)}, bf16[528,1664]{1,0:T(8,128)(2,1)}) custom-call(bf16[528,1664]{1,0:T(8,128)(2,1)} %get-tuple-element.226.n_ref.refs_8_, bf16[832,1664]{1,0:T(8,128)(2,1)} %pad_maximum_fusion.w_ref, f32[1,624]{1,0:T(1,128)} %reshape.174.b_ref), custom_call_target="tpu_custom_call" | custom-call | flops 47130869760 | bytes 215544960 | tf_op jit(solution)/shard_map/attend_fwd/pallas_call | solution.py:197
  39.4 8.7 %attend_fwd.9 = (bf16[528,624]{1,0:T(8,128)(2,1)}, bf16[528,208]{1,0:T(8,128)(2,1)}, f32[8,512]{1,0:T(8,128)}, f32[8,128]{1,0:T(8,128)}, bf16[528,1664]{1,0:T(8,128)(2,1)}) custom-call(bf16[528,1664]{1,0:T(8,128)(2,1)} %collective-permute-done.1.n_ref.refs_9_, bf16[832,1664]{1,0:T(8,128)(2,1)} %pad_maximum_fusion.w_ref, f32[1,624]{1,0:T(1,128)} %reshape.174.b_ref), custom_call_target="tpu_custom_call" | custom-call | flops 47130869760 | bytes 215544960 | tf_op jit(solution)/shard_map/attend_fwd/pallas_call | solution.py:197
  49.5 3.0 pack.3
  52.5 15.6 %collective-permute-done.2 = bf16[208,1664]{1,0:T(8,128)(2,1)S(1)} collective-permute-done((bf16[208,1664]{1,0:T(8,128)(2,1)S(1)}, bf16[208,1664]{1,0:T(8,128)(2,1)S(1)}, u32[]{:S(2)}, u32[]{:S(2)}) %collective-permute-start.2) | collective-permute-done | bytes 692256 | tf_op jit(solution)/shard_map/ppermute | solution.py:654
  69.0 8.8 %attend_fwd.10 = (bf16[528,624]{1,0:T(8,128)(2,1)}, bf16[528,208]{1,0:T(8,128)(2,1)}, f32[8,512]{1,0:T(8,128)}, f32[8,128]{1,0:T(8,128)}, bf16[528,1664]{1,0:T(8,128)(2,1)}) custom-call(bf16[528,1664]{1,0:T(8,128)(2,1)} %collective-permute-done.n_ref.refs_10_, bf16[832,1664]{1,0:T(8,128)(2,1)} %pad_maximum_fusion.w_ref, f32[1,624]{1,0:T(1,128)} %reshape.174.b_ref), custom_call_target="tpu_custom_call" | custom-call | flops 47130869760 | bytes 215544960 | tf_op jit(solution)/shard_map/attend_fwd/pallas_call | solution.py:197
  82.6 8.6 %attend_fwd.11 = (bf16[528,624]{1,0:T(8,128)(2,1)}, bf16[528,208]{1,0:T(8,128)(2,1)}, f32[8,512]{1,0:T(8,128)}, f32[8,128]{1,0:T(8,128)}, bf16[528,1664]{1,0:T(8,128)(2,1)}) custom-call(bf16[528,1664]{1,0:T(8,128)(2,1)} %copy-done.51, bf16[832,1664]{1,0:T(8,128)(2,1)} %pad_maximum_fusion.w_ref, f32[1,624]{1,0:T(1,128)} %reshape.174.b_ref), custom_call_target="tpu_custom_call" | custom-call | flops 47130869760 | bytes 215544960 | tf_op jit(solution)/shard_map/attend_fwd/pallas_call | solution.py:197
  100.1 12.1 %collective-permute-done.6 = bf16[208,1664]{1,0:T(8,128)(2,1)} collective-permute-done((bf16[208,1664]{1,0:T(8,128)(2,1)S(1)}, bf16[208,1664]{1,0:T(8,128)(2,1)}, u32[]{:S(2)}, u32[]{:S(2)}) %collective-permute-start.6) | collective-permute-done | bytes 692256 | tf_op jit(solution)/shard_map/ppermute | solution.py:654
  119.0 9.1 %attend_fwd.12 = (bf16[528,624]{1,0:T(8,128)(2,1)}, bf16[528,208]{1,0:T(8,128)(2,1)}, f32[8,512]{1,0:T(8,128)}, f32[8,128]{1,0:T(8,128)}, bf16[528,1664]{1,0:T(8,128)(2,1)}) custom-call(bf16[528,1664]{1,0:T(8,128)(2,1)} %copy-done.51, bf16[832,1664]{1,0:T(8,128)(2,1)} %copy-done.12, f32[1,624]{1,0:T(1,128)} %reshape.176.b_ref, ...), custom_call_target="tpu_custom_call" | custom-call | flops 47130869760 | bytes 268260480 | tf_op jit(solution)/shard_map/attend_fwd/pallas_call | solution.py:197
  128.2 9.1 %attend_fwd.13 = (bf16[528,624]{1,0:T(8,128)(2,1)}, bf16[528,208]{1,0:T(8,128)(2,1)}, f32[8,512]{1,0:T(8,128)}, f32[8,128]{1,0:T(8,128)}, bf16[528,1664]{1,0:T(8,128)(2,1)}) custom-call(bf16[528,1664]{1,0:T(8,128)(2,1)} %collective-permute-done.1.n_ref.refs_9_, bf16[832,1664]{1,0:T(8,128)(2,1)} %copy-done.12, f32[1,624]{1,0:T(1,128)} %reshape.176.b_ref, ...), custom_call_target="tpu_custom_call" | custom-call | flops 47130869760 | bytes 268260480 | tf_op jit(solution)/shard_map/attend_fwd/pallas_call | solution.py:197
  139.0 10.1 %attend_fwd.14 = (bf16[528,624]{1,0:T(8,128)(2,1)}, bf16[528,208]{1,0:T(8,128)(2,1)}, f32[8,512]{1,0:T(8,128)}, f32[8,128]{1,0:T(8,128)}, bf16[528,1664]{1,0:T(8,128)(2,1)}) custom-call(bf16[528,1664]{1,0:T(8,128)(2,1)} %collective-permute-done.n_ref.refs_10_, bf16[832,1664]{1,0:T(8,128)(2,1)} %copy-done.12, f32[1,624]{1,0:T(1,128)} %reshape.176.b_ref, ...), custom_call_target="tpu_custom_call" | custom-call | flops 47130869760 | bytes 320976000 | tf_op jit(solution)/shard_map/attend_fwd/pallas_call | solution.py:197
  151.5 11.4 %collective-permute-done.12.c0.refs_4_ = bf16[528,1664]{1,0:T(8,128)(2,1)} collective-permute-done((bf16[528,1664]{1,0:T(8,128)(2,1)}, bf16[528,1664]{1,0:T(8,128)(2,1)}, u32[]{:S(2)}, u32[]{:S(2)}) %collective-permute-start.12) | collective-permute-done | bytes 1757216 | tf_op jit(solution)/shard_map/ppermute | solution.py:654
  163.0 9.7 %attend_fwd.15 = (bf16[528,624]{1,0:T(8,128)(2,1)}, bf16[528,208]{1,0:T(8,128)(2,1)}, f32[8,512]{1,0:T(8,128)}, f32[8,128]{1,0:T(8,128)}, bf16[528,1664]{1,0:T(8,128)(2,1)}) custom-call(bf16[528,1664]{1,0:T(8,128)(2,1)} %get-tuple-element.226.n_ref.refs_8_, bf16[832,1664]{1,0:T(8,128)(2,1)} %copy-done.12, f32[1,624]{1,0:T(1,128)} %reshape.176.b_ref, ...), custom_call_target="tpu_custom_call" | custom-call | flops 47130869760 | bytes 268260480 | tf_op jit(solution)/shard_map/attend_fwd/pallas_call | solution.py:197
  172.7 9.9 %collective-permute-start.14 = (bf16[1664,256]{1,0:T(8,128)(2,1)}, bf16[1664,256]{1,0:T(8,128)(2,1)S(1)}, u32[]{:S(2)}, u32[]{:S(2)}) collective-permute-start(bf16[1664,256]{1,0:T(8,128)(2,1)} %collective-permute-done.13), channel_id=1, source_target_pairs={{0,8},{1,9},{2,10},{3,11},{4,12},{5,13},{6,14},{7,15},{8,0},{9,1},... | collective-permute-start | bytes 2555912 | tf_op jit(solution)/shard_map/ppermute | solution.py:654
  182.5 4.0 constant_dynamic-slice_fusion.9.up_ref
  187.3 2.7 collective-permute-start.15
  190.0 4.0 constant_dynamic-slice_fusion.8.down_ref.refs_0_
  196.2 5.6 collective-permute-done.14
  204.9 2.9 collective-permute-done.15
  208.8 2.7 collective-permute-done.17.c_ref
  212.7 8.6 %norm_second.1 = (f32[528,1664]{1,0:T(8,128)}, bf16[528,1664]{1,0:T(8,128)(2,1)}) custom-call(bf16[528,1664]{1,0:T(8,128)(2,1)} %get-tuple-element.354.x_ref, bf16[528,1664]{1,0:T(8,128)(2,1)} %get-tuple-element.227.a_ref, bf16[528,1664]{1,0:T(8,128)(2,1)} %copy-done.14, bf16[528,1664]{1,0:T(8,128)(2,1)} %copy-done.16, f32[1,1664]{1,0:T(1,128)} %reshape.177.bias_ref, ...), custom_call_target="tpu_custom_call" | custom-call | bytes 369607680 | tf_op jit(solution)/shard_map/norm_second/pallas_call | solution.py:197
  232.7 21.2 %mlp.4 = (bf16[1056,2048]{1,0:T(8,128)(2,1)}, bf16[1056,2048]{1,0:T(8,128)(2,1)}, bf16[528,1664]{1,0:T(8,128)(2,1)}, bf16[528,1664]{1,0:T(8,128)(2,1)}, f32[1,1024]{1,0:T(1,128)}) custom-call(bf16[528,1664]{1,0:T(8,128)(2,1)} %get-tuple-element.240.n0.refs_2_, bf16[528,1664]{1,0:T(8,128)(2,1)} %copy-done.52, ...), custom_call_target="tpu_custom_call" | custom-call | flops 323884154880 | bytes 780533760 | tf_op jit(solution)/shard_map/mlp/pallas_call | solution.py:197
  256.9 9.8 %collective-permute-done.19 = bf16[1664,512]{1,0:T(8,128)(2,1)} collective-permute-done((bf16[1664,512]{1,0:T(8,128)(2,1)}, bf16[1664,512]{1,0:T(8,128)(2,1)}, u32[]{:S(2)}, u32[]{:S(2)}) %collective-permute-start.19) | collective-permute-done | bytes 1703968 | tf_op jit(solution)/shard_map/ppermute | solution.py:654
  277.0 22.6 %mlp.5 = (bf16[1056,2048]{1,0:T(8,128)(2,1)}, bf16[1056,2048]{1,0:T(8,128)(2,1)}, bf16[528,1664]{1,0:T(8,128)(2,1)}, bf16[528,1664]{1,0:T(8,128)(2,1)}, f32[1,1024]{1,0:T(1,128)}) custom-call(bf16[528,1664]{1,0:T(8,128)(2,1)} %get-tuple-element.240.n0.refs_2_, bf16[528,1664]{1,0:T(8,128)(2,1)} %copy-done.52, ...), custom_call_target="tpu_custom_call", output_to_operand_aliasing={{0}: (9, {}), {1}: (10, {})} | custom-call | flops 323884154880 | bytes 1145487360 | tf_op jit(solution)/shard_map/mlp/pallas_call | solution.py:197
  299.7 13.5 %row_product.2 = (bf16[528,1664]{1,0:T(8,128)(2,1)}, bf16[528,1664]{1,0:T(8,128)(2,1)}) custom-call(bf16[1056,2048]{1,0:T(8,128)(2,1)} %get-tuple-element.267.act_ref.refs_0_, bf16[1024,1664]{1,0:T(8,128)(2,1)} %constant_dynamic-slice_fusion.8.down_ref.refs_0_, bf16[1024,1664]{1,0:T(8,128)(2,1)} %copy-done.4), custom_call_target="tpu_custom_call" | custom-call | flops 215922769920 | bytes 439664640 | tf_op jit(solution)/shard_map/row_product/pallas_call | solution.py:197
  313.7 21.1 %mlp.6 = (bf16[1056,2048]{1,0:T(8,128)(2,1)}, bf16[1056,2048]{1,0:T(8,128)(2,1)}, bf16[528,1664]{1,0:T(8,128)(2,1)}, bf16[528,1664]{1,0:T(8,128)(2,1)}, f32[1,1024]{1,0:T(1,128)}) custom-call(bf16[528,1664]{1,0:T(8,128)(2,1)} %collective-permute-done.21.n0.refs_4_, bf16[528,1664]{1,0:T(8,128)(2,1)} %collective-permute-done.22.n1.refs_5_, ...), custom_call_target="tpu_custom_call" | custom-call | flops 323884154880 | bytes 780533760 | tf_op jit(solution)/shard_map/mlp/pallas_call | solution.py:197
  334.8 22.6 %mlp.7 = (bf16[1056,2048]{1,0:T(8,128)(2,1)}, bf16[1056,2048]{1,0:T(8,128)(2,1)}, bf16[528,1664]{1,0:T(8,128)(2,1)}, bf16[528,1664]{1,0:T(8,128)(2,1)}, f32[1,1024]{1,0:T(1,128)}) custom-call(bf16[528,1664]{1,0:T(8,128)(2,1)} %collective-permute-done.21.n0.refs_4_, ...), custom_call_target="tpu_custom_call", output_to_operand_aliasing={{0}: (9, {}), {1}: (10, {})} | custom-call | flops 323884154880 | bytes 1145487360 | tf_op jit(solution)/shard_map/mlp/pallas_call | solution.py:197
  358.0 15.8 %wgrad.4 = bf16[1024,1664]{1,0:T(8,128)(2,1)} custom-call(s32[2]{0:T(128)} %pad_add_fusion.3.index_ref, bf16[1056,2048]{1,0:T(8,128)(2,1)} %get-tuple-element.267.act_ref.refs_0_, bf16[1056,2048]{1,0:T(8,128)(2,1)} %get-tuple-element.271.refs_1_.act_ref, bf16[528,1664]{1,0:T(8,128)(2,1)} %get-tuple-element.219.c0.refs_2_.add_ref, ...), custom_call_target="tpu_custom_call" | custom-call | flops 215922769920 | bytes 442859520 | tf_op jit(solution)/shard_map/wgrad/pallas_call | solution.py:487
  379.0 3.1 add_convert_fusion.1
  383.9 16.0 %wgrad.5 = bf16[1024,1664]{1,0:T(8,128)(2,1)} custom-call(s32[2]{0:T(128)} %pad_add_fusion.2.index_ref, bf16[1056,2048]{1,0:T(8,128)(2,1)} %get-tuple-element.273.refs_0_, bf16[1056,2048]{1,0:T(8,128)(2,1)} %get-tuple-element.266.refs_1_, bf16[528,1664]{1,0:T(8,128)(2,1)} %get-tuple-element.240.n0.refs_2_, bf16[528,1664]{1,0:T(8,128)(2,1)} %copy-done.52, ...), custom_call_target="tpu_custom_call" | custom-call | flops 215922769920 | bytes 442859520 | tf_op jit(solution)/shard_map/wgrad/pallas_call | solution.py:487
  401.3 15.7 %wgrad.6 = bf16[1024,1664]{1,0:T(8,128)(2,1)} custom-call(s32[2]{0:T(128)} %pad_add_fusion.1.index_ref, bf16[1056,2048]{1,0:T(8,128)(2,1)} %get-tuple-element.267.act_ref.refs_0_, bf16[1056,2048]{1,0:T(8,128)(2,1)} %get-tuple-element.271.refs_1_.act_ref, bf16[528,1664]{1,0:T(8,128)(2,1)} %get-tuple-element.219.c0.refs_2_.add_ref, ...), custom_call_target="tpu_custom_call" | custom-call | flops 215922769920 | bytes 442859520 | tf_op jit(solution)/shard_map/wgrad/pallas_call | solution.py:487
  417.0 5.4 collective-permute-done.26.c_ref
  422.5 10.9 %norm_back.2 = (f32[528,1664]{1,0:T(8,128)}, bf16[528,1664]{1,0:T(8,128)(2,1)}, f32[8,1664]{1,0:T(8,128)}, f32[8,1664]{1,0:T(8,128)}, f32[8,1664]{1,0:T(8,128)}) custom-call(f32[528,1664]{1,0:T(8,128)} %get-tuple-element.312.x_ref.refs_0_, bf16[528,1664]{1,0:T(8,128)(2,1)} %get-tuple-element.269.a_ref, bf16[528,1664]{1,0:T(8,128)(2,1)} %collective-permute-done.23.b_ref, ...), custom_call_target="tpu_custom_call" | custom-call | bytes 479431680 | tf_op jit(solution)/shard_map/norm_back/pallas_call | solution.py:197
  433.3 13.4 %row_product.3 = (bf16[528,1664]{1,0:T(8,128)(2,1)}, bf16[528,1664]{1,0:T(8,128)(2,1)}) custom-call(bf16[1056,2048]{1,0:T(8,128)(2,1)} %get-tuple-element.271.refs_1_.act_ref, bf16[1024,1664]{1,0:T(8,128)(2,1)} %constant_dynamic-slice_fusion.8.down_ref.refs_0_, bf16[1024,1664]{1,0:T(8,128)(2,1)} %copy-done.4), custom_call_target="tpu_custom_call" | custom-call | flops 215922769920 | bytes 439664640 | tf_op jit(solution)/shard_map/row_product/pallas_call | solution.py:197
  449.0 15.9 %wgrad.7 = bf16[1024,1664]{1,0:T(8,128)(2,1)} custom-call(s32[2]{0:T(128)} %pad_add_fusion.index_ref, bf16[1056,2048]{1,0:T(8,128)(2,1)} %get-tuple-element.273.refs_0_, bf16[1056,2048]{1,0:T(8,128)(2,1)} %get-tuple-element.266.refs_1_, bf16[528,1664]{1,0:T(8,128)(2,1)} %get-tuple-element.240.n0.refs_2_, bf16[528,1664]{1,0:T(8,128)(2,1)} %copy-done.52, ...), custom_call_target="tpu_custom_call" | custom-call | flops 215922769920 | bytes 442859520 | tf_op jit(solution)/shard_map/wgrad/pallas_call | solution.py:487
  464.9 4.6 add_convert_fusion.5
  470.9 9.8 %attend_bwd.8 = (bf16[528,624]{1,0:T(8,128)(2,1)}, f32[1,624]{1,0:T(1,128)}, bf16[528,1664]{1,0:T(8,128)(2,1)}) custom-call(bf16[528,1664]{1,0:T(8,128)(2,1)} %get-tuple-element.332.g_ref.refs_12_, bf16[528,624]{1,0:T(8,128)(2,1)} %get-tuple-element.277.qkv_ref, f32[8,512]{1,0:T(8,128)} %get-tuple-element.278.lse_ref, f32[8,128]{1,0:T(8,128)} %get-tuple-element.279.lset_ref, ...), custom_call_target="tpu_custom_call" | custom-call | flops 52038205440 | bytes 228723840 | tf_op jit(solution)/shard_map/attend_bwd/pallas_call | solution.py:197
  482.5 9.7 %attend_bwd.9 = (bf16[528,624]{1,0:T(8,128)(2,1)}, f32[1,624]{1,0:T(1,128)}, bf16[528,1664]{1,0:T(8,128)(2,1)}) custom-call(bf16[528,1664]{1,0:T(8,128)(2,1)} %collective-permute-done.31.g_ref.refs_13_, bf16[528,624]{1,0:T(8,128)(2,1)} %get-tuple-element.285.qkv_ref, f32[8,512]{1,0:T(8,128)} %get-tuple-element.286.lse_ref, ...), custom_call_target="tpu_custom_call" | custom-call | flops 52038205440 | bytes 228723840 | tf_op jit(solution)/shard_map/attend_bwd/pallas_call | solution.py:197
  492.3 4.7 add_convert_fusion.7
  497.5 3.1 add_convert_fusion
  501.0 9.8 %attend_bwd.10 = (bf16[528,624]{1,0:T(8,128)(2,1)}, f32[1,624]{1,0:T(1,128)}, bf16[528,1664]{1,0:T(8,128)(2,1)}) custom-call(bf16[528,1664]{1,0:T(8,128)(2,1)} %collective-permute-done.29.g_ref.refs_14_, bf16[528,624]{1,0:T(8,128)(2,1)} %get-tuple-element.292.qkv_ref, f32[8,512]{1,0:T(8,128)} %get-tuple-element.293.lse_ref, ...), custom_call_target="tpu_custom_call" | custom-call | flops 52038205440 | bytes 228723840 | tf_op jit(solution)/shard_map/attend_bwd/pallas_call | solution.py:197
  518.0 10.0 %attend_bwd.11 = (bf16[528,624]{1,0:T(8,128)(2,1)}, f32[1,624]{1,0:T(1,128)}, bf16[528,1664]{1,0:T(8,128)(2,1)}) custom-call(bf16[528,1664]{1,0:T(8,128)(2,1)} %copy-done.53, bf16[528,624]{1,0:T(8,128)(2,1)} %get-tuple-element.298.qkv_ref, f32[8,512]{1,0:T(8,128)} %get-tuple-element.299.lse_ref, f32[8,128]{1,0:T(8,128)} %get-tuple-element.300.lset_ref, ...), custom_call_target="tpu_custom_call" | custom-call | flops 52038205440 | bytes 228723840 | tf_op jit(solution)/shard_map/attend_bwd/pallas_call | solution.py:197
  528.1 20.1 %attend_wgrad.2 = bf16[832,1664]{1,0:T(8,128)(2,1)} custom-call(bf16[528,624]{1,0:T(8,128)(2,1)} %get-tuple-element.302.refs_0_, bf16[528,624]{1,0:T(8,128)(2,1)} %get-tuple-element.303.refs_1_, bf16[528,624]{1,0:T(8,128)(2,1)} %get-tuple-element.304.refs_2_, bf16[528,624]{1,0:T(8,128)(2,1)} %get-tuple-element.305.refs_3_, ...), custom_call_target="tpu_custom_call" | custom-call | flops 175437250560 | bytes 610222080 | tf_op jit(solution)/shard_map/attend_wgrad/pallas_call | solution.py:197
  553.2 5.5 collective-permute-done.35.refs_3_
  558.6 5.8 unpack.2
  564.4 10.5 %attend_bwd.12 = (bf16[528,624]{1,0:T(8,128)(2,1)}, f32[1,624]{1,0:T(1,128)}, bf16[528,1664]{1,0:T(8,128)(2,1)}) custom-call(bf16[528,1664]{1,0:T(8,128)(2,1)} %copy-done.53, bf16[528,624]{1,0:T(8,128)(2,1)} %get-tuple-element.315.qkv_ref, f32[8,512]{1,0:T(8,128)} %get-tuple-element.316.lse_ref, f32[8,128]{1,0:T(8,128)} %get-tuple-element.317.lset_ref, ...), custom_call_target="tpu_custom_call" | custom-call | flops 52038205440 | bytes 281439360 | tf_op jit(solution)/shard_map/attend_bwd/pallas_call | solution.py:197
  576.9 10.2 %attend_bwd.13 = (bf16[528,624]{1,0:T(8,128)(2,1)}, f32[1,624]{1,0:T(1,128)}, bf16[528,1664]{1,0:T(8,128)(2,1)}) custom-call(bf16[528,1664]{1,0:T(8,128)(2,1)} %collective-permute-done.31.g_ref.refs_13_, bf16[528,624]{1,0:T(8,128)(2,1)} %get-tuple-element.321.qkv_ref, f32[8,512]{1,0:T(8,128)} %get-tuple-element.322.lse_ref, ...), custom_call_target="tpu_custom_call" | custom-call | flops 52038205440 | bytes 281439360 | tf_op jit(solution)/shard_map/attend_bwd/pallas_call | solution.py:197
  589.9 7.8 collective-permute-done.38
  600.1 10.7 %attend_bwd.14 = (bf16[528,624]{1,0:T(8,128)(2,1)}, f32[1,624]{1,0:T(1,128)}, bf16[528,1664]{1,0:T(8,128)(2,1)}) custom-call(bf16[528,1664]{1,0:T(8,128)(2,1)} %collective-permute-done.29.g_ref.refs_14_, bf16[528,624]{1,0:T(8,128)(2,1)} %get-tuple-element.327.qkv_ref, f32[8,512]{1,0:T(8,128)} %get-tuple-element.328.lse_ref, ...), custom_call_target="tpu_custom_call" | custom-call | flops 52038205440 | bytes 334154880 | tf_op jit(solution)/shard_map/attend_bwd/pallas_call | solution.py:197
  610.8 2.8 fusion
  614.3 10.3 %attend_bwd.15 = (bf16[528,624]{1,0:T(8,128)(2,1)}, f32[1,624]{1,0:T(1,128)}, bf16[528,1664]{1,0:T(8,128)(2,1)}) custom-call(bf16[528,1664]{1,0:T(8,128)(2,1)} %get-tuple-element.332.g_ref.refs_12_, bf16[528,624]{1,0:T(8,128)(2,1)} %get-tuple-element.333.qkv_ref, f32[8,512]{1,0:T(8,128)} %get-tuple-element.334.lse_ref, ...), custom_call_target="tpu_custom_call" | custom-call | flops 52038205440 | bytes 281439360 | tf_op jit(solution)/shard_map/attend_bwd/pallas_call | solution.py:197
  639.1 2.8 constant_dynamic-update-slice_fusion.6.refs_0_
  641.8 20.1 %attend_wgrad.3 = bf16[832,1664]{1,0:T(8,128)(2,1)} custom-call(bf16[528,624]{1,0:T(8,128)(2,1)} %get-tuple-element.341.refs_0_, bf16[528,624]{1,0:T(8,128)(2,1)} %get-tuple-element.342.refs_1_, bf16[528,624]{1,0:T(8,128)(2,1)} %get-tuple-element.343.refs_2_, bf16[528,624]{1,0:T(8,128)(2,1)} %get-tuple-element.344.refs_3_, ...), custom_call_target="tpu_custom_call" | custom-call | flops 175437250560 | bytes 610222080 | tf_op jit(solution)/shard_map/attend_wgrad/pallas_call | solution.py:197
  673.6 9.0 %place.2 = f32[2048,1664]{1,0:T(8,128)} custom-call(s32[8]{0:T(128)} %stack.131.at_ref, bf16[1024,1664]{1,0:T(8,128)(2,1)} %constant_dynamic-update-slice_fusion.6.refs_0_, bf16[1024,1664]{1,0:T(8,128)(2,1)} %collective-permute-done.45.refs_1_), custom_call_target="tpu_custom_call" | custom-call | bytes 613417920 | tf_op jit(solution)/shard_map/place/pallas_call | solution.py:197
  683.1 9.9 %norm_back.3 = (f32[8,1664]{1,0:T(8,128)}, bf16[528,1664]{1,0:T(8,128)(2,1)}, f32[8,1664]{1,0:T(8,128)}, f32[8,1664]{1,0:T(8,128)}, f32[8,1664]{1,0:T(8,128)}) custom-call(bf16[528,1664]{1,0:T(8,128)(2,1)} %get-tuple-element.354.x_ref, bf16[528,1664]{1,0:T(8,128)(2,1)} %get-tuple-element.336.a_ref, bf16[528,1664]{1,0:T(8,128)(2,1)} %collective-permute-done.40.b_ref, ...), custom_call_target="tpu_custom_call" | custom-call | bytes 375598080 | tf_op jit(solution)/shard_map/norm_back/pallas_call | solution.py:197
  695.7 4.6 collective-permute-done.48
  702.8 2.8 unpack.3
  715.7 21.4 %collective-permute-done.53 = bf16[512,1664]{1,0:T(8,128)(2,1)S(1)} collective-permute-done((bf16[512,1664]{1,0:T(8,128)(2,1)}, bf16[512,1664]{1,0:T(8,128)(2,1)S(1)}, u32[]{:S(2)}, u32[]{:S(2)}) %collective-permute-start.53) | collective-permute-done | bytes 1703968 | tf_op jit(solution)/shard_map/ppermute | solution.py:654
  739.3 12.6 %collective-permute-done.55 = bf16[208,1664]{1,0:T(8,128)(2,1)S(1)} collective-permute-done((bf16[208,1664]{1,0:T(8,128)(2,1)S(1)}, bf16[208,1664]{1,0:T(8,128)(2,1)S(1)}, u32[]{:S(2)}, u32[]{:S(2)}) %collective-permute-start.55) | collective-permute-done | bytes 692256 | tf_op jit(solution)/shard_map/ppermute | solution.py:654
  753.7 12.7 %collective-permute-done.57 = bf16[208,1664]{1,0:T(8,128)(2,1)S(1)} collective-permute-done((bf16[208,1664]{1,0:T(8,128)(2,1)S(1)}, bf16[208,1664]{1,0:T(8,128)(2,1)S(1)}, u32[]{:S(2)}, u32[]{:S(2)}) %collective-permute-start.57) | collective-permute-done | bytes 692256 | tf_op jit(solution)/shard_map/ppermute | solution.py:654
  768.4 10.8 %place.3 = f32[1664,2048]{1,0:T(8,128)} custom-call(s32[8]{0:T(128)} %stack.142.at_ref, bf16[1024,1664]{1,0:T(8,128)(2,1)} %constant_dynamic-update-slice_fusion.12.refs_0_, bf16[1024,1664]{1,0:T(8,128)(2,1)} %collective-permute-done.58.refs_1_), custom_call_target="tpu_custom_call" | custom-call | bytes 613417920 | tf_op jit(solution)/shard_map/place/pallas_call | solution.py:197
  787.1 7.9 place_heads.1
  (339 shorter events, 170.4 us)
Async XLA Ops:
  11.7 27.7 %collective-permute-start.1 = (bf16[528,1664]{1,0:T(8,128)(2,1)}, bf16[528,1664]{1,0:T(8,128)(2,1)}, u32[]{:S(2)}, u32[]{:S(2)}) collective-permute-start(bf16[528,1664]{1,0:T(8,128)(2,1)} %get-tuple-element.226.n_ref.refs_8_), channel_id=1, source_target_pairs={{0,4},{1,5},{2,6},{3,7},{4,0},{5,1},{6,2},{7,3},{8,12},{9,13},{10,... | collective-permute-start | bytes 5271560 | tf_op jit(solution)/shard_map/ppermute | solution.py:654
  12.1 56.9 %collective-permute-start = (bf16[528,1664]{1,0:T(8,128)(2,1)}, bf16[528,1664]{1,0:T(8,128)(2,1)}, u32[]{:S(2)}, u32[]{:S(2)}) collective-permute-start(bf16[528,1664]{1,0:T(8,128)(2,1)} %get-tuple-element.226.n_ref.refs_8_), channel_id=1, source_target_pairs={{0,1},{1,0},{2,3},{3,2},{4,5},{5,4},{6,7},{7,6},{8,9},{9,8},{10,11... | collective-permute-start | bytes 5271560 | tf_op jit(solution)/shard_map/ppermute | solution.py:654
  16.1 52.0 %collective-permute-start.2 = (bf16[208,1664]{1,0:T(8,128)(2,1)S(1)}, bf16[208,1664]{1,0:T(8,128)(2,1)S(1)}, u32[]{:S(2)}, u32[]{:S(2)}) collective-permute-start(bf16[208,1664]{1,0:T(8,128)(2,1)S(1)} %get-tuple-element.394), channel_id=1, source_target_pairs={{0,2},{1,3},{2,0},{3,1},{4,6},{5,7},{6,4},{7,5},{8,10},{9,11},{10,... | collective-permute-start | bytes 2076680 | tf_op jit(solution)/shard_map/ppermute | solution.py:654
  37.2 80.3 %collective-permute-start.8 = (f32[1440]{0:T(1024)}, f32[1440]{0:T(1024)}, u32[]{:S(2)}, u32[]{:S(2)}) collective-permute-start(f32[1440]{0:T(1024)} %pad_maximum_fusion.1), channel_id=1, source_target_pairs={{0,2},{1,3},{2,0},{3,1},{4,6},{5,7},{6,4},{7,5},{8,10},{9,11},{10,... | collective-permute-start | bytes 17288 | tf_op jit(solution)/shard_map/ppermute | solution.py:654
  69.0 12.3 %collective-permute-start.3 = (bf16[528,1664]{1,0:T(8,128)(2,1)}, bf16[528,1664]{1,0:T(8,128)(2,1)S(1)}, u32[]{:S(2)}, u32[]{:S(2)}) collective-permute-start(bf16[528,1664]{1,0:T(8,128)(2,1)} %collective-permute-done.n_ref.refs_10_), channel_id=1, source_target_pairs={{0,4},{1,5},{2,6},{3,7},{4,0},{5,1},{6,2},{7,3},{8,12},{9,13},{10,... | collective-permute-start | bytes 5271560 | tf_op jit(solution)/shard_map/ppermute | solution.py:654
  77.9 18.4 %collective-permute-start.5 = (bf16[208,1664]{1,0:T(8,128)(2,1)S(1)}, bf16[208,1664]{1,0:T(8,128)(2,1)}, u32[]{:S(2)}, u32[]{:S(2)}) collective-permute-start(bf16[208,1664]{1,0:T(8,128)(2,1)S(1)} %collective-permute-done.2), channel_id=1, source_target_pairs={{0,8},{1,9},{2,10},{3,11},{4,12},{5,13},{6,14},{7,15},{8,0},{9,1},... | collective-permute-start | bytes 2076680 | tf_op jit(solution)/shard_map/ppermute | solution.py:654
  79.5 32.6 %collective-permute-start.6 = (bf16[208,1664]{1,0:T(8,128)(2,1)S(1)}, bf16[208,1664]{1,0:T(8,128)(2,1)}, u32[]{:S(2)}, u32[]{:S(2)}) collective-permute-start(bf16[208,1664]{1,0:T(8,128)(2,1)S(1)} %collective-permute-done.2), channel_id=1, source_target_pairs={{0,16},{1,17},{2,18},{3,19},{4,20},{5,21},{6,22},{7,23},{8,24},{9,... | collective-permute-start | bytes 2076680 | tf_op jit(solution)/shard_map/ppermute | solution.py:654
  81.1 34.5 %collective-permute-start.7 = (bf16[208,1664]{1,0:T(8,128)(2,1)S(1)}, bf16[208,1664]{1,0:T(8,128)(2,1)}, u32[]{:S(2)}, u32[]{:S(2)}) collective-permute-start(bf16[208,1664]{1,0:T(8,128)(2,1)S(1)} %collective-permute-done.2), channel_id=1, source_target_pairs={{0,24},{1,25},{2,26},{3,27},{4,28},{5,29},{6,30},{7,31},{8,16},{9,... | collective-permute-start | bytes 2076680 | tf_op jit(solution)/shard_map/ppermute | solution.py:654
  81.4 46.8 %collective-permute-start.9 = (bf16[528,1664]{1,0:T(8,128)(2,1)}, bf16[528,1664]{1,0:T(8,128)(2,1)}, u32[]{:S(2)}, u32[]{:S(2)}) collective-permute-start(bf16[528,1664]{1,0:T(8,128)(2,1)} %get-tuple-element.219.c0.refs_2_.add_ref), channel_id=1, source_target_pairs={{0,4},{1,5},{2,6},{3,7},{4,0},{5,1},{6,2},{7,3},{8,12},{9,13},{10,... | collective-permute-start | bytes 5271560 | tf_op jit(solution)/shard_map/ppermute | solution.py:654
  96.2 22.1 %copy-start.41 = (f32[208]{0:T(256)S(1)}, f32[208]{0:T(256)}, u32[]{:S(2)}) copy-start(f32[208]{0:T(256)} %copy-done.40) | copy-start | bytes 2500
  96.3 66.6 %collective-permute-start.12 = (bf16[528,1664]{1,0:T(8,128)(2,1)}, bf16[528,1664]{1,0:T(8,128)(2,1)}, u32[]{:S(2)}, u32[]{:S(2)}) collective-permute-start(bf16[528,1664]{1,0:T(8,128)(2,1)} %get-tuple-element.219.c0.refs_2_.add_ref), channel_id=1, source_target_pairs={{0,1},{1,0},{2,3},{3,2},{4,5},{5,4},{6,7},{7,6},{8,9},{9,8},{10,11... | collective-permute-start | bytes 5271560 | tf_op jit(solution)/shard_map/ppermute | solution.py:654
  112.1 50.8 %collective-permute-start.13 = (bf16[1664,256]{1,0:T(8,128)(2,1)}, bf16[1664,256]{1,0:T(8,128)(2,1)}, u32[]{:S(2)}, u32[]{:S(2)}) collective-permute-start(bf16[1664,256]{1,0:T(8,128)(2,1)} %constant_dynamic-slice_fusion.11), channel_id=1, source_target_pairs={{0,2},{1,3},{2,0},{3,1},{4,6},{5,7},{6,4},{7,5},{8,10},{9,11},{10,... | collective-permute-start | bytes 2555912 | tf_op jit(solution)/shard_map/ppermute | solution.py:654
  115.6 71.7 %collective-permute-start.4 = (bf16[256,1664]{1,0:T(8,128)(2,1)}, bf16[256,1664]{1,0:T(8,128)(2,1)}, u32[]{:S(2)}, u32[]{:S(2)}) collective-permute-start(bf16[256,1664]{1,0:T(8,128)(2,1)} %constant_dynamic-slice_fusion.10), channel_id=1, source_target_pairs={{0,2},{1,3},{2,0},{3,1},{4,6},{5,7},{6,4},{7,5},{8,10},{9,11},{10,... | collective-permute-start | bytes 2555912 | tf_op jit(solution)/shard_map/ppermute | solution.py:654
  128.2 9.6 %collective-permute-start.10 = (bf16[528,1664]{1,0:T(8,128)(2,1)}, bf16[528,1664]{1,0:T(8,128)(2,1)S(1)}, u32[]{:S(2)}, u32[]{:S(2)}) collective-permute-start(bf16[528,1664]{1,0:T(8,128)(2,1)} %get-tuple-element.218), channel_id=1, source_target_pairs={{0,4},{1,5},{2,6},{3,7},{4,0},{5,1},{6,2},{7,3},{8,12},{9,13},{10,... | collective-permute-start | bytes 5271560 | tf_op jit(solution)/shard_map/ppermute | solution.py:654
  137.3 25.6 %collective-permute-start.11 = (bf16[528,1664]{1,0:T(8,128)(2,1)}, bf16[528,1664]{1,0:T(8,128)(2,1)S(1)}, u32[]{:S(2)}, u32[]{:S(2)}) collective-permute-start(bf16[528,1664]{1,0:T(8,128)(2,1)} %get-tuple-element.221), channel_id=1, source_target_pairs={{0,4},{1,5},{2,6},{3,7},{4,0},{5,1},{6,2},{7,3},{8,12},{9,13},{10,... | collective-permute-start | bytes 5271560 | tf_op jit(solution)/shard_map/ppermute | solution.py:654
  149.1 62.4 %collective-permute-start.17 = (bf16[528,1664]{1,0:T(8,128)(2,1)}, bf16[528,1664]{1,0:T(8,128)(2,1)S(1)}, u32[]{:S(2)}, u32[]{:S(2)}) collective-permute-start(bf16[528,1664]{1,0:T(8,128)(2,1)} %get-tuple-element.223), channel_id=1, source_target_pairs={{0,1},{1,0},{2,3},{3,2},{4,5},{5,4},{6,7},{7,6},{8,9},{9,8},{10,11... | collective-permute-start | bytes 5271560 | tf_op jit(solution)/shard_map/ppermute | solution.py:654
  162.9 45.9 %collective-permute-start.16 = (bf16[528,1664]{1,0:T(8,128)(2,1)}, bf16[528,1664]{1,0:T(8,128)(2,1)}, u32[]{:S(2)}, u32[]{:S(2)}) collective-permute-start(bf16[528,1664]{1,0:T(8,128)(2,1)} %collective-permute-done.12.c0.refs_4_), channel_id=1, source_target_pairs={{0,4},{1,5},{2,6},{3,7},{4,0},{5,1},{6,2},{7,3},{8,12},{9,13},{10,... | collective-permute-start | bytes 5271560 | tf_op jit(solution)/shard_map/ppermute | solution.py:654
  172.7 29.1 %collective-permute-start.14 = (bf16[1664,256]{1,0:T(8,128)(2,1)}, bf16[1664,256]{1,0:T(8,128)(2,1)S(1)}, u32[]{:S(2)}, u32[]{:S(2)}) collective-permute-start(bf16[1664,256]{1,0:T(8,128)(2,1)} %collective-permute-done.13), channel_id=1, source_target_pairs={{0,8},{1,9},{2,10},{3,11},{4,12},{5,13},{6,14},{7,15},{8,0},{9,1},... | collective-permute-start | bytes 2555912 | tf_op jit(solution)/shard_map/ppermute | solution.py:654
  187.3 20.5 %collective-permute-start.15 = (bf16[256,1664]{1,0:T(8,128)(2,1)}, bf16[256,1664]{1,0:T(8,128)(2,1)S(1)}, u32[]{:S(2)}, u32[]{:S(2)}) collective-permute-start(bf16[256,1664]{1,0:T(8,128)(2,1)} %collective-permute-done.4), channel_id=1, source_target_pairs={{0,16},{1,17},{2,18},{3,19},{4,20},{5,21},{6,22},{7,23},{8,24},{9,... | collective-permute-start | bytes 2555912 | tf_op jit(solution)/shard_map/ppermute | solution.py:654
  221.2 10.3 %collective-permute-start.18 = (bf16[528,1664]{1,0:T(8,128)(2,1)}, bf16[528,1664]{1,0:T(8,128)(2,1)S(1)}, u32[]{:S(2)}, u32[]{:S(2)}) collective-permute-start(bf16[528,1664]{1,0:T(8,128)(2,1)} %get-tuple-element.240.n0.refs_2_), channel_id=1, source_target_pairs={{0,4},{1,5},{2,6},{3,7},{4,0},{5,1},{6,2},{7,3},{8,12},{9,13},{10,... | collective-permute-start | bytes 5271560 | tf_op jit(solution)/shard_map/ppermute | solution.py:654
  226.8 39.9 %collective-permute-start.19 = (bf16[1664,512]{1,0:T(8,128)(2,1)}, bf16[1664,512]{1,0:T(8,128)(2,1)}, u32[]{:S(2)}, u32[]{:S(2)}) collective-permute-start(bf16[1664,512]{1,0:T(8,128)(2,1)} %constant_dynamic-update-slice_fusion), channel_id=1, source_target_pairs={{0,16},{1,17},{2,18},{3,19},{4,20},{5,21},{6,22},{7,23},{8,24},{9,... | collective-permute-start | bytes 5111816 | tf_op jit(solution)/shard_map/ppermute | solution.py:654
  228.4 44.4 %collective-permute-start.20 = (bf16[512,1664]{1,0:T(8,128)(2,1)}, bf16[512,1664]{1,0:T(8,128)(2,1)}, u32[]{:S(2)}, u32[]{:S(2)}) collective-permute-start(bf16[512,1664]{1,0:T(8,128)(2,1)} %constant_dynamic-update-slice_fusion.2), channel_id=1, source_target_pairs={{0,8},{1,9},{2,10},{3,11},{4,12},{5,13},{6,14},{7,15},{8,0},{9,1},... | collective-permute-start | bytes 5111816 | tf_op jit(solution)/shard_map/ppermute | solution.py:654
  229.7 69.9 %collective-permute-start.21 = (bf16[528,1664]{1,0:T(8,128)(2,1)}, bf16[528,1664]{1,0:T(8,128)(2,1)}, u32[]{:S(2)}, u32[]{:S(2)}) collective-permute-start(bf16[528,1664]{1,0:T(8,128)(2,1)} %get-tuple-element.240.n0.refs_2_), channel_id=1, source_target_pairs={{0,1},{1,0},{2,3},{3,2},{4,5},{5,4},{6,7},{7,6},{8,9},{9,8},{10,11... | collective-permute-start | bytes 5271560 | tf_op jit(solution)/shard_map/ppermute | solution.py:654
  299.6 14.1 %collective-permute-start.22 = (bf16[528,1664]{1,0:T(8,128)(2,1)}, bf16[528,1664]{1,0:T(8,128)(2,1)}, u32[]{:S(2)}, u32[]{:S(2)}) collective-permute-start(bf16[528,1664]{1,0:T(8,128)(2,1)} %collective-permute-done.21.n0.refs_4_), channel_id=1, source_target_pairs={{0,4},{1,5},{2,6},{3,7},{4,0},{5,1},{6,2},{7,3},{8,12},{9,13},{10,... | collective-permute-start | bytes 5271560 | tf_op jit(solution)/shard_map/ppermute | solution.py:654
  313.2 21.6 %collective-permute-start.24 = (bf16[528,1664]{1,0:T(8,128)(2,1)}, bf16[528,1664]{1,0:T(8,128)(2,1)}, u32[]{:S(2)}, u32[]{:S(2)}) collective-permute-start(bf16[528,1664]{1,0:T(8,128)(2,1)} %get-tuple-element.249), channel_id=1, source_target_pairs={{0,4},{1,5},{2,6},{3,7},{4,0},{5,1},{6,2},{7,3},{8,12},{9,13},{10,... | collective-permute-start | bytes 5271560 | tf_op jit(solution)/shard_map/ppermute | solution.py:654
  313.7 21.1 %collective-permute-start.23 = (bf16[528,1664]{1,0:T(8,128)(2,1)}, bf16[528,1664]{1,0:T(8,128)(2,1)}, u32[]{:S(2)}, u32[]{:S(2)}) collective-permute-start(bf16[528,1664]{1,0:T(8,128)(2,1)} %get-tuple-element.253), channel_id=1, source_target_pairs={{0,4},{1,5},{2,6},{3,7},{4,0},{5,1},{6,2},{7,3},{8,12},{9,13},{10,... | collective-permute-start | bytes 5271560 | tf_op jit(solution)/shard_map/ppermute | solution.py:654
  357.4 21.6 %collective-permute-start.25 = (bf16[528,1664]{1,0:T(8,128)(2,1)}, bf16[528,1664]{1,0:T(8,128)(2,1)}, u32[]{:S(2)}, u32[]{:S(2)}) collective-permute-start(bf16[528,1664]{1,0:T(8,128)(2,1)} %get-tuple-element.264), channel_id=1, source_target_pairs={{0,4},{1,5},{2,6},{3,7},{4,0},{5,1},{6,2},{7,3},{8,12},{9,13},{10,... | collective-permute-start | bytes 5271560 | tf_op jit(solution)/shard_map/ppermute | solution.py:654
  358.0 21.0 %copy-start.17 = (bf16[528,1664]{1,0:T(8,128)(2,1)S(1)}, bf16[528,1664]{1,0:T(8,128)(2,1)}, u32[]{:S(2)}) copy-start(bf16[528,1664]{1,0:T(8,128)(2,1)} %get-tuple-element.263) | copy-start | bytes 5271556
  373.9 91.0 %collective-permute-start.28 = (bf16[1024,1664]{1,0:T(8,128)(2,1)}, bf16[1024,1664]{1,0:T(8,128)(2,1)}, u32[]{:S(2)}, u32[]{:S(2)}) collective-permute-start(bf16[1024,1664]{1,0:T(8,128)(2,1)} %wgrad.4), channel_id=1, source_target_pairs={{0,16},{1,17},{2,18},{3,19},{4,20},{5,21},{6,22},{7,23},{8,24},{9,... | collective-permute-start | bytes 10223624 | tf_op jit(solution)/shard_map/ppermute | solution.py:654
  382.1 40.3 %collective-permute-start.26 = (bf16[528,1664]{1,0:T(8,128)(2,1)}, bf16[528,1664]{1,0:T(8,128)(2,1)}, u32[]{:S(2)}, u32[]{:S(2)}) collective-permute-start(bf16[528,1664]{1,0:T(8,128)(2,1)} %add_convert_fusion.1), channel_id=1, source_target_pairs={{0,1},{1,0},{2,3},{3,2},{4,5},{5,4},{6,7},{7,6},{8,9},{9,8},{10,11... | collective-permute-start | bytes 5271560 | tf_op jit(solution)/shard_map/ppermute | solution.py:654
  399.9 92.3 %collective-permute-start.27 = (bf16[1024,1664]{1,0:T(8,128)(2,1)}, bf16[1024,1664]{1,0:T(8,128)(2,1)}, u32[]{:S(2)}, u32[]{:S(2)}) collective-permute-start(bf16[1024,1664]{1,0:T(8,128)(2,1)} %wgrad.5), channel_id=1, source_target_pairs={{0,8},{1,9},{2,10},{3,11},{4,12},{5,13},{6,14},{7,15},{8,0},{9,1},... | collective-permute-start | bytes 10223624 | tf_op jit(solution)/shard_map/ppermute | solution.py:654
  446.8 50.8 %collective-permute-start.32 = (bf16[528,1664]{1,0:T(8,128)(2,1)}, bf16[528,1664]{1,0:T(8,128)(2,1)}, u32[]{:S(2)}, u32[]{:S(2)}) collective-permute-start(bf16[528,1664]{1,0:T(8,128)(2,1)} %get-tuple-element.272), channel_id=1, source_target_pairs={{0,4},{1,5},{2,6},{3,7},{4,0},{5,1},{6,2},{7,3},{8,12},{9,13},{10,... | collective-permute-start | bytes 5271560 | tf_op jit(solution)/shard_map/ppermute | solution.py:654
  446.8 35.8 %collective-permute-start.31 = (bf16[528,1664]{1,0:T(8,128)(2,1)}, bf16[528,1664]{1,0:T(8,128)(2,1)}, u32[]{:S(2)}, u32[]{:S(2)}) collective-permute-start(bf16[528,1664]{1,0:T(8,128)(2,1)} %get-tuple-element.332.g_ref.refs_12_), channel_id=1, source_target_pairs={{0,4},{1,5},{2,6},{3,7},{4,0},{5,1},{6,2},{7,3},{8,12},{9,13},{10,... | collective-permute-start | bytes 5271560 | tf_op jit(solution)/shard_map/ppermute | solution.py:654
  447.3 53.7 %collective-permute-start.29 = (bf16[528,1664]{1,0:T(8,128)(2,1)}, bf16[528,1664]{1,0:T(8,128)(2,1)}, u32[]{:S(2)}, u32[]{:S(2)}) collective-permute-start(bf16[528,1664]{1,0:T(8,128)(2,1)} %get-tuple-element.332.g_ref.refs_12_), channel_id=1, source_target_pairs={{0,1},{1,0},{2,3},{3,2},{4,5},{5,4},{6,7},{7,6},{8,9},{9,8},{10,11... | collective-permute-start | bytes 5271560 | tf_op jit(solution)/shard_map/ppermute | solution.py:654
  469.5 42.3 %collective-permute-start.33 = (bf16[512,1664]{1,0:T(8,128)(2,1)}, bf16[512,1664]{1,0:T(8,128)(2,1)}, u32[]{:S(2)}, u32[]{:S(2)}) collective-permute-start(bf16[512,1664]{1,0:T(8,128)(2,1)} %bitcast.22), channel_id=1, source_target_pairs={{0,8},{1,9},{2,10},{3,11},{4,12},{5,13},{6,14},{7,15},{8,0},{9,1},... | collective-permute-start | bytes 5111816 | tf_op jit(solution)/shard_map/ppermute | solution.py:654
  496.9 54.4 %collective-permute-start.34 = (bf16[512,1664]{1,0:T(8,128)(2,1)}, bf16[512,1664]{1,0:T(8,128)(2,1)}, u32[]{:S(2)}, u32[]{:S(2)}) collective-permute-start(bf16[512,1664]{1,0:T(8,128)(2,1)} %bitcast.26), channel_id=1, source_target_pairs={{0,16},{1,17},{2,18},{3,19},{4,20},{5,21},{6,22},{7,23},{8,24},{9,... | collective-permute-start | bytes 5111816 | tf_op jit(solution)/shard_map/ppermute | solution.py:654
  500.6 58.0 %collective-permute-start.35 = (bf16[528,1664]{1,0:T(8,128)(2,1)}, bf16[528,1664]{1,0:T(8,128)(2,1)}, u32[]{:S(2)}, u32[]{:S(2)}) collective-permute-start(bf16[528,1664]{1,0:T(8,128)(2,1)} %add_convert_fusion), channel_id=1, source_target_pairs={{0,1},{1,0},{2,3},{3,2},{4,5},{5,4},{6,7},{7,6},{8,9},{9,8},{10,11... | collective-permute-start | bytes 5271560 | tf_op jit(solution)/shard_map/ppermute | solution.py:654
  501.0 15.8 %collective-permute-start.30 = (bf16[528,1664]{1,0:T(8,128)(2,1)}, bf16[528,1664]{1,0:T(8,128)(2,1)S(1)}, u32[]{:S(2)}, u32[]{:S(2)}) collective-permute-start(bf16[528,1664]{1,0:T(8,128)(2,1)} %collective-permute-done.29.g_ref.refs_14_), channel_id=1, source_target_pairs={{0,4},{1,5},{2,6},{3,7},{4,0},{5,1},{6,2},{7,3},{8,12},{9,13},{10,... | collective-permute-start | bytes 5271560 | tf_op jit(solution)/shard_map/ppermute | solution.py:654
  515.1 59.8 %collective-permute-start.36 = (bf16[256,1664]{1,0:T(8,128)(2,1)}, bf16[256,1664]{1,0:T(8,128)(2,1)}, u32[]{:S(2)}, u32[]{:S(2)}) collective-permute-start(bf16[256,1664]{1,0:T(8,128)(2,1)} %get-tuple-element.406), channel_id=1, source_target_pairs={{0,2},{1,3},{2,0},{3,1},{4,6},{5,7},{6,4},{7,5},{8,10},{9,11},{10,... | collective-permute-start | bytes 2555912 | tf_op jit(solution)/shard_map/ppermute | solution.py:654
  550.9 60.0 %collective-permute-start.37 = (bf16[416,1664]{1,0:T(8,128)(2,1)}, bf16[416,1664]{1,0:T(8,128)(2,1)}, u32[]{:S(2)}, u32[]{:S(2)}) collective-permute-start(bf16[416,1664]{1,0:T(8,128)(2,1)} %constant_dynamic-slice_fusion.6), channel_id=1, source_target_pairs={{0,16},{1,17},{2,18},{3,19},{4,20},{5,21},{6,22},{7,23},{8,24},{9,... | collective-permute-start | bytes 4153352 | tf_op jit(solution)/shard_map/ppermute | solution.py:654
  574.9 25.2 %collective-permute-start.39 = (bf16[528,1664]{1,0:T(8,128)(2,1)}, bf16[528,1664]{1,0:T(8,128)(2,1)}, u32[]{:S(2)}, u32[]{:S(2)}) collective-permute-start(bf16[528,1664]{1,0:T(8,128)(2,1)} %get-tuple-element.318), channel_id=1, source_target_pairs={{0,4},{1,5},{2,6},{3,7},{4,0},{5,1},{6,2},{7,3},{8,12},{9,13},{10,... | collective-permute-start | bytes 5271560 | tf_op jit(solution)/shard_map/ppermute | solution.py:654
  576.3 21.4 %collective-permute-start.38 = (bf16[256,1664]{1,0:T(8,128)(2,1)S(1)}, bf16[256,1664]{1,0:T(8,128)(2,1)S(1)}, u32[]{:S(2)}, u32[]{:S(2)}) collective-permute-start(bf16[256,1664]{1,0:T(8,128)(2,1)S(1)} %add_convert_fusion.9), channel_id=1, source_target_pairs={{0,8},{1,9},{2,10},{3,11},{4,12},{5,13},{6,14},{7,15},{8,0},{9,1},... | collective-permute-start | bytes 2555912 | tf_op jit(solution)/shard_map/ppermute | solution.py:654
  587.1 27.2 %collective-permute-start.40 = (bf16[528,1664]{1,0:T(8,128)(2,1)}, bf16[528,1664]{1,0:T(8,128)(2,1)}, u32[]{:S(2)}, u32[]{:S(2)}) collective-permute-start(bf16[528,1664]{1,0:T(8,128)(2,1)} %get-tuple-element.324), channel_id=1, source_target_pairs={{0,4},{1,5},{2,6},{3,7},{4,0},{5,1},{6,2},{7,3},{8,12},{9,13},{10,... | collective-permute-start | bytes 5271560 | tf_op jit(solution)/shard_map/ppermute | solution.py:654
  588.7 39.7 %collective-permute-start.41 = (bf16[256,1664]{1,0:T(8,128)(2,1)}, bf16[256,1664]{1,0:T(8,128)(2,1)}, u32[]{:S(2)}, u32[]{:S(2)}) collective-permute-start(bf16[256,1664]{1,0:T(8,128)(2,1)} %get-tuple-element.404), channel_id=1, source_target_pairs={{0,2},{1,3},{2,0},{3,1},{4,6},{5,7},{6,4},{7,5},{8,10},{9,11},{10,... | collective-permute-start | bytes 2555912 | tf_op jit(solution)/shard_map/ppermute | solution.py:654
  598.7 40.4 %collective-permute-start.43 = (bf16[512,1664]{1,0:T(8,128)(2,1)}, bf16[512,1664]{1,0:T(8,128)(2,1)}, u32[]{:S(2)}, u32[]{:S(2)}) collective-permute-start(bf16[512,1664]{1,0:T(8,128)(2,1)} %constant_dynamic-update-slice_fusion.4), channel_id=1, source_target_pairs={{0,16},{1,17},{2,18},{3,19},{4,20},{5,21},{6,22},{7,23},{8,24},{9,... | collective-permute-start | bytes 5111816 | tf_op jit(solution)/shard_map/ppermute | solution.py:654
  610.8 71.8 %collective-permute-start.46 = (bf16[528,1664]{1,0:T(8,128)(2,1)}, bf16[528,1664]{1,0:T(8,128)(2,1)}, u32[]{:S(2)}, u32[]{:S(2)}) collective-permute-start(bf16[528,1664]{1,0:T(8,128)(2,1)} %get-tuple-element.330), channel_id=1, source_target_pairs={{0,1},{1,0},{2,3},{3,2},{4,5},{5,4},{6,7},{7,6},{8,9},{9,8},{10,11... | collective-permute-start | bytes 5271560 | tf_op jit(solution)/shard_map/ppermute | solution.py:654
  613.6 18.7 %collective-permute-start.42 = (bf16[208,1664]{1,0:T(8,128)(2,1)}, bf16[208,1664]{1,0:T(8,128)(2,1)}, u32[]{:S(2)}, u32[]{:S(2)}) collective-permute-start(bf16[208,1664]{1,0:T(8,128)(2,1)} %get-tuple-element.408), channel_id=1, source_target_pairs={{0,8},{1,9},{2,10},{3,11},{4,12},{5,13},{6,14},{7,15},{8,0},{9,1},... | collective-permute-start | bytes 2076680 | tf_op jit(solution)/shard_map/ppermute | solution.py:654
  630.7 38.4 %collective-permute-start.44 = (bf16[256,1664]{1,0:T(8,128)(2,1)}, bf16[256,1664]{1,0:T(8,128)(2,1)}, u32[]{:S(2)}, u32[]{:S(2)}) collective-permute-start(bf16[256,1664]{1,0:T(8,128)(2,1)} %add_convert_fusion.8), channel_id=1, source_target_pairs={{0,16},{1,17},{2,18},{3,19},{4,20},{5,21},{6,22},{7,23},{8,24},{9,... | collective-permute-start | bytes 2555912 | tf_op jit(solution)/shard_map/ppermute | solution.py:654
  634.4 61.2 %collective-permute-start.50 = (bf16[208,1664]{1,0:T(8,128)(2,1)}, bf16[208,1664]{1,0:T(8,128)(2,1)}, u32[]{:S(2)}, u32[]{:S(2)}) collective-permute-start(bf16[208,1664]{1,0:T(8,128)(2,1)} %add_convert_fusion.11), channel_id=1, source_target_pairs={{0,2},{1,3},{2,0},{3,1},{4,6},{5,7},{6,4},{7,5},{8,10},{9,11},{10,... | collective-permute-start | bytes 2076680 | tf_op jit(solution)/shard_map/ppermute | solution.py:654
  641.8 30.2 %collective-permute-start.45 = (bf16[1024,1664]{1,0:T(8,128)(2,1)}, bf16[1024,1664]{1,0:T(8,128)(2,1)}, u32[]{:S(2)}, u32[]{:S(2)}) collective-permute-start(bf16[1024,1664]{1,0:T(8,128)(2,1)} %constant_dynamic-update-slice_fusion.6.refs_0_), channel_id=1, source_target_pairs={{0,4},{1,5},{2,6},{3,7},{4,0},{5,1},{6,2},{7,3},{8,12},{9,13},{10,... | collective-permute-start | bytes 10223624 | tf_op jit(solution)/shard_map/ppermute | solution.py:654
  666.3 29.4 %collective-permute-start.49 = (bf16[208,1664]{1,0:T(8,128)(2,1)}, bf16[208,1664]{1,0:T(8,128)(2,1)}, u32[]{:S(2)}, u32[]{:S(2)}) collective-permute-start(bf16[208,1664]{1,0:T(8,128)(2,1)} %constant_dynamic-slice_fusion.2), channel_id=1, source_target_pairs={{0,24},{1,25},{2,26},{3,27},{4,28},{5,29},{6,30},{7,31},{8,16},{9,... | collective-permute-start | bytes 2076680 | tf_op jit(solution)/shard_map/ppermute | solution.py:654
  669.1 31.1 %collective-permute-start.48 = (bf16[208,1664]{1,0:T(8,128)(2,1)}, bf16[208,1664]{1,0:T(8,128)(2,1)}, u32[]{:S(2)}, u32[]{:S(2)}) collective-permute-start(bf16[208,1664]{1,0:T(8,128)(2,1)} %constant_dynamic-slice_fusion.3), channel_id=1, source_target_pairs={{0,16},{1,17},{2,18},{3,19},{4,20},{5,21},{6,22},{7,23},{8,24},{9,... | collective-permute-start | bytes 2076680 | tf_op jit(solution)/shard_map/ppermute | solution.py:654
  672.1 28.6 %collective-permute-start.47 = (bf16[208,1664]{1,0:T(8,128)(2,1)S(1)}, bf16[208,1664]{1,0:T(8,128)(2,1)}, u32[]{:S(2)}, u32[]{:S(2)}) collective-permute-start(bf16[208,1664]{1,0:T(8,128)(2,1)S(1)} %constant_dynamic-slice_fusion.4), channel_id=1, source_target_pairs={{0,8},{1,9},{2,10},{3,11},{4,12},{5,13},{6,14},{7,15},{8,0},{9,1},... | collective-permute-start | bytes 2076680 | tf_op jit(solution)/shard_map/ppermute | solution.py:654
  682.6 54.5 %collective-permute-start.53 = (bf16[512,1664]{1,0:T(8,128)(2,1)}, bf16[512,1664]{1,0:T(8,128)(2,1)S(1)}, u32[]{:S(2)}, u32[]{:S(2)}) collective-permute-start(bf16[512,1664]{1,0:T(8,128)(2,1)} %copy-done.19), channel_id=1, source_target_pairs={{0,8},{1,9},{2,10},{3,11},{4,12},{5,13},{6,14},{7,15},{8,0},{9,1},... | collective-permute-start | bytes 5111816 | tf_op jit(solution)/shard_map/ppermute | solution.py:654
  695.6 10.0 %collective-permute-start.51 = (f32[21504]{0:T(1024)S(1)}, f32[21504]{0:T(1024)S(1)}, u32[]{:S(2)}, u32[]{:S(2)}) collective-permute-start(f32[21504]{0:T(1024)S(1)} %constant_dynamic-update-slice_fusion.23), channel_id=1, source_target_pairs={{0,4},{1,5},{2,6},{3,7},{4,0},{5,1},{6,2},{7,3},{8,12},{9,13},{10,... | collective-permute-start | bytes 258056 | tf_op jit(solution)/shard_map/ppermute | solution.py:654
  705.6 4.6 collective-permute-start.52
  705.7 46.2 %collective-permute-start.55 = (bf16[208,1664]{1,0:T(8,128)(2,1)S(1)}, bf16[208,1664]{1,0:T(8,128)(2,1)S(1)}, u32[]{:S(2)}, u32[]{:S(2)}) collective-permute-start(bf16[208,1664]{1,0:T(8,128)(2,1)S(1)} %add_convert_fusion.10), channel_id=1, source_target_pairs={{0,8},{1,9},{2,10},{3,11},{4,12},{5,13},{6,14},{7,15},{8,0},{9,1},... | collective-permute-start | bytes 2076680 | tf_op jit(solution)/shard_map/ppermute | solution.py:654
  706.7 46.2 %collective-permute-start.56 = (bf16[208,1664]{1,0:T(8,128)(2,1)S(1)}, bf16[208,1664]{1,0:T(8,128)(2,1)S(1)}, u32[]{:S(2)}, u32[]{:S(2)}) collective-permute-start(bf16[208,1664]{1,0:T(8,128)(2,1)S(1)} %add_convert_fusion.10), channel_id=1, source_target_pairs={{0,16},{1,17},{2,18},{3,19},{4,20},{5,21},{6,22},{7,23},{8,24},{9,... | collective-permute-start | bytes 2076680 | tf_op jit(solution)/shard_map/ppermute | solution.py:654
  707.7 58.7 %collective-permute-start.57 = (bf16[208,1664]{1,0:T(8,128)(2,1)S(1)}, bf16[208,1664]{1,0:T(8,128)(2,1)S(1)}, u32[]{:S(2)}, u32[]{:S(2)}) collective-permute-start(bf16[208,1664]{1,0:T(8,128)(2,1)S(1)} %add_convert_fusion.10), channel_id=1, source_target_pairs={{0,24},{1,25},{2,26},{3,27},{4,28},{5,29},{6,30},{7,31},{8,16},{9,... | collective-permute-start | bytes 2076680 | tf_op jit(solution)/shard_map/ppermute | solution.py:654
  710.2 28.2 %collective-permute-start.54 = (f32[21504]{0:T(1024)S(1)}, f32[21504]{0:T(1024)S(1)}, u32[]{:S(2)}, u32[]{:S(2)}) collective-permute-start(f32[21504]{0:T(1024)S(1)} %add.490), channel_id=1, source_target_pairs={{0,2},{1,3},{2,0},{3,1},{4,6},{5,7},{6,4},{7,5},{8,10},{9,11},{10,... | collective-permute-start | bytes 258056 | tf_op jit(solution)/shard_map/ppermute | solution.py:654
  738.4 30.1 %collective-permute-start.58 = (bf16[1024,1664]{1,0:T(8,128)(2,1)}, bf16[1024,1664]{1,0:T(8,128)(2,1)}, u32[]{:S(2)}, u32[]{:S(2)}) collective-permute-start(bf16[1024,1664]{1,0:T(8,128)(2,1)} %constant_dynamic-update-slice_fusion.12.refs_0_), channel_id=1, source_target_pairs={{0,4},{1,5},{2,6},{3,7},{4,0},{5,1},{6,2},{7,3},{8,12},{9,13},{10,... | collective-permute-start | bytes 10223624 | tf_op jit(solution)/shard_map/ppermute | solution.py:654
  767.3 19.8 %collective-permute-start.61 = (bf16[832,1664]{1,0:T(8,128)(2,1)}, bf16[832,1664]{1,0:T(8,128)(2,1)}, u32[]{:S(2)}, u32[]{:S(2)}) collective-permute-start(bf16[832,1664]{1,0:T(8,128)(2,1)} %constant_dynamic-update-slice_fusion.15.refs_0_), channel_id=1, source_target_pairs={{0,4},{1,5},{2,6},{3,7},{4,0},{5,1},{6,2},{7,3},{8,12},{9,13},{10,... | collective-permute-start | bytes 8306696 | tf_op jit(solution)/shard_map/ppermute | solution.py:654
  767.3 11.9 %collective-permute-start.59 = (f32[21504]{0:T(1024)S(1)}, f32[21504]{0:T(1024)S(1)}, u32[]{:S(2)}, u32[]{:S(2)}) collective-permute-start(f32[21504]{0:T(1024)S(1)} %add.491), channel_id=1, source_target_pairs={{0,8},{1,9},{2,10},{3,11},{4,12},{5,13},{6,14},{7,15},{8,0},{9,1},... | collective-permute-start | bytes 258056 | tf_op jit(solution)/shard_map/ppermute | solution.py:654
  779.9 15.2 %collective-permute-start.60 = (f32[21504]{0:T(1024)}, f32[21504]{0:T(1024)}, u32[]{:S(2)}, u32[]{:S(2)}) collective-permute-start(f32[21504]{0:T(1024)} %add.500), channel_id=1, source_target_pairs={{0,16},{1,17},{2,18},{3,19},{4,20},{5,21},{6,22},{7,23},{8,24},{9,... | collective-permute-start | bytes 258056 | tf_op jit(solution)/shard_map/ppermute | solution.py:654
  (53 other events, 438.9 us)
